TPU v7x, 32 devices: a whole 2x2x4 slice. The times are simulated.
32 devices in a mesh: gx: 4 (over y, core), gy: 4 (over z), gz: 2 (over x).
Axes of the slice: x: 2, y: 2, z: 4, core: 2. Of those that a mesh axis runs over, the one named last changes fastest.
Arguments:
- rhs: float32 [3, 64, 64, 256], P(None, 'gx', 'gy', 'gz'), may hold values from -24 to 24
- blocks: float32 [9, 64, 64, 256], P(None, 'gx', 'gy', 'gz'), may hold values from -1 to 14, as said below
- couplings: float32 [6, 64, 64, 256], P(None, 'gx', 'gy', 'gz'), may hold values from 0.25 to 1
- agg_ids: int32 [2, 64, 64], P('gz', 'gx', 'gy'), may hold values from 0 to 1023, as said below
- coarse_inv: float32 [36, 4, 1024], P(None, 'gx', ('gy', 'gz')), may hold values from -0.15 to 4, as said below
Outputs:
- solution: float32 [3, 64, 64, 256], P(None, 'gx', 'gy', 'gz')
Inputs may be any that keep to these rules, and one draw needn't show every extreme that they name: `agg_ids`: of the pencils of one device, at most 64 have ids in one owner's range (128 consecutive ids starting at a multiple of 128); in every x slab one such range gets exactly 64 pencils from every device of that slab. `blocks`: diagonal entries of each block lie in 8.5 to 14, off-diagonal entries in -1 to 1. `coarse_inv`: diagonal entries of each 6 x 6 matrix lie in 1 to 4, off-diagonal entries in -0.15 to 0.15.
All inputs are finite; a program needn't handle non-finite values.
Results may differ from a plain program's by a relative error of at most 0.00005.
Values sent between devices are 32-bit elements; how exact they have to be, the bound alone decides.
No kernel may reach another device: no remote copies, remote signals or barrier semaphores. Data moves between devices by JAX's collectives and lax.ppermute only.
A program may use at most 64 MiB of HBM per device.

v0:
```python
import jax
import jax.numpy as jnp
from jax import lax
from jax.sharding import PartitionSpec as P

CZ = 128
AGG_DEV = 128


damping = 0.8


def padded_2(block, sides, width):
    for axis, dim in sides:
        count = lax.axis_size(axis)
        forward = [(i, i + 1) for i in range(count - 1)]
        backward = [(target, source) for source, target in forward]
        low = lax.ppermute(
            lax.slice_in_dim(block, block.shape[dim] - width, None, axis=dim), axis, forward
        )
        high = lax.ppermute(lax.slice_in_dim(block, 0, width, axis=dim), axis, backward)
        block = jnp.concatenate([low, block, high], axis=dim)
    return block


def invert_blocks(m):
    a, b, c, d, e, f, g, h, i = [m[k] for k in range(9)]
    co_a = e * i - f * h
    co_b = f * g - d * i
    co_c = d * h - e * g
    determ = a * co_a + b * co_b + c * co_c
    rows = [
        co_a,
        c * h - b * i,
        b * f - c * e,
        co_b,
        a * i - c * g,
        c * d - a * f,
        co_c,
        b * g - a * h,
        a * e - b * d,
    ]
    return jnp.stack(rows) / determ


def block_times(m, v):
    return jnp.stack(
        [m[3 * r] * v[0] + m[3 * r + 1] * v[1] + m[3 * r + 2] * v[2] for r in range(3)]
    )


def stencil_apply(padded, field, blocks, couplings):
    beside = (
        couplings[0][None] * padded[:, :-2, 1:-1, 1:-1]
        + couplings[1][None] * padded[:, 2:, 1:-1, 1:-1]
    )
    beside = (
        beside
        + couplings[2][None] * padded[:, 1:-1, :-2, 1:-1]
        + couplings[3][None] * padded[:, 1:-1, 2:, 1:-1]
    )
    beside = (
        beside
        + couplings[4][None] * padded[:, 1:-1, 1:-1, :-2]
        + couplings[5][None] * padded[:, 1:-1, 1:-1, 2:]
    )
    return block_times(blocks, field) - beside


def mode_table(length):
    steps = jnp.arange(length).astype(jnp.float32)
    along = (steps - (length - 1) / 2.0) / (length / 2.0)
    first_mode = jnp.full((length,), length ** (-0.5), jnp.float32)
    return jnp.stack([first_mode, along * (3.0 / length) ** 0.5], axis=1)


def apply_coarse(coarse_inv, coarse_six):
    matrices = coarse_inv.reshape(6, 6, coarse_six.shape[1])
    return jnp.sum(matrices * coarse_six[None], axis=1)


def shards(rhs, blocks, couplings, agg_ids, coarse_inv):
    highest = lax.Precision.HIGHEST
    inverse = invert_blocks(blocks)

    def operate(field):
        padded = padded_2(field, (("gx", 1), ("gy", 2), ("gz", 3)), 1)
        return stencil_apply(padded, field, blocks, couplings)

    first = damping * block_times(inverse, rhs)
    second = first + damping * block_times(inverse, rhs - operate(first))
    resid = rhs - operate(second)
    modes = mode_table(CZ)
    size_x = rhs.shape[1]
    size_y = rhs.shape[2]
    count = size_x * size_y
    owners = lax.axis_size("gy") * lax.axis_size("gz")
    slot_cap = max(2, 2 * count // owners)
    aggregate = agg_ids.reshape(count)
    owner_of = aggregate // AGG_DEV
    local_id = aggregate % AGG_DEV
    member = (owner_of[:, None] == jnp.arange(owners, dtype=jnp.int32)[None, :]).astype(jnp.int32)
    before = jnp.cumsum(member, axis=0) - member
    place = jnp.sum(before * member, axis=1)
    slot = owner_of * slot_cap + place
    total_slots = owners * slot_cap
    source = jnp.zeros((total_slots,), jnp.int32).at[slot].set(jnp.arange(count, dtype=jnp.int32))
    filled = jnp.zeros((total_slots,), jnp.bool_).at[slot].set(True)
    outgoing_ids = jnp.where(filled, local_id[source], -1).reshape(owners, slot_cap)
    pencil_coarse = jnp.einsum("cxyk,km->xycm", resid, modes, precision=highest).reshape(count, 6)
    outgoing = jnp.where(filled[:, None], pencil_coarse[source], 0.0).reshape(owners, slot_cap, 6)
    arrived, arrived_ids = (
        lax.all_to_all(outgoing, ("gy", "gz"), split_axis=0, concat_axis=0, tiled=True),
        lax.all_to_all(outgoing_ids, ("gy", "gz"), split_axis=0, concat_axis=0, tiled=True),
    )
    slot_coarse = arrived.reshape(total_slots, 6)
    selector = (
        jnp.arange(AGG_DEV, dtype=jnp.int32)[:, None] == arrived_ids.reshape(total_slots)[None, :]
    ).astype(jnp.float32)
    coarse = jnp.dot(selector, slot_coarse, precision=highest, preferred_element_type=jnp.float32)
    correction = apply_coarse(coarse_inv, coarse.T)
    slot_corr = jnp.dot(
        selector.T, correction.T, precision=highest, preferred_element_type=jnp.float32
    )
    returned = lax.all_to_all(
        slot_corr.reshape(owners, slot_cap, 6),
        ("gy", "gz"),
        split_axis=0,
        concat_axis=0,
        tiled=True,
    )
    pencil_corr = returned.reshape(total_slots, 6)[slot]
    pencil_corr = pencil_corr.reshape(size_x, size_y, 3, 2)
    prolonged = jnp.einsum("xycm,km->cxyk", pencil_corr, modes, precision=highest)
    third = second + (prolonged - damping * block_times(inverse, operate(prolonged)))
    return third + damping * block_times(inverse, rhs - operate(third))


def solution(mesh):
    return jax.shard_map(
        shards,
        mesh=mesh,
        in_specs=(
            P(None, "gx", "gy", "gz"),
            P(None, "gx", "gy", "gz"),
            P(None, "gx", "gy", "gz"),
            P("gz", "gx", "gy"),
            P(None, "gx", ("gy", "gz")),
        ),
        out_specs=P(None, "gx", "gy", "gz"),
        check_vma=False,
    )
```

profile of v0, /device:TPU:0, one launch (start us, length us, event | category | flops | bytes accessed | tf_op | source)
XLA Modules:
  0.0 201.5 jit_solution(10488955296157497248)
XLA Ops:
  4.5 3.0 %collective-permute-start = (f32[3,1,16,128]{3,2,0,1:T(8,128)}, f32[3,1,16,128]{3,2,0,1:T(8,128)}, u32[]{:S(2)}, u32[]{:S(2)}) collective-permute-start(f32[3,1,16,128]{3,2,0,1:T(8,128)} %get-tuple-element.61), channel_id=1, source_target_pairs={{0,8},{8,16},{16,24},{1,9},{9,17},{17,25},{2,10},{10,18},{18,26},{... | collective-permute-start | bytes 73736 | tf_op jit(solution)/shard_map/ppermute | solution.py:18
  18.7 4.3 %collective-permute-start.2 = (f32[3,18,1,128]{3,2,0,1:T(1,128)S(1)}, f32[3,18,1,128]{3,2,0,1:T(1,128)S(1)}, u32[]{:S(2)}, u32[]{:S(2)}) collective-permute-start(f32[3,18,1,128]{3,2,0,1:T(1,128)S(1)} %get-tuple-element.53), channel_id=1, source_target_pairs={{0,2},{2,4},{4,6},{1,3},{3,5},{5,7},{8,10},{10,12},{12,14},{9,11},... | collective-permute-start | bytes 82952 | tf_op jit(solution)/shard_map/ppermute | solution.py:18
  24.5 4.2 %collective-permute-done.3 = f32[3,18,1,128]{3,2,0,1:T(1,128)S(1)} collective-permute-done((f32[3,18,1,128]{3,2,0,1:T(1,128)S(1)}, f32[3,18,1,128]{3,2,0,1:T(1,128)S(1)}, u32[]{:S(2)}, u32[]{:S(2)}) %collective-permute-start.3) | collective-permute-done | bytes 27680 | tf_op jit(solution)/shard_map/ppermute | solution.py:21
  33.6 4.0 %collective-permute-start.4 = (f32[3,18,18,1]{2,3,1,0:T(1,128)}, f32[3,18,18,1]{2,3,1,0:T(1,128)}, u32[]{:S(2)}, u32[]{:S(2)}) collective-permute-start(f32[3,18,18,1]{2,3,1,0:T(1,128)} %copy.99), channel_id=1, source_target_pairs={{0,1},{2,3},{4,5},{6,7},{8,9},{10,11},{12,13},{14,15},{16,17},{18,... | collective-permute-start | bytes 11672 | tf_op jit(solution)/shard_map/ppermute | solution.py:18
  41.6 2.2 %scatter_custom_fusion = pred[512]{0:T(512)(128)(4,1)} fusion(s32[256]{0:T(256)} %bitcast.315, pred[256]{0:T(512)(128)(4,1)S(1)} %broadcast.177, pred[]{:T(512)} %constant.48.clone.1), kind=kCustom, calls=%fused_computation.317 | custom fusion | bytes 1024 | tf_op jit(solution)/shard_map/scatter | solution.py:108
  43.8 3.5 %gather_fusion = s32[512]{0:T(512)S(1)} fusion(s32[256]{0:T(256)S(1)} %get-tuple-element.63, s32[1024]{0:T(1024)S(1)} %get-tuple-element.66), kind=kCustom, calls=%fused_computation | custom fusion | bytes 6144 | tf_op jit(solution)/shard_map/gather | solution.py:109
  55.4 2.6 %collective-permute-start.6 = (f32[3,1,16,128]{3,2,0,1:T(8,128)}, f32[3,1,16,128]{3,2,0,1:T(8,128)}, u32[]{:S(2)}, u32[]{:S(2)}) collective-permute-start(f32[3,1,16,128]{3,2,0,1:T(8,128)} %get-tuple-element.59), channel_id=1, source_target_pairs={{0,8},{8,16},{16,24},{1,9},{9,17},{17,25},{2,10},{10,18},{18,26},{... | collective-permute-start | bytes 73736 | tf_op jit(solution)/shard_map/ppermute | solution.py:18
  60.0 6.3 %all-to-all-start = ((s32[8,1,64]{2,1,0:T(1,128)}), s32[8,1,64]{2,1,0:T(1,128)S(1)}, u32[]{:S(2)}, u32[]{:S(2)}) async-start(s32[8,1,64]{2,1,0:T(1,128)} %all_to_all.12), calls=%async_computation | async-start | bytes 8192 | tf_op jit(solution)/shard_map/all_to_all | solution.py:114
  67.7 4.5 %collective-permute-start.8 = (f32[3,18,1,128]{3,2,0,1:T(1,128)}, f32[3,18,1,128]{3,2,0,1:T(1,128)}, u32[]{:S(2)}, u32[]{:S(2)}) collective-permute-start(f32[3,18,1,128]{3,2,0,1:T(1,128)} %get-tuple-element.51), channel_id=1, source_target_pairs={{0,2},{2,4},{4,6},{1,3},{3,5},{5,7},{8,10},{10,12},{12,14},{9,11},... | collective-permute-start | bytes 82952 | tf_op jit(solution)/shard_map/ppermute | solution.py:18
  74.8 3.5 %collective-permute-done.9 = f32[3,18,1,128]{3,2,0,1:T(1,128)} collective-permute-done((f32[3,18,1,128]{3,2,0,1:T(1,128)}, f32[3,18,1,128]{3,2,0,1:T(1,128)}, u32[]{:S(2)}, u32[]{:S(2)}) %collective-permute-start.9) | collective-permute-done | bytes 27680 | tf_op jit(solution)/shard_map/ppermute | solution.py:21
  82.5 4.0 %collective-permute-start.10 = (f32[3,18,18,1]{2,3,1,0:T(1,128)}, f32[3,18,18,1]{2,3,1,0:T(1,128)}, u32[]{:S(2)}, u32[]{:S(2)}) collective-permute-start(f32[3,18,18,1]{2,3,1,0:T(1,128)} %copy.104), channel_id=1, source_target_pairs={{0,1},{2,3},{4,5},{6,7},{8,9},{10,11},{12,13},{14,15},{16,17},{18,... | collective-permute-start | bytes 11672 | tf_op jit(solution)/shard_map/ppermute | solution.py:18
  96.7 4.6 %convolution_bitcast_fusion.1 = f32[16,16,3,2]{1,3,0,2:T(2,128)S(1)} fusion(f32[128,1]{0,1:T(1,128)} %add_multiply_fusion, f32[3,18,18,1]{3,2,0,1:T(8,128)} %copy.107, f32[3,18,1,128]{3,2,0,1:T(1,128)} %collective-permute-done.9, f32[3,18,1,128]{3,2,0,1:T(1,128)} %collective-permute-done.8, f32[3,1,16,128]{3,2,0,1:T(8,128)} %collective-permute-done.7, ...), kind=kOutput, calls=%fused_computation.6 | convolution fusion | flops 5603328 | bytes 2084960 | tf_op jit(solution)/shard_map/cxyk,km->xycm/dot_general | solution.py:110
  103.4 3.8 %all-to-all-start.1 = ((f32[8,1,384]{2,1,0:T(1,128)}), f32[8,1,384]{2,1,0:T(1,128)S(1)}, u32[]{:S(2)}, u32[]{:S(2)}) async-start(f32[8,1,384]{2,1,0:T(1,128)} %reshape.248), calls=%async_computation.1 | async-start | bytes 24576 | tf_op jit(solution)/shard_map/all_to_all | solution.py:113
  108.5 5.3 %all-to-all-done.1 = f32[8,1,384]{2,1,0:T(1,128)S(1)} async-done(((f32[8,1,384]{2,1,0:T(1,128)}), f32[8,1,384]{2,1,0:T(1,128)S(1)}, u32[]{:S(2)}, u32[]{:S(2)}) %all-to-all-start.1) | async-done | bytes 12320 | tf_op jit(solution)/shard_map/all_to_all | solution.py:113
  115.9 8.9 %all_to_all.19 = f32[8,1,384]{2,1,0:T(1,128)S(1)} all-to-all(f32[8,1,384]{2,1,0:T(1,128)S(1)} %reshape.250), channel_id=1, replica_groups=mesh['gx'=4,'gy'=4,'gz'=2] {'gy','gz'}, dimensions={0} | all-to-all | bytes 24576 | tf_op jit(solution)/shard_map/all_to_all | solution.py:125
  130.8 7.4 %collective-permute-done.13 = f32[3,1,16,128]{3,2,0,1:T(8,128)S(1)} collective-permute-done((f32[3,1,16,128]{3,2,0,1:T(8,128)S(1)}, f32[3,1,16,128]{3,2,0,1:T(8,128)S(1)}, u32[]{:S(2)}, u32[]{:S(2)}) %collective-permute-start.13) | collective-permute-done | bytes 24608 | tf_op jit(solution)/shard_map/ppermute | solution.py:21
  138.2 2.4 %collective-permute-start.14 = (f32[3,18,1,128]{3,2,0,1:T(1,128)S(1)}, f32[3,18,1,128]{3,2,0,1:T(1,128)S(1)}, u32[]{:S(2)}, u32[]{:S(2)}) collective-permute-start(f32[3,18,1,128]{3,2,0,1:T(1,128)S(1)} %get-tuple-element.49), channel_id=1, source_target_pairs={{0,2},{2,4},{4,6},{1,3},{3,5},{5,7},{8,10},{10,12},{12,14},{9,11},... | collective-permute-start | bytes 82952 | tf_op jit(solution)/shard_map/ppermute | solution.py:18
  142.2 4.2 %collective-permute-done.15 = f32[3,18,1,128]{3,2,0,1:T(1,128)S(1)} collective-permute-done((f32[3,18,1,128]{3,2,0,1:T(1,128)S(1)}, f32[3,18,1,128]{3,2,0,1:T(1,128)S(1)}, u32[]{:S(2)}, u32[]{:S(2)}) %collective-permute-start.15) | collective-permute-done | bytes 27680 | tf_op jit(solution)/shard_map/ppermute | solution.py:21
  150.5 3.1 %collective-permute-start.16 = (f32[3,18,18,1]{2,3,1,0:T(1,128)}, f32[3,18,18,1]{2,3,1,0:T(1,128)}, u32[]{:S(2)}, u32[]{:S(2)}) collective-permute-start(f32[3,18,18,1]{2,3,1,0:T(1,128)} %copy.118), channel_id=1, source_target_pairs={{0,1},{2,3},{4,5},{6,7},{8,9},{10,11},{12,13},{14,15},{16,17},{18,... | collective-permute-start | bytes 11672 | tf_op jit(solution)/shard_map/ppermute | solution.py:18
  170.6 3.7 %collective-permute-done.19 = f32[3,1,16,128]{3,2,0,1:T(8,128)S(1)} collective-permute-done((f32[3,1,16,128]{3,2,0,1:T(8,128)S(1)}, f32[3,1,16,128]{3,2,0,1:T(8,128)S(1)}, u32[]{:S(2)}, u32[]{:S(2)}) %collective-permute-start.19) | collective-permute-done | bytes 24608 | tf_op jit(solution)/shard_map/ppermute | solution.py:21
  174.3 2.4 %collective-permute-start.20 = (f32[3,18,1,128]{3,2,0,1:T(1,128)S(1)}, f32[3,18,1,128]{3,2,0,1:T(1,128)S(1)}, u32[]{:S(2)}, u32[]{:S(2)}) collective-permute-start(f32[3,18,1,128]{3,2,0,1:T(1,128)S(1)} %get-tuple-element.47), channel_id=1, source_target_pairs={{0,2},{2,4},{4,6},{1,3},{3,5},{5,7},{8,10},{10,12},{12,14},{9,11},... | collective-permute-start | bytes 82952 | tf_op jit(solution)/shard_map/ppermute | solution.py:18
  178.3 4.2 %collective-permute-done.21 = f32[3,18,1,128]{3,2,0,1:T(1,128)S(1)} collective-permute-done((f32[3,18,1,128]{3,2,0,1:T(1,128)S(1)}, f32[3,18,1,128]{3,2,0,1:T(1,128)S(1)}, u32[]{:S(2)}, u32[]{:S(2)}) %collective-permute-start.21) | collective-permute-done | bytes 27680 | tf_op jit(solution)/shard_map/ppermute | solution.py:21
  186.4 3.9 %collective-permute-start.22 = (f32[3,18,18,1]{2,3,1,0:T(1,128)}, f32[3,18,18,1]{2,3,1,0:T(1,128)}, u32[]{:S(2)}, u32[]{:S(2)}) collective-permute-start(f32[3,18,18,1]{2,3,1,0:T(1,128)} %copy.122), channel_id=1, source_target_pairs={{0,1},{2,3},{4,5},{6,7},{8,9},{10,11},{12,13},{14,15},{16,17},{18,... | collective-permute-start | bytes 11672 | tf_op jit(solution)/shard_map/ppermute | solution.py:18
  194.6 2.9 %collective-permute-done.23 = f32[3,18,18,1]{2,3,1,0:T(1,128)} collective-permute-done((f32[3,18,18,1]{2,3,1,0:T(1,128)}, f32[3,18,18,1]{2,3,1,0:T(1,128)}, u32[]{:S(2)}, u32[]{:S(2)}) %collective-permute-start.23) | collective-permute-done | bytes 3920 | tf_op jit(solution)/shard_map/ppermute | solution.py:21
  (223 shorter events, 102.0 us)
Async XLA Ops:
  4.5 13.4 %collective-permute-start = (f32[3,1,16,128]{3,2,0,1:T(8,128)}, f32[3,1,16,128]{3,2,0,1:T(8,128)}, u32[]{:S(2)}, u32[]{:S(2)}) collective-permute-start(f32[3,1,16,128]{3,2,0,1:T(8,128)} %get-tuple-element.61), channel_id=1, source_target_pairs={{0,8},{8,16},{16,24},{1,9},{9,17},{17,25},{2,10},{10,18},{18,26},{... | collective-permute-start | bytes 73736 | tf_op jit(solution)/shard_map/ppermute | solution.py:18
  7.5 10.4 %collective-permute-start.1 = (f32[3,1,16,128]{3,2,0,1:T(8,128)}, f32[3,1,16,128]{3,2,0,1:T(8,128)}, u32[]{:S(2)}, u32[]{:S(2)}) collective-permute-start(f32[3,1,16,128]{3,2,0,1:T(8,128)} %get-tuple-element.62), channel_id=1, source_target_pairs={{8,0},{16,8},{24,16},{9,1},{17,9},{25,17},{10,2},{18,10},{26,18},{... | collective-permute-start | bytes 73736 | tf_op jit(solution)/shard_map/ppermute | solution.py:21
  18.7 5.8 %collective-permute-start.2 = (f32[3,18,1,128]{3,2,0,1:T(1,128)S(1)}, f32[3,18,1,128]{3,2,0,1:T(1,128)S(1)}, u32[]{:S(2)}, u32[]{:S(2)}) collective-permute-start(f32[3,18,1,128]{3,2,0,1:T(1,128)S(1)} %get-tuple-element.53), channel_id=1, source_target_pairs={{0,2},{2,4},{4,6},{1,3},{3,5},{5,7},{8,10},{10,12},{12,14},{9,11},... | collective-permute-start | bytes 82952 | tf_op jit(solution)/shard_map/ppermute | solution.py:18
  23.0 5.8 %collective-permute-start.3 = (f32[3,18,1,128]{3,2,0,1:T(1,128)S(1)}, f32[3,18,1,128]{3,2,0,1:T(1,128)S(1)}, u32[]{:S(2)}, u32[]{:S(2)}) collective-permute-start(f32[3,18,1,128]{3,2,0,1:T(1,128)S(1)} %get-tuple-element.54), channel_id=1, source_target_pairs={{2,0},{4,2},{6,4},{3,1},{5,3},{7,5},{10,8},{12,10},{14,12},{11,9},... | collective-permute-start | bytes 82952 | tf_op jit(solution)/shard_map/ppermute | solution.py:21
  33.6 13.7 %collective-permute-start.4 = (f32[3,18,18,1]{2,3,1,0:T(1,128)}, f32[3,18,18,1]{2,3,1,0:T(1,128)}, u32[]{:S(2)}, u32[]{:S(2)}) collective-permute-start(f32[3,18,18,1]{2,3,1,0:T(1,128)} %copy.99), channel_id=1, source_target_pairs={{0,1},{2,3},{4,5},{6,7},{8,9},{10,11},{12,13},{14,15},{16,17},{18,... | collective-permute-start | bytes 11672 | tf_op jit(solution)/shard_map/ppermute | solution.py:18
  39.7 9.6 %collective-permute-start.5 = (f32[3,18,18,1]{2,3,1,0:T(1,128)}, f32[3,18,18,1]{2,3,1,0:T(1,128)}, u32[]{:S(2)}, u32[]{:S(2)}) collective-permute-start(f32[3,18,18,1]{2,3,1,0:T(1,128)} %copy.101), channel_id=1, source_target_pairs={{1,0},{3,2},{5,4},{7,6},{9,8},{11,10},{13,12},{15,14},{17,16},{19,... | collective-permute-start | bytes 11672 | tf_op jit(solution)/shard_map/ppermute | solution.py:21
  55.4 10.9 %collective-permute-start.6 = (f32[3,1,16,128]{3,2,0,1:T(8,128)}, f32[3,1,16,128]{3,2,0,1:T(8,128)}, u32[]{:S(2)}, u32[]{:S(2)}) collective-permute-start(f32[3,1,16,128]{3,2,0,1:T(8,128)} %get-tuple-element.59), channel_id=1, source_target_pairs={{0,8},{8,16},{16,24},{1,9},{9,17},{17,25},{2,10},{10,18},{18,26},{... | collective-permute-start | bytes 73736 | tf_op jit(solution)/shard_map/ppermute | solution.py:18
  58.0 8.3 %collective-permute-start.7 = (f32[3,1,16,128]{3,2,0,1:T(8,128)}, f32[3,1,16,128]{3,2,0,1:T(8,128)}, u32[]{:S(2)}, u32[]{:S(2)}) collective-permute-start(f32[3,1,16,128]{3,2,0,1:T(8,128)} %get-tuple-element.60), channel_id=1, source_target_pairs={{8,0},{16,8},{24,16},{9,1},{17,9},{25,17},{10,2},{18,10},{26,18},{... | collective-permute-start | bytes 73736 | tf_op jit(solution)/shard_map/ppermute | solution.py:21
  60.0 43.4 %all-to-all-start = ((s32[8,1,64]{2,1,0:T(1,128)}), s32[8,1,64]{2,1,0:T(1,128)S(1)}, u32[]{:S(2)}, u32[]{:S(2)}) async-start(s32[8,1,64]{2,1,0:T(1,128)} %all_to_all.12), calls=%async_computation | async-start | bytes 8192 | tf_op jit(solution)/shard_map/all_to_all | solution.py:114
  67.7 7.1 %collective-permute-start.8 = (f32[3,18,1,128]{3,2,0,1:T(1,128)}, f32[3,18,1,128]{3,2,0,1:T(1,128)}, u32[]{:S(2)}, u32[]{:S(2)}) collective-permute-start(f32[3,18,1,128]{3,2,0,1:T(1,128)} %get-tuple-element.51), channel_id=1, source_target_pairs={{0,2},{2,4},{4,6},{1,3},{3,5},{5,7},{8,10},{10,12},{12,14},{9,11},... | collective-permute-start | bytes 82952 | tf_op jit(solution)/shard_map/ppermute | solution.py:18
  72.2 6.1 %collective-permute-start.9 = (f32[3,18,1,128]{3,2,0,1:T(1,128)}, f32[3,18,1,128]{3,2,0,1:T(1,128)}, u32[]{:S(2)}, u32[]{:S(2)}) collective-permute-start(f32[3,18,1,128]{3,2,0,1:T(1,128)} %get-tuple-element.52), channel_id=1, source_target_pairs={{2,0},{4,2},{6,4},{3,1},{5,3},{7,5},{10,8},{12,10},{14,12},{11,9},... | collective-permute-start | bytes 82952 | tf_op jit(solution)/shard_map/ppermute | solution.py:21
  82.5 8.1 %collective-permute-start.10 = (f32[3,18,18,1]{2,3,1,0:T(1,128)}, f32[3,18,18,1]{2,3,1,0:T(1,128)}, u32[]{:S(2)}, u32[]{:S(2)}) collective-permute-start(f32[3,18,18,1]{2,3,1,0:T(1,128)} %copy.104), channel_id=1, source_target_pairs={{0,1},{2,3},{4,5},{6,7},{8,9},{10,11},{12,13},{14,15},{16,17},{18,... | collective-permute-start | bytes 11672 | tf_op jit(solution)/shard_map/ppermute | solution.py:18
  88.6 6.1 %collective-permute-start.11 = (f32[3,18,18,1]{2,3,1,0:T(1,128)}, f32[3,18,18,1]{2,3,1,0:T(1,128)}, u32[]{:S(2)}, u32[]{:S(2)}) collective-permute-start(f32[3,18,18,1]{2,3,1,0:T(1,128)} %copy.106), channel_id=1, source_target_pairs={{1,0},{3,2},{5,4},{7,6},{9,8},{11,10},{13,12},{15,14},{17,16},{19,... | collective-permute-start | bytes 11672 | tf_op jit(solution)/shard_map/ppermute | solution.py:21
  103.4 10.3 %all-to-all-start.1 = ((f32[8,1,384]{2,1,0:T(1,128)}), f32[8,1,384]{2,1,0:T(1,128)S(1)}, u32[]{:S(2)}, u32[]{:S(2)}) async-start(f32[8,1,384]{2,1,0:T(1,128)} %reshape.248), calls=%async_computation.1 | async-start | bytes 24576 | tf_op jit(solution)/shard_map/all_to_all | solution.py:113
  129.5 8.7 %collective-permute-start.13 = (f32[3,1,16,128]{3,2,0,1:T(8,128)S(1)}, f32[3,1,16,128]{3,2,0,1:T(8,128)S(1)}, u32[]{:S(2)}, u32[]{:S(2)}) collective-permute-start(f32[3,1,16,128]{3,2,0,1:T(8,128)S(1)} %get-tuple-element.58), channel_id=1, source_target_pairs={{8,0},{16,8},{24,16},{9,1},{17,9},{25,17},{10,2},{18,10},{26,18},{... | collective-permute-start | bytes 73736 | tf_op jit(solution)/shard_map/ppermute | solution.py:21
  138.2 3.9 %collective-permute-start.14 = (f32[3,18,1,128]{3,2,0,1:T(1,128)S(1)}, f32[3,18,1,128]{3,2,0,1:T(1,128)S(1)}, u32[]{:S(2)}, u32[]{:S(2)}) collective-permute-start(f32[3,18,1,128]{3,2,0,1:T(1,128)S(1)} %get-tuple-element.49), channel_id=1, source_target_pairs={{0,2},{2,4},{4,6},{1,3},{3,5},{5,7},{8,10},{10,12},{12,14},{9,11},... | collective-permute-start | bytes 82952 | tf_op jit(solution)/shard_map/ppermute | solution.py:18
  140.6 5.8 %collective-permute-start.15 = (f32[3,18,1,128]{3,2,0,1:T(1,128)S(1)}, f32[3,18,1,128]{3,2,0,1:T(1,128)S(1)}, u32[]{:S(2)}, u32[]{:S(2)}) collective-permute-start(f32[3,18,1,128]{3,2,0,1:T(1,128)S(1)} %get-tuple-element.50), channel_id=1, source_target_pairs={{2,0},{4,2},{6,4},{3,1},{5,3},{7,5},{10,8},{12,10},{14,12},{11,9},... | collective-permute-start | bytes 82952 | tf_op jit(solution)/shard_map/ppermute | solution.py:21
  150.5 7.3 %collective-permute-start.16 = (f32[3,18,18,1]{2,3,1,0:T(1,128)}, f32[3,18,18,1]{2,3,1,0:T(1,128)}, u32[]{:S(2)}, u32[]{:S(2)}) collective-permute-start(f32[3,18,18,1]{2,3,1,0:T(1,128)} %copy.118), channel_id=1, source_target_pairs={{0,1},{2,3},{4,5},{6,7},{8,9},{10,11},{12,13},{14,15},{16,17},{18,... | collective-permute-start | bytes 11672 | tf_op jit(solution)/shard_map/ppermute | solution.py:18
  155.7 6.2 %collective-permute-start.17 = (f32[3,18,18,1]{2,3,1,0:T(1,128)}, f32[3,18,18,1]{2,3,1,0:T(1,128)}, u32[]{:S(2)}, u32[]{:S(2)}) collective-permute-start(f32[3,18,18,1]{2,3,1,0:T(1,128)} %copy.120), channel_id=1, source_target_pairs={{1,0},{3,2},{5,4},{7,6},{9,8},{11,10},{13,12},{15,14},{17,16},{19,... | collective-permute-start | bytes 11672 | tf_op jit(solution)/shard_map/ppermute | solution.py:21
  169.3 5.0 %collective-permute-start.19 = (f32[3,1,16,128]{3,2,0,1:T(8,128)S(1)}, f32[3,1,16,128]{3,2,0,1:T(8,128)S(1)}, u32[]{:S(2)}, u32[]{:S(2)}) collective-permute-start(f32[3,1,16,128]{3,2,0,1:T(8,128)S(1)} %get-tuple-element.56), channel_id=1, source_target_pairs={{8,0},{16,8},{24,16},{9,1},{17,9},{25,17},{10,2},{18,10},{26,18},{... | collective-permute-start | bytes 73736 | tf_op jit(solution)/shard_map/ppermute | solution.py:21
  174.3 3.9 %collective-permute-start.20 = (f32[3,18,1,128]{3,2,0,1:T(1,128)S(1)}, f32[3,18,1,128]{3,2,0,1:T(1,128)S(1)}, u32[]{:S(2)}, u32[]{:S(2)}) collective-permute-start(f32[3,18,1,128]{3,2,0,1:T(1,128)S(1)} %get-tuple-element.47), channel_id=1, source_target_pairs={{0,2},{2,4},{4,6},{1,3},{3,5},{5,7},{8,10},{10,12},{12,14},{9,11},... | collective-permute-start | bytes 82952 | tf_op jit(solution)/shard_map/ppermute | solution.py:18
  176.7 5.8 %collective-permute-start.21 = (f32[3,18,1,128]{3,2,0,1:T(1,128)S(1)}, f32[3,18,1,128]{3,2,0,1:T(1,128)S(1)}, u32[]{:S(2)}, u32[]{:S(2)}) collective-permute-start(f32[3,18,1,128]{3,2,0,1:T(1,128)S(1)} %get-tuple-element.48), channel_id=1, source_target_pairs={{2,0},{4,2},{6,4},{3,1},{5,3},{7,5},{10,8},{12,10},{14,12},{11,9},... | collective-permute-start | bytes 82952 | tf_op jit(solution)/shard_map/ppermute | solution.py:21
  186.4 7.0 %collective-permute-start.22 = (f32[3,18,18,1]{2,3,1,0:T(1,128)}, f32[3,18,18,1]{2,3,1,0:T(1,128)}, u32[]{:S(2)}, u32[]{:S(2)}) collective-permute-start(f32[3,18,18,1]{2,3,1,0:T(1,128)} %copy.122), channel_id=1, source_target_pairs={{0,1},{2,3},{4,5},{6,7},{8,9},{10,11},{12,13},{14,15},{16,17},{18,... | collective-permute-start | bytes 11672 | tf_op jit(solution)/shard_map/ppermute | solution.py:18
  191.3 6.2 %collective-permute-start.23 = (f32[3,18,18,1]{2,3,1,0:T(1,128)}, f32[3,18,18,1]{2,3,1,0:T(1,128)}, u32[]{:S(2)}, u32[]{:S(2)}) collective-permute-start(f32[3,18,18,1]{2,3,1,0:T(1,128)} %copy.124), channel_id=1, source_target_pairs={{1,0},{3,2},{5,4},{7,6},{9,8},{11,10},{13,12},{15,14},{17,16},{19,... | collective-permute-start | bytes 11672 | tf_op jit(solution)/shard_map/ppermute | solution.py:21
  (43 other events, 455.4 us)
where the time goes:
time: 204 us; the launch traced here: 202 us
  starting transfers between devices  62.8 us (31%)
  local copies, waits for them, and re-layouts  59.6 us (29%)
  waiting for transfers between devices  40 us (20%)
  other arithmetic  22.7 us (11%)
  blocking collectives  8.92 us (4%)
  matrix products  6.67 us (3%)
    ppermute x12, starting transfers between devices, padded_2(): lax.ppermute(lax.slice_in_dim(block, block.shape[dim] - width, None, axis...  37.4 us
    ppermute x12, waiting for transfers between devices, padded_2(): lax.ppermute(lax.slice_in_dim(block, 0, width, axis=dim), axis, backward)  34.1 us
    ppermute x12, starting transfers between devices, padded_2(): lax.ppermute(lax.slice_in_dim(block, 0, width, axis=dim), axis, backward)  15.4 us
    slice x12, local copies, waits for them, and re-layouts, padded_2(): lax.slice_in_dim(block, block.shape[dim] - width, None, axis=dim)  14.6 us
    all_to_all x1, blocking collectives, shards(): lax.all_to_all(slot_corr.reshape(owners, slot_cap, 6), ('gy', 'gz'), spli...  8.92 us
    ppermute x4, local copies, waits for them, and re-layouts, padded_2(): lax.ppermute(lax.slice_in_dim(block, block.shape[dim] - width, None, axis...  7.33 us
    ppermute x4, local copies, waits for them, and re-layouts, padded_2(): lax.ppermute(lax.slice_in_dim(block, 0, width, axis=dim), axis, backward)  7.31 us
    slice x4, local copies, waits for them, and re-layouts, padded_2(): lax.slice_in_dim(block, 0, width, axis=dim)  7.29 us
  transfers between devices with their start and end apart: 26, of which 13 were waited for; matrix products, arithmetic and copies ran while one was open for 25% of the time, Pallas kernels for 0%

commit v1 on v0

v1 whole, which is shorter than its diff:
```python
import functools

import jax
import jax.numpy as jnp
from jax import lax
from jax.experimental import pallas as pl
from jax.experimental.pallas import tpu as pltpu
from jax.sharding import PartitionSpec as P

DAMPING = 0.8
HIGHEST = lax.Precision.HIGHEST
AXES = ("gx", "gy", "gz")


def dot_tt(a, b):
    return lax.dot_general(
        a, b, (((1,), (1,)), ((), ())), precision=HIGHEST, preferred_element_type=jnp.float32
    )


def dot_00(a, b):
    return lax.dot_general(
        a, b, (((0,), (0,)), ((), ())), precision=HIGHEST, preferred_element_type=jnp.float32
    )


def lane_iota(rows, lanes):
    return lax.broadcasted_iota(jnp.int32, (rows, lanes), 1)


def row_iota(rows, lanes):
    return lax.broadcasted_iota(jnp.int32, (rows, lanes), 0)


def mode_rows(rows, length):
    k = lane_iota(rows, length).astype(jnp.float32)
    m1 = (k - (length - 1) / 2.0) / (length / 2.0) * (3.0 / length) ** 0.5
    m0 = jnp.full((rows, length), length ** (-0.5), jnp.float32)
    return m0, m1


def is_even(axis):
    return lax.rem(lax.axis_index(axis), 2) == 0


def damped_inverse(m):
    a, b, c, d, e, f, g, h, i = m
    co_a = e * i - f * h
    co_b = f * g - d * i
    co_c = d * h - e * g
    determ = a * co_a + b * co_b + c * co_c
    scale = DAMPING / determ
    rows = [
        co_a,
        c * h - b * i,
        b * f - c * e,
        co_b,
        a * i - c * g,
        c * d - a * f,
        co_c,
        b * g - a * h,
        a * e - b * d,
    ]
    return [r * scale for r in rows]


def times(m, v):
    return [m[3 * r] * v[0] + m[3 * r + 1] * v[1] + m[3 * r + 2] * v[2] for r in range(3)]


class Dims:
    def __init__(self, nx, ny, nz):
        self.nx, self.ny, self.nz = nx, ny, nz
        self.rows = nx * ny


def put_faces(dims, field, sends):
    xe, xo, ye, yo, ze, zo = sends
    nx, ny, nz = dims.nx, dims.ny, dims.nz
    even_x, even_y, even_z = [is_even(a) for a in AXES]
    x_e = jnp.where(even_x, nx - 1, 0)
    x_o = (nx - 1) - x_e
    y_e = jnp.where(even_y, ny - 1, 0)
    y_o = (ny - 1) - y_e
    z_e = jnp.where(even_z, nz - 1, 0)
    z_o = (nz - 1) - z_e
    row = row_iota(8, nz)
    lane = lane_iota(8, nz)
    pick = jnp.where(
        ((row == 0) & (lane == z_e)) | ((row == 1) & (lane == z_o)), 1.0, 0.0
    ).astype(jnp.float32)
    for c in range(3):
        for ref, x in ((xe, x_e), (xo, x_o)):
            ref[c] = field[c, pl.ds(pl.multiple_of(x * ny, ny), ny), :]
        for ref, y in ((ye, y_e), (yo, y_o)):
            ref[c] = field[c, pl.ds(y, nx, stride=ny), :]
        z = dot_tt(pick, field[c])
        ze[c : c + 1, :] = z[0:1]
        zo[c : c + 1, :] = z[1:2]


class Halo:
    def __init__(self, dims, recv):
        xe, xo, ye, yo, ze, zo = recv
        self.dims = dims
        self.even = [is_even(a) for a in AXES]
        self.x, self.y = (xe, xo), (ye, yo)
        nz = dims.nz
        even_z = self.even[2]
        row = row_iota(8, nz)
        lane = lane_iota(8, nz)
        place = jnp.where(
            ((row == 0) & (lane == nz - 1)) | ((row == 1) & (lane == 0)), 1.0, 0.0
        ).astype(jnp.float32)
        low = jnp.where(even_z, zo[...], ze[...])
        high = jnp.where(even_z, ze[...], zo[...])
        row = row_iota(8, dims.rows)
        self.z = []
        for c in range(3):
            pair = jnp.where(row == 0, low[c : c + 1], jnp.where(row == 1, high[c : c + 1], 0.0))
            self.z.append(dot_00(pair, place))

    def x_face(self, c, high):
        e, o = self.x[0][c], self.x[1][c]
        return jnp.where(self.even[0], e, o) if high else jnp.where(self.even[0], o, e)

    def y_row(self, c, x, high):
        e, o = self.y[0][c, x : x + 1, :], self.y[1][c, x : x + 1, :]
        return jnp.where(self.even[1], e, o) if high else jnp.where(self.even[1], o, e)

    def z_tile(self, c, x):
        ny = self.dims.ny
        return self.z[c][x * ny : (x + 1) * ny]


def apply_tile(dims, x, center, x_low, x_high, y_tile, z_tile, blocks, coup):
    ny, nz = dims.ny, dims.nz
    row = row_iota(ny, nz)
    lane = lane_iota(ny, nz)
    own = times(blocks, center)
    out = []
    for c in range(3):
        v = center[c]
        beside = coup[0] * x_low[c] + coup[1] * x_high[c]
        y_minus = pltpu.roll(jnp.where(row == ny - 1, y_tile[c][0], v), 1, 0)
        y_plus = pltpu.roll(jnp.where(row == 0, y_tile[c][1], v), ny - 1, 0)
        beside = beside + coup[2] * y_minus + coup[3] * y_plus
        z_minus = pltpu.roll(jnp.where(lane == nz - 1, z_tile[c], v), 1, 1)
        z_plus = pltpu.roll(jnp.where(lane == 0, z_tile[c], v), nz - 1, 1)
        beside = beside + coup[4] * z_minus + coup[5] * z_plus
        out.append(own[c] - beside)
    return out


def tile(dims, ref, c, x):
    return ref[c, x * dims.ny : (x + 1) * dims.ny, :]


def tiles(dims, ref, count, x):
    return [tile(dims, ref, c, x) for c in range(count)]


def apply_at(dims, x, field, halo, blocks, coup):
    center = tiles(dims, field, 3, x)
    x_low = tiles(dims, field, 3, x - 1) if x > 0 else [halo.x_face(c, False) for c in range(3)]
    x_high = (
        tiles(dims, field, 3, x + 1)
        if x < dims.nx - 1
        else [halo.x_face(c, True) for c in range(3)]
    )
    y_tile = [(halo.y_row(c, x, False), halo.y_row(c, x, True)) for c in range(3)]
    z_tile = [halo.z_tile(c, x) for c in range(3)]
    return center, apply_tile(dims, x, center, x_low, x_high, y_tile, z_tile, blocks, coup)


def first_kernel(dims, rhs, blocks, first, inverse, *sends):
    for x in range(dims.nx):
        inv = damped_inverse(tiles(dims, blocks, 9, x))
        rows = slice(x * dims.ny, (x + 1) * dims.ny)
        for k in range(9):
            inverse[k, rows, :] = inv[k]
        v = times(inv, tiles(dims, rhs, 3, x))
        for c in range(3):
            first[c, rows, :] = v[c]
    put_faces(dims, first, sends)


def smooth(dims, rhs, blocks, couplings, inverse, field, recv, out):
    halo = Halo(dims, recv)
    for x in range(dims.nx):
        center, applied = apply_at(
            dims, x, field, halo, tiles(dims, blocks, 9, x), tiles(dims, couplings, 6, x)
        )
        left = tiles(dims, rhs, 3, x)
        step = times(tiles(dims, inverse, 9, x), [left[c] - applied[c] for c in range(3)])
        rows = slice(x * dims.ny, (x + 1) * dims.ny)
        for c in range(3):
            out[c, rows, :] = center[c] + step[c]


def second_kernel(dims, rhs, blocks, couplings, inverse, first, *refs):
    recv, (second, *sends) = refs[:6], refs[6:]
    smooth(dims, rhs, blocks, couplings, inverse, first, recv, second)
    put_faces(dims, second, sends)


def last_kernel(dims, rhs, blocks, couplings, inverse, third, *refs):
    recv, out = refs[:6], refs[6]
    smooth(dims, rhs, blocks, couplings, inverse, third, recv, out)


def coarse_kernel(dims, rhs, blocks, couplings, second, ids, coarse_inv, *refs):
    recv, packet, resid = refs[:6], refs[6], refs[7]
    halo = Halo(dims, recv)
    for x in range(dims.nx):
        _, applied = apply_at(
            dims, x, second, halo, tiles(dims, blocks, 9, x), tiles(dims, couplings, 6, x)
        )
        left = tiles(dims, rhs, 3, x)
        rows = slice(x * dims.ny, (x + 1) * dims.ny)
        for c in range(3):
            resid[c, rows, :] = left[c] - applied[c]
    m0, m1 = mode_rows(8, dims.nz)
    row = row_iota(8, dims.nz)
    modes = jnp.where(row == 0, m0, jnp.where(row == 1, m1, 0.0))
    for c in range(3):
        packet[0, 2 * c : 2 * c + 2, :] = dot_tt(modes, resid[c])[0:2]
    packet[0, 6:7, :] = ids[...].astype(jnp.float32)
    packet[0, 7:8, :] = jnp.zeros((1, dims.rows), jnp.float32)
    half = coarse_inv.shape[0] // 2
    own = coarse_inv.shape[1]
    packet[0, 8 : 8 + half, 0:own] = coarse_inv[0:half]
    packet[0, 8 : 8 + half, own : 2 * own] = coarse_inv[half : 2 * half]


def split3(v):
    high = v.astype(jnp.bfloat16)
    rest = v - high.astype(jnp.float32)
    mid = rest.astype(jnp.bfloat16)
    low = (rest - mid.astype(jnp.float32)).astype(jnp.bfloat16)
    return jnp.concatenate([high, mid, low], axis=0)


def gray(j):
    return lax.bitwise_xor(j, lax.shift_right_logical(j, 1))


def gray_inverse(v, bits):
    out = v
    for b in range(1, bits):
        out = lax.bitwise_xor(out, lax.shift_right_logical(v, b))
    return out


def bits_of(n):
    return max(1, (n - 1).bit_length())


def solve_kernel(dims, sizes, own, packets, own_out, y_out, z_out, coarse, correction):
    n_y, n_z = sizes
    owners = n_y * n_z
    rows = dims.rows
    my_y, my_z = lax.axis_index("gy"), lax.axis_index("gz")
    half = 18

    def owner_at(j):
        jz = lax.rem(j, n_z)
        jy = lax.div(j, n_z)
        return lax.bitwise_xor(my_y, gray(jy)) * n_z + lax.bitwise_xor(my_z, gray(jz))

    def member(j, ids):
        base = (owner_at(j) * own).astype(jnp.float32)
        agg = row_iota(own, rows).astype(jnp.float32) + base
        return jnp.where(agg == ids, 1.0, 0.0).astype(jnp.bfloat16)

    coarse[...] = jnp.zeros_like(coarse)

    def add(d, carry):
        pack = packets[d, 0:8, :]
        ids = pack[6:7]
        parts = split3(jnp.where(row_iota(8, rows) < 6, pack, 0.0))

        def one(j, carry):
            s = lax.dot_general(
                parts,
                member(j, ids),
                (((1,), (1,)), ((), ())),
                preferred_element_type=jnp.float32,
            )
            coarse[j] = coarse[j] + (s[0:8] + (s[8:16] + s[16:24]))
            return carry

        return lax.fori_loop(0, owners, one, carry, unroll=8)

    lax.fori_loop(0, owners, add, 0)

    def correct(j, carry):
        v = coarse[j]
        out = []
        for i in range(6):
            total = None
            for k in range(6):
                at = 6 * i + k
                r, side = 8 + at % half, at // half
                term = packets[j, r : r + 1, side * own : (side + 1) * own] * v[k : k + 1]
                total = term if total is None else total + term
            out.append(total)
        out += [jnp.zeros((2, own), jnp.float32)]
        correction[j] = split3(jnp.concatenate(out, axis=0))
        return carry

    lax.fori_loop(0, owners, correct, 0)

    def gather(y, z):
        inside = (y >= 0) & (y < n_y) & (z >= 0) & (z < n_z)
        y = jnp.clip(y, 0, n_y - 1)
        z = jnp.clip(z, 0, n_z - 1)
        jy = gray_inverse(lax.bitwise_xor(my_y, y), bits_of(n_y))
        jz = gray_inverse(lax.bitwise_xor(my_z, z), bits_of(n_z))
        ids = packets[jy * n_z + jz, 6:7, :]

        def one(j, total):
            return total + lax.dot_general(
                correction[j],
                member(j, ids),
                (((1,), (0,)), ((), ())),
                preferred_element_type=jnp.float32,
            )

        s = lax.fori_loop(0, owners, one, jnp.zeros((24, rows), jnp.float32), unroll=8)
        return jnp.where(inside, s[0:8] + (s[8:16] + s[16:24]), 0.0)

    own_out[...] = gather(my_y, my_z)
    place = lax.rem(lane_iota(8, rows), dims.ny)
    low, high = gather(my_y - 1, my_z), gather(my_y + 1, my_z)
    y_out[...] = jnp.where(place == dims.ny - 1, low, jnp.where(place == 0, high, 0.0))
    z_out[0] = gather(my_y, my_z - 1)
    z_out[1] = gather(my_y, my_z + 1)


def third_kernel(dims, blocks, couplings, inverse, second, own, y_mix, z_mix, xe, xo, *refs):
    third, sends, (field, y_field, z_field) = refs[0], refs[1:7], refs[7:]
    nx, ny, nz, rows = dims.nx, dims.ny, dims.nz, dims.rows
    m0, m1 = mode_rows(8, nz)
    row = row_iota(8, nz)
    lane = lane_iota(8, nz)
    last = jnp.where(lane == nz - 1, 1.0, 0.0)
    start = jnp.where(lane == 0, 1.0, 0.0)
    zero = jnp.zeros((8, nz), jnp.float32)
    even_x = is_even("gx")
    x_low = jnp.where(even_x, xo[...], xe[...])
    x_high = jnp.where(even_x, xe[...], xo[...])
    x_field = []
    row_r = row_iota(8, rows)
    for c in range(3):
        modes = jnp.where(row == 2 * c, m0, jnp.where(row == 2 * c + 1, m1, zero))
        field[c] = dot_00(own[...], modes)
        y_field[c] = dot_00(y_mix[...], modes)
        z_field[c] = dot_00(z_mix[0], modes * last) + dot_00(z_mix[1], modes * start)
        x_field.append(
            (dot_00(x_low, modes)[rows - ny : rows], dot_00(x_high, modes)[0:ny])
        )
    for x in range(nx):
        center = tiles(dims, field, 3, x)
        low = tiles(dims, field, 3, x - 1) if x > 0 else [x_field[c][0] for c in range(3)]
        high = tiles(dims, field, 3, x + 1) if x < nx - 1 else [x_field[c][1] for c in range(3)]
        y_tile = [(tile(dims, y_field, c, x),) * 2 for c in range(3)]
        z_tile = tiles(dims, z_field, 3, x)
        applied = apply_tile(
            dims,
            x,
            center,
            low,
            high,
            y_tile,
            z_tile,
            tiles(dims, blocks, 9, x),
            tiles(dims, couplings, 6, x),
        )
        step = times(tiles(dims, inverse, 9, x), applied)
        at = slice(x * ny, (x + 1) * ny)
        for c in range(3):
            third[c, at, :] = second[c, at, :] + (center[c] - step[c])
    put_faces(dims, third, sends)


def pairs(count, start):
    out = []
    for i in range(start, count - 1, 2):
        out += [(i, i + 1), (i + 1, i)]
    return out


def swap(value, axis, start):
    count = lax.axis_size(axis)
    which = pairs(count, start)
    return lax.ppermute(value, axis, which) if which else jnp.zeros_like(value)


def exchange(sends):
    xe, xo, ye, yo, ze, zo = sends
    ze, zo = swap(ze, "gz", 0), swap(zo, "gz", 1)
    yo, ye = swap(yo, "gy", 1), swap(ye, "gy", 0)
    xo, xe = swap(xo, "gx", 1), swap(xe, "gx", 0)
    return xe, xo, ye, yo, ze, zo


def gather_slab(packet):
    for axis in ("gz", "gy"):
        count = lax.axis_size(axis)
        mask = 1
        while mask < count:
            which = [(i, i ^ mask) for i in range(count)]
            packet = jnp.concatenate([packet, lax.ppermute(packet, axis, which)], axis=0)
            mask = 2 * mask + 1
    return packet


def call(body, name, out_shapes, scratch, *args):
    return pl.pallas_call(
        body,
        name=name,
        out_shape=[jax.ShapeDtypeStruct(s, jnp.float32) for s in out_shapes],
        in_specs=[pl.BlockSpec(memory_space=pltpu.VMEM)] * len(args),
        out_specs=[pl.BlockSpec(memory_space=pltpu.VMEM)] * len(out_shapes),
        scratch_shapes=scratch,
        compiler_params=pltpu.CompilerParams(vmem_limit_bytes=24 * 1024 * 1024),
    )(*args)


def shards(rhs, blocks, couplings, agg_ids, coarse_inv):
    _, nx, ny, nz = rhs.shape
    dims = Dims(nx, ny, nz)
    rows = nx * ny
    rhs = rhs.reshape(3, rows, nz)
    blocks = blocks.reshape(9, rows, nz)
    couplings = couplings.reshape(6, rows, nz)
    ids = agg_ids.reshape(1, rows)
    own = coarse_inv.shape[2]
    coarse_inv = coarse_inv.reshape(36, own)
    n_y, n_z = lax.axis_size("gy"), lax.axis_size("gz")
    owners = n_y * n_z
    vector = (3, rows, nz)
    faces = [(3, ny, nz)] * 2 + [(3, nx, nz)] * 2 + [(8, rows)] * 2
    part = functools.partial

    first, inverse, *sends = call(
        part(first_kernel, dims), "first", [vector, (9, rows, nz)] + faces, [], rhs, blocks
    )
    recv = exchange(sends)
    second, *sends = call(
        part(second_kernel, dims),
        "second",
        [vector] + faces,
        [],
        rhs,
        blocks,
        couplings,
        inverse,
        first,
        *recv,
    )
    recv = exchange(sends)
    (packet,) = call(
        part(coarse_kernel, dims),
        "coarse",
        [(1, 8 + 18, rows)],
        [pltpu.VMEM(vector, jnp.float32)],
        rhs,
        blocks,
        couplings,
        second,
        ids,
        coarse_inv,
        *recv,
    )
    packets = gather_slab(packet)
    corr, y_mix, z_mix = call(
        part(solve_kernel, dims, (n_y, n_z), own),
        "solve",
        [(8, rows), (8, rows), (2, 8, rows)],
        [
            pltpu.VMEM((owners, 8, own), jnp.float32),
            pltpu.VMEM((owners, 24, own), jnp.bfloat16),
        ],
        packets,
    )
    xo, xe = swap(corr, "gx", 1), swap(corr, "gx", 0)
    third, *sends = call(
        part(third_kernel, dims),
        "third",
        [vector] + faces,
        [pltpu.VMEM(vector, jnp.float32)] * 3,
        blocks,
        couplings,
        inverse,
        second,
        corr,
        y_mix,
        z_mix,
        xe,
        xo,
    )
    recv = exchange(sends)
    (out,) = call(
        part(last_kernel, dims),
        "last",
        [vector],
        [],
        rhs,
        blocks,
        couplings,
        inverse,
        third,
        *recv,
    )
    return out.reshape(3, nx, ny, nz)


def solution(mesh):
    return jax.shard_map(
        shards,
        mesh=mesh,
        in_specs=(
            P(None, "gx", "gy", "gz"),
            P(None, "gx", "gy", "gz"),
            P(None, "gx", "gy", "gz"),
            P("gz", "gx", "gy"),
            P(None, "gx", ("gy", "gz")),
        ),
        out_specs=P(None, "gx", "gy", "gz"),
        check_vma=False,
    )
```

time: 204 us -> 70.2 us (0.34)
  the two profiles are of different devices: /device:TPU:0 before, /device:TPU:12 now
where the time goes in v1:
time: 70.2 us; the launch traced here: 69.6 us
  starting transfers between devices  30.9 us (44%)
  waiting for transfers between devices  17.4 us (25%)
  Pallas kernels  13.8 us (20%)
  local copies, waits for them, and re-layouts  7.36 us (10%)
    ppermute x17, starting transfers between devices, swap(): return lax.ppermute(value, axis, which) if which else jnp.zeros_like(value)  25.6 us
    pallas_call x6, Pallas kernels, call(): pl.pallas_call(body, name=name, out_shape=[jax.ShapeDtypeStruct(s, jnp.fl...  13.8 us
    ppermute x3, waiting for transfers between devices, gather_slab(): lax.ppermute(packet, axis, which)  9.91 us
    ppermute x17, waiting for transfers between devices, swap(): return lax.ppermute(value, axis, which) if which else jnp.zeros_like(value)  7.5 us
    unnamed x21, local copies, waits for them, and re-layouts  6.01 us
    ppermute x3, starting transfers between devices, gather_slab(): lax.ppermute(packet, axis, which)  5.26 us
  transfers between devices with their start and end apart: 20, of which 8 were waited for; matrix products, arithmetic and copies ran while one was open for 3% of the time, Pallas kernels for 0%

profile of v1, /device:TPU:12, one launch (start us, length us, event | category | flops | bytes accessed | tf_op | source)
XLA Modules:
  0.0 69.6 jit_solution(11216466342916997725)
XLA Ops:
  2.3 1.3 %first.1 = (f32[3,256,128]{2,1,0:T(8,128)S(1)}, f32[9,256,128]{2,1,0:T(8,128)S(1)}, f32[3,16,128]{2,1,0:T(8,128)S(1)}, f32[3,16,128]{2,1,0:T(8,128)S(1)}, f32[3,...) custom-call(f32[3,256,128]{2,1,0:T(8,128)S(1)} %bitcast.16, ...), custom_call_target="tpu_custom_call" | custom-call | tf_op jit(solution)/shard_map/first/pallas_call | solution.py:420
  3.6 2.5 %collective-permute-start.1 = (f32[3,16,128]{2,1,0:T(8,128)S(1)}, f32[3,16,128]{2,1,0:T(8,128)S(1)}, u32[]{:S(2)}, u32[]{:S(2)}) collective-permute-start(f32[3,16,128]{2,1,0:T(8,128)S(1)} %get-tuple-element.30), channel_id=1, source_target_pairs={{8,16},{16,8},{9,17},{17,9},{10,18},{18,10},{11,19},{19,11},{12,20... | collective-permute-start | bytes 73736 | tf_op jit(solution)/shard_map/ppermute | solution.py:397
  6.2 5.0 %collective-permute-start.3 = (f32[3,16,128]{2,1,0:T(8,128)S(1)}, f32[3,16,128]{2,1,0:T(8,128)S(1)}, u32[]{:S(2)}, u32[]{:S(2)}) collective-permute-start(f32[3,16,128]{2,1,0:T(8,128)S(1)} %get-tuple-element.32), channel_id=1, source_target_pairs={{2,4},{4,2},{3,5},{5,3},{10,12},{12,10},{11,13},{13,11},{18,20},{2... | collective-permute-start | bytes 73736 | tf_op jit(solution)/shard_map/ppermute | solution.py:397
  11.2 1.6 %collective-permute-start.4 = (f32[8,256]{1,0:T(8,128)S(1)}, f32[8,256]{1,0:T(8,128)S(1)}, u32[]{:S(2)}, u32[]{:S(2)}) collective-permute-start(f32[8,256]{1,0:T(8,128)S(1)} %get-tuple-element.33), channel_id=1, source_target_pairs={{0,1},{1,0},{2,3},{3,2},{4,5},{5,4},{6,7},{7,6},{8,9},{9,8},{10,11... | collective-permute-start | bytes 24584 | tf_op jit(solution)/shard_map/ppermute | solution.py:397
  12.8 2.2 %collective-permute-done.4.refs_4_ = f32[8,256]{1,0:T(8,128)S(1)} collective-permute-done((f32[8,256]{1,0:T(8,128)S(1)}, f32[8,256]{1,0:T(8,128)S(1)}, u32[]{:S(2)}, u32[]{:S(2)}) %collective-permute-start.4) | collective-permute-done | bytes 8224 | tf_op jit(solution)/shard_map/ppermute | solution.py:397
  15.0 2.1 %second.1 = (f32[3,256,128]{2,1,0:T(8,128)S(1)}, f32[3,16,128]{2,1,0:T(8,128)}, f32[3,16,128]{2,1,0:T(8,128)}, f32[3,16,128]{2,1,0:T(8,128)}, f32[3,16,128]{2,1,...) custom-call(f32[3,256,128]{2,1,0:T(8,128)S(1)} %bitcast.17, f32[9,256,128]{2,1,0:T(8,128)S(1)} %bitcast.8, ...), custom_call_target="tpu_custom_call" | custom-call | tf_op jit(solution)/shard_map/second/pallas_call | solution.py:420
  17.9 1.9 %collective-permute-start.6 = (f32[3,16,128]{2,1,0:T(8,128)}, f32[3,16,128]{2,1,0:T(8,128)}, u32[]{:S(2)}, u32[]{:S(2)}) collective-permute-start(f32[3,16,128]{2,1,0:T(8,128)} %get-tuple-element.36), channel_id=1, source_target_pairs={{8,16},{16,8},{9,17},{17,9},{10,18},{18,10},{11,19},{19,11},{12,20... | collective-permute-start | bytes 73736 | tf_op jit(solution)/shard_map/ppermute | solution.py:397
  19.9 1.9 %collective-permute-start.8 = (f32[3,16,128]{2,1,0:T(8,128)}, f32[3,16,128]{2,1,0:T(8,128)}, u32[]{:S(2)}, u32[]{:S(2)}) collective-permute-start(f32[3,16,128]{2,1,0:T(8,128)} %get-tuple-element.38), channel_id=1, source_target_pairs={{2,4},{4,2},{3,5},{5,3},{10,12},{12,10},{11,13},{13,11},{18,20},{2... | collective-permute-start | bytes 73736 | tf_op jit(solution)/shard_map/ppermute | solution.py:397
  21.8 1.6 %collective-permute-start.9 = (f32[8,256]{1,0:T(8,128)}, f32[8,256]{1,0:T(8,128)S(1)}, u32[]{:S(2)}, u32[]{:S(2)}) collective-permute-start(f32[8,256]{1,0:T(8,128)} %get-tuple-element.39), channel_id=1, source_target_pairs={{0,1},{1,0},{2,3},{3,2},{4,5},{5,4},{6,7},{7,6},{8,9},{9,8},{10,11... | collective-permute-start | bytes 24584 | tf_op jit(solution)/shard_map/ppermute | solution.py:397
  24.0 1.3 %reshape.21.ids = s32[1,256]{1,0:T(1,128)} reshape(s32[1,16,16]{2,1,0:T(8,128)} %param.8) | data formatting | bytes 2048 | tf_op jit(solution)/shard_map/reshape | solution.py:438
  28.3 2.1 %coarse.1 = f32[1,26,256]{2,1,0:T(8,128)S(1)} custom-call(f32[3,256,128]{2,1,0:T(8,128)S(1)} %bitcast.18, f32[9,256,128]{2,1,0:T(8,128)S(1)} %bitcast.9, f32[6,256,128]{2,1,0:T(8,128)S(1)} %bitcast.13, f32[3,256,128]{2,1,0:T(8,128)S(1)} %copy-done.6, s32[1,256]{1,0:T(1,128)S(1)} %copy-done.8, f32[36,128]{1,0:T(8,128)S(1)} %bitcast.20, ...), custom_call_target="tpu_custom_call" | custom-call | tf_op jit(solution)/shard_map/coarse/pallas_call | solution.py:420
  30.4 1.5 %collective-permute-start.10 = (f32[1,26,256]{2,1,0:T(8,128)S(1)}, f32[1,26,256]{2,1,0:T(8,128)S(1)}, u32[]{:S(2)}, u32[]{:S(2)}) collective-permute-start(f32[1,26,256]{2,1,0:T(8,128)S(1)} %coarse.1), channel_id=1, source_target_pairs={{0,1},{1,0},{2,3},{3,2},{4,5},{5,4},{6,7},{7,6},{8,9},{9,8},{10,11... | collective-permute-start | bytes 79880 | tf_op jit(solution)/shard_map/ppermute | solution.py:414
  31.9 2.4 %collective-permute-done.10 = f32[1,26,256]{2,1,0:T(8,128)S(1)} collective-permute-done((f32[1,26,256]{2,1,0:T(8,128)S(1)}, f32[1,26,256]{2,1,0:T(8,128)S(1)}, u32[]{:S(2)}, u32[]{:S(2)}) %collective-permute-start.10) | collective-permute-done | bytes 26656 | tf_op jit(solution)/shard_map/ppermute | solution.py:414
  35.5 3.1 %collective-permute-done.11 = f32[2,26,256]{2,1,0:T(8,128)S(1)} collective-permute-done((f32[2,26,256]{2,1,0:T(8,128)S(1)}, f32[2,26,256]{2,1,0:T(8,128)S(1)}, u32[]{:S(2)}, u32[]{:S(2)}) %collective-permute-start.11) | collective-permute-done | bytes 53280 | tf_op jit(solution)/shard_map/ppermute | solution.py:414
  38.6 2.6 %collective-permute-start.12 = (f32[4,26,256]{2,1,0:T(8,128)S(1)}, f32[4,26,256]{2,1,0:T(8,128)S(1)}, u32[]{:S(2)}, u32[]{:S(2)}) collective-permute-start(f32[4,26,256]{2,1,0:T(8,128)S(1)} %pad_maximum_fusion.1), channel_id=1, source_target_pairs={{0,6},{2,4},{4,2},{6,0},{1,7},{3,5},{5,3},{7,1},{8,14},{10,12},{12... | collective-permute-start | bytes 319496 | tf_op jit(solution)/shard_map/ppermute | solution.py:414
  41.2 4.4 %collective-permute-done.12 = f32[4,26,256]{2,1,0:T(8,128)S(1)} collective-permute-done((f32[4,26,256]{2,1,0:T(8,128)S(1)}, f32[4,26,256]{2,1,0:T(8,128)S(1)}, u32[]{:S(2)}, u32[]{:S(2)}) %collective-permute-start.12) | collective-permute-done | bytes 106528 | tf_op jit(solution)/shard_map/ppermute | solution.py:414
  45.6 3.1 %solve.1 = (f32[8,256]{1,0:T(8,128)S(1)}, f32[8,256]{1,0:T(8,128)S(1)}, f32[2,8,256]{2,1,0:T(8,128)S(1)}) custom-call(f32[8,26,256]{2,1,0:T(8,128)S(1)} %pad_maximum_fusion.packets), custom_call_target="tpu_custom_call" | custom-call | tf_op jit(solution)/shard_map/solve/pallas_call | solution.py:420
  48.7 3.3 %collective-permute-start.14 = (f32[8,256]{1,0:T(8,128)S(1)}, f32[8,256]{1,0:T(8,128)S(1)}, u32[]{:S(2)}, u32[]{:S(2)}) collective-permute-start(f32[8,256]{1,0:T(8,128)S(1)} %get-tuple-element.40.own), channel_id=1, source_target_pairs={{8,16},{16,8},{9,17},{17,9},{10,18},{18,10},{11,19},{19,11},{12,20... | collective-permute-start | bytes 24584 | tf_op jit(solution)/shard_map/ppermute | solution.py:397
  52.0 1.7 %collective-permute-done.14.xo = f32[8,256]{1,0:T(8,128)S(1)} collective-permute-done((f32[8,256]{1,0:T(8,128)S(1)}, f32[8,256]{1,0:T(8,128)S(1)}, u32[]{:S(2)}, u32[]{:S(2)}) %collective-permute-start.14) | collective-permute-done | bytes 8224 | tf_op jit(solution)/shard_map/ppermute | solution.py:397
  53.7 3.5 %third.1 = (f32[3,256,128]{2,1,0:T(8,128)S(1)}, f32[3,16,128]{2,1,0:T(8,128)S(1)}, f32[3,16,128]{2,1,0:T(8,128)S(1)}, f32[3,16,128]{2,1,0:T(8,128)S(1)}, f32[3,1...) custom-call(f32[9,256,128]{2,1,0:T(8,128)S(1)} %bitcast.10, f32[6,256,128]{2,1,0:T(8,128)S(1)} %bitcast.14, ...), custom_call_target="tpu_custom_call" | custom-call | tf_op jit(solution)/shard_map/third/pallas_call | solution.py:420
  57.2 3.3 %collective-permute-start.16 = (f32[3,16,128]{2,1,0:T(8,128)S(1)}, f32[3,16,128]{2,1,0:T(8,128)S(1)}, u32[]{:S(2)}, u32[]{:S(2)}) collective-permute-start(f32[3,16,128]{2,1,0:T(8,128)S(1)} %get-tuple-element.45), channel_id=1, source_target_pairs={{8,16},{16,8},{9,17},{17,9},{10,18},{18,10},{11,19},{19,11},{12,20... | collective-permute-start | bytes 73736 | tf_op jit(solution)/shard_map/ppermute | solution.py:397
  60.6 3.6 %collective-permute-start.18 = (f32[3,16,128]{2,1,0:T(8,128)S(1)}, f32[3,16,128]{2,1,0:T(8,128)S(1)}, u32[]{:S(2)}, u32[]{:S(2)}) collective-permute-start(f32[3,16,128]{2,1,0:T(8,128)S(1)} %get-tuple-element.47), channel_id=1, source_target_pairs={{2,4},{4,2},{3,5},{5,3},{10,12},{12,10},{11,13},{13,11},{18,20},{2... | collective-permute-start | bytes 73736 | tf_op jit(solution)/shard_map/ppermute | solution.py:397
  64.9 3.1 %collective-permute-done.19.refs_4_ = f32[8,256]{1,0:T(8,128)S(1)} collective-permute-done((f32[8,256]{1,0:T(8,128)S(1)}, f32[8,256]{1,0:T(8,128)S(1)}, u32[]{:S(2)}, u32[]{:S(2)}) %collective-permute-start.19) | collective-permute-done | bytes 8224 | tf_op jit(solution)/shard_map/ppermute | solution.py:397
  67.9 1.7 %last.1 = f32[3,256,128]{2,1,0:T(8,128)} custom-call(f32[3,256,128]{2,1,0:T(8,128)S(1)} %bitcast.19, f32[9,256,128]{2,1,0:T(8,128)S(1)} %bitcast.11, f32[6,256,128]{2,1,0:T(8,128)S(1)} %bitcast.15, f32[9,256,128]{2,1,0:T(8,128)S(1)} %get-tuple-element.27.inverse, f32[3,256,128]{2,1,0:T(8,128)S(1)} %get-tuple-element.43.third, ...), custom_call_target="tpu_custom_call" | custom-call | tf_op jit(solution)/shard_map/last/pallas_call | solution.py:420
  (48 shorter events, 8.7 us)
Async XLA Ops:
  2.3 12.7 %copy-start.2 = (f32[6,16,16,128]{3,2,1,0:T(8,128)S(1)}, f32[6,16,16,128]{3,2,1,0:T(8,128)}, u32[]{:S(2)}) copy-start(f32[6,16,16,128]{3,2,1,0:T(8,128)} %param.7) | copy-start | bytes 2359300
  3.6 11.4 %collective-permute-start = (f32[3,16,128]{2,1,0:T(8,128)S(1)}, f32[3,16,128]{2,1,0:T(8,128)S(1)}, u32[]{:S(2)}, u32[]{:S(2)}) collective-permute-start(f32[3,16,128]{2,1,0:T(8,128)S(1)} %get-tuple-element.29), channel_id=1, source_target_pairs={{0,8},{8,0},{16,24},{24,16},{1,9},{9,1},{17,25},{25,17},{2,10},{10... | collective-permute-start | bytes 73736 | tf_op jit(solution)/shard_map/ppermute | solution.py:397
  3.6 11.4 %collective-permute-start.1 = (f32[3,16,128]{2,1,0:T(8,128)S(1)}, f32[3,16,128]{2,1,0:T(8,128)S(1)}, u32[]{:S(2)}, u32[]{:S(2)}) collective-permute-start(f32[3,16,128]{2,1,0:T(8,128)S(1)} %get-tuple-element.30), channel_id=1, source_target_pairs={{8,16},{16,8},{9,17},{17,9},{10,18},{18,10},{11,19},{19,11},{12,20... | collective-permute-start | bytes 73736 | tf_op jit(solution)/shard_map/ppermute | solution.py:397
  6.1 8.8 %collective-permute-start.2 = (f32[3,16,128]{2,1,0:T(8,128)S(1)}, f32[3,16,128]{2,1,0:T(8,128)S(1)}, u32[]{:S(2)}, u32[]{:S(2)}) collective-permute-start(f32[3,16,128]{2,1,0:T(8,128)S(1)} %get-tuple-element.31), channel_id=1, source_target_pairs={{0,2},{2,0},{4,6},{6,4},{1,3},{3,1},{5,7},{7,5},{8,10},{10,8},{12,... | collective-permute-start | bytes 73736 | tf_op jit(solution)/shard_map/ppermute | solution.py:397
  6.2 8.8 %collective-permute-start.3 = (f32[3,16,128]{2,1,0:T(8,128)S(1)}, f32[3,16,128]{2,1,0:T(8,128)S(1)}, u32[]{:S(2)}, u32[]{:S(2)}) collective-permute-start(f32[3,16,128]{2,1,0:T(8,128)S(1)} %get-tuple-element.32), channel_id=1, source_target_pairs={{2,4},{4,2},{3,5},{5,3},{10,12},{12,10},{11,13},{13,11},{18,20},{2... | collective-permute-start | bytes 73736 | tf_op jit(solution)/shard_map/ppermute | solution.py:397
  11.2 3.7 %collective-permute-start.4 = (f32[8,256]{1,0:T(8,128)S(1)}, f32[8,256]{1,0:T(8,128)S(1)}, u32[]{:S(2)}, u32[]{:S(2)}) collective-permute-start(f32[8,256]{1,0:T(8,128)S(1)} %get-tuple-element.33), channel_id=1, source_target_pairs={{0,1},{1,0},{2,3},{3,2},{4,5},{5,4},{6,7},{7,6},{8,9},{9,8},{10,11... | collective-permute-start | bytes 24584 | tf_op jit(solution)/shard_map/ppermute | solution.py:397
  15.0 8.4 %copy-start.9 = (f32[36,1,128]{2,1,0:T(1,128)S(1)}, f32[36,1,128]{2,1,0:T(1,128)}, u32[]{:S(2)}) copy-start(f32[36,1,128]{2,1,0:T(1,128)} %param.9) | copy-start | bytes 55300
  15.0 11.0 %copy-start.1 = (f32[9,16,16,128]{3,2,1,0:T(8,128)S(1)}, f32[9,16,16,128]{3,2,1,0:T(8,128)}, u32[]{:S(2)}) copy-start(f32[9,16,16,128]{3,2,1,0:T(8,128)} %param.6) | copy-start | bytes 3538948
  15.0 10.9 %copy-start.4 = (f32[3,16,16,128]{3,2,1,0:T(8,128)S(1)}, f32[3,16,16,128]{3,2,1,0:T(8,128)}, u32[]{:S(2)}) copy-start(f32[3,16,16,128]{3,2,1,0:T(8,128)} %param.5) | copy-start | bytes 1179652
  17.9 7.9 %collective-permute-start.5 = (f32[3,16,128]{2,1,0:T(8,128)}, f32[3,16,128]{2,1,0:T(8,128)}, u32[]{:S(2)}, u32[]{:S(2)}) collective-permute-start(f32[3,16,128]{2,1,0:T(8,128)} %get-tuple-element.35), channel_id=1, source_target_pairs={{0,8},{8,0},{16,24},{24,16},{1,9},{9,1},{17,25},{25,17},{2,10},{10... | collective-permute-start | bytes 73736 | tf_op jit(solution)/shard_map/ppermute | solution.py:397
  17.9 7.9 %collective-permute-start.6 = (f32[3,16,128]{2,1,0:T(8,128)}, f32[3,16,128]{2,1,0:T(8,128)}, u32[]{:S(2)}, u32[]{:S(2)}) collective-permute-start(f32[3,16,128]{2,1,0:T(8,128)} %get-tuple-element.36), channel_id=1, source_target_pairs={{8,16},{16,8},{9,17},{17,9},{10,18},{18,10},{11,19},{19,11},{12,20... | collective-permute-start | bytes 73736 | tf_op jit(solution)/shard_map/ppermute | solution.py:397
  19.8 6.0 %collective-permute-start.7 = (f32[3,16,128]{2,1,0:T(8,128)}, f32[3,16,128]{2,1,0:T(8,128)}, u32[]{:S(2)}, u32[]{:S(2)}) collective-permute-start(f32[3,16,128]{2,1,0:T(8,128)} %get-tuple-element.37), channel_id=1, source_target_pairs={{0,2},{2,0},{4,6},{6,4},{1,3},{3,1},{5,7},{7,5},{8,10},{10,8},{12,... | collective-permute-start | bytes 73736 | tf_op jit(solution)/shard_map/ppermute | solution.py:397
  19.9 6.0 %collective-permute-start.8 = (f32[3,16,128]{2,1,0:T(8,128)}, f32[3,16,128]{2,1,0:T(8,128)}, u32[]{:S(2)}, u32[]{:S(2)}) collective-permute-start(f32[3,16,128]{2,1,0:T(8,128)} %get-tuple-element.38), channel_id=1, source_target_pairs={{2,4},{4,2},{3,5},{5,3},{10,12},{12,10},{11,13},{13,11},{18,20},{2... | collective-permute-start | bytes 73736 | tf_op jit(solution)/shard_map/ppermute | solution.py:397
  21.8 3.9 %collective-permute-start.9 = (f32[8,256]{1,0:T(8,128)}, f32[8,256]{1,0:T(8,128)S(1)}, u32[]{:S(2)}, u32[]{:S(2)}) collective-permute-start(f32[8,256]{1,0:T(8,128)} %get-tuple-element.39), channel_id=1, source_target_pairs={{0,1},{1,0},{2,3},{3,2},{4,5},{5,4},{6,7},{7,6},{8,9},{9,8},{10,11... | collective-permute-start | bytes 24584 | tf_op jit(solution)/shard_map/ppermute | solution.py:397
  30.4 3.9 %collective-permute-start.10 = (f32[1,26,256]{2,1,0:T(8,128)S(1)}, f32[1,26,256]{2,1,0:T(8,128)S(1)}, u32[]{:S(2)}, u32[]{:S(2)}) collective-permute-start(f32[1,26,256]{2,1,0:T(8,128)S(1)} %coarse.1), channel_id=1, source_target_pairs={{0,1},{1,0},{2,3},{3,2},{4,5},{5,4},{6,7},{7,6},{8,9},{9,8},{10,11... | collective-permute-start | bytes 79880 | tf_op jit(solution)/shard_map/ppermute | solution.py:414
  34.3 4.3 %collective-permute-start.11 = (f32[2,26,256]{2,1,0:T(8,128)S(1)}, f32[2,26,256]{2,1,0:T(8,128)S(1)}, u32[]{:S(2)}, u32[]{:S(2)}) collective-permute-start(f32[2,26,256]{2,1,0:T(8,128)S(1)} %pad_maximum_fusion.2), channel_id=1, source_target_pairs={{0,2},{2,0},{4,6},{6,4},{1,3},{3,1},{5,7},{7,5},{8,10},{10,8},{12,... | collective-permute-start | bytes 159752 | tf_op jit(solution)/shard_map/ppermute | solution.py:414
  38.6 7.0 %collective-permute-start.12 = (f32[4,26,256]{2,1,0:T(8,128)S(1)}, f32[4,26,256]{2,1,0:T(8,128)S(1)}, u32[]{:S(2)}, u32[]{:S(2)}) collective-permute-start(f32[4,26,256]{2,1,0:T(8,128)S(1)} %pad_maximum_fusion.1), channel_id=1, source_target_pairs={{0,6},{2,4},{4,2},{6,0},{1,7},{3,5},{5,3},{7,1},{8,14},{10,12},{12... | collective-permute-start | bytes 319496 | tf_op jit(solution)/shard_map/ppermute | solution.py:414
  48.7 3.3 %collective-permute-start.13 = (f32[8,256]{1,0:T(8,128)S(1)}, f32[8,256]{1,0:T(8,128)S(1)}, u32[]{:S(2)}, u32[]{:S(2)}) collective-permute-start(f32[8,256]{1,0:T(8,128)S(1)} %get-tuple-element.40.own), channel_id=1, source_target_pairs={{0,8},{8,0},{16,24},{24,16},{1,9},{9,1},{17,25},{25,17},{2,10},{10... | collective-permute-start | bytes 24584 | tf_op jit(solution)/shard_map/ppermute | solution.py:397
  48.7 5.0 %collective-permute-start.14 = (f32[8,256]{1,0:T(8,128)S(1)}, f32[8,256]{1,0:T(8,128)S(1)}, u32[]{:S(2)}, u32[]{:S(2)}) collective-permute-start(f32[8,256]{1,0:T(8,128)S(1)} %get-tuple-element.40.own), channel_id=1, source_target_pairs={{8,16},{16,8},{9,17},{17,9},{10,18},{18,10},{11,19},{19,11},{12,20... | collective-permute-start | bytes 24584 | tf_op jit(solution)/shard_map/ppermute | solution.py:397
  57.2 10.7 %collective-permute-start.15 = (f32[3,16,128]{2,1,0:T(8,128)S(1)}, f32[3,16,128]{2,1,0:T(8,128)S(1)}, u32[]{:S(2)}, u32[]{:S(2)}) collective-permute-start(f32[3,16,128]{2,1,0:T(8,128)S(1)} %get-tuple-element.44), channel_id=1, source_target_pairs={{0,8},{8,0},{16,24},{24,16},{1,9},{9,1},{17,25},{25,17},{2,10},{10... | collective-permute-start | bytes 73736 | tf_op jit(solution)/shard_map/ppermute | solution.py:397
  57.2 10.7 %collective-permute-start.16 = (f32[3,16,128]{2,1,0:T(8,128)S(1)}, f32[3,16,128]{2,1,0:T(8,128)S(1)}, u32[]{:S(2)}, u32[]{:S(2)}) collective-permute-start(f32[3,16,128]{2,1,0:T(8,128)S(1)} %get-tuple-element.45), channel_id=1, source_target_pairs={{8,16},{16,8},{9,17},{17,9},{10,18},{18,10},{11,19},{19,11},{12,20... | collective-permute-start | bytes 73736 | tf_op jit(solution)/shard_map/ppermute | solution.py:397
  60.5 7.5 %collective-permute-start.17 = (f32[3,16,128]{2,1,0:T(8,128)S(1)}, f32[3,16,128]{2,1,0:T(8,128)S(1)}, u32[]{:S(2)}, u32[]{:S(2)}) collective-permute-start(f32[3,16,128]{2,1,0:T(8,128)S(1)} %get-tuple-element.46), channel_id=1, source_target_pairs={{0,2},{2,0},{4,6},{6,4},{1,3},{3,1},{5,7},{7,5},{8,10},{10,8},{12,... | collective-permute-start | bytes 73736 | tf_op jit(solution)/shard_map/ppermute | solution.py:397
  60.6 7.3 %collective-permute-start.18 = (f32[3,16,128]{2,1,0:T(8,128)S(1)}, f32[3,16,128]{2,1,0:T(8,128)S(1)}, u32[]{:S(2)}, u32[]{:S(2)}) collective-permute-start(f32[3,16,128]{2,1,0:T(8,128)S(1)} %get-tuple-element.47), channel_id=1, source_target_pairs={{2,4},{4,2},{3,5},{5,3},{10,12},{12,10},{11,13},{13,11},{18,20},{2... | collective-permute-start | bytes 73736 | tf_op jit(solution)/shard_map/ppermute | solution.py:397
  64.2 3.7 %collective-permute-start.19 = (f32[8,256]{1,0:T(8,128)S(1)}, f32[8,256]{1,0:T(8,128)S(1)}, u32[]{:S(2)}, u32[]{:S(2)}) collective-permute-start(f32[8,256]{1,0:T(8,128)S(1)} %get-tuple-element.48), channel_id=1, source_target_pairs={{0,1},{1,0},{2,3},{3,2},{4,5},{5,4},{6,7},{7,6},{8,9},{9,8},{10,11... | collective-permute-start | bytes 24584 | tf_op jit(solution)/shard_map/ppermute | solution.py:397
  (6 other events, 5.4 us)

commit v2 on v1

--- a/solution.py
+++ b/solution.py
@@ -8,20 +8,46 @@
 from jax.sharding import PartitionSpec as P
 
 DAMPING = 0.8
-HIGHEST = lax.Precision.HIGHEST
 AXES = ("gx", "gy", "gz")
+VMEM_LIMIT = 12 * 1024 * 1024
 
 
 def dot_tt(a, b):
     return lax.dot_general(
-        a, b, (((1,), (1,)), ((), ())), precision=HIGHEST, preferred_element_type=jnp.float32
+        a, b, (((1,), (1,)), ((), ())), preferred_element_type=jnp.float32
     )
 
 
 def dot_00(a, b):
     return lax.dot_general(
-        a, b, (((0,), (0,)), ((), ())), precision=HIGHEST, preferred_element_type=jnp.float32
-    )
+        a, b, (((0,), (0,)), ((), ())), preferred_element_type=jnp.float32
+    )
+
+
+def parts3(v):
+    high = v.astype(jnp.bfloat16)
+    rest = v - high.astype(jnp.float32)
+    mid = rest.astype(jnp.bfloat16)
+    low = (rest - mid.astype(jnp.float32)).astype(jnp.bfloat16)
+    return high, mid, low
+
+
+def split3(v):
+    return jnp.concatenate(parts3(v), axis=0)
+
+
+def pairs6(v):
+    high, mid, low = parts3(v)
+    return jnp.concatenate([high, high, high, mid, mid, low], axis=0)
+
+
+def pairs6_right(v):
+    high, mid, low = parts3(v)
+    return jnp.concatenate([high, mid, low, high, mid, high], axis=0)
+
+
+def triple(v):
+    return jnp.concatenate([v, v, v], axis=0)
 
 
 def lane_iota(rows, lanes):
@@ -89,12 +115,13 @@
     pick = jnp.where(
         ((row == 0) & (lane == z_e)) | ((row == 1) & (lane == z_o)), 1.0, 0.0
     ).astype(jnp.float32)
+    pick = pick.astype(jnp.bfloat16)
     for c in range(3):
         for ref, x in ((xe, x_e), (xo, x_o)):
             ref[c] = field[c, pl.ds(pl.multiple_of(x * ny, ny), ny), :]
         for ref, y in ((ye, y_e), (yo, y_o)):
             ref[c] = field[c, pl.ds(y, nx, stride=ny), :]
-        z = dot_tt(pick, field[c])
+        z = sum(dot_tt(pick, part) for part in parts3(field[c]))
         ze[c : c + 1, :] = z[0:1]
         zo[c : c + 1, :] = z[1:2]
 
@@ -107,18 +134,17 @@
         self.x, self.y = (xe, xo), (ye, yo)
         nz = dims.nz
         even_z = self.even[2]
-        row = row_iota(8, nz)
-        lane = lane_iota(8, nz)
-        place = jnp.where(
-            ((row == 0) & (lane == nz - 1)) | ((row == 1) & (lane == 0)), 1.0, 0.0
-        ).astype(jnp.float32)
         low = jnp.where(even_z, zo[...], ze[...])
         high = jnp.where(even_z, ze[...], zo[...])
         row = row_iota(8, dims.rows)
-        self.z = []
-        for c in range(3):
-            pair = jnp.where(row == 0, low[c : c + 1], jnp.where(row == 1, high[c : c + 1], 0.0))
-            self.z.append(dot_00(pair, place))
+        both = jnp.where(row < 3, low, jnp.where(row < 6, pltpu.roll(high, 3, 0), 0.0))
+        row = row_iota(8, nz)
+        lane = lane_iota(8, nz)
+        place = [
+            ((row == c) & (lane == nz - 1)) | ((row == 3 + c) & (lane == 0)) for c in range(3)
+        ]
+        place = jnp.where(jnp.concatenate(place, axis=1), 1.0, 0.0)
+        self.z = dot_00(split3(both), triple(place).astype(jnp.bfloat16))
 
     def x_face(self, c, high):
         e, o = self.x[0][c], self.x[1][c]
@@ -129,8 +155,8 @@
         return jnp.where(self.even[1], e, o) if high else jnp.where(self.even[1], o, e)
 
     def z_tile(self, c, x):
-        ny = self.dims.ny
-        return self.z[c][x * ny : (x + 1) * ny]
+        ny, nz = self.dims.ny, self.dims.nz
+        return self.z[x * ny : (x + 1) * ny, c * nz : (c + 1) * nz]
 
 
 def apply_tile(dims, x, center, x_low, x_high, y_tile, z_tile, blocks, coup):
@@ -209,7 +235,7 @@
     smooth(dims, rhs, blocks, couplings, inverse, third, recv, out)
 
 
-def coarse_kernel(dims, rhs, blocks, couplings, second, ids, coarse_inv, *refs):
+def coarse_kernel(dims, rhs, blocks, couplings, second, ids, *refs):
     recv, packet, resid = refs[:6], refs[6], refs[7]
     halo = Halo(dims, recv)
     for x in range(dims.nx):
@@ -222,23 +248,28 @@
             resid[c, rows, :] = left[c] - applied[c]
     m0, m1 = mode_rows(8, dims.nz)
     row = row_iota(8, dims.nz)
-    modes = jnp.where(row == 0, m0, jnp.where(row == 1, m1, 0.0))
+    modes = split3(jnp.where(row == 0, m0, jnp.where(row == 1, m1, 0.0)))
     for c in range(3):
-        packet[0, 2 * c : 2 * c + 2, :] = dot_tt(modes, resid[c])[0:2]
-    packet[0, 6:7, :] = ids[...].astype(jnp.float32)
+        s = sum(dot_tt(modes, part) for part in parts3(resid[c]))
+        packet[0, 2 * c : 2 * c + 2, :] = (s[0:8] + (s[8:16] + s[16:24]))[0:2]
+    packet[0, 6:7, :] = pencil_row(dims, ids[0].astype(jnp.float32))
     packet[0, 7:8, :] = jnp.zeros((1, dims.rows), jnp.float32)
-    half = coarse_inv.shape[0] // 2
-    own = coarse_inv.shape[1]
-    packet[0, 8 : 8 + half, 0:own] = coarse_inv[0:half]
-    packet[0, 8 : 8 + half, own : 2 * own] = coarse_inv[half : 2 * half]
-
-
-def split3(v):
-    high = v.astype(jnp.bfloat16)
-    rest = v - high.astype(jnp.float32)
-    mid = rest.astype(jnp.bfloat16)
-    low = (rest - mid.astype(jnp.float32)).astype(jnp.bfloat16)
-    return jnp.concatenate([high, mid, low], axis=0)
+
+
+def pencil_row(dims, square):
+    nx, ny, rows = dims.nx, dims.ny, dims.rows
+    lane = lane_iota(ny, rows)
+    spread = jnp.where(lax.rem(lane, ny) == row_iota(ny, rows), 1.0, 0.0)
+    wide = lax.dot_general(
+        square,
+        spread,
+        (((1,), (0,)), ((), ())),
+        precision=lax.Precision.HIGHEST,
+        preferred_element_type=jnp.float32,
+    )
+    lane = lane_iota(nx, rows)
+    keep = lax.div(lane, ny) == row_iota(nx, rows)
+    return jnp.sum(jnp.where(keep, wide, 0.0), axis=0, keepdims=True)
 
 
 def gray(j):
@@ -256,12 +287,14 @@
     return max(1, (n - 1).bit_length())
 
 
-def solve_kernel(dims, sizes, own, packets, own_out, y_out, z_out, coarse, correction):
+def solve_kernel(dims, sizes, own, packets, inverses, own_out, y_out, z_out, coarse, correction):
     n_y, n_z = sizes
     owners = n_y * n_z
     rows = dims.rows
     my_y, my_z = lax.axis_index("gy"), lax.axis_index("gz")
-    half = 18
+    local = row_iota(own, rows).astype(jnp.bfloat16)
+    one_b = jnp.ones((own, rows), jnp.bfloat16)
+    zero_b = jnp.zeros((own, rows), jnp.bfloat16)
 
     def owner_at(j):
         jz = lax.rem(j, n_z)
@@ -270,102 +303,108 @@
 
     def member(j, ids):
         base = (owner_at(j) * own).astype(jnp.float32)
-        agg = row_iota(own, rows).astype(jnp.float32) + base
-        return jnp.where(agg == ids, 1.0, 0.0).astype(jnp.bfloat16)
+        rel = jnp.clip(ids - base, -1.0, float(own)).astype(jnp.bfloat16)
+        return jnp.where(local == rel, one_b, zero_b)
 
     coarse[...] = jnp.zeros_like(coarse)
 
     def add(d, carry):
-        pack = packets[d, 0:8, :]
+        pack = packets[d]
         ids = pack[6:7]
         parts = split3(jnp.where(row_iota(8, rows) < 6, pack, 0.0))
-
-        def one(j, carry):
-            s = lax.dot_general(
-                parts,
-                member(j, ids),
-                (((1,), (1,)), ((), ())),
-                preferred_element_type=jnp.float32,
-            )
-            coarse[j] = coarse[j] + (s[0:8] + (s[8:16] + s[16:24]))
-            return carry
-
-        return lax.fori_loop(0, owners, one, carry, unroll=8)
-
-    lax.fori_loop(0, owners, add, 0)
-
-    def correct(j, carry):
-        v = coarse[j]
-        out = []
+        for j in range(owners):
+            s = dot_tt(parts, member(j, ids))
+            coarse[8 * j : 8 * j + 8] = coarse[8 * j : 8 * j + 8] + (s[0:8] + (s[8:16] + s[16:24]))
+        return carry
+
+    lax.fori_loop(0, owners, add, 0, unroll=2)
+
+    for block in range(owners // 8):
+        v = [coarse[pl.ds(64 * block + k, 8, stride=8), :] for k in range(6)]
         for i in range(6):
             total = None
             for k in range(6):
-                at = 6 * i + k
-                r, side = 8 + at % half, at // half
-                term = packets[j, r : r + 1, side * own : (side + 1) * own] * v[k : k + 1]
-                total = term if total is None else total + term
-            out.append(total)
-        out += [jnp.zeros((2, own), jnp.float32)]
-        correction[j] = split3(jnp.concatenate(out, axis=0))
-        return carry
-
-    lax.fori_loop(0, owners, correct, 0)
-
-    def gather(y, z):
+                m = inverses[pl.ds(36 * 8 * block + 6 * i + k, 8, stride=36), :]
+                total = m * v[k] if total is None else total + m * v[k]
+            correction[pl.ds(64 * block + i, 8, stride=8), :] = total
+        for i in (6, 7):
+            correction[pl.ds(64 * block + i, 8, stride=8), :] = jnp.zeros_like(total)
+
+    def ids_of(y, z):
         inside = (y >= 0) & (y < n_y) & (z >= 0) & (z < n_z)
         y = jnp.clip(y, 0, n_y - 1)
         z = jnp.clip(z, 0, n_z - 1)
         jy = gray_inverse(lax.bitwise_xor(my_y, y), bits_of(n_y))
         jz = gray_inverse(lax.bitwise_xor(my_z, z), bits_of(n_z))
-        ids = packets[jy * n_z + jz, 6:7, :]
-
-        def one(j, total):
-            return total + lax.dot_general(
-                correction[j],
-                member(j, ids),
+        return jnp.where(inside, packets[jy * n_z + jz, 6:7, :], -1.0)
+
+    place = lax.rem(lane_iota(1, rows), dims.ny)
+    low, high = ids_of(my_y - 1, my_z), ids_of(my_y + 1, my_z)
+    wanted = [
+        ids_of(my_y, my_z),
+        jnp.where(place == dims.ny - 1, low, jnp.where(place == 0, high, -1.0)),
+        ids_of(my_y, my_z - 1),
+        ids_of(my_y, my_z + 1),
+    ]
+    if n_z == 2:
+        wanted = wanted[:2] + [ids_of(my_y, 1 - my_z)]
+    totals = [jnp.zeros((24, rows), jnp.float32) for _ in wanted]
+    for j in range(owners):
+        left = split3(correction[8 * j : 8 * j + 8])
+        for t in range(len(wanted)):
+            totals[t] = totals[t] + lax.dot_general(
+                left,
+                member(j, wanted[t]),
                 (((1,), (0,)), ((), ())),
                 preferred_element_type=jnp.float32,
             )
-
-        s = lax.fori_loop(0, owners, one, jnp.zeros((24, rows), jnp.float32), unroll=8)
-        return jnp.where(inside, s[0:8] + (s[8:16] + s[16:24]), 0.0)
-
-    own_out[...] = gather(my_y, my_z)
-    place = lax.rem(lane_iota(8, rows), dims.ny)
-    low, high = gather(my_y - 1, my_z), gather(my_y + 1, my_z)
-    y_out[...] = jnp.where(place == dims.ny - 1, low, jnp.where(place == 0, high, 0.0))
-    z_out[0] = gather(my_y, my_z - 1)
-    z_out[1] = gather(my_y, my_z + 1)
+    totals = [s[0:8] + (s[8:16] + s[16:24]) for s in totals]
+    own_out[...] = totals[0]
+    y_out[...] = totals[1]
+    if n_z == 2:
+        z_out[0] = jnp.where(my_z == 1, totals[2], 0.0)
+        z_out[1] = jnp.where(my_z == 0, totals[2], 0.0)
+    else:
+        z_out[0] = totals[2]
+        z_out[1] = totals[3]
 
 
 def third_kernel(dims, blocks, couplings, inverse, second, own, y_mix, z_mix, xe, xo, *refs):
-    third, sends, (field, y_field, z_field) = refs[0], refs[1:7], refs[7:]
-    nx, ny, nz, rows = dims.nx, dims.ny, dims.nz, dims.rows
+    third, sends, (field, y_field, z_field, x_field) = refs[0], refs[1:7], refs[7:]
+    nx, ny, nz = dims.nx, dims.ny, dims.nz
     m0, m1 = mode_rows(8, nz)
     row = row_iota(8, nz)
-    lane = lane_iota(8, nz)
-    last = jnp.where(lane == nz - 1, 1.0, 0.0)
-    start = jnp.where(lane == 0, 1.0, 0.0)
-    zero = jnp.zeros((8, nz), jnp.float32)
+    lane = lane_iota(8, 3 * nz)
     even_x = is_even("gx")
-    x_low = jnp.where(even_x, xo[...], xe[...])
-    x_high = jnp.where(even_x, xe[...], xo[...])
-    x_field = []
-    row_r = row_iota(8, rows)
-    for c in range(3):
-        modes = jnp.where(row == 2 * c, m0, jnp.where(row == 2 * c + 1, m1, zero))
-        field[c] = dot_00(own[...], modes)
-        y_field[c] = dot_00(y_mix[...], modes)
-        z_field[c] = dot_00(z_mix[0], modes * last) + dot_00(z_mix[1], modes * start)
-        x_field.append(
-            (dot_00(x_low, modes)[rows - ny : rows], dot_00(x_high, modes)[0:ny])
-        )
+    side = nx * ny // 2
+    x_low = jnp.where(even_x, xo[:, side:], xe[:, side:])
+    x_high = jnp.where(even_x, xe[:, :side], xo[:, :side])
+    x_mix = jnp.where(lane_iota(8, side) < ny, x_high, x_low)
+    modes = jnp.concatenate(
+        [
+            jnp.where(row == 2 * c, m0, jnp.where(row == 2 * c + 1, m1, 0.0))
+            for c in range(3)
+        ],
+        axis=1,
+    )
+    at = lax.rem(lane, nz)
+    wide = pairs6_right(modes)
+    last = pairs6_right(jnp.where(at == nz - 1, modes, 0.0))
+    start = pairs6_right(jnp.where(at == 0, modes, 0.0))
+    field[...] = dot_00(pairs6(own[...]), wide)
+    y_field[...] = dot_00(pairs6(y_mix[...]), wide)
+    z_field[...] = dot_00(pairs6(z_mix[0]), last) + dot_00(pairs6(z_mix[1]), start)
+    x_field[...] = dot_00(pairs6(x_mix), wide)
+
+    def at_x(ref, x):
+        return [ref[x * ny : (x + 1) * ny, c * nz : (c + 1) * nz] for c in range(3)]
+
     for x in range(nx):
-        center = tiles(dims, field, 3, x)
-        low = tiles(dims, field, 3, x - 1) if x > 0 else [x_field[c][0] for c in range(3)]
-        high = tiles(dims, field, 3, x + 1) if x < nx - 1 else [x_field[c][1] for c in range(3)]
-        y_tile = [(tile(dims, y_field, c, x),) * 2 for c in range(3)]
-        z_tile = tiles(dims, z_field, 3, x)
+        center = at_x(field, x)
+        low = at_x(field, x - 1) if x > 0 else at_x(x_field, side // ny - 1)
+        high = at_x(field, x + 1) if x < nx - 1 else at_x(x_field, 0)
+        y_tile = [(v, v) for v in at_x(y_field, x)]
+        z_tile = at_x(z_field, x)
         applied = apply_tile(
             dims,
             x,
@@ -411,7 +450,9 @@
         mask = 1
         while mask < count:
             which = [(i, i ^ mask) for i in range(count)]
-            packet = jnp.concatenate([packet, lax.ppermute(packet, axis, which)], axis=0)
+            arrived = lax.ppermute(packet, axis, which)
+            tail = (-1,) + packet.shape[-2:] if packet.shape[1] == 8 else (-1, packet.shape[-1])
+            packet = jnp.concatenate([packet.reshape(tail), arrived.reshape(tail)], axis=0)
             mask = 2 * mask + 1
     return packet
 
@@ -424,7 +465,7 @@
         in_specs=[pl.BlockSpec(memory_space=pltpu.VMEM)] * len(args),
         out_specs=[pl.BlockSpec(memory_space=pltpu.VMEM)] * len(out_shapes),
         scratch_shapes=scratch,
-        compiler_params=pltpu.CompilerParams(vmem_limit_bytes=24 * 1024 * 1024),
+        compiler_params=pltpu.CompilerParams(vmem_limit_bytes=VMEM_LIMIT),
     )(*args)
 
 
@@ -435,9 +476,8 @@
     rhs = rhs.reshape(3, rows, nz)
     blocks = blocks.reshape(9, rows, nz)
     couplings = couplings.reshape(6, rows, nz)
-    ids = agg_ids.reshape(1, rows)
     own = coarse_inv.shape[2]
-    coarse_inv = coarse_inv.reshape(36, own)
+    inverses = gather_slab(coarse_inv)
     n_y, n_z = lax.axis_size("gy"), lax.axis_size("gz")
     owners = n_y * n_z
     vector = (3, rows, nz)
@@ -464,14 +504,13 @@
     (packet,) = call(
         part(coarse_kernel, dims),
         "coarse",
-        [(1, 8 + 18, rows)],
+        [(1, 8, rows)],
         [pltpu.VMEM(vector, jnp.float32)],
         rhs,
         blocks,
         couplings,
         second,
-        ids,
-        coarse_inv,
+        agg_ids,
         *recv,
     )
     packets = gather_slab(packet)
@@ -480,17 +519,19 @@
         "solve",
         [(8, rows), (8, rows), (2, 8, rows)],
         [
-            pltpu.VMEM((owners, 8, own), jnp.float32),
-            pltpu.VMEM((owners, 24, own), jnp.bfloat16),
+            pltpu.VMEM((owners * 8, own), jnp.float32),
+            pltpu.VMEM((owners * 8, own), jnp.float32),
         ],
         packets,
+        inverses,
     )
     xo, xe = swap(corr, "gx", 1), swap(corr, "gx", 0)
     third, *sends = call(
         part(third_kernel, dims),
         "third",
         [vector] + faces,
-        [pltpu.VMEM(vector, jnp.float32)] * 3,
+        [pltpu.VMEM((rows, 3 * nz), jnp.float32)] * 3
+        + [pltpu.VMEM((rows // 2, 3 * nz), jnp.float32)],
         blocks,
         couplings,
         inverse,

time: 70.2 us -> 61.6 us (0.88)
  the two profiles are of different devices: /device:TPU:12 before, /device:TPU:9 now
where the time goes in v2:
time: 61.6 us; the launch traced here: 61.2 us
  starting transfers between devices  38.3 us (62%)
  waiting for transfers between devices  11.4 us (19%)
  Pallas kernels  8.96 us (15%)
  local copies, waits for them, and re-layouts  2.29 us (4%)
    ppermute x17, starting transfers between devices, swap(): return lax.ppermute(value, axis, which) if which else jnp.zeros_like(value)  33.5 us
    pallas_call x6, Pallas kernels, call(): pl.pallas_call(body, name=name, out_shape=[jax.ShapeDtypeStruct(s, jnp.fl...  8.96 us
    ppermute x6, waiting for transfers between devices, gather_slab(): arrived = lax.ppermute(packet, axis, which)  5.87 us
    ppermute x17, waiting for transfers between devices, swap(): return lax.ppermute(value, axis, which) if which else jnp.zeros_like(value)  5.55 us
    ppermute x6, starting transfers between devices, gather_slab(): arrived = lax.ppermute(packet, axis, which)  4.84 us
    unnamed x15, local copies, waits for them, and re-layouts  2.29 us
  transfers between devices with their start and end apart: 23, of which 10 were waited for; matrix products, arithmetic and copies ran while one was open for 0% of the time, Pallas kernels for 0%

profile of v2, /device:TPU:9, one launch (start us, length us, event | category | flops | bytes accessed | tf_op | source)
XLA Modules:
  0.0 61.2 jit_solution(10119888059741916115)
XLA Ops:
  4.1 3.0 %collective-permute-start.1 = (f32[3,16,128]{2,1,0:T(8,128)S(1)}, f32[3,16,128]{2,1,0:T(8,128)S(1)}, u32[]{:S(2)}, u32[]{:S(2)}) collective-permute-start(f32[3,16,128]{2,1,0:T(8,128)S(1)} %get-tuple-element.30), channel_id=1, source_target_pairs={{8,16},{16,8},{9,17},{17,9},{10,18},{18,10},{11,19},{19,11},{12,20... | collective-permute-start | bytes 73736 | tf_op jit(solution)/shard_map/ppermute | solution.py:436
  7.4 4.3 %collective-permute-start.3 = (f32[3,16,128]{2,1,0:T(8,128)S(1)}, f32[3,16,128]{2,1,0:T(8,128)S(1)}, u32[]{:S(2)}, u32[]{:S(2)}) collective-permute-start(f32[3,16,128]{2,1,0:T(8,128)S(1)} %get-tuple-element.32), channel_id=1, source_target_pairs={{2,4},{4,2},{3,5},{5,3},{10,12},{12,10},{11,13},{13,11},{18,20},{2... | collective-permute-start | bytes 73736 | tf_op jit(solution)/shard_map/ppermute | solution.py:436
  11.7 1.3 %collective-permute-start.4 = (f32[8,256]{1,0:T(8,128)S(1)}, f32[8,256]{1,0:T(8,128)S(1)}, u32[]{:S(2)}, u32[]{:S(2)}) collective-permute-start(f32[8,256]{1,0:T(8,128)S(1)} %get-tuple-element.33), channel_id=1, source_target_pairs={{0,1},{1,0},{2,3},{3,2},{4,5},{5,4},{6,7},{7,6},{8,9},{9,8},{10,11... | collective-permute-start | bytes 24584 | tf_op jit(solution)/shard_map/ppermute | solution.py:436
  13.0 1.3 %collective-permute-done.4.refs_4_ = f32[8,256]{1,0:T(8,128)S(1)} collective-permute-done((f32[8,256]{1,0:T(8,128)S(1)}, f32[8,256]{1,0:T(8,128)S(1)}, u32[]{:S(2)}, u32[]{:S(2)}) %collective-permute-start.4) | collective-permute-done | bytes 8224 | tf_op jit(solution)/shard_map/ppermute | solution.py:436
  14.3 1.6 %second.1 = (f32[3,256,128]{2,1,0:T(8,128)S(1)}, f32[3,16,128]{2,1,0:T(8,128)S(1)}, f32[3,16,128]{2,1,0:T(8,128)S(1)}, f32[3,16,128]{2,1,0:T(8,128)S(1)}, f32[3,...) custom-call(f32[3,256,128]{2,1,0:T(8,128)S(1)} %bitcast.18, f32[9,256,128]{2,1,0:T(8,128)S(1)} %bitcast.9, ...), custom_call_target="tpu_custom_call" | custom-call | tf_op jit(solution)/shard_map/second/pallas_call | solution.py:461
  15.9 4.2 %collective-permute-start.6 = (f32[3,16,128]{2,1,0:T(8,128)S(1)}, f32[3,16,128]{2,1,0:T(8,128)S(1)}, u32[]{:S(2)}, u32[]{:S(2)}) collective-permute-start(f32[3,16,128]{2,1,0:T(8,128)S(1)} %get-tuple-element.36), channel_id=1, source_target_pairs={{8,16},{16,8},{9,17},{17,9},{10,18},{18,10},{11,19},{19,11},{12,20... | collective-permute-start | bytes 73736 | tf_op jit(solution)/shard_map/ppermute | solution.py:436
  20.2 1.9 %collective-permute-start.8 = (f32[3,16,128]{2,1,0:T(8,128)S(1)}, f32[3,16,128]{2,1,0:T(8,128)S(1)}, u32[]{:S(2)}, u32[]{:S(2)}) collective-permute-start(f32[3,16,128]{2,1,0:T(8,128)S(1)} %get-tuple-element.38), channel_id=1, source_target_pairs={{2,4},{4,2},{3,5},{5,3},{10,12},{12,10},{11,13},{13,11},{18,20},{2... | collective-permute-start | bytes 73736 | tf_op jit(solution)/shard_map/ppermute | solution.py:436
  22.2 1.3 %collective-permute-start.9 = (f32[8,256]{1,0:T(8,128)S(1)}, f32[8,256]{1,0:T(8,128)S(1)}, u32[]{:S(2)}, u32[]{:S(2)}) collective-permute-start(f32[8,256]{1,0:T(8,128)S(1)} %get-tuple-element.39), channel_id=1, source_target_pairs={{0,1},{1,0},{2,3},{3,2},{4,5},{5,4},{6,7},{7,6},{8,9},{9,8},{10,11... | collective-permute-start | bytes 24584 | tf_op jit(solution)/shard_map/ppermute | solution.py:436
  23.4 1.3 %collective-permute-done.9.refs_4_ = f32[8,256]{1,0:T(8,128)S(1)} collective-permute-done((f32[8,256]{1,0:T(8,128)S(1)}, f32[8,256]{1,0:T(8,128)S(1)}, u32[]{:S(2)}, u32[]{:S(2)}) %collective-permute-start.9) | collective-permute-done | bytes 8224 | tf_op jit(solution)/shard_map/ppermute | solution.py:436
  25.7 1.3 %collective-permute-start.10 = (f32[1,8,256]{2,1,0:T(8,128)S(1)}, f32[1,8,256]{2,1,0:T(8,128)S(1)}, u32[]{:S(2)}, u32[]{:S(2)}) collective-permute-start(f32[1,8,256]{2,1,0:T(8,128)S(1)} %coarse.1), channel_id=1, source_target_pairs={{0,1},{1,0},{2,3},{3,2},{4,5},{5,4},{6,7},{7,6},{8,9},{9,8},{10,11... | collective-permute-start | bytes 24584 | tf_op jit(solution)/shard_map/ppermute | solution.py:453
  29.8 1.4 %collective-permute-done.11 = f32[2,8,256]{2,1,0:T(8,128)S(1)} collective-permute-done((f32[2,8,256]{2,1,0:T(8,128)S(1)}, f32[2,8,256]{2,1,0:T(8,128)S(1)}, u32[]{:S(2)}, u32[]{:S(2)}) %collective-permute-start.11) | collective-permute-done | bytes 16416 | tf_op jit(solution)/shard_map/ppermute | solution.py:453
  31.3 1.4 %collective-permute-start.12 = (f32[4,8,256]{2,1,0:T(8,128)S(1)}, f32[4,8,256]{2,1,0:T(8,128)S(1)}, u32[]{:S(2)}, u32[]{:S(2)}) collective-permute-start(f32[4,8,256]{2,1,0:T(8,128)S(1)} %pad_maximum_fusion.4), channel_id=1, source_target_pairs={{0,6},{2,4},{4,2},{6,0},{1,7},{3,5},{5,3},{7,1},{8,14},{10,12},{12... | collective-permute-start | bytes 98312 | tf_op jit(solution)/shard_map/ppermute | solution.py:453
  32.9 1.5 %collective-permute-start.15 = (f32[144,128]{1,0:T(8,128)S(1)}, f32[144,128]{1,0:T(8,128)S(1)}, u32[]{:S(2)}, u32[]{:S(2)}) collective-permute-start(f32[144,128]{1,0:T(8,128)S(1)} %pad_maximum_fusion.1), channel_id=1, source_target_pairs={{0,6},{2,4},{4,2},{6,0},{1,7},{3,5},{5,3},{7,1},{8,14},{10,12},{12... | collective-permute-start | bytes 221192 | tf_op jit(solution)/shard_map/ppermute | solution.py:453
  34.4 2.0 %collective-permute-done.15 = f32[144,128]{1,0:T(8,128)S(1)} collective-permute-done((f32[144,128]{1,0:T(8,128)S(1)}, f32[144,128]{1,0:T(8,128)S(1)}, u32[]{:S(2)}, u32[]{:S(2)}) %collective-permute-start.15) | collective-permute-done | bytes 73760 | tf_op jit(solution)/shard_map/ppermute | solution.py:453
  36.5 2.3 %solve.1 = (f32[8,256]{1,0:T(8,128)S(1)}, f32[8,256]{1,0:T(8,128)S(1)}, f32[2,8,256]{2,1,0:T(8,128)S(1)}) custom-call(f32[8,8,256]{2,1,0:T(8,128)S(1)} %pad_maximum_fusion.2.packets, f32[288,128]{1,0:T(8,128)S(1)} %pad_maximum_fusion.inverses), custom_call_target="tpu_custom_call" | custom-call | tf_op jit(solution)/shard_map/solve/pallas_call | solution.py:461
  38.7 3.2 %collective-permute-start.16 = (f32[8,256]{1,0:T(8,128)S(1)}, f32[8,256]{1,0:T(8,128)S(1)}, u32[]{:S(2)}, u32[]{:S(2)}) collective-permute-start(f32[8,256]{1,0:T(8,128)S(1)} %get-tuple-element.40.own), channel_id=1, source_target_pairs={{0,8},{8,0},{16,24},{24,16},{1,9},{9,1},{17,25},{25,17},{2,10},{10... | collective-permute-start | bytes 24584 | tf_op jit(solution)/shard_map/ppermute | solution.py:436
  41.9 3.4 %collective-permute-start.17 = (f32[8,256]{1,0:T(8,128)S(1)}, f32[8,256]{1,0:T(8,128)S(1)}, u32[]{:S(2)}, u32[]{:S(2)}) collective-permute-start(f32[8,256]{1,0:T(8,128)S(1)} %get-tuple-element.40.own), channel_id=1, source_target_pairs={{8,16},{16,8},{9,17},{17,9},{10,18},{18,10},{11,19},{19,11},{12,20... | collective-permute-start | bytes 24584 | tf_op jit(solution)/shard_map/ppermute | solution.py:436
  45.3 1.5 %collective-permute-done.17.xo = f32[8,256]{1,0:T(8,128)S(1)} collective-permute-done((f32[8,256]{1,0:T(8,128)S(1)}, f32[8,256]{1,0:T(8,128)S(1)}, u32[]{:S(2)}, u32[]{:S(2)}) %collective-permute-start.17) | collective-permute-done | bytes 8224 | tf_op jit(solution)/shard_map/ppermute | solution.py:436
  46.9 1.7 %third.1 = (f32[3,256,128]{2,1,0:T(8,128)S(1)}, f32[3,16,128]{2,1,0:T(8,128)S(1)}, f32[3,16,128]{2,1,0:T(8,128)S(1)}, f32[3,16,128]{2,1,0:T(8,128)S(1)}, f32[3,1...) custom-call(f32[9,256,128]{2,1,0:T(8,128)S(1)} %bitcast.11, f32[6,256,128]{2,1,0:T(8,128)S(1)} %bitcast.15, ...), custom_call_target="tpu_custom_call" | custom-call | tf_op jit(solution)/shard_map/third/pallas_call | solution.py:461
  48.5 3.4 %collective-permute-start.19 = (f32[3,16,128]{2,1,0:T(8,128)S(1)}, f32[3,16,128]{2,1,0:T(8,128)S(1)}, u32[]{:S(2)}, u32[]{:S(2)}) collective-permute-start(f32[3,16,128]{2,1,0:T(8,128)S(1)} %get-tuple-element.45), channel_id=1, source_target_pairs={{8,16},{16,8},{9,17},{17,9},{10,18},{18,10},{11,19},{19,11},{12,20... | collective-permute-start | bytes 73736 | tf_op jit(solution)/shard_map/ppermute | solution.py:436
  52.0 2.2 %collective-permute-start.20 = (f32[3,16,128]{2,1,0:T(8,128)S(1)}, f32[3,16,128]{2,1,0:T(8,128)S(1)}, u32[]{:S(2)}, u32[]{:S(2)}) collective-permute-start(f32[3,16,128]{2,1,0:T(8,128)S(1)} %get-tuple-element.46), channel_id=1, source_target_pairs={{0,2},{2,0},{4,6},{6,4},{1,3},{3,1},{5,7},{7,5},{8,10},{10,8},{12,... | collective-permute-start | bytes 73736 | tf_op jit(solution)/shard_map/ppermute | solution.py:436
  54.1 3.1 %collective-permute-start.21 = (f32[3,16,128]{2,1,0:T(8,128)S(1)}, f32[3,16,128]{2,1,0:T(8,128)S(1)}, u32[]{:S(2)}, u32[]{:S(2)}) collective-permute-start(f32[3,16,128]{2,1,0:T(8,128)S(1)} %get-tuple-element.47), channel_id=1, source_target_pairs={{2,4},{4,2},{3,5},{5,3},{10,12},{12,10},{11,13},{13,11},{18,20},{2... | collective-permute-start | bytes 73736 | tf_op jit(solution)/shard_map/ppermute | solution.py:436
  58.4 1.3 %collective-permute-done.22.refs_4_ = f32[8,256]{1,0:T(8,128)S(1)} collective-permute-done((f32[8,256]{1,0:T(8,128)S(1)}, f32[8,256]{1,0:T(8,128)S(1)}, u32[]{:S(2)}, u32[]{:S(2)}) %collective-permute-start.22) | collective-permute-done | bytes 8224 | tf_op jit(solution)/shard_map/ppermute | solution.py:436
  59.8 1.4 %last.1 = f32[3,256,128]{2,1,0:T(8,128)} custom-call(f32[3,256,128]{2,1,0:T(8,128)S(1)} %bitcast.20, f32[9,256,128]{2,1,0:T(8,128)S(1)} %bitcast.12, f32[6,256,128]{2,1,0:T(8,128)S(1)} %bitcast.16, f32[9,256,128]{2,1,0:T(8,128)S(1)} %get-tuple-element.27.inverse, f32[3,256,128]{2,1,0:T(8,128)S(1)} %get-tuple-element.43.third, ...), custom_call_target="tpu_custom_call" | custom-call | tf_op jit(solution)/shard_map/last/pallas_call | solution.py:461
  (50 shorter events, 9.8 us)
Async XLA Ops:
  3.4 10.8 %collective-permute-start = (f32[3,16,128]{2,1,0:T(8,128)S(1)}, f32[3,16,128]{2,1,0:T(8,128)S(1)}, u32[]{:S(2)}, u32[]{:S(2)}) collective-permute-start(f32[3,16,128]{2,1,0:T(8,128)S(1)} %get-tuple-element.29), channel_id=1, source_target_pairs={{0,8},{8,0},{16,24},{24,16},{1,9},{9,1},{17,25},{25,17},{2,10},{10... | collective-permute-start | bytes 73736 | tf_op jit(solution)/shard_map/ppermute | solution.py:436
  4.1 10.2 %collective-permute-start.1 = (f32[3,16,128]{2,1,0:T(8,128)S(1)}, f32[3,16,128]{2,1,0:T(8,128)S(1)}, u32[]{:S(2)}, u32[]{:S(2)}) collective-permute-start(f32[3,16,128]{2,1,0:T(8,128)S(1)} %get-tuple-element.30), channel_id=1, source_target_pairs={{8,16},{16,8},{9,17},{17,9},{10,18},{18,10},{11,19},{19,11},{12,20... | collective-permute-start | bytes 73736 | tf_op jit(solution)/shard_map/ppermute | solution.py:436
  7.2 7.1 %collective-permute-start.2 = (f32[3,16,128]{2,1,0:T(8,128)S(1)}, f32[3,16,128]{2,1,0:T(8,128)S(1)}, u32[]{:S(2)}, u32[]{:S(2)}) collective-permute-start(f32[3,16,128]{2,1,0:T(8,128)S(1)} %get-tuple-element.31), channel_id=1, source_target_pairs={{0,2},{2,0},{4,6},{6,4},{1,3},{3,1},{5,7},{7,5},{8,10},{10,8},{12,... | collective-permute-start | bytes 73736 | tf_op jit(solution)/shard_map/ppermute | solution.py:436
  7.4 6.9 %collective-permute-start.3 = (f32[3,16,128]{2,1,0:T(8,128)S(1)}, f32[3,16,128]{2,1,0:T(8,128)S(1)}, u32[]{:S(2)}, u32[]{:S(2)}) collective-permute-start(f32[3,16,128]{2,1,0:T(8,128)S(1)} %get-tuple-element.32), channel_id=1, source_target_pairs={{2,4},{4,2},{3,5},{5,3},{10,12},{12,10},{11,13},{13,11},{18,20},{2... | collective-permute-start | bytes 73736 | tf_op jit(solution)/shard_map/ppermute | solution.py:436
  11.7 2.6 %collective-permute-start.4 = (f32[8,256]{1,0:T(8,128)S(1)}, f32[8,256]{1,0:T(8,128)S(1)}, u32[]{:S(2)}, u32[]{:S(2)}) collective-permute-start(f32[8,256]{1,0:T(8,128)S(1)} %get-tuple-element.33), channel_id=1, source_target_pairs={{0,1},{1,0},{2,3},{3,2},{4,5},{5,4},{6,7},{7,6},{8,9},{9,8},{10,11... | collective-permute-start | bytes 24584 | tf_op jit(solution)/shard_map/ppermute | solution.py:436
  15.9 8.8 %collective-permute-start.5 = (f32[3,16,128]{2,1,0:T(8,128)S(1)}, f32[3,16,128]{2,1,0:T(8,128)S(1)}, u32[]{:S(2)}, u32[]{:S(2)}) collective-permute-start(f32[3,16,128]{2,1,0:T(8,128)S(1)} %get-tuple-element.35), channel_id=1, source_target_pairs={{0,8},{8,0},{16,24},{24,16},{1,9},{9,1},{17,25},{25,17},{2,10},{10... | collective-permute-start | bytes 73736 | tf_op jit(solution)/shard_map/ppermute | solution.py:436
  15.9 8.8 %collective-permute-start.6 = (f32[3,16,128]{2,1,0:T(8,128)S(1)}, f32[3,16,128]{2,1,0:T(8,128)S(1)}, u32[]{:S(2)}, u32[]{:S(2)}) collective-permute-start(f32[3,16,128]{2,1,0:T(8,128)S(1)} %get-tuple-element.36), channel_id=1, source_target_pairs={{8,16},{16,8},{9,17},{17,9},{10,18},{18,10},{11,19},{19,11},{12,20... | collective-permute-start | bytes 73736 | tf_op jit(solution)/shard_map/ppermute | solution.py:436
  20.2 4.6 %collective-permute-start.7 = (f32[3,16,128]{2,1,0:T(8,128)S(1)}, f32[3,16,128]{2,1,0:T(8,128)S(1)}, u32[]{:S(2)}, u32[]{:S(2)}) collective-permute-start(f32[3,16,128]{2,1,0:T(8,128)S(1)} %get-tuple-element.37), channel_id=1, source_target_pairs={{0,2},{2,0},{4,6},{6,4},{1,3},{3,1},{5,7},{7,5},{8,10},{10,8},{12,... | collective-permute-start | bytes 73736 | tf_op jit(solution)/shard_map/ppermute | solution.py:436
  20.2 4.6 %collective-permute-start.8 = (f32[3,16,128]{2,1,0:T(8,128)S(1)}, f32[3,16,128]{2,1,0:T(8,128)S(1)}, u32[]{:S(2)}, u32[]{:S(2)}) collective-permute-start(f32[3,16,128]{2,1,0:T(8,128)S(1)} %get-tuple-element.38), channel_id=1, source_target_pairs={{2,4},{4,2},{3,5},{5,3},{10,12},{12,10},{11,13},{13,11},{18,20},{2... | collective-permute-start | bytes 73736 | tf_op jit(solution)/shard_map/ppermute | solution.py:436
  22.2 2.6 %collective-permute-start.9 = (f32[8,256]{1,0:T(8,128)S(1)}, f32[8,256]{1,0:T(8,128)S(1)}, u32[]{:S(2)}, u32[]{:S(2)}) collective-permute-start(f32[8,256]{1,0:T(8,128)S(1)} %get-tuple-element.39), channel_id=1, source_target_pairs={{0,1},{1,0},{2,3},{3,2},{4,5},{5,4},{6,7},{7,6},{8,9},{9,8},{10,11... | collective-permute-start | bytes 24584 | tf_op jit(solution)/shard_map/ppermute | solution.py:436
  24.8 22.1 %copy-start.1 = (f32[9,16,16,128]{3,2,1,0:T(8,128)S(1)}, f32[9,16,16,128]{3,2,1,0:T(8,128)}, u32[]{:S(2)}) copy-start(f32[9,16,16,128]{3,2,1,0:T(8,128)} %param.6) | copy-start | bytes 3538948
  25.7 2.6 %collective-permute-start.10 = (f32[1,8,256]{2,1,0:T(8,128)S(1)}, f32[1,8,256]{2,1,0:T(8,128)S(1)}, u32[]{:S(2)}, u32[]{:S(2)}) collective-permute-start(f32[1,8,256]{2,1,0:T(8,128)S(1)} %coarse.1), channel_id=1, source_target_pairs={{0,1},{1,0},{2,3},{3,2},{4,5},{5,4},{6,7},{7,6},{8,9},{9,8},{10,11... | collective-permute-start | bytes 24584 | tf_op jit(solution)/shard_map/ppermute | solution.py:453
  27.0 2.6 %collective-permute-start.13 = (f32[36,1,128]{2,0,1:T(8,128)S(1)}, f32[36,1,128]{2,0,1:T(8,128)S(1)}, u32[]{:S(2)}, u32[]{:S(2)}) collective-permute-start(f32[36,1,128]{2,0,1:T(8,128)S(1)} %copy.10), channel_id=1, source_target_pairs={{0,1},{1,0},{2,3},{3,2},{4,5},{5,4},{6,7},{7,6},{8,9},{9,8},{10,11... | collective-permute-start | bytes 55304 | tf_op jit(solution)/shard_map/ppermute | solution.py:453
  28.3 3.0 %collective-permute-start.11 = (f32[2,8,256]{2,1,0:T(8,128)S(1)}, f32[2,8,256]{2,1,0:T(8,128)S(1)}, u32[]{:S(2)}, u32[]{:S(2)}) collective-permute-start(f32[2,8,256]{2,1,0:T(8,128)S(1)} %pad_maximum_fusion.5), channel_id=1, source_target_pairs={{0,2},{2,0},{4,6},{6,4},{1,3},{3,1},{5,7},{7,5},{8,10},{10,8},{12,... | collective-permute-start | bytes 49160 | tf_op jit(solution)/shard_map/ppermute | solution.py:453
  29.6 3.3 %collective-permute-start.14 = (f32[72,128]{1,0:T(8,128)S(1)}, f32[72,128]{1,0:T(8,128)S(1)}, u32[]{:S(2)}, u32[]{:S(2)}) collective-permute-start(f32[72,128]{1,0:T(8,128)S(1)} %pad_maximum_fusion.3), channel_id=1, source_target_pairs={{0,2},{2,0},{4,6},{6,4},{1,3},{3,1},{5,7},{7,5},{8,10},{10,8},{12,... | collective-permute-start | bytes 110600 | tf_op jit(solution)/shard_map/ppermute | solution.py:453
  31.3 3.2 %collective-permute-start.12 = (f32[4,8,256]{2,1,0:T(8,128)S(1)}, f32[4,8,256]{2,1,0:T(8,128)S(1)}, u32[]{:S(2)}, u32[]{:S(2)}) collective-permute-start(f32[4,8,256]{2,1,0:T(8,128)S(1)} %pad_maximum_fusion.4), channel_id=1, source_target_pairs={{0,6},{2,4},{4,2},{6,0},{1,7},{3,5},{5,3},{7,1},{8,14},{10,12},{12... | collective-permute-start | bytes 98312 | tf_op jit(solution)/shard_map/ppermute | solution.py:453
  32.9 3.5 %collective-permute-start.15 = (f32[144,128]{1,0:T(8,128)S(1)}, f32[144,128]{1,0:T(8,128)S(1)}, u32[]{:S(2)}, u32[]{:S(2)}) collective-permute-start(f32[144,128]{1,0:T(8,128)S(1)} %pad_maximum_fusion.1), channel_id=1, source_target_pairs={{0,6},{2,4},{4,2},{6,0},{1,7},{3,5},{5,3},{7,1},{8,14},{10,12},{12... | collective-permute-start | bytes 221192 | tf_op jit(solution)/shard_map/ppermute | solution.py:453
  38.7 6.6 %collective-permute-start.16 = (f32[8,256]{1,0:T(8,128)S(1)}, f32[8,256]{1,0:T(8,128)S(1)}, u32[]{:S(2)}, u32[]{:S(2)}) collective-permute-start(f32[8,256]{1,0:T(8,128)S(1)} %get-tuple-element.40.own), channel_id=1, source_target_pairs={{0,8},{8,0},{16,24},{24,16},{1,9},{9,1},{17,25},{25,17},{2,10},{10... | collective-permute-start | bytes 24584 | tf_op jit(solution)/shard_map/ppermute | solution.py:436
  41.9 5.0 %collective-permute-start.17 = (f32[8,256]{1,0:T(8,128)S(1)}, f32[8,256]{1,0:T(8,128)S(1)}, u32[]{:S(2)}, u32[]{:S(2)}) collective-permute-start(f32[8,256]{1,0:T(8,128)S(1)} %get-tuple-element.40.own), channel_id=1, source_target_pairs={{8,16},{16,8},{9,17},{17,9},{10,18},{18,10},{11,19},{19,11},{12,20... | collective-permute-start | bytes 24584 | tf_op jit(solution)/shard_map/ppermute | solution.py:436
  48.5 11.2 %collective-permute-start.18 = (f32[3,16,128]{2,1,0:T(8,128)S(1)}, f32[3,16,128]{2,1,0:T(8,128)S(1)}, u32[]{:S(2)}, u32[]{:S(2)}) collective-permute-start(f32[3,16,128]{2,1,0:T(8,128)S(1)} %get-tuple-element.44), channel_id=1, source_target_pairs={{0,8},{8,0},{16,24},{24,16},{1,9},{9,1},{17,25},{25,17},{2,10},{10... | collective-permute-start | bytes 73736 | tf_op jit(solution)/shard_map/ppermute | solution.py:436
  48.5 11.2 %collective-permute-start.19 = (f32[3,16,128]{2,1,0:T(8,128)S(1)}, f32[3,16,128]{2,1,0:T(8,128)S(1)}, u32[]{:S(2)}, u32[]{:S(2)}) collective-permute-start(f32[3,16,128]{2,1,0:T(8,128)S(1)} %get-tuple-element.45), channel_id=1, source_target_pairs={{8,16},{16,8},{9,17},{17,9},{10,18},{18,10},{11,19},{19,11},{12,20... | collective-permute-start | bytes 73736 | tf_op jit(solution)/shard_map/ppermute | solution.py:436
  52.0 7.8 %collective-permute-start.20 = (f32[3,16,128]{2,1,0:T(8,128)S(1)}, f32[3,16,128]{2,1,0:T(8,128)S(1)}, u32[]{:S(2)}, u32[]{:S(2)}) collective-permute-start(f32[3,16,128]{2,1,0:T(8,128)S(1)} %get-tuple-element.46), channel_id=1, source_target_pairs={{0,2},{2,0},{4,6},{6,4},{1,3},{3,1},{5,7},{7,5},{8,10},{10,8},{12,... | collective-permute-start | bytes 73736 | tf_op jit(solution)/shard_map/ppermute | solution.py:436
  54.1 5.7 %collective-permute-start.21 = (f32[3,16,128]{2,1,0:T(8,128)S(1)}, f32[3,16,128]{2,1,0:T(8,128)S(1)}, u32[]{:S(2)}, u32[]{:S(2)}) collective-permute-start(f32[3,16,128]{2,1,0:T(8,128)S(1)} %get-tuple-element.47), channel_id=1, source_target_pairs={{2,4},{4,2},{3,5},{5,3},{10,12},{12,10},{11,13},{13,11},{18,20},{2... | collective-permute-start | bytes 73736 | tf_op jit(solution)/shard_map/ppermute | solution.py:436
  57.2 2.6 %collective-permute-start.22 = (f32[8,256]{1,0:T(8,128)S(1)}, f32[8,256]{1,0:T(8,128)S(1)}, u32[]{:S(2)}, u32[]{:S(2)}) collective-permute-start(f32[8,256]{1,0:T(8,128)S(1)} %get-tuple-element.48), channel_id=1, source_target_pairs={{0,1},{1,0},{2,3},{3,2},{4,5},{5,4},{6,7},{7,6},{8,9},{9,8},{10,11... | collective-permute-start | bytes 24584 | tf_op jit(solution)/shard_map/ppermute | solution.py:436
  (6 other events, 39.9 us)

commit v3 on v2

v3 whole, which is shorter than its diff:
```python
import functools

import jax
import jax.numpy as jnp
from jax import lax
from jax.experimental import pallas as pl
from jax.experimental.pallas import tpu as pltpu
from jax.sharding import PartitionSpec as P

DAMPING = 0.8
AXES = ("gx", "gy", "gz")
VMEM_LIMIT = 12 * 1024 * 1024


def dot_tt(a, b):
    return lax.dot_general(
        a, b, (((1,), (1,)), ((), ())), preferred_element_type=jnp.float32
    )


def dot_00(a, b):
    return lax.dot_general(
        a, b, (((0,), (0,)), ((), ())), preferred_element_type=jnp.float32
    )


def parts3(v):
    high = v.astype(jnp.bfloat16)
    rest = v - high.astype(jnp.float32)
    mid = rest.astype(jnp.bfloat16)
    low = (rest - mid.astype(jnp.float32)).astype(jnp.bfloat16)
    return high, mid, low


def split3(v):
    return jnp.concatenate(parts3(v), axis=0)


def pairs6(v):
    high, mid, low = parts3(v)
    return jnp.concatenate([high, high, high, mid, mid, low], axis=0)


def pairs6_right(v):
    high, mid, low = parts3(v)
    return jnp.concatenate([high, mid, low, high, mid, high], axis=0)


def lane_iota(rows, lanes):
    return lax.broadcasted_iota(jnp.int32, (rows, lanes), 1)


def row_iota(rows, lanes):
    return lax.broadcasted_iota(jnp.int32, (rows, lanes), 0)


def mode_rows(rows, length):
    k = lane_iota(rows, length).astype(jnp.float32)
    m1 = (k - (length - 1) / 2.0) / (length / 2.0) * (3.0 / length) ** 0.5
    m0 = jnp.full((rows, length), length ** (-0.5), jnp.float32)
    return m0, m1


def is_even(axis):
    return lax.rem(lax.axis_index(axis), 2) == 0


def damped_inverse(m):
    a, b, c, d, e, f, g, h, i = m
    co_a = e * i - f * h
    co_b = f * g - d * i
    co_c = d * h - e * g
    determ = a * co_a + b * co_b + c * co_c
    scale = DAMPING / determ
    rows = [
        co_a,
        c * h - b * i,
        b * f - c * e,
        co_b,
        a * i - c * g,
        c * d - a * f,
        co_c,
        b * g - a * h,
        a * e - b * d,
    ]
    return [r * scale for r in rows]


def times(m, v):
    return [m[3 * r] * v[0] + m[3 * r + 1] * v[1] + m[3 * r + 2] * v[2] for r in range(3)]


class Dims:
    def __init__(self, nx, ny, nz):
        self.nx, self.ny, self.nz = nx, ny, nz
        self.rows = nx * ny
        self.groups = self.rows // 8


def tile(ref, c, x, size):
    return ref[c, x * size : (x + 1) * size, :]


def tiles(ref, count, x, size):
    return [tile(ref, c, x, size) for c in range(count)]


def flat_tiles(ref, start, count, size):
    return [ref[(start + c) * size : (start + c + 1) * size, :] for c in range(count)]


def face_index(axis, count):
    even = jnp.where(is_even(axis), count - 1, 0)
    return even, (count - 1) - even


def put_faces(dims, fields, sends):
    xe, xo, ye, yo = sends
    nx, ny = dims.nx, dims.ny
    x_at = face_index("gx", nx)
    y_at = face_index("gy", ny)
    at = 0
    for field in fields:
        for c in range(field.shape[0]):
            for ref, x in zip((xe, xo), x_at):
                ref[at * ny : (at + 1) * ny, :] = field[c, pl.ds(pl.multiple_of(x * ny, ny), ny), :]
            for ref, y in zip((ye, yo), y_at):
                ref[at * nx : (at + 1) * nx, :] = field[c, pl.ds(y, nx, stride=ny), :]
            at += 1


def put_z(dims, field, sends):
    groups, nz = dims.groups, dims.nz
    lane = lane_iota(8, nz)
    for ref, k in zip(sends, face_index("gz", nz)):
        total = []
        for c in range(3):
            face = jnp.zeros((8, nz), jnp.float32)
            for g in range(groups):
                to = c * groups + g
                v = pltpu.roll(field[c, 8 * g : 8 * g + 8, :], lax.rem(to + nz - k, nz), 1)
                face = jnp.where(lane == to, v, face)
            total.append(face)
        ref[...] = total[0] + total[1] + total[2]


def neighbour(axis, pair, high):
    e, o = pair
    even = is_even(axis)
    return jnp.where(even, e, o) if high else jnp.where(even, o, e)


class ZHalo:
    def __init__(self, dims, recv):
        self.dims = dims
        self.recv = [r[...] for r in recv]
        if len(recv) == 2:
            self.low = neighbour("gz", self.recv, False)
            self.high = neighbour("gz", self.recv, True)
        else:
            self.low = self.high = None
            self.at = jnp.where(is_even("gz"), 0, dims.nz - 1)

    def tile(self, c, x):
        dims = self.dims
        nz = dims.nz
        lane = lane_iota(8, nz)
        per = dims.ny // 8
        out = []
        for g in range(x * per, (x + 1) * per):
            at = c * dims.groups + g
            if self.low is None:
                v = pltpu.roll(self.recv[0], lax.rem(self.at + nz - at, nz), 1)
                out.append(jnp.where(lane == self.at, v, 0.0))
            else:
                low = pltpu.roll(self.low, (nz - 1 - at) % nz, 1)
                high = pltpu.roll(self.high, (nz - at) % nz, 1)
                out.append(jnp.where(lane == nz - 1, low, high))
        return jnp.concatenate(out, axis=0) if per > 1 else out[0]


def shifted(v, low, high, axis):
    size = v.shape[axis]
    at = lax.broadcasted_iota(jnp.int32, v.shape, axis)
    below = pltpu.roll(jnp.where(at == size - 1, low, v), 1, axis)
    above = pltpu.roll(jnp.where(at == 0, high, v), size - 1, axis)
    return below, above


def beside(coup, x_pair, y_pair, z_pair):
    return (
        coup[0] * x_pair[0]
        + coup[1] * x_pair[1]
        + (coup[2] * y_pair[0] + coup[3] * y_pair[1])
        + (coup[4] * z_pair[0] + coup[5] * z_pair[1])
    )


def sums_at(dims, x, field, x_halo, y_halo, z_halo, coup):
    nx, ny = dims.nx, dims.ny
    center = tiles(field, 3, x, ny)
    out = []
    for c in range(3):
        low = tile(field, c, x - 1, ny) if x > 0 else x_halo(c, False)
        high = tile(field, c, x + 1, ny) if x < nx - 1 else x_halo(c, True)
        y_pair = shifted(center[c], y_halo(c, x, False), y_halo(c, x, True), 0)
        z = z_halo.tile(c, x)
        z_pair = shifted(center[c], z, z, 1)
        out.append(beside(coup, (low, high), y_pair, z_pair))
    return center, out


def received(dims, recv):
    xe, xo, ye, yo = recv
    nx, ny = dims.nx, dims.ny

    def x_halo(c, high):
        pair = [r[c * ny : (c + 1) * ny, :] for r in (xe, xo)]
        return neighbour("gx", pair, high)

    def y_halo(c, x, high):
        pair = [r[c * nx + x : c * nx + x + 1, :] for r in (ye, yo)]
        return neighbour("gy", pair, high)

    return x_halo, y_halo


def rows_at(dims, x):
    return slice(x * dims.ny, (x + 1) * dims.ny)


def first_kernel(dims, counts, *refs):
    n_inv, n_z = counts
    rhs, blocks, couplings = refs[:3]
    pieces, refs = refs[3 : 3 + n_inv], refs[3 + n_inv :]
    first, inverse, xe, xo, ye, yo = refs[:6]
    for x in range(dims.nx):
        inv = damped_inverse(tiles(blocks, 9, x, dims.ny))
        at = rows_at(dims, x)
        for k in range(9):
            inverse[k, at, :] = inv[k]
        v = times(inv, tiles(rhs, 3, x, dims.ny))
        for c in range(3):
            first[c, at, :] = v[c]
    put_faces(dims, (first, inverse, couplings), (xe, xo, ye, yo))
    put_z(dims, first, refs[6 : 6 + n_z])
    at = 18 * dims.nx
    for piece in pieces:
        ye[at : at + piece.shape[0], :] = piece[:, 0, :]
        at += piece.shape[0]


def second_kernel(dims, counts, inverse, couplings, first, *refs):
    n_inv, n_z = counts
    pieces, refs = refs[:n_inv], refs[n_inv:]
    recv, z_recv, refs = refs[:4], refs[4 : 4 + n_z], refs[4 + n_z :]
    second, sums, *sends = refs[:6]
    z_sends, inverses = refs[6 : 6 + n_z], refs[6 + n_z]
    x_halo, y_halo = received(dims, recv)
    z_halo = ZHalo(dims, z_recv)
    for x in range(dims.nx):
        coup = tiles(couplings, 6, x, dims.ny)
        center, total = sums_at(dims, x, first, x_halo, y_halo, z_halo, coup)
        step = times(tiles(inverse, 9, x, dims.ny), total)
        at = rows_at(dims, x)
        for c in range(3):
            sums[c, at, :] = total[c]
            second[c, at, :] = (2.0 - DAMPING) * center[c] + step[c]
    put_faces(dims, (second,), sends)
    put_z(dims, second, z_sends)
    at = 0
    for piece in pieces:
        inverses[at : at + piece.shape[0], :] = piece[:, 0, :]
        at += piece.shape[0]
    start = 18 * dims.nx
    inverses[at : 2 * at, :] = recv[2][start : start + at, :]


def coarse_kernel(dims, n_z, rhs, sums, couplings, second, ids, *refs):
    recv, z_recv, (packet, resid) = refs[:4], refs[4 : 4 + n_z], refs[4 + n_z :]
    x_halo, y_halo = received(dims, recv)
    z_halo = ZHalo(dims, z_recv)
    rest = 1.0 - DAMPING * (2.0 - DAMPING)
    for x in range(dims.nx):
        coup = tiles(couplings, 6, x, dims.ny)
        _, total = sums_at(dims, x, second, x_halo, y_halo, z_halo, coup)
        at = rows_at(dims, x)
        for c in range(3):
            resid[c, at, :] = rest * rhs[c, at, :] + (total[c] - DAMPING * sums[c, at, :])
    m0, m1 = mode_rows(8, dims.nz)
    row = row_iota(8, dims.nz)
    modes = split3(jnp.where(row == 0, m0, jnp.where(row == 1, m1, 0.0)))
    for c in range(3):
        s = sum(dot_tt(modes, part) for part in parts3(resid[c]))
        packet[0, 2 * c : 2 * c + 2, :] = (s[0:8] + (s[8:16] + s[16:24]))[0:2]
    packet[0, 6:7, :] = pencil_row(dims, ids[0].astype(jnp.float32))
    packet[0, 7:8, :] = jnp.zeros((1, dims.rows), jnp.float32)


def pencil_row(dims, square):
    nx, ny, rows = dims.nx, dims.ny, dims.rows
    lane = lane_iota(ny, rows)
    spread = jnp.where(lax.rem(lane, ny) == row_iota(ny, rows), 1.0, 0.0)
    wide = lax.dot_general(
        square,
        spread,
        (((1,), (0,)), ((), ())),
        precision=lax.Precision.HIGHEST,
        preferred_element_type=jnp.float32,
    )
    lane = lane_iota(nx, rows)
    keep = lax.div(lane, ny) == row_iota(nx, rows)
    return jnp.sum(jnp.where(keep, wide, 0.0), axis=0, keepdims=True)


def gray(j):
    return lax.bitwise_xor(j, lax.shift_right_logical(j, 1))


def gray_inverse(v, bits):
    out = v
    for b in range(1, bits):
        out = lax.bitwise_xor(out, lax.shift_right_logical(v, b))
    return out


def bits_of(n):
    return max(1, (n - 1).bit_length())


def solve_kernel(dims, sizes, own, packets, inverses, stack, y_z, coarse, correction):
    n_y, n_z = sizes
    owners = n_y * n_z
    rows = dims.rows
    my_y, my_z = lax.axis_index("gy"), lax.axis_index("gz")
    local = row_iota(own, rows).astype(jnp.bfloat16)
    one_b = jnp.ones((own, rows), jnp.bfloat16)
    zero_b = jnp.zeros((own, rows), jnp.bfloat16)

    def owner_at(j):
        jz = lax.rem(j, n_z)
        jy = lax.div(j, n_z)
        return lax.bitwise_xor(my_y, gray(jy)) * n_z + lax.bitwise_xor(my_z, gray(jz))

    def member(j, ids):
        base = (owner_at(j) * own).astype(jnp.float32)
        rel = jnp.clip(ids - base, -1.0, float(own)).astype(jnp.bfloat16)
        return jnp.where(local == rel, one_b, zero_b)

    coarse[...] = jnp.zeros_like(coarse)

    def add(d, carry):
        pack = packets[d]
        ids = pack[6:7]
        parts = split3(jnp.where(row_iota(8, rows) < 6, pack, 0.0))
        for j in range(owners):
            s = dot_tt(parts, member(j, ids))
            coarse[8 * j : 8 * j + 8] = coarse[8 * j : 8 * j + 8] + (s[0:8] + (s[8:16] + s[16:24]))
        return carry

    lax.fori_loop(0, owners, add, 0, unroll=2)

    for block in range(owners // 8):
        v = [coarse[pl.ds(64 * block + k, 8, stride=8), :] for k in range(6)]
        for i in range(6):
            total = None
            for k in range(6):
                m = inverses[pl.ds(36 * 8 * block + 6 * i + k, 8, stride=36), :]
                total = m * v[k] if total is None else total + m * v[k]
            correction[pl.ds(64 * block + i, 8, stride=8), :] = total
        for i in (6, 7):
            correction[pl.ds(64 * block + i, 8, stride=8), :] = jnp.zeros_like(total)

    def ids_of(y, z):
        inside = (y >= 0) & (y < n_y) & (z >= 0) & (z < n_z)
        y = jnp.clip(y, 0, n_y - 1)
        z = jnp.clip(z, 0, n_z - 1)
        jy = gray_inverse(lax.bitwise_xor(my_y, y), bits_of(n_y))
        jz = gray_inverse(lax.bitwise_xor(my_z, z), bits_of(n_z))
        return jnp.where(inside, packets[jy * n_z + jz, 6:7, :], -1.0)

    upper = lax.rem(lane_iota(1, rows), dims.ny) >= dims.ny // 2

    def y_ids(z):
        return jnp.where(upper, ids_of(my_y - 1, z), ids_of(my_y + 1, z))

    beyond = [1 - my_z] if n_z == 2 else [my_z - 1, my_z + 1]
    wanted = [ids_of(my_y, my_z), y_ids(my_z)]
    wanted += [ids_of(my_y, z) for z in beyond] + [y_ids(z) for z in beyond]
    totals = [jnp.zeros((24, rows), jnp.float32) for _ in wanted]
    for j in range(owners):
        left = split3(correction[8 * j : 8 * j + 8])
        for t in range(len(wanted)):
            totals[t] = totals[t] + lax.dot_general(
                left,
                member(j, wanted[t]),
                (((1,), (0,)), ((), ())),
                preferred_element_type=jnp.float32,
            )
    totals = [s[0:8] + (s[8:16] + s[16:24]) for s in totals]
    stack[0:8] = totals[0]
    stack[8:16] = totals[1]
    if n_z == 2:
        low = my_z == 1
        for ref, at, value in ((stack, 16, totals[2]), (y_z, 0, totals[3])):
            ref[at : at + 8] = jnp.where(low, value, 0.0)
            ref[at + 8 : at + 16] = jnp.where(low, 0.0, value)
    else:
        stack[16:24], stack[24:32] = totals[2], totals[3]
        y_z[0:8], y_z[8:16] = totals[4], totals[5]


def third_kernel(dims, n_z, inverse, couplings, second, stack, y_z, *refs):
    stacks, fat, thin, refs = refs[:2], refs[2:6], refs[6:10], refs[10:]
    third, x_third, y_third = refs[:3]
    z_sends, refs = refs[3 : 3 + n_z], refs[3 + n_z :]
    field, y_field, z_field, yz_field, x_field, xy_field, xz_field = refs
    nx, ny, nz = dims.nx, dims.ny, dims.nz
    side = nx * ny // 2
    m0, m1 = mode_rows(8, nz)
    row = row_iota(8, nz)
    modes = jnp.concatenate(
        [
            jnp.where(row == 2 * c, m0, jnp.where(row == 2 * c + 1, m1, 0.0))
            for c in range(3)
        ],
        axis=1,
    )
    at = lax.rem(lane_iota(8, 3 * nz), nz)
    wide = pairs6_right(modes)
    last = pairs6_right(jnp.where(at == nz - 1, modes, 0.0))
    start = pairs6_right(jnp.where(at == 0, modes, 0.0))
    x_low = neighbour("gx", [s[:, side:] for s in stacks], False)
    x_high = neighbour("gx", [s[:, :side] for s in stacks], True)
    x_mix = jnp.where(lane_iota(4 * 8, side) < side // 2, x_high, x_low)

    def expand(v, ends=None):
        if ends is None:
            return dot_00(pairs6(v), wide)
        return dot_00(pairs6(v), last) + dot_00(pairs6(ends), start)

    for ref, value in (
        (field, expand(stack[0:8])),
        (y_field, expand(stack[8:16])),
        (z_field, expand(stack[16:24], stack[24:32])),
        (yz_field, expand(y_z[0:8], y_z[8:16])),
        (x_field, expand(x_mix[0:8])),
        (xy_field, expand(x_mix[8:16])),
        (xz_field, expand(x_mix[16:24], x_mix[24:32])),
    ):
        for c in range(3):
            ref[c] = value[:, c * nz : (c + 1) * nz]

    def at_x(own, outer, c, x):
        if 0 <= x < nx:
            return tile(own, c, x, ny)
        return tile(outer, c, side // ny + x if x < 0 else x - nx, ny)

    def update(inv, coup, center, base, pairs):
        step = times(inv, [beside(coup, *pairs(c)) for c in range(3)])
        return [base[c] + ((1.0 - DAMPING) * center[c] + step[c]) for c in range(3)]

    for x in range(-1, nx + 1):
        center = [at_x(field, x_field, c, x) for c in range(3)]

        def pairs(c, x=x, center=center):
            y = at_x(y_field, xy_field, c, x)
            z = at_x(z_field, xz_field, c, x)
            x_pair = (at_x(field, x_field, c, x - 1), at_x(field, x_field, c, x + 1))
            return x_pair, shifted(center[c], y, y, 0), shifted(center[c], z, z, 1)

        if 0 <= x < nx:
            out = update(
                tiles(inverse, 9, x, ny),
                tiles(couplings, 6, x, ny),
                center,
                tiles(second, 3, x, ny),
                pairs,
            )
            for c in range(3):
                third[c, rows_at(dims, x), :] = out[c]
        else:
            high = x == nx
            halo = [
                neighbour("gx", [r[c * ny : (c + 1) * ny, :] for r in fat[:2]], high)
                for c in range(3, 18)
            ]
            base = [
                neighbour("gx", [r[c * ny : (c + 1) * ny, :] for r in thin[:2]], high)
                for c in range(3)
            ]
            out = update(halo[:9], halo[9:], center, base, pairs)
            for c in range(3):
                x_third[int(high), c * ny : (c + 1) * ny, :] = out[c]
    for high in (False, True):
        inner, near, far = (ny - 1, 0, 1) if high else (0, ny - 1, ny - 2)

        def line(ref, c, y):
            return ref[c, pl.ds(y, nx, stride=ny), :]

        center = [line(y_field, c, near) for c in range(3)]

        def pairs(c, center=center, inner=inner, near=near, far=far, high=high):
            low_row = xy_field[c, side - ny + near : side - ny + near + 1, :]
            high_row = xy_field[c, near : near + 1, :]
            y_pair = (line(y_field, c, far), line(field, c, inner))
            z = line(yz_field, c, near)
            return (
                shifted(center[c], low_row, high_row, 0),
                y_pair[::-1] if high else y_pair,
                shifted(center[c], z, z, 1),
            )

        halo = [
            neighbour("gy", [r[c * nx : (c + 1) * nx, :] for r in fat[2:]], high)
            for c in range(3, 18)
        ]
        base = [
            neighbour("gy", [r[c * nx : (c + 1) * nx, :] for r in thin[2:]], high)
            for c in range(3)
        ]
        out = update(halo[:9], halo[9:], center, base, pairs)
        for c in range(3):
            y_third[int(high), c * nx : (c + 1) * nx, :] = out[c]
    put_z(dims, third, z_sends)


def last_kernel(dims, inverse, couplings, first, third, x_third, y_third, *refs):
    z_recv, out = refs[:-1], refs[-1]
    nx, ny = dims.nx, dims.ny

    def x_halo(c, high):
        return x_third[int(high), c * ny : (c + 1) * ny, :]

    def y_halo(c, x, high):
        return y_third[int(high), c * nx + x : c * nx + x + 1, :]

    z_halo = ZHalo(dims, z_recv)
    for x in range(nx):
        coup = tiles(couplings, 6, x, ny)
        center, total = sums_at(dims, x, third, x_halo, y_halo, z_halo, coup)
        step = times(tiles(inverse, 9, x, ny), total)
        at = rows_at(dims, x)
        for c in range(3):
            out[c, at, :] = first[c, at, :] + ((1.0 - DAMPING) * center[c] + step[c])


def pairs_of(count, start):
    out = []
    for i in range(start, count - 1, 2):
        out += [(i, i + 1), (i + 1, i)]
    return out


def swap(value, axis, start):
    return lax.ppermute(value, axis, pairs_of(lax.axis_size(axis), start))


def exchange(sends, z_sends):
    xe, xo, ye, yo = sends
    z_recv = [swap(v, "gz", k) for k, v in enumerate(z_sends)]
    yo, ye = swap(yo, "gy", 1), swap(ye, "gy", 0)
    xo, xe = swap(xo, "gx", 1), swap(xe, "gx", 0)
    return [xe, xo, ye, yo], z_recv


def stages(axis, first=0):
    masks = []
    mask = 1
    while mask < lax.axis_size(axis):
        masks.append([(i, i ^ mask) for i in range(lax.axis_size(axis))])
        mask = 2 * mask + 1
    return masks[first:]


def gather_along(value, axis, first=0):
    for which in stages(axis, first):
        value = jnp.concatenate([value, lax.ppermute(value, axis, which)], axis=0)
    return value


def call(body, name, out_shapes, scratch, *args):
    return pl.pallas_call(
        body,
        name=name,
        out_shape=[jax.ShapeDtypeStruct(s, jnp.float32) for s in out_shapes],
        in_specs=[pl.BlockSpec(memory_space=pltpu.VMEM)] * len(args),
        out_specs=[pl.BlockSpec(memory_space=pltpu.VMEM)] * len(out_shapes),
        scratch_shapes=scratch,
        compiler_params=pltpu.CompilerParams(vmem_limit_bytes=VMEM_LIMIT),
    )(*args)


def shards(rhs, blocks, couplings, agg_ids, coarse_inv):
    _, nx, ny, nz = rhs.shape
    dims = Dims(nx, ny, nz)
    rows = nx * ny
    rhs = rhs.reshape(3, rows, nz)
    blocks = blocks.reshape(9, rows, nz)
    couplings = couplings.reshape(6, rows, nz)
    own = coarse_inv.shape[2]
    n_y, n_z = lax.axis_size("gy"), lax.axis_size("gz")
    owners = n_y * n_z
    z_count = 1 if n_z == 2 else 2
    vector = (3, rows, nz)
    part = functools.partial
    f32 = jnp.float32

    def faces(count, extra=0):
        return [(count * ny, nz)] * 2 + [(count * nx + extra, nz), (count * nx, nz)]

    z_faces = [(8, nz)] * z_count
    pieces = [coarse_inv]
    for which in stages("gz"):
        joined = jnp.concatenate(pieces, axis=0) if len(pieces) > 1 else pieces[0]
        pieces.append(lax.ppermute(joined, "gz", which))
    counts = (len(pieces), z_count)
    inv_rows = 36 * n_z

    first, inverse, *sends = call(
        part(first_kernel, dims, counts),
        "first",
        [vector, (9, rows, nz)] + faces(18, inv_rows) + z_faces,
        [],
        rhs,
        blocks,
        couplings,
        *pieces,
    )
    fat, z_recv = exchange(sends[:4], sends[4:])
    second, sums, *sends = call(
        part(second_kernel, dims, counts),
        "second",
        [vector, vector] + faces(3) + z_faces + [(2 * inv_rows, own)],
        [],
        inverse,
        couplings,
        first,
        *pieces,
        *fat,
        *z_recv,
    )
    inverses = gather_along(sends[-1], "gy", 1)
    thin, z_recv = exchange(sends[:4], sends[4:-1])
    (packet,) = call(
        part(coarse_kernel, dims, z_count),
        "coarse",
        [(1, 8, rows)],
        [pltpu.VMEM(vector, f32)],
        rhs,
        sums,
        couplings,
        second,
        agg_ids,
        *thin,
        *z_recv,
    )
    packets = gather_along(gather_along(packet, "gz"), "gy")
    stack, y_z = call(
        part(solve_kernel, dims, (n_y, n_z), own),
        "solve",
        [(4 * 8, rows), (2 * 8, rows)],
        [pltpu.VMEM((owners * 8, own), f32)] * 2,
        packets,
        inverses,
    )
    xo, xe = swap(stack, "gx", 1), swap(stack, "gx", 0)
    third, x_third, y_third, *z_sends = call(
        part(third_kernel, dims, z_count),
        "third",
        [vector, (2, 3 * ny, nz), (2, 3 * nx, nz)] + z_faces,
        [pltpu.VMEM(vector, f32)] * 4 + [pltpu.VMEM((3, rows // 2, nz), f32)] * 3,
        inverse,
        couplings,
        second,
        stack,
        y_z,
        xe,
        xo,
        *fat,
        *thin,
    )
    z_recv = [swap(v, "gz", k) for k, v in enumerate(z_sends)]
    (out,) = call(
        part(last_kernel, dims),
        "last",
        [vector],
        [],
        inverse,
        couplings,
        first,
        third,
        x_third,
        y_third,
        *z_recv,
    )
    return out.reshape(3, nx, ny, nz)


def solution(mesh):
    return jax.shard_map(
        shards,
        mesh=mesh,
        in_specs=(
            P(None, "gx", "gy", "gz"),
            P(None, "gx", "gy", "gz"),
            P(None, "gx", "gy", "gz"),
            P("gz", "gx", "gy"),
            P(None, "gx", ("gy", "gz")),
        ),
        out_specs=P(None, "gx", "gy", "gz"),
        check_vma=False,
    )
```

time: 61.6 us -> 61.5 us (level)
  the two profiles are of different devices: /device:TPU:9 before, /device:TPU:0 now
where the time goes in v3:
time: 61.5 us; the launch traced here: 61.1 us
  starting transfers between devices  31.2 us (51%)
  waiting for transfers between devices  15.5 us (25%)
  Pallas kernels  10.1 us (16%)
  local copies, waits for them, and re-layouts  4.13 us (7%)
    ppermute x13, starting transfers between devices, swap(): return lax.ppermute(value, axis, pairs_of(lax.axis_size(axis), start))  20.4 us
    pallas_call x6, Pallas kernels, call(): pl.pallas_call(body, name=name, out_shape=[jax.ShapeDtypeStruct(s, jnp.fl...  10.1 us
    ppermute x4, starting transfers between devices, gather_along(): value = jnp.concatenate([value, lax.ppermute(value, axis, which)], axis=0)  7.86 us
    ppermute x13, waiting for transfers between devices, swap(): return lax.ppermute(value, axis, pairs_of(lax.axis_size(axis), start))  7.23 us
    ppermute x4, waiting for transfers between devices, gather_along(): value = jnp.concatenate([value, lax.ppermute(value, axis, which)], axis=0)  6.33 us
    unnamed x14, local copies, waits for them, and re-layouts  4.13 us
    ppermute x1, starting transfers between devices, shards(): pieces.append(lax.ppermute(joined, 'gz', which))  2.97 us
    ppermute x1, waiting for transfers between devices, shards(): pieces.append(lax.ppermute(joined, 'gz', which))  1.95 us
  transfers between devices with their start and end apart: 18, of which 9 were waited for; matrix products, arithmetic and copies ran while one was open for 0% of the time, Pallas kernels for 0%

profile of v3, /device:TPU:0, one launch (start us, length us, event | category | flops | bytes accessed | tf_op | source)
XLA Modules:
  0.0 61.1 jit_solution(11343681508670592542)
XLA Ops:
  0.0 3.0 %collective-permute-start = (f32[36,1,128]{2,1,0:T(1,128)}, f32[36,1,128]{2,1,0:T(1,128)S(1)}, u32[]{:S(2)}, u32[]{:S(2)}) collective-permute-start(f32[36,1,128]{2,1,0:T(1,128)} %refs_0_.1), channel_id=1, source_target_pairs={{0,1},{1,0},{2,3},{3,2},{4,5},{5,4},{6,7},{7,6},{8,9},{9,8},{10,11... | collective-permute-start | bytes 55304 | tf_op jit(solution)/shard_map/ppermute | solution.py:616
  3.0 1.9 %collective-permute-done.refs_4_.refs_1_ = f32[36,1,128]{2,1,0:T(1,128)S(1)} collective-permute-done((f32[36,1,128]{2,1,0:T(1,128)}, f32[36,1,128]{2,1,0:T(1,128)S(1)}, u32[]{:S(2)}, u32[]{:S(2)}) %collective-permute-start) | collective-permute-done | bytes 18464 | tf_op jit(solution)/shard_map/ppermute | solution.py:616
  4.9 1.1 %copy-done = f32[6,16,16,128]{3,2,1,0:T(8,128)S(1)} copy-done((f32[6,16,16,128]{3,2,1,0:T(8,128)S(1)}, f32[6,16,16,128]{3,2,1,0:T(8,128)}, u32[]{:S(2)}) %copy-start) | copy-done | bytes 786456
  6.1 1.0 %copy-done.2 = f32[3,16,16,128]{3,2,1,0:T(8,128)S(1)} copy-done((f32[3,16,16,128]{3,2,1,0:T(8,128)S(1)}, f32[3,16,16,128]{3,2,1,0:T(8,128)}, u32[]{:S(2)}) %copy-start.2) | copy-done | bytes 393240
  7.0 1.3 %copy-done.3 = f32[9,16,16,128]{3,2,1,0:T(8,128)S(1)} copy-done((f32[9,16,16,128]{3,2,1,0:T(8,128)S(1)}, f32[9,16,16,128]{3,2,1,0:T(8,128)}, u32[]{:S(2)}) %copy-start.3) | copy-done | bytes 1179672
  9.7 2.2 %collective-permute-start.3 = (f32[360,128]{1,0:T(8,128)S(1)}, f32[360,128]{1,0:T(8,128)S(1)}, u32[]{:S(2)}, u32[]{:S(2)}) collective-permute-start(f32[360,128]{1,0:T(8,128)S(1)} %get-tuple-element.30), channel_id=1, source_target_pairs={{0,2},{2,0},{4,6},{6,4},{1,3},{3,1},{5,7},{7,5},{8,10},{10,8},{12,... | collective-permute-start | bytes 552968 | tf_op jit(solution)/shard_map/ppermute | solution.py:556
  13.2 1.6 %collective-permute-start.5 = (f32[8,128]{1,0:T(8,128)S(1)}, f32[8,128]{1,0:T(8,128)S(1)}, u32[]{:S(2)}, u32[]{:S(2)}) collective-permute-start(f32[8,128]{1,0:T(8,128)S(1)} %get-tuple-element.32), channel_id=1, source_target_pairs={{0,1},{1,0},{2,3},{3,2},{4,5},{5,4},{6,7},{7,6},{8,9},{9,8},{10,11... | collective-permute-start | bytes 12296 | tf_op jit(solution)/shard_map/ppermute | solution.py:556
  14.7 2.1 %collective-permute-done.5.refs_6_ = f32[8,128]{1,0:T(8,128)S(1)} collective-permute-done((f32[8,128]{1,0:T(8,128)S(1)}, f32[8,128]{1,0:T(8,128)S(1)}, u32[]{:S(2)}, u32[]{:S(2)}) %collective-permute-start.5) | collective-permute-done | bytes 4128 | tf_op jit(solution)/shard_map/ppermute | solution.py:556
  16.9 2.7 %second.1 = (f32[3,256,128]{2,1,0:T(8,128)S(1)}, f32[3,256,128]{2,1,0:T(8,128)S(1)}, f32[48,128]{1,0:T(8,128)S(1)}, f32[48,128]{1,0:T(8,128)S(1)}, f32[48,128]{1...) custom-call(f32[9,256,128]{2,1,0:T(8,128)S(1)} %get-tuple-element.26.inverse, ...), custom_call_target="tpu_custom_call" | custom-call | tf_op jit(solution)/shard_map/second/pallas_call | solution.py:583
  19.6 2.0 %collective-permute-start.6 = (f32[48,128]{1,0:T(8,128)S(1)}, f32[48,128]{1,0:T(8,128)S(1)}, u32[]{:S(2)}, u32[]{:S(2)}) collective-permute-start(f32[48,128]{1,0:T(8,128)S(1)} %get-tuple-element.35), channel_id=1, source_target_pairs={{0,8},{8,0},{16,24},{24,16},{1,9},{9,1},{17,25},{25,17},{2,10},{10... | collective-permute-start | bytes 73736 | tf_op jit(solution)/shard_map/ppermute | solution.py:556
  22.3 4.0 %collective-permute-start.8 = (f32[48,128]{1,0:T(8,128)S(1)}, f32[48,128]{1,0:T(8,128)S(1)}, u32[]{:S(2)}, u32[]{:S(2)}) collective-permute-start(f32[48,128]{1,0:T(8,128)S(1)} %get-tuple-element.37), channel_id=1, source_target_pairs={{0,2},{2,0},{4,6},{6,4},{1,3},{3,1},{5,7},{7,5},{8,10},{10,8},{12,... | collective-permute-start | bytes 73736 | tf_op jit(solution)/shard_map/ppermute | solution.py:556
  26.9 1.6 %collective-permute-start.10 = (f32[8,128]{1,0:T(8,128)S(1)}, f32[8,128]{1,0:T(8,128)S(1)}, u32[]{:S(2)}, u32[]{:S(2)}) collective-permute-start(f32[8,128]{1,0:T(8,128)S(1)} %get-tuple-element.39), channel_id=1, source_target_pairs={{0,1},{1,0},{2,3},{3,2},{4,5},{5,4},{6,7},{7,6},{8,9},{9,8},{10,11... | collective-permute-start | bytes 12296 | tf_op jit(solution)/shard_map/ppermute | solution.py:556
  28.5 2.1 %collective-permute-done.10.refs_4_ = f32[8,128]{1,0:T(8,128)S(1)} collective-permute-done((f32[8,128]{1,0:T(8,128)S(1)}, f32[8,128]{1,0:T(8,128)S(1)}, u32[]{:S(2)}, u32[]{:S(2)}) %collective-permute-start.10) | collective-permute-done | bytes 4128 | tf_op jit(solution)/shard_map/ppermute | solution.py:556
  31.4 1.5 %collective-permute-start.11 = (f32[1,8,256]{2,1,0:T(8,128)S(1)}, f32[1,8,256]{2,1,0:T(8,128)S(1)}, u32[]{:S(2)}, u32[]{:S(2)}) collective-permute-start(f32[1,8,256]{2,1,0:T(8,128)S(1)} %coarse.1), channel_id=1, source_target_pairs={{0,1},{1,0},{2,3},{3,2},{4,5},{5,4},{6,7},{7,6},{8,9},{9,8},{10,11... | collective-permute-start | bytes 24584 | tf_op jit(solution)/shard_map/ppermute | solution.py:578
  32.9 2.2 %collective-permute-done.11 = f32[1,8,256]{2,1,0:T(8,128)S(1)} collective-permute-done((f32[1,8,256]{2,1,0:T(8,128)S(1)}, f32[1,8,256]{2,1,0:T(8,128)S(1)}, u32[]{:S(2)}, u32[]{:S(2)}) %collective-permute-start.11) | collective-permute-done | bytes 8224 | tf_op jit(solution)/shard_map/ppermute | solution.py:578
  35.1 3.0 %collective-permute-start.12 = (f32[2,8,256]{2,1,0:T(8,128)S(1)}, f32[2,8,256]{2,1,0:T(8,128)S(1)}, u32[]{:S(2)}, u32[]{:S(2)}) collective-permute-start(f32[2,8,256]{2,1,0:T(8,128)S(1)} %pad_maximum_fusion.3), channel_id=1, source_target_pairs={{0,2},{2,0},{4,6},{6,4},{1,3},{3,1},{5,7},{7,5},{8,10},{10,8},{12,... | collective-permute-start | bytes 49160 | tf_op jit(solution)/shard_map/ppermute | solution.py:578
  38.0 1.2 %collective-permute-start.14 = (f32[144,128]{1,0:T(8,128)S(1)}, f32[144,128]{1,0:T(8,128)S(1)}, u32[]{:S(2)}, u32[]{:S(2)}) collective-permute-start(f32[144,128]{1,0:T(8,128)S(1)} %get-tuple-element.40), channel_id=1, source_target_pairs={{0,6},{2,4},{4,2},{6,0},{1,7},{3,5},{5,3},{7,1},{8,14},{10,12},{12... | collective-permute-start | bytes 221192 | tf_op jit(solution)/shard_map/ppermute | solution.py:578
  39.8 2.1 %collective-permute-start.13 = (f32[4,8,256]{2,1,0:T(8,128)S(1)}, f32[4,8,256]{2,1,0:T(8,128)S(1)}, u32[]{:S(2)}, u32[]{:S(2)}) collective-permute-start(f32[4,8,256]{2,1,0:T(8,128)S(1)} %pad_maximum_fusion.2), channel_id=1, source_target_pairs={{0,6},{2,4},{4,2},{6,0},{1,7},{3,5},{5,3},{7,1},{8,14},{10,12},{12... | collective-permute-start | bytes 98312 | tf_op jit(solution)/shard_map/ppermute | solution.py:578
  41.9 2.8 %collective-permute-done.14 = f32[144,128]{1,0:T(8,128)S(1)} collective-permute-done((f32[144,128]{1,0:T(8,128)S(1)}, f32[144,128]{1,0:T(8,128)S(1)}, u32[]{:S(2)}, u32[]{:S(2)}) %collective-permute-start.14) | collective-permute-done | bytes 73760 | tf_op jit(solution)/shard_map/ppermute | solution.py:578
  45.6 2.3 %solve.1 = (f32[32,256]{1,0:T(8,128)S(1)}, f32[16,256]{1,0:T(8,128)S(1)}) custom-call(f32[8,8,256]{2,1,0:T(8,128)S(1)} %pad_maximum_fusion.1.packets, f32[288,128]{1,0:T(8,128)S(1)} %pad_maximum_fusion.inverses), custom_call_target="tpu_custom_call" | custom-call | tf_op jit(solution)/shard_map/solve/pallas_call | solution.py:583
  48.6 4.3 %collective-permute-start.15 = (f32[32,256]{1,0:T(8,128)S(1)}, f32[32,256]{1,0:T(8,128)S(1)}, u32[]{:S(2)}, u32[]{:S(2)}) collective-permute-start(f32[32,256]{1,0:T(8,128)S(1)} %get-tuple-element.41.stack), channel_id=1, source_target_pairs={{0,8},{8,0},{16,24},{24,16},{1,9},{9,1},{17,25},{25,17},{2,10},{10... | collective-permute-start | bytes 98312 | tf_op jit(solution)/shard_map/ppermute | solution.py:556
  54.7 1.6 %collective-permute-start.17 = (f32[8,128]{1,0:T(8,128)S(1)}, f32[8,128]{1,0:T(8,128)S(1)}, u32[]{:S(2)}, u32[]{:S(2)}) collective-permute-start(f32[8,128]{1,0:T(8,128)S(1)} %get-tuple-element.46), channel_id=1, source_target_pairs={{0,1},{1,0},{2,3},{3,2},{4,5},{5,4},{6,7},{7,6},{8,9},{9,8},{10,11... | collective-permute-start | bytes 12296 | tf_op jit(solution)/shard_map/ppermute | solution.py:556
  56.3 2.1 %collective-permute-done.17.refs_0_ = f32[8,128]{1,0:T(8,128)S(1)} collective-permute-done((f32[8,128]{1,0:T(8,128)S(1)}, f32[8,128]{1,0:T(8,128)S(1)}, u32[]{:S(2)}, u32[]{:S(2)}) %collective-permute-start.17) | collective-permute-done | bytes 4128 | tf_op jit(solution)/shard_map/ppermute | solution.py:556
  58.4 2.7 %last.1 = f32[3,256,128]{2,1,0:T(8,128)} custom-call(f32[9,256,128]{2,1,0:T(8,128)S(1)} %get-tuple-element.26.inverse, f32[6,256,128]{2,1,0:T(8,128)S(1)} %bitcast.8, f32[3,256,128]{2,1,0:T(8,128)S(1)} %get-tuple-element.27.first, f32[3,256,128]{2,1,0:T(8,128)S(1)} %get-tuple-element.43.third, f32[2,48,128]{2,1,0:T(8,128)S(1)} %get-tuple-element.44.x_third, ...), custom_call_target="tpu_custom_call" | custom-call | tf_op jit(solution)/shard_map/last/pallas_call | solution.py:583
  (36 shorter events, 8.7 us)
Async XLA Ops:
  0.0 4.9 %collective-permute-start = (f32[36,1,128]{2,1,0:T(1,128)}, f32[36,1,128]{2,1,0:T(1,128)S(1)}, u32[]{:S(2)}, u32[]{:S(2)}) collective-permute-start(f32[36,1,128]{2,1,0:T(1,128)} %refs_0_.1), channel_id=1, source_target_pairs={{0,1},{1,0},{2,3},{3,2},{4,5},{5,4},{6,7},{7,6},{8,9},{9,8},{10,11... | collective-permute-start | bytes 55304 | tf_op jit(solution)/shard_map/ppermute | solution.py:616
  4.9 1.1 %copy-start = (f32[6,16,16,128]{3,2,1,0:T(8,128)S(1)}, f32[6,16,16,128]{3,2,1,0:T(8,128)}, u32[]{:S(2)}) copy-start(f32[6,16,16,128]{3,2,1,0:T(8,128)} %param.7) | copy-start | bytes 2359300
  6.1 1.0 %copy-start.2 = (f32[3,16,16,128]{3,2,1,0:T(8,128)S(1)}, f32[3,16,16,128]{3,2,1,0:T(8,128)}, u32[]{:S(2)}) copy-start(f32[3,16,16,128]{3,2,1,0:T(8,128)} %param.5) | copy-start | bytes 1179652
  7.0 1.3 %copy-start.3 = (f32[9,16,16,128]{3,2,1,0:T(8,128)S(1)}, f32[9,16,16,128]{3,2,1,0:T(8,128)}, u32[]{:S(2)}) copy-start(f32[9,16,16,128]{3,2,1,0:T(8,128)} %param.6) | copy-start | bytes 3538948
  9.0 7.8 %copy-start.1 = (f32[6,16,16,128]{3,2,1,0:T(8,128)S(1)}, f32[6,16,16,128]{3,2,1,0:T(8,128)}, u32[]{:S(2)}) copy-start(f32[6,16,16,128]{3,2,1,0:T(8,128)} %param.7) | copy-start | bytes 2359300
  9.0 7.8 %copy-start.5 = (f32[36,1,128]{2,1,0:T(1,128)S(1)}, f32[36,1,128]{2,1,0:T(1,128)}, u32[]{:S(2)}) copy-start(f32[36,1,128]{2,1,0:T(1,128)} %refs_0_.1) | copy-start | bytes 55300
  9.7 7.2 %collective-permute-start.3 = (f32[360,128]{1,0:T(8,128)S(1)}, f32[360,128]{1,0:T(8,128)S(1)}, u32[]{:S(2)}, u32[]{:S(2)}) collective-permute-start(f32[360,128]{1,0:T(8,128)S(1)} %get-tuple-element.30), channel_id=1, source_target_pairs={{0,2},{2,0},{4,6},{6,4},{1,3},{3,1},{5,7},{7,5},{8,10},{10,8},{12,... | collective-permute-start | bytes 552968 | tf_op jit(solution)/shard_map/ppermute | solution.py:556
  11.8 5.0 %collective-permute-start.1 = (f32[288,128]{1,0:T(8,128)S(1)}, f32[288,128]{1,0:T(8,128)S(1)}, u32[]{:S(2)}, u32[]{:S(2)}) collective-permute-start(f32[288,128]{1,0:T(8,128)S(1)} %get-tuple-element.28), channel_id=1, source_target_pairs={{0,8},{8,0},{16,24},{24,16},{1,9},{9,1},{17,25},{25,17},{2,10},{10... | collective-permute-start | bytes 442376 | tf_op jit(solution)/shard_map/ppermute | solution.py:556
  11.8 5.0 %collective-permute-start.2 = (f32[288,128]{1,0:T(8,128)S(1)}, f32[288,128]{1,0:T(8,128)S(1)}, u32[]{:S(2)}, u32[]{:S(2)}) collective-permute-start(f32[288,128]{1,0:T(8,128)S(1)} %get-tuple-element.29), channel_id=1, source_target_pairs={{8,16},{16,8},{9,17},{17,9},{10,18},{18,10},{11,19},{19,11},{12,20... | collective-permute-start | bytes 442376 | tf_op jit(solution)/shard_map/ppermute | solution.py:556
  12.5 4.4 %collective-permute-start.4 = (f32[288,128]{1,0:T(8,128)S(1)}, f32[288,128]{1,0:T(8,128)S(1)}, u32[]{:S(2)}, u32[]{:S(2)}) collective-permute-start(f32[288,128]{1,0:T(8,128)S(1)} %get-tuple-element.31), channel_id=1, source_target_pairs={{2,4},{4,2},{3,5},{5,3},{10,12},{12,10},{11,13},{13,11},{18,20},{2... | collective-permute-start | bytes 442376 | tf_op jit(solution)/shard_map/ppermute | solution.py:556
  13.2 3.7 %collective-permute-start.5 = (f32[8,128]{1,0:T(8,128)S(1)}, f32[8,128]{1,0:T(8,128)S(1)}, u32[]{:S(2)}, u32[]{:S(2)}) collective-permute-start(f32[8,128]{1,0:T(8,128)S(1)} %get-tuple-element.32), channel_id=1, source_target_pairs={{0,1},{1,0},{2,3},{3,2},{4,5},{5,4},{6,7},{7,6},{8,9},{9,8},{10,11... | collective-permute-start | bytes 12296 | tf_op jit(solution)/shard_map/ppermute | solution.py:556
  16.9 13.7 %copy-start.6 = (s32[1,16,16]{2,1,0:T(8,128)S(1)}, s32[1,16,16]{2,1,0:T(8,128)}, u32[]{:S(2)}) copy-start(s32[1,16,16]{2,1,0:T(8,128)} %ids.1) | copy-start | bytes 3076
  19.6 11.0 %collective-permute-start.6 = (f32[48,128]{1,0:T(8,128)S(1)}, f32[48,128]{1,0:T(8,128)S(1)}, u32[]{:S(2)}, u32[]{:S(2)}) collective-permute-start(f32[48,128]{1,0:T(8,128)S(1)} %get-tuple-element.35), channel_id=1, source_target_pairs={{0,8},{8,0},{16,24},{24,16},{1,9},{9,1},{17,25},{25,17},{2,10},{10... | collective-permute-start | bytes 73736 | tf_op jit(solution)/shard_map/ppermute | solution.py:556
  21.6 9.0 %collective-permute-start.7 = (f32[48,128]{1,0:T(8,128)S(1)}, f32[48,128]{1,0:T(8,128)S(1)}, u32[]{:S(2)}, u32[]{:S(2)}) collective-permute-start(f32[48,128]{1,0:T(8,128)S(1)} %get-tuple-element.36), channel_id=1, source_target_pairs={{8,16},{16,8},{9,17},{17,9},{10,18},{18,10},{11,19},{19,11},{12,20... | collective-permute-start | bytes 73736 | tf_op jit(solution)/shard_map/ppermute | solution.py:556
  22.3 8.3 %collective-permute-start.8 = (f32[48,128]{1,0:T(8,128)S(1)}, f32[48,128]{1,0:T(8,128)S(1)}, u32[]{:S(2)}, u32[]{:S(2)}) collective-permute-start(f32[48,128]{1,0:T(8,128)S(1)} %get-tuple-element.37), channel_id=1, source_target_pairs={{0,2},{2,0},{4,6},{6,4},{1,3},{3,1},{5,7},{7,5},{8,10},{10,8},{12,... | collective-permute-start | bytes 73736 | tf_op jit(solution)/shard_map/ppermute | solution.py:556
  26.2 4.3 %collective-permute-start.9 = (f32[48,128]{1,0:T(8,128)S(1)}, f32[48,128]{1,0:T(8,128)S(1)}, u32[]{:S(2)}, u32[]{:S(2)}) collective-permute-start(f32[48,128]{1,0:T(8,128)S(1)} %get-tuple-element.38), channel_id=1, source_target_pairs={{2,4},{4,2},{3,5},{5,3},{10,12},{12,10},{11,13},{13,11},{18,20},{2... | collective-permute-start | bytes 73736 | tf_op jit(solution)/shard_map/ppermute | solution.py:556
  26.9 3.7 %collective-permute-start.10 = (f32[8,128]{1,0:T(8,128)S(1)}, f32[8,128]{1,0:T(8,128)S(1)}, u32[]{:S(2)}, u32[]{:S(2)}) collective-permute-start(f32[8,128]{1,0:T(8,128)S(1)} %get-tuple-element.39), channel_id=1, source_target_pairs={{0,1},{1,0},{2,3},{3,2},{4,5},{5,4},{6,7},{7,6},{8,9},{9,8},{10,11... | collective-permute-start | bytes 12296 | tf_op jit(solution)/shard_map/ppermute | solution.py:556
  31.4 3.7 %collective-permute-start.11 = (f32[1,8,256]{2,1,0:T(8,128)S(1)}, f32[1,8,256]{2,1,0:T(8,128)S(1)}, u32[]{:S(2)}, u32[]{:S(2)}) collective-permute-start(f32[1,8,256]{2,1,0:T(8,128)S(1)} %coarse.1), channel_id=1, source_target_pairs={{0,1},{1,0},{2,3},{3,2},{4,5},{5,4},{6,7},{7,6},{8,9},{9,8},{10,11... | collective-permute-start | bytes 24584 | tf_op jit(solution)/shard_map/ppermute | solution.py:578
  35.1 4.7 %collective-permute-start.12 = (f32[2,8,256]{2,1,0:T(8,128)S(1)}, f32[2,8,256]{2,1,0:T(8,128)S(1)}, u32[]{:S(2)}, u32[]{:S(2)}) collective-permute-start(f32[2,8,256]{2,1,0:T(8,128)S(1)} %pad_maximum_fusion.3), channel_id=1, source_target_pairs={{0,2},{2,0},{4,6},{6,4},{1,3},{3,1},{5,7},{7,5},{8,10},{10,8},{12,... | collective-permute-start | bytes 49160 | tf_op jit(solution)/shard_map/ppermute | solution.py:578
  38.0 6.6 %collective-permute-start.14 = (f32[144,128]{1,0:T(8,128)S(1)}, f32[144,128]{1,0:T(8,128)S(1)}, u32[]{:S(2)}, u32[]{:S(2)}) collective-permute-start(f32[144,128]{1,0:T(8,128)S(1)} %get-tuple-element.40), channel_id=1, source_target_pairs={{0,6},{2,4},{4,2},{6,0},{1,7},{3,5},{5,3},{7,1},{8,14},{10,12},{12... | collective-permute-start | bytes 221192 | tf_op jit(solution)/shard_map/ppermute | solution.py:578
  39.8 5.8 %collective-permute-start.13 = (f32[4,8,256]{2,1,0:T(8,128)S(1)}, f32[4,8,256]{2,1,0:T(8,128)S(1)}, u32[]{:S(2)}, u32[]{:S(2)}) collective-permute-start(f32[4,8,256]{2,1,0:T(8,128)S(1)} %pad_maximum_fusion.2), channel_id=1, source_target_pairs={{0,6},{2,4},{4,2},{6,0},{1,7},{3,5},{5,3},{7,1},{8,14},{10,12},{12... | collective-permute-start | bytes 98312 | tf_op jit(solution)/shard_map/ppermute | solution.py:578
  47.9 5.0 %collective-permute-start.16 = (f32[32,256]{1,0:T(8,128)S(1)}, f32[32,256]{1,0:T(8,128)S(1)}, u32[]{:S(2)}, u32[]{:S(2)}) collective-permute-start(f32[32,256]{1,0:T(8,128)S(1)} %get-tuple-element.41.stack), channel_id=1, source_target_pairs={{8,16},{16,8},{9,17},{17,9},{10,18},{18,10},{11,19},{19,11},{12,20... | collective-permute-start | bytes 98312 | tf_op jit(solution)/shard_map/ppermute | solution.py:556
  48.6 5.2 %collective-permute-start.15 = (f32[32,256]{1,0:T(8,128)S(1)}, f32[32,256]{1,0:T(8,128)S(1)}, u32[]{:S(2)}, u32[]{:S(2)}) collective-permute-start(f32[32,256]{1,0:T(8,128)S(1)} %get-tuple-element.41.stack), channel_id=1, source_target_pairs={{0,8},{8,0},{16,24},{24,16},{1,9},{9,1},{17,25},{25,17},{2,10},{10... | collective-permute-start | bytes 98312 | tf_op jit(solution)/shard_map/ppermute | solution.py:556
  54.7 3.7 %collective-permute-start.17 = (f32[8,128]{1,0:T(8,128)S(1)}, f32[8,128]{1,0:T(8,128)S(1)}, u32[]{:S(2)}, u32[]{:S(2)}) collective-permute-start(f32[8,128]{1,0:T(8,128)S(1)} %get-tuple-element.46), channel_id=1, source_target_pairs={{0,1},{1,0},{2,3},{3,2},{4,5},{5,4},{6,7},{7,6},{8,9},{9,8},{10,11... | collective-permute-start | bytes 12296 | tf_op jit(solution)/shard_map/ppermute | solution.py:556
  (1 other events, 0.7 us)

commit v4 on v3

--- a/solution.py
+++ b/solution.py
@@ -114,34 +114,44 @@
     return even, (count - 1) - even
 
 
+def inner_odd(axis, value):
+    count = lax.axis_size(axis)
+    at = lax.axis_index(axis)
+    return jnp.where((at > 0) & (at < count - 1), value, 0.0)
+
+
 def put_faces(dims, fields, sends):
     xe, xo, ye, yo = sends
     nx, ny = dims.nx, dims.ny
-    x_at = face_index("gx", nx)
-    y_at = face_index("gy", ny)
+    x_e, x_o = face_index("gx", nx)
+    y_e, y_o = face_index("gy", ny)
     at = 0
     for field in fields:
         for c in range(field.shape[0]):
-            for ref, x in zip((xe, xo), x_at):
-                ref[at * ny : (at + 1) * ny, :] = field[c, pl.ds(pl.multiple_of(x * ny, ny), ny), :]
-            for ref, y in zip((ye, yo), y_at):
-                ref[at * nx : (at + 1) * nx, :] = field[c, pl.ds(y, nx, stride=ny), :]
+            x_rows = slice(at * ny, (at + 1) * ny)
+            y_rows = slice(at * nx, (at + 1) * nx)
+            xe[x_rows, :] = field[c, pl.ds(pl.multiple_of(x_e * ny, ny), ny), :]
+            v = field[c, pl.ds(pl.multiple_of(x_o * ny, ny), ny), :]
+            xo[x_rows, :] = inner_odd("gx", v)
+            ye[y_rows, :] = field[c, pl.ds(y_e, nx, stride=ny), :]
+            yo[y_rows, :] = inner_odd("gy", field[c, pl.ds(y_o, nx, stride=ny), :])
             at += 1
 
 
 def put_z(dims, field, sends):
     groups, nz = dims.groups, dims.nz
     lane = lane_iota(8, nz)
-    for ref, k in zip(sends, face_index("gz", nz)):
+    for odd, (ref, k) in enumerate(zip(sends, face_index("gz", nz))):
+        to = lax.rem(lane + nz - k, nz)
         total = []
         for c in range(3):
             face = jnp.zeros((8, nz), jnp.float32)
             for g in range(groups):
-                to = c * groups + g
-                v = pltpu.roll(field[c, 8 * g : 8 * g + 8, :], lax.rem(to + nz - k, nz), 1)
-                face = jnp.where(lane == to, v, face)
+                at = c * groups + g
+                face = jnp.where(to == at, pltpu.roll(field[c, 8 * g : 8 * g + 8, :], at, 1), face)
             total.append(face)
-        ref[...] = total[0] + total[1] + total[2]
+        face = pltpu.roll(total[0] + total[1] + total[2], lax.rem(nz - k, nz), 1)
+        ref[0:8, :] = inner_odd("gz", face) if odd else face
 
 
 def neighbour(axis, pair, high):
@@ -153,13 +163,14 @@
 class ZHalo:
     def __init__(self, dims, recv):
         self.dims = dims
-        self.recv = [r[...] for r in recv]
+        self.recv = [r[0:8, :] for r in recv]
         if len(recv) == 2:
             self.low = neighbour("gz", self.recv, False)
             self.high = neighbour("gz", self.recv, True)
         else:
             self.low = self.high = None
             self.at = jnp.where(is_even("gz"), 0, dims.nz - 1)
+            self.moved = pltpu.roll(self.recv[0], self.at, 1)
 
     def tile(self, c, x):
         dims = self.dims
@@ -170,7 +181,7 @@
         for g in range(x * per, (x + 1) * per):
             at = c * dims.groups + g
             if self.low is None:
-                v = pltpu.roll(self.recv[0], lax.rem(self.at + nz - at, nz), 1)
+                v = pltpu.roll(self.moved, (nz - at) % nz, 1)
                 out.append(jnp.where(lane == self.at, v, 0.0))
             else:
                 low = pltpu.roll(self.low, (nz - 1 - at) % nz, 1)
@@ -229,12 +240,37 @@
     return slice(x * dims.ny, (x + 1) * dims.ny)
 
 
-def first_kernel(dims, counts, *refs):
-    n_inv, n_z = counts
-    rhs, blocks, couplings = refs[:3]
-    pieces, refs = refs[3 : 3 + n_inv], refs[3 + n_inv :]
-    first, inverse, xe, xo, ye, yo = refs[:6]
+def put_inverses(ref, start, pieces):
+    for piece in pieces:
+        ref[start : start + 36, :] = piece
+        start += 36
+
+
+CHUNKS = 4
+
+
+def first_kernel(dims, n_z, *refs):
+    rhs_in, blocks_in, couplings_in, coarse_inv = refs[:4]
+    first, inverse, rhs, couplings, xe, xo, ye, yo = refs[4:12]
+    z_sends, (blocks, sems) = refs[12 : 12 + n_z], refs[12 + n_z :]
+    step = dims.rows // CHUNKS
+
+    def copy(k, src, dst, rows):
+        return pltpu.make_async_copy(src.at[:, rows, :], dst.at[:, rows, :], sems.at[k])
+
+    copies = []
+    for k in range(CHUNKS):
+        rows = pl.ds(k * step, step)
+        copies.append(copy(2 * k, blocks_in, blocks, rows))
+        copies.append(copy(2 * k + 1, rhs_in, rhs, rows))
+    copies.append(copy(2 * CHUNKS, couplings_in, couplings, pl.ds(0, dims.rows)))
+    for c in copies:
+        c.start()
     for x in range(dims.nx):
+        if x % (dims.nx // CHUNKS) == 0:
+            k = x // (dims.nx // CHUNKS)
+            copies[2 * k].wait()
+            copies[2 * k + 1].wait()
         inv = damped_inverse(tiles(blocks, 9, x, dims.ny))
         at = rows_at(dims, x)
         for k in range(9):
@@ -242,20 +278,19 @@
         v = times(inv, tiles(rhs, 3, x, dims.ny))
         for c in range(3):
             first[c, at, :] = v[c]
+    copies[-1].wait()
     put_faces(dims, (first, inverse, couplings), (xe, xo, ye, yo))
-    put_z(dims, first, refs[6 : 6 + n_z])
-    at = 18 * dims.nx
-    for piece in pieces:
-        ye[at : at + piece.shape[0], :] = piece[:, 0, :]
-        at += piece.shape[0]
-
-
-def second_kernel(dims, counts, inverse, couplings, first, *refs):
-    n_inv, n_z = counts
-    pieces, refs = refs[:n_inv], refs[n_inv:]
+    put_z(dims, first, z_sends)
+    own = coarse_inv[:, 0, :]
+    put_inverses(ye, 18 * dims.nx, [own])
+    put_inverses(yo, 18 * dims.nx, [own])
+    put_inverses(z_sends[0], 8, [own])
+
+
+def second_kernel(dims, n_z, inverse, couplings, first, *refs):
     recv, z_recv, refs = refs[:4], refs[4 : 4 + n_z], refs[4 + n_z :]
     second, sums, *sends = refs[:6]
-    z_sends, inverses = refs[6 : 6 + n_z], refs[6 + n_z]
+    z_sends = refs[6:]
     x_halo, y_halo = received(dims, recv)
     z_halo = ZHalo(dims, z_recv)
     for x in range(dims.nx):
@@ -268,16 +303,13 @@
             second[c, at, :] = (2.0 - DAMPING) * center[c] + step[c]
     put_faces(dims, (second,), sends)
     put_z(dims, second, z_sends)
-    at = 0
-    for piece in pieces:
-        inverses[at : at + piece.shape[0], :] = piece[:, 0, :]
-        at += piece.shape[0]
-    start = 18 * dims.nx
-    inverses[at : 2 * at, :] = recv[2][start : start + at, :]
+    even_block, odd_block = [r[18 * dims.nx : 18 * dims.nx + 36, :] for r in recv[2:]]
+    put_inverses(sends[2], 3 * dims.nx, [odd_block])
+    put_inverses(z_sends[0], 8, [even_block, odd_block])
 
 
 def coarse_kernel(dims, n_z, rhs, sums, couplings, second, ids, *refs):
-    recv, z_recv, (packet, resid) = refs[:4], refs[4 : 4 + n_z], refs[4 + n_z :]
+    recv, z_recv, (packets, packet, resid) = refs[:4], refs[4 : 4 + n_z], refs[4 + n_z :]
     x_halo, y_halo = received(dims, recv)
     z_halo = ZHalo(dims, z_recv)
     rest = 1.0 - DAMPING * (2.0 - DAMPING)
@@ -292,9 +324,11 @@
     modes = split3(jnp.where(row == 0, m0, jnp.where(row == 1, m1, 0.0)))
     for c in range(3):
         s = sum(dot_tt(modes, part) for part in parts3(resid[c]))
-        packet[0, 2 * c : 2 * c + 2, :] = (s[0:8] + (s[8:16] + s[16:24]))[0:2]
-    packet[0, 6:7, :] = pencil_row(dims, ids[0].astype(jnp.float32))
-    packet[0, 7:8, :] = jnp.zeros((1, dims.rows), jnp.float32)
+        packet[2 * c : 2 * c + 2, :] = (s[0:8] + (s[8:16] + s[16:24]))[0:2]
+    packet[6:7, :] = pencil_row(dims, ids[0].astype(jnp.float32))
+    packet[7:8, :] = jnp.zeros((1, dims.rows), jnp.float32)
+    for d in range(packets.shape[0]):
+        packets[d] = packet[...]
 
 
 def pencil_row(dims, square):
@@ -313,34 +347,75 @@
     return jnp.sum(jnp.where(keep, wide, 0.0), axis=0, keepdims=True)
 
 
-def gray(j):
-    return lax.bitwise_xor(j, lax.shift_right_logical(j, 1))
-
-
-def gray_inverse(v, bits):
-    out = v
-    for b in range(1, bits):
-        out = lax.bitwise_xor(out, lax.shift_right_logical(v, b))
-    return out
-
-
-def bits_of(n):
-    return max(1, (n - 1).bit_length())
-
-
-def solve_kernel(dims, sizes, own, packets, inverses, stack, y_z, coarse, correction):
+def partner(index, count, odd):
+    if odd:
+        return ((index + 1) % count ^ 1) - 1 + (((index + 1) % count ^ 1) == 0) * count
+    return index ^ 1
+
+
+def follow(index, count, word):
+    for odd in word:
+        index = partner(index, count, odd)
+    return index
+
+
+def words_of(count):
+    words, seen = [], set()
+    for length in range(count):
+        for start in (False, True):
+            word = tuple(bool(start) ^ bool(k % 2) for k in range(length))
+            to = follow(0, count, word)
+            if to not in seen:
+                seen.add(to)
+                words.append(word)
+    return words
+
+
+def blocks_of(n_y, n_z):
+    e, o, none = (False,), (True,), ()
+    held = [(none, none), (e, none), (o, none), (none, e), (e, e), (o, e), (e + o, none)]
+    found = {(follow(0, n_y, y), follow(0, n_z, z)) for y, z in held}
+    rest = []
+    for y in words_of(n_y):
+        for z in words_of(n_z):
+            at = (follow(0, n_y, y), follow(0, n_z, z))
+            if at not in found:
+                found.add(at)
+                rest.append((y, z))
+    return held, rest
+
+
+def solve_kernel(dims, sizes, own, packets, coarse_inv, *refs):
     n_y, n_z = sizes
     owners = n_y * n_z
     rows = dims.rows
+    held, rest = blocks_of(n_y, n_z)
+    pieces, refs = refs[: 5 + len(rest)], refs[5 + len(rest) :]
+    stack, y_z, coarse, correction, inverses = refs
+    put_inverses(inverses, 0, [coarse_inv[:, 0, :]])
+    at = 36
+    fat_ye, fat_yo, fat_z, thin_ye, thin_z = pieces[:5]
+    for ref, start, count in (
+        (fat_ye, 18 * dims.nx, 36),
+        (fat_yo, 18 * dims.nx, 36),
+        (fat_z, 8, 36),
+        (thin_z, 8, 72),
+        (thin_ye, 3 * dims.nx, 36),
+    ):
+        inverses[at : at + count, :] = ref[start : start + count, :]
+        at += count
+    for piece in pieces[5:]:
+        put_inverses(inverses, at, [piece[:, 0, :]])
+        at += 36
+    order = held + rest
     my_y, my_z = lax.axis_index("gy"), lax.axis_index("gz")
     local = row_iota(own, rows).astype(jnp.bfloat16)
     one_b = jnp.ones((own, rows), jnp.bfloat16)
     zero_b = jnp.zeros((own, rows), jnp.bfloat16)
 
     def owner_at(j):
-        jz = lax.rem(j, n_z)
-        jy = lax.div(j, n_z)
-        return lax.bitwise_xor(my_y, gray(jy)) * n_z + lax.bitwise_xor(my_z, gray(jz))
+        y, z = order[j]
+        return follow(my_y, n_y, y) * n_z + follow(my_z, n_z, z)
 
     def member(j, ids):
         base = (owner_at(j) * own).astype(jnp.float32)
@@ -375,9 +450,7 @@
         inside = (y >= 0) & (y < n_y) & (z >= 0) & (z < n_z)
         y = jnp.clip(y, 0, n_y - 1)
         z = jnp.clip(z, 0, n_z - 1)
-        jy = gray_inverse(lax.bitwise_xor(my_y, y), bits_of(n_y))
-        jz = gray_inverse(lax.bitwise_xor(my_z, z), bits_of(n_z))
-        return jnp.where(inside, packets[jy * n_z + jz, 6:7, :], -1.0)
+        return jnp.where(inside, packets[y * n_z + z, 6:7, :], -1.0)
 
     upper = lax.rem(lane_iota(1, rows), dims.ny) >= dims.ny // 2
 
@@ -430,8 +503,11 @@
     wide = pairs6_right(modes)
     last = pairs6_right(jnp.where(at == nz - 1, modes, 0.0))
     start = pairs6_right(jnp.where(at == 0, modes, 0.0))
+    my_x, n_x = lax.axis_index("gx"), lax.axis_size("gx")
     x_low = neighbour("gx", [s[:, side:] for s in stacks], False)
     x_high = neighbour("gx", [s[:, :side] for s in stacks], True)
+    x_low = jnp.where(my_x > 0, x_low, 0.0)
+    x_high = jnp.where(my_x < n_x - 1, x_high, 0.0)
     x_mix = jnp.where(lane_iota(4 * 8, side) < side // 2, x_high, x_low)
 
     def expand(v, ends=None):
@@ -545,47 +621,39 @@
             out[c, at, :] = first[c, at, :] + ((1.0 - DAMPING) * center[c] + step[c])
 
 
-def pairs_of(count, start):
-    out = []
-    for i in range(start, count - 1, 2):
-        out += [(i, i + 1), (i + 1, i)]
-    return out
-
-
-def swap(value, axis, start):
-    return lax.ppermute(value, axis, pairs_of(lax.axis_size(axis), start))
+def swap(value, axis, odd):
+    count = lax.axis_size(axis)
+    return lax.ppermute(value, axis, [(partner(i, count, odd), i) for i in range(count)])
 
 
 def exchange(sends, z_sends):
     xe, xo, ye, yo = sends
+    xe = swap(xe, "gx", 0)
     z_recv = [swap(v, "gz", k) for k, v in enumerate(z_sends)]
-    yo, ye = swap(yo, "gy", 1), swap(ye, "gy", 0)
-    xo, xe = swap(xo, "gx", 1), swap(xe, "gx", 0)
+    ye, yo = swap(ye, "gy", 0), swap(yo, "gy", 1)
+    xo = swap(xo, "gx", 1)
     return [xe, xo, ye, yo], z_recv
 
 
-def stages(axis, first=0):
-    masks = []
-    mask = 1
-    while mask < lax.axis_size(axis):
-        masks.append([(i, i ^ mask) for i in range(lax.axis_size(axis))])
-        mask = 2 * mask + 1
-    return masks[first:]
-
-
-def gather_along(value, axis, first=0):
-    for which in stages(axis, first):
-        value = jnp.concatenate([value, lax.ppermute(value, axis, which)], axis=0)
-    return value
-
-
-def call(body, name, out_shapes, scratch, *args):
+def fetch(value, word_y, word_z):
+    n_y, n_z = lax.axis_size("gy"), lax.axis_size("gz")
+    which = []
+    for y in range(n_y):
+        for z in range(n_z):
+            source = follow(y, n_y, word_y) * n_z + follow(z, n_z, word_z)
+            which.append((source, y * n_z + z))
+    return lax.ppermute(value, ("gy", "gz"), which)
+
+
+def call(body, name, out_shapes, scratch, *args, in_hbm=0):
+    near = pl.BlockSpec(memory_space=pltpu.VMEM)
+    far = pl.BlockSpec(memory_space=pl.ANY)
     return pl.pallas_call(
         body,
         name=name,
         out_shape=[jax.ShapeDtypeStruct(s, jnp.float32) for s in out_shapes],
-        in_specs=[pl.BlockSpec(memory_space=pltpu.VMEM)] * len(args),
-        out_specs=[pl.BlockSpec(memory_space=pltpu.VMEM)] * len(out_shapes),
+        in_specs=[far] * in_hbm + [near] * (len(args) - in_hbm),
+        out_specs=[near] * len(out_shapes),
         scratch_shapes=scratch,
         compiler_params=pltpu.CompilerParams(vmem_limit_bytes=VMEM_LIMIT),
     )(*args)
@@ -606,69 +674,71 @@
     part = functools.partial
     f32 = jnp.float32
 
-    def faces(count, extra=0):
-        return [(count * ny, nz)] * 2 + [(count * nx + extra, nz), (count * nx, nz)]
-
-    z_faces = [(8, nz)] * z_count
-    pieces = [coarse_inv]
-    for which in stages("gz"):
-        joined = jnp.concatenate(pieces, axis=0) if len(pieces) > 1 else pieces[0]
-        pieces.append(lax.ppermute(joined, "gz", which))
-    counts = (len(pieces), z_count)
-    inv_rows = 36 * n_z
-
-    first, inverse, *sends = call(
-        part(first_kernel, dims, counts),
+    def faces(count, even, odd):
+        return [(count * ny, nz)] * 2 + [(count * nx + even, nz), (count * nx + odd, nz)]
+
+    def z_faces(extra):
+        return [(8 + extra, nz)] + [(8, nz)] * (z_count - 1)
+
+    _, rest = blocks_of(n_y, n_z)
+    pieces = [fetch(coarse_inv, y, z) for y, z in rest]
+    first, inverse, rhs, couplings, *sends = call(
+        part(first_kernel, dims, z_count),
         "first",
-        [vector, (9, rows, nz)] + faces(18, inv_rows) + z_faces,
-        [],
+        [vector, (9, rows, nz), vector, (6, rows, nz)] + faces(18, 36, 36) + z_faces(36),
+        [pltpu.VMEM((9, rows, nz), f32), pltpu.SemaphoreType.DMA((2 * CHUNKS + 1,))],
         rhs,
         blocks,
         couplings,
-        *pieces,
-    )
-    fat, z_recv = exchange(sends[:4], sends[4:])
+        coarse_inv,
+        in_hbm=3,
+    )
+    fat, fat_z = exchange(sends[:4], sends[4:])
     second, sums, *sends = call(
-        part(second_kernel, dims, counts),
+        part(second_kernel, dims, z_count),
         "second",
-        [vector, vector] + faces(3) + z_faces + [(2 * inv_rows, own)],
+        [vector, vector] + faces(3, 36, 0) + z_faces(72),
         [],
         inverse,
         couplings,
         first,
-        *pieces,
         *fat,
-        *z_recv,
-    )
-    inverses = gather_along(sends[-1], "gy", 1)
-    thin, z_recv = exchange(sends[:4], sends[4:-1])
-    (packet,) = call(
+        *fat_z,
+    )
+    thin, thin_z = exchange(sends[:4], sends[4:])
+    (packets,) = call(
         part(coarse_kernel, dims, z_count),
         "coarse",
-        [(1, 8, rows)],
-        [pltpu.VMEM(vector, f32)],
+        [(owners, 8, rows)],
+        [pltpu.VMEM((8, rows), f32), pltpu.VMEM(vector, f32)],
         rhs,
         sums,
         couplings,
         second,
         agg_ids,
         *thin,
-        *z_recv,
-    )
-    packets = gather_along(gather_along(packet, "gz"), "gy")
+        *thin_z,
+    )
+    packets = lax.all_to_all(packets, ("gy", "gz"), 0, 0, tiled=True)
     stack, y_z = call(
         part(solve_kernel, dims, (n_y, n_z), own),
         "solve",
         [(4 * 8, rows), (2 * 8, rows)],
-        [pltpu.VMEM((owners * 8, own), f32)] * 2,
+        [pltpu.VMEM((owners * 8, own), f32)] * 2 + [pltpu.VMEM((owners * 36, own), f32)],
         packets,
-        inverses,
-    )
-    xo, xe = swap(stack, "gx", 1), swap(stack, "gx", 0)
+        coarse_inv,
+        fat[2],
+        fat[3],
+        fat_z[0],
+        thin[2],
+        thin_z[0],
+        *pieces,
+    )
+    xe, xo = swap(stack, "gx", 0), swap(stack, "gx", 1)
     third, x_third, y_third, *z_sends = call(
         part(third_kernel, dims, z_count),
         "third",
-        [vector, (2, 3 * ny, nz), (2, 3 * nx, nz)] + z_faces,
+        [vector, (2, 3 * ny, nz), (2, 3 * nx, nz)] + z_faces(0),
         [pltpu.VMEM(vector, f32)] * 4 + [pltpu.VMEM((3, rows // 2, nz), f32)] * 3,
         inverse,
         couplings,

time: 61.5 us -> 60 us (0.976)
  starting transfers between devices: 31.2 us -> 25 us
  local copies, waits for them, and re-layouts: 4.13 us -> 10.2 us
  Pallas kernels: 10.1 us -> 9.07 us
    ppermute x18 -> x14, starting transfers between devices: 31.2 us -> 21.1 us  [the longest x13 17.2 us: swap(): lax.ppermute(value, axis, [(partner(i, count, odd), i) for i in range(cou...]
    unnamed x14 -> x34, local copies, waits for them, and re-layouts: 4.13 us -> 10.2 us
    all_to_all x0 -> x1, starting transfers between devices: none -> 3.91 us  [shards(): packets = lax.all_to_all(packets, ('gy', 'gz'), 0, 0, tiled=True)]
    pallas_call x6, Pallas kernels: 10.1 us -> 9.07 us  [call(): pl.pallas_call(body, name=name, out_shape=[jax.ShapeDtypeStruct(s, jnp.fl...]
    ppermute x18 -> x14, waiting for transfers between devices: 15.5 us -> 14.8 us  [the longest x13 12.5 us: swap(): lax.ppermute(value, axis, [(partner(i, count, odd), i) for i in range(cou...]
  transfers between devices with their start and end apart: 18 -> 15, of which waited for: 9 -> 8; matrix products, arithmetic and copies ran while one was open for 0% -> 0% of each run, Pallas kernels for 0% -> 0%
where the time goes in v4:
time: 60 us; the launch traced here: 59.3 us
  starting transfers between devices  25 us (42%)
  waiting for transfers between devices  15 us (25%)
  local copies, waits for them, and re-layouts  10.2 us (17%)
  Pallas kernels  9.07 us (15%)
    ppermute x13, starting transfers between devices, swap(): lax.ppermute(value, axis, [(partner(i, count, odd), i) for i in range(cou...  17.2 us
    ppermute x13, waiting for transfers between devices, swap(): lax.ppermute(value, axis, [(partner(i, count, odd), i) for i in range(cou...  12.5 us
    unnamed x34, local copies, waits for them, and re-layouts  10.2 us
    pallas_call x6, Pallas kernels, call(): pl.pallas_call(body, name=name, out_shape=[jax.ShapeDtypeStruct(s, jnp.fl...  9.07 us
    all_to_all x1, starting transfers between devices, shards(): packets = lax.all_to_all(packets, ('gy', 'gz'), 0, 0, tiled=True)  3.91 us
    ppermute x1, starting transfers between devices, fetch(): return lax.ppermute(value, ('gy', 'gz'), which)  3.82 us
    ppermute x1, waiting for transfers between devices, fetch(): return lax.ppermute(value, ('gy', 'gz'), which)  2.29 us
  transfers between devices with their start and end apart: 15, of which 8 were waited for; matrix products, arithmetic and copies ran while one was open for 0% of the time, Pallas kernels for 0%

profile of v4, /device:TPU:0, one launch (start us, length us, event | category | flops | bytes accessed | tf_op | source)
XLA Modules:
  0.0 59.3 jit_solution(16639236017779935404)
XLA Ops:
  0.0 1.3 %copy-done = f32[9,16,16,128]{3,2,1,0:T(8,128)S(1)} copy-done((f32[9,16,16,128]{3,2,1,0:T(8,128)S(1)}, f32[9,16,16,128]{3,2,1,0:T(8,128)}, u32[]{:S(2)}) %copy-start) | copy-done | bytes 1179672
  1.3 1.1 %copy-done.1 = f32[6,16,16,128]{3,2,1,0:T(8,128)S(1)} copy-done((f32[6,16,16,128]{3,2,1,0:T(8,128)S(1)}, f32[6,16,16,128]{3,2,1,0:T(8,128)}, u32[]{:S(2)}) %copy-start.1) | copy-done | bytes 786456
  2.4 1.0 %copy-done.2 = f32[3,16,16,128]{3,2,1,0:T(8,128)S(1)} copy-done((f32[3,16,16,128]{3,2,1,0:T(8,128)S(1)}, f32[3,16,16,128]{3,2,1,0:T(8,128)}, u32[]{:S(2)}) %copy-start.2) | copy-done | bytes 393240
  4.1 1.0 %first.1 = (f32[3,256,128]{2,1,0:T(8,128)S(1)}, f32[9,256,128]{2,1,0:T(8,128)S(1)}, f32[3,256,128]{2,1,0:T(8,128)S(1)}, f32[6,256,128]{2,1,0:T(8,128)S(1)}, f32[...) custom-call(f32[3,256,128]{2,1,0:T(8,128)S(1)} %bitcast.6, ...), custom_call_target="tpu_custom_call" | custom-call | tf_op jit(solution)/shard_map/first/pallas_call | solution.py:651
  5.1 3.1 %collective-permute-start.2 = (f32[324,128]{1,0:T(8,128)S(1)}, f32[324,128]{1,0:T(8,128)S(1)}, u32[]{:S(2)}, u32[]{:S(2)}) collective-permute-start(f32[324,128]{1,0:T(8,128)S(1)} %get-tuple-element.32), channel_id=1, source_target_pairs={{2,0},{0,2},{6,4},{4,6},{3,1},{1,3},{7,5},{5,7},{10,8},{8,10},{14,... | collective-permute-start | bytes 497672 | tf_op jit(solution)/shard_map/ppermute | solution.py:626
  8.2 2.5 %collective-permute-start.3 = (f32[324,128]{1,0:T(8,128)S(1)}, f32[324,128]{1,0:T(8,128)S(1)}, u32[]{:S(2)}, u32[]{:S(2)}) collective-permute-start(f32[324,128]{1,0:T(8,128)S(1)} %get-tuple-element.33), channel_id=1, source_target_pairs={{6,0},{4,2},{2,4},{0,6},{7,1},{5,3},{3,5},{1,7},{14,8},{12,10},{10... | collective-permute-start | bytes 497672 | tf_op jit(solution)/shard_map/ppermute | solution.py:626
  10.7 1.6 %collective-permute-start.1 = (f32[288,128]{1,0:T(8,128)S(1)}, f32[288,128]{1,0:T(8,128)S(1)}, u32[]{:S(2)}, u32[]{:S(2)}) collective-permute-start(f32[288,128]{1,0:T(8,128)S(1)} %get-tuple-element.31), channel_id=1, source_target_pairs={{24,0},{16,8},{8,16},{0,24},{25,1},{17,9},{9,17},{1,25},{26,2},{18... | collective-permute-start | bytes 442376 | tf_op jit(solution)/shard_map/ppermute | solution.py:626
  12.4 1.5 %collective-permute-start.4 = (f32[44,128]{1,0:T(8,128)S(1)}, f32[44,128]{1,0:T(8,128)S(1)}, u32[]{:S(2)}, u32[]{:S(2)}) collective-permute-start(f32[44,128]{1,0:T(8,128)S(1)} %get-tuple-element.34), channel_id=1, source_target_pairs={{1,0},{0,1},{3,2},{2,3},{5,4},{4,5},{7,6},{6,7},{9,8},{8,9},{11,10... | collective-permute-start | bytes 67592 | tf_op jit(solution)/shard_map/ppermute | solution.py:626
  13.8 2.3 %collective-permute-done.4.refs_4_.refs_2_ = f32[44,128]{1,0:T(8,128)S(1)} collective-permute-done((f32[44,128]{1,0:T(8,128)S(1)}, f32[44,128]{1,0:T(8,128)S(1)}, u32[]{:S(2)}, u32[]{:S(2)}) %collective-permute-start.4) | collective-permute-done | bytes 22560 | tf_op jit(solution)/shard_map/ppermute | solution.py:626
  16.2 2.2 %collective-permute-done.3.refs_3_.refs_1_.refs_5_ = f32[324,128]{1,0:T(8,128)S(1)} collective-permute-done((f32[324,128]{1,0:T(8,128)S(1)}, f32[324,128]{1,0:T(8,128)S(1)}, u32[]{:S(2)}, u32[]{:S(2)}) %collective-permute-start.3) | collective-permute-done | bytes 165920 | tf_op jit(solution)/shard_map/ppermute | solution.py:626
  18.4 1.8 %second.1 = (f32[3,256,128]{2,1,0:T(8,128)S(1)}, f32[3,256,128]{2,1,0:T(8,128)S(1)}, f32[48,128]{1,0:T(8,128)S(1)}, f32[48,128]{1,0:T(8,128)S(1)}, f32[84,128]{1...) custom-call(f32[9,256,128]{2,1,0:T(8,128)S(1)} %get-tuple-element.27.inverse, ...), custom_call_target="tpu_custom_call" | custom-call | tf_op jit(solution)/shard_map/second/pallas_call | solution.py:651
  20.8 1.5 %collective-permute-start.9 = (f32[80,128]{1,0:T(8,128)S(1)}, f32[80,128]{1,0:T(8,128)S(1)}, u32[]{:S(2)}, u32[]{:S(2)}) collective-permute-start(f32[80,128]{1,0:T(8,128)S(1)} %get-tuple-element.42), channel_id=1, source_target_pairs={{1,0},{0,1},{3,2},{2,3},{5,4},{4,5},{7,6},{6,7},{9,8},{8,9},{11,10... | collective-permute-start | bytes 122888 | tf_op jit(solution)/shard_map/ppermute | solution.py:626
  22.3 1.6 %collective-permute-start.6 = (f32[48,128]{1,0:T(8,128)S(1)}, f32[48,128]{1,0:T(8,128)S(1)}, u32[]{:S(2)}, u32[]{:S(2)}) collective-permute-start(f32[48,128]{1,0:T(8,128)S(1)} %get-tuple-element.39), channel_id=1, source_target_pairs={{24,0},{16,8},{8,16},{0,24},{25,1},{17,9},{9,17},{1,25},{26,2},{18... | collective-permute-start | bytes 73736 | tf_op jit(solution)/shard_map/ppermute | solution.py:626
  23.9 2.6 %collective-permute-start.8 = (f32[48,128]{1,0:T(8,128)S(1)}, f32[48,128]{1,0:T(8,128)S(1)}, u32[]{:S(2)}, u32[]{:S(2)}) collective-permute-start(f32[48,128]{1,0:T(8,128)S(1)} %get-tuple-element.41), channel_id=1, source_target_pairs={{6,0},{4,2},{2,4},{0,6},{7,1},{5,3},{3,5},{1,7},{14,8},{12,10},{10... | collective-permute-start | bytes 73736 | tf_op jit(solution)/shard_map/ppermute | solution.py:626
  26.6 3.0 %collective-permute-done.8.refs_3_.refs_9_ = f32[48,128]{1,0:T(8,128)S(1)} collective-permute-done((f32[48,128]{1,0:T(8,128)S(1)}, f32[48,128]{1,0:T(8,128)S(1)}, u32[]{:S(2)}, u32[]{:S(2)}) %collective-permute-start.8) | collective-permute-done | bytes 24608 | tf_op jit(solution)/shard_map/ppermute | solution.py:626
  32.2 3.9 %all-to-all-start = ((f32[8,8,256]{2,1,0:T(8,128)}), f32[8,8,256]{2,1,0:T(8,128)S(1)}, u32[]{:S(2)}, u32[]{:S(2)}) async-start(f32[8,8,256]{2,1,0:T(8,128)} %copy-done.3), calls=%async_computation | async-start | bytes 131072 | tf_op jit(solution)/shard_map/all_to_all | solution.py:722
  36.2 3.8 %collective-permute-start.10 = (f32[36,1,128]{2,1,0:T(1,128)S(1)}, f32[36,1,128]{2,1,0:T(1,128)S(1)}, u32[]{:S(2)}, u32[]{:S(2)}) collective-permute-start(f32[36,1,128]{2,1,0:T(1,128)S(1)} %copy-done.13), channel_id=1, source_target_pairs={{5,0},{4,1},{7,2},{6,3},{1,4},{0,5},{3,6},{2,7},{13,8},{12,9},{15,... | collective-permute-start | bytes 55304 | tf_op jit(solution)/shard_map/ppermute | solution.py:645
  40.0 2.3 %collective-permute-done.10.refs_5_ = f32[36,1,128]{2,1,0:T(1,128)S(1)} collective-permute-done((f32[36,1,128]{2,1,0:T(1,128)S(1)}, f32[36,1,128]{2,1,0:T(1,128)S(1)}, u32[]{:S(2)}, u32[]{:S(2)}) %collective-permute-start.10) | collective-permute-done | bytes 18464 | tf_op jit(solution)/shard_map/ppermute | solution.py:645
  44.5 2.3 %solve.1 = (f32[32,256]{1,0:T(8,128)S(1)}, f32[16,256]{1,0:T(8,128)S(1)}) custom-call(f32[8,8,256]{2,1,0:T(8,128)S(1)} %all-to-all-done.packets, f32[36,1,128]{2,1,0:T(1,128)S(1)} %copy-done.13, f32[324,128]{1,0:T(8,128)S(1)} %collective-permute-done.2.refs_2_.refs_0_.refs_4_, f32[324,128]{1,0:T(8,128)S(1)} %collective-permute-done.3.refs_3_.refs_1_.refs_5_, ...), custom_call_target="tpu_custom_call" | custom-call | tf_op jit(solution)/shard_map/solve/pallas_call | solution.py:651
  48.1 2.2 %collective-permute-done.12.refs_1_ = f32[32,256]{1,0:T(8,128)S(1)} collective-permute-done((f32[32,256]{1,0:T(8,128)S(1)}, f32[32,256]{1,0:T(8,128)S(1)}, u32[]{:S(2)}, u32[]{:S(2)}) %collective-permute-start.12) | collective-permute-done | bytes 32800 | tf_op jit(solution)/shard_map/ppermute | solution.py:626
  52.6 1.1 %third.1 = (f32[3,256,128]{2,1,0:T(8,128)S(1)}, f32[2,48,128]{2,1,0:T(8,128)S(1)}, f32[2,48,128]{2,1,0:T(8,128)S(1)}, f32[8,128]{1,0:T(8,128)S(1)}) custom-call(f32[9,256,128]{2,1,0:T(8,128)S(1)} %get-tuple-element.27.inverse, f32[6,256,128]{2,1,0:T(8,128)S(1)} %get-tuple-element.28.couplings, f32[3,256,128]{2,1,0:T(8,128)S(1)} %get-tuple-element.35.second, ...), custom_call_target="tpu_custom_call" | custom-call | tf_op jit(solution)/shard_map/third/pallas_call | solution.py:651
  53.6 1.5 %collective-permute-start.13 = (f32[8,128]{1,0:T(8,128)S(1)}, f32[8,128]{1,0:T(8,128)S(1)}, u32[]{:S(2)}, u32[]{:S(2)}) collective-permute-start(f32[8,128]{1,0:T(8,128)S(1)} %get-tuple-element.48), channel_id=1, source_target_pairs={{1,0},{0,1},{3,2},{2,3},{5,4},{4,5},{7,6},{6,7},{9,8},{8,9},{11,10... | collective-permute-start | bytes 12296 | tf_op jit(solution)/shard_map/ppermute | solution.py:626
  55.1 2.1 %collective-permute-done.13.refs_0_ = f32[8,128]{1,0:T(8,128)S(1)} collective-permute-done((f32[8,128]{1,0:T(8,128)S(1)}, f32[8,128]{1,0:T(8,128)S(1)}, u32[]{:S(2)}, u32[]{:S(2)}) %collective-permute-start.13) | collective-permute-done | bytes 4128 | tf_op jit(solution)/shard_map/ppermute | solution.py:626
  57.2 2.1 %last.1 = f32[3,256,128]{2,1,0:T(8,128)} custom-call(f32[9,256,128]{2,1,0:T(8,128)S(1)} %get-tuple-element.27.inverse, f32[6,256,128]{2,1,0:T(8,128)S(1)} %get-tuple-element.28.couplings, f32[3,256,128]{2,1,0:T(8,128)S(1)} %get-tuple-element.29.first, f32[3,256,128]{2,1,0:T(8,128)S(1)} %get-tuple-element.45.third, ...), custom_call_target="tpu_custom_call" | custom-call | tf_op jit(solution)/shard_map/last/pallas_call | solution.py:651
  (46 shorter events, 9.7 us)
Async XLA Ops:
  0.0 1.3 %copy-start = (f32[9,16,16,128]{3,2,1,0:T(8,128)S(1)}, f32[9,16,16,128]{3,2,1,0:T(8,128)}, u32[]{:S(2)}) copy-start(f32[9,16,16,128]{3,2,1,0:T(8,128)} %param.6) | copy-start | bytes 3538948
  1.3 1.1 %copy-start.1 = (f32[6,16,16,128]{3,2,1,0:T(8,128)S(1)}, f32[6,16,16,128]{3,2,1,0:T(8,128)}, u32[]{:S(2)}) copy-start(f32[6,16,16,128]{3,2,1,0:T(8,128)} %param.7) | copy-start | bytes 2359300
  2.4 1.0 %copy-start.2 = (f32[3,16,16,128]{3,2,1,0:T(8,128)S(1)}, f32[3,16,16,128]{3,2,1,0:T(8,128)}, u32[]{:S(2)}) copy-start(f32[3,16,16,128]{3,2,1,0:T(8,128)} %param.5) | copy-start | bytes 1179652
  5.1 11.1 %collective-permute-start.2 = (f32[324,128]{1,0:T(8,128)S(1)}, f32[324,128]{1,0:T(8,128)S(1)}, u32[]{:S(2)}, u32[]{:S(2)}) collective-permute-start(f32[324,128]{1,0:T(8,128)S(1)} %get-tuple-element.32), channel_id=1, source_target_pairs={{2,0},{0,2},{6,4},{4,6},{3,1},{1,3},{7,5},{5,7},{10,8},{8,10},{14,... | collective-permute-start | bytes 497672 | tf_op jit(solution)/shard_map/ppermute | solution.py:626
  8.2 10.2 %collective-permute-start.3 = (f32[324,128]{1,0:T(8,128)S(1)}, f32[324,128]{1,0:T(8,128)S(1)}, u32[]{:S(2)}, u32[]{:S(2)}) collective-permute-start(f32[324,128]{1,0:T(8,128)S(1)} %get-tuple-element.33), channel_id=1, source_target_pairs={{6,0},{4,2},{2,4},{0,6},{7,1},{5,3},{3,5},{1,7},{14,8},{12,10},{10... | collective-permute-start | bytes 497672 | tf_op jit(solution)/shard_map/ppermute | solution.py:626
  10.7 5.5 %collective-permute-start = (f32[288,128]{1,0:T(8,128)S(1)}, f32[288,128]{1,0:T(8,128)S(1)}, u32[]{:S(2)}, u32[]{:S(2)}) collective-permute-start(f32[288,128]{1,0:T(8,128)S(1)} %get-tuple-element.30), channel_id=1, source_target_pairs={{8,0},{0,8},{24,16},{16,24},{9,1},{1,9},{25,17},{17,25},{10,2},{2,... | collective-permute-start | bytes 442376 | tf_op jit(solution)/shard_map/ppermute | solution.py:626
  10.7 5.5 %collective-permute-start.1 = (f32[288,128]{1,0:T(8,128)S(1)}, f32[288,128]{1,0:T(8,128)S(1)}, u32[]{:S(2)}, u32[]{:S(2)}) collective-permute-start(f32[288,128]{1,0:T(8,128)S(1)} %get-tuple-element.31), channel_id=1, source_target_pairs={{24,0},{16,8},{8,16},{0,24},{25,1},{17,9},{9,17},{1,25},{26,2},{18... | collective-permute-start | bytes 442376 | tf_op jit(solution)/shard_map/ppermute | solution.py:626
  12.4 3.8 %collective-permute-start.4 = (f32[44,128]{1,0:T(8,128)S(1)}, f32[44,128]{1,0:T(8,128)S(1)}, u32[]{:S(2)}, u32[]{:S(2)}) collective-permute-start(f32[44,128]{1,0:T(8,128)S(1)} %get-tuple-element.34), channel_id=1, source_target_pairs={{1,0},{0,1},{3,2},{2,3},{5,4},{4,5},{7,6},{6,7},{9,8},{8,9},{11,10... | collective-permute-start | bytes 67592 | tf_op jit(solution)/shard_map/ppermute | solution.py:626
  16.2 4.0 %copy-start.10 = (f32[44,128]{1,0:T(8,128)}, f32[44,128]{1,0:T(8,128)S(1)}, u32[]{:S(2)}) copy-start(f32[44,128]{1,0:T(8,128)S(1)} %collective-permute-done.4.refs_4_.refs_2_) | copy-start | bytes 67588
  18.4 11.1 %copy-start.16 = (s32[1,16,16]{2,1,0:T(8,128)S(1)}, s32[1,16,16]{2,1,0:T(8,128)}, u32[]{:S(2)}) copy-start(s32[1,16,16]{2,1,0:T(8,128)} %ids.1) | copy-start | bytes 3076
  20.2 15.9 %copy-start.13 = (f32[36,1,128]{2,1,0:T(1,128)S(1)}, f32[36,1,128]{2,1,0:T(1,128)}, u32[]{:S(2)}) copy-start(f32[36,1,128]{2,1,0:T(1,128)} %coarse_inv.1) | copy-start | bytes 55300
  20.2 9.4 %collective-permute-start.7 = (f32[84,128]{1,0:T(8,128)S(1)}, f32[84,128]{1,0:T(8,128)S(1)}, u32[]{:S(2)}, u32[]{:S(2)}) collective-permute-start(f32[84,128]{1,0:T(8,128)S(1)} %get-tuple-element.40), channel_id=1, source_target_pairs={{2,0},{0,2},{6,4},{4,6},{3,1},{1,3},{7,5},{5,7},{10,8},{8,10},{14,... | collective-permute-start | bytes 129032 | tf_op jit(solution)/shard_map/ppermute | solution.py:626
  20.8 8.8 %collective-permute-start.9 = (f32[80,128]{1,0:T(8,128)S(1)}, f32[80,128]{1,0:T(8,128)S(1)}, u32[]{:S(2)}, u32[]{:S(2)}) collective-permute-start(f32[80,128]{1,0:T(8,128)S(1)} %get-tuple-element.42), channel_id=1, source_target_pairs={{1,0},{0,1},{3,2},{2,3},{5,4},{4,5},{7,6},{6,7},{9,8},{8,9},{11,10... | collective-permute-start | bytes 122888 | tf_op jit(solution)/shard_map/ppermute | solution.py:626
  22.3 4.3 %collective-permute-start.5 = (f32[48,128]{1,0:T(8,128)S(1)}, f32[48,128]{1,0:T(8,128)S(1)}, u32[]{:S(2)}, u32[]{:S(2)}) collective-permute-start(f32[48,128]{1,0:T(8,128)S(1)} %get-tuple-element.38), channel_id=1, source_target_pairs={{8,0},{0,8},{24,16},{16,24},{9,1},{1,9},{25,17},{17,25},{10,2},{2,... | collective-permute-start | bytes 73736 | tf_op jit(solution)/shard_map/ppermute | solution.py:626
  22.3 4.3 %collective-permute-start.6 = (f32[48,128]{1,0:T(8,128)S(1)}, f32[48,128]{1,0:T(8,128)S(1)}, u32[]{:S(2)}, u32[]{:S(2)}) collective-permute-start(f32[48,128]{1,0:T(8,128)S(1)} %get-tuple-element.39), channel_id=1, source_target_pairs={{24,0},{16,8},{8,16},{0,24},{25,1},{17,9},{9,17},{1,25},{26,2},{18... | collective-permute-start | bytes 73736 | tf_op jit(solution)/shard_map/ppermute | solution.py:626
  23.9 5.6 %collective-permute-start.8 = (f32[48,128]{1,0:T(8,128)S(1)}, f32[48,128]{1,0:T(8,128)S(1)}, u32[]{:S(2)}, u32[]{:S(2)}) collective-permute-start(f32[48,128]{1,0:T(8,128)S(1)} %get-tuple-element.41), channel_id=1, source_target_pairs={{6,0},{4,2},{2,4},{0,6},{7,1},{5,3},{3,5},{1,7},{14,8},{12,10},{10... | collective-permute-start | bytes 73736 | tf_op jit(solution)/shard_map/ppermute | solution.py:626
  29.6 2.7 %copy-start.8 = (f32[48,128]{1,0:T(8,128)}, f32[48,128]{1,0:T(8,128)S(1)}, u32[]{:S(2)}) copy-start(f32[48,128]{1,0:T(8,128)S(1)} %collective-permute-done.8.refs_3_.refs_9_) | copy-start | bytes 73732
  32.2 10.8 %all-to-all-start = ((f32[8,8,256]{2,1,0:T(8,128)}), f32[8,8,256]{2,1,0:T(8,128)S(1)}, u32[]{:S(2)}, u32[]{:S(2)}) async-start(f32[8,8,256]{2,1,0:T(8,128)} %copy-done.3), calls=%async_computation | async-start | bytes 131072 | tf_op jit(solution)/shard_map/all_to_all | solution.py:722
  36.2 6.1 %collective-permute-start.10 = (f32[36,1,128]{2,1,0:T(1,128)S(1)}, f32[36,1,128]{2,1,0:T(1,128)S(1)}, u32[]{:S(2)}, u32[]{:S(2)}) collective-permute-start(f32[36,1,128]{2,1,0:T(1,128)S(1)} %copy-done.13), channel_id=1, source_target_pairs={{5,0},{4,1},{7,2},{6,3},{1,4},{0,5},{3,6},{2,7},{13,8},{12,9},{15,... | collective-permute-start | bytes 55304 | tf_op jit(solution)/shard_map/ppermute | solution.py:645
  43.1 0.7 %copy-start.11 = (f32[44,128]{1,0:T(8,128)S(1)}, f32[44,128]{1,0:T(8,128)}, u32[]{:S(2)}) copy-start(f32[44,128]{1,0:T(8,128)} %copy-done.10) | copy-start | bytes 67588
  46.9 1.3 %collective-permute-start.11 = (f32[32,256]{1,0:T(8,128)S(1)}, f32[32,256]{1,0:T(8,128)S(1)}, u32[]{:S(2)}, u32[]{:S(2)}) collective-permute-start(f32[32,256]{1,0:T(8,128)S(1)} %get-tuple-element.43.stack), channel_id=1, source_target_pairs={{8,0},{0,8},{24,16},{16,24},{9,1},{1,9},{25,17},{17,25},{10,2},{2,... | collective-permute-start | bytes 98312 | tf_op jit(solution)/shard_map/ppermute | solution.py:626
  46.9 3.4 %collective-permute-start.12 = (f32[32,256]{1,0:T(8,128)S(1)}, f32[32,256]{1,0:T(8,128)S(1)}, u32[]{:S(2)}, u32[]{:S(2)}) collective-permute-start(f32[32,256]{1,0:T(8,128)S(1)} %get-tuple-element.43.stack), channel_id=1, source_target_pairs={{24,0},{16,8},{8,16},{0,24},{25,1},{17,9},{9,17},{1,25},{26,2},{18... | collective-permute-start | bytes 98312 | tf_op jit(solution)/shard_map/ppermute | solution.py:626
  50.3 0.7 %copy-start.5 = (f32[48,128]{1,0:T(8,128)S(1)}, f32[48,128]{1,0:T(8,128)}, u32[]{:S(2)}) copy-start(f32[48,128]{1,0:T(8,128)} %copy-done.4) | copy-start | bytes 73732
  53.6 3.6 %collective-permute-start.13 = (f32[8,128]{1,0:T(8,128)S(1)}, f32[8,128]{1,0:T(8,128)S(1)}, u32[]{:S(2)}, u32[]{:S(2)}) collective-permute-start(f32[8,128]{1,0:T(8,128)S(1)} %get-tuple-element.48), channel_id=1, source_target_pairs={{1,0},{0,1},{3,2},{2,3},{5,4},{4,5},{7,6},{6,7},{9,8},{8,9},{11,10... | collective-permute-start | bytes 12296 | tf_op jit(solution)/shard_map/ppermute | solution.py:626
  (8 other events, 5.4 us)

commit v5 on v4

--- a/solution.py
+++ b/solution.py
@@ -250,9 +250,9 @@
 
 
 def first_kernel(dims, n_z, *refs):
-    rhs_in, blocks_in, couplings_in, coarse_inv = refs[:4]
-    first, inverse, rhs, couplings, xe, xo, ye, yo = refs[4:12]
-    z_sends, (blocks, sems) = refs[12 : 12 + n_z], refs[12 + n_z :]
+    rhs_in, blocks_in, couplings_in, coarse_inv_in, ids_in = refs[:5]
+    first, inverse, rhs, couplings, own, ids, xe, xo, ye, yo = refs[5:15]
+    z_sends, (blocks, coarse_inv, square, sems) = refs[15 : 15 + n_z], refs[15 + n_z :]
     step = dims.rows // CHUNKS
 
     def copy(k, src, dst, rows):
@@ -264,6 +264,8 @@
         copies.append(copy(2 * k, blocks_in, blocks, rows))
         copies.append(copy(2 * k + 1, rhs_in, rhs, rows))
     copies.append(copy(2 * CHUNKS, couplings_in, couplings, pl.ds(0, dims.rows)))
+    copies.append(pltpu.make_async_copy(coarse_inv_in, coarse_inv, sems.at[2 * CHUNKS + 1]))
+    copies.append(pltpu.make_async_copy(ids_in, square, sems.at[2 * CHUNKS + 2]))
     for c in copies:
         c.start()
     for x in range(dims.nx):
@@ -278,13 +280,15 @@
         v = times(inv, tiles(rhs, 3, x, dims.ny))
         for c in range(3):
             first[c, at, :] = v[c]
-    copies[-1].wait()
+    for c in copies[-3:]:
+        c.wait()
     put_faces(dims, (first, inverse, couplings), (xe, xo, ye, yo))
     put_z(dims, first, z_sends)
-    own = coarse_inv[:, 0, :]
-    put_inverses(ye, 18 * dims.nx, [own])
-    put_inverses(yo, 18 * dims.nx, [own])
-    put_inverses(z_sends[0], 8, [own])
+    own[...] = coarse_inv[:, 0, :]
+    put_inverses(ye, 18 * dims.nx, [own[...]])
+    put_inverses(yo, 18 * dims.nx, [own[...]])
+    put_inverses(z_sends[0], 8, [own[...]])
+    ids[...] = pencil_row(dims, square[0].astype(jnp.float32))
 
 
 def second_kernel(dims, n_z, inverse, couplings, first, *refs):
@@ -309,7 +313,7 @@
 
 
 def coarse_kernel(dims, n_z, rhs, sums, couplings, second, ids, *refs):
-    recv, z_recv, (packets, packet, resid) = refs[:4], refs[4 : 4 + n_z], refs[4 + n_z :]
+    recv, z_recv, (packet, resid) = refs[:4], refs[4 : 4 + n_z], refs[4 + n_z :]
     x_halo, y_halo = received(dims, recv)
     z_halo = ZHalo(dims, z_recv)
     rest = 1.0 - DAMPING * (2.0 - DAMPING)
@@ -324,11 +328,9 @@
     modes = split3(jnp.where(row == 0, m0, jnp.where(row == 1, m1, 0.0)))
     for c in range(3):
         s = sum(dot_tt(modes, part) for part in parts3(resid[c]))
-        packet[2 * c : 2 * c + 2, :] = (s[0:8] + (s[8:16] + s[16:24]))[0:2]
-    packet[6:7, :] = pencil_row(dims, ids[0].astype(jnp.float32))
-    packet[7:8, :] = jnp.zeros((1, dims.rows), jnp.float32)
-    for d in range(packets.shape[0]):
-        packets[d] = packet[...]
+        packet[0, 2 * c : 2 * c + 2, :] = (s[0:8] + (s[8:16] + s[16:24]))[0:2]
+    packet[0, 6:7, :] = ids[...]
+    packet[0, 7:8, :] = jnp.zeros((1, dims.rows), jnp.float32)
 
 
 def pencil_row(dims, square):
@@ -385,14 +387,16 @@
     return held, rest
 
 
-def solve_kernel(dims, sizes, own, packets, coarse_inv, *refs):
+def solve_kernel(dims, sizes, own, *refs):
     n_y, n_z = sizes
     owners = n_y * n_z
     rows = dims.rows
+    my_y, my_z = lax.axis_index("gy"), lax.axis_index("gz")
+    arrived, coarse_inv, refs = refs[:n_y], refs[n_y], refs[n_y + 1 :]
     held, rest = blocks_of(n_y, n_z)
     pieces, refs = refs[: 5 + len(rest)], refs[5 + len(rest) :]
-    stack, y_z, coarse, correction, inverses = refs
-    put_inverses(inverses, 0, [coarse_inv[:, 0, :]])
+    stack, y_z, coarse, correction, inverses, packets = refs
+    put_inverses(inverses, 0, [coarse_inv[...]])
     at = 36
     fat_ye, fat_yo, fat_z, thin_ye, thin_z = pieces[:5]
     for ref, start, count in (
@@ -408,7 +412,9 @@
         put_inverses(inverses, at, [piece[:, 0, :]])
         at += 36
     order = held + rest
-    my_y, my_z = lax.axis_index("gy"), lax.axis_index("gz")
+    for y, ref in zip(words_of(n_y), arrived):
+        for k, z in enumerate(words_of(n_z)):
+            packets[follow(my_y, n_y, y) * n_z + follow(my_z, n_z, z)] = ref[k]
     local = row_iota(own, rows).astype(jnp.bfloat16)
     one_b = jnp.ones((own, rows), jnp.bfloat16)
     zero_b = jnp.zeros((own, rows), jnp.bfloat16)
@@ -647,7 +653,7 @@
 
 def call(body, name, out_shapes, scratch, *args, in_hbm=0):
     near = pl.BlockSpec(memory_space=pltpu.VMEM)
-    far = pl.BlockSpec(memory_space=pl.ANY)
+    far = pl.BlockSpec(memory_space=pltpu.HBM)
     return pl.pallas_call(
         body,
         name=name,
@@ -682,16 +688,23 @@
 
     _, rest = blocks_of(n_y, n_z)
     pieces = [fetch(coarse_inv, y, z) for y, z in rest]
-    first, inverse, rhs, couplings, *sends = call(
+    first, inverse, rhs, couplings, own_inv, ids, *sends = call(
         part(first_kernel, dims, z_count),
         "first",
-        [vector, (9, rows, nz), vector, (6, rows, nz)] + faces(18, 36, 36) + z_faces(36),
-        [pltpu.VMEM((9, rows, nz), f32), pltpu.SemaphoreType.DMA((2 * CHUNKS + 1,))],
-        rhs,
-        blocks,
-        couplings,
-        coarse_inv,
-        in_hbm=3,
+        [vector, (9, rows, nz), vector, (6, rows, nz), (36, own), (1, rows)]
+        + faces(18, 36, 36)
+        + z_faces(36),
+        [
+            pltpu.VMEM((9, rows, nz), f32),
+            pltpu.VMEM(coarse_inv.shape, f32),
+            pltpu.VMEM(agg_ids.shape, jnp.int32),
+            pltpu.SemaphoreType.DMA((2 * CHUNKS + 3,)),
+        ],
+        *[
+            pltpu.with_memory_space_constraint(v, pltpu.HBM)
+            for v in (rhs, blocks, couplings, coarse_inv, agg_ids)
+        ],
+        in_hbm=5,
     )
     fat, fat_z = exchange(sends[:4], sends[4:])
     second, sums, *sends = call(
@@ -706,27 +719,30 @@
         *fat_z,
     )
     thin, thin_z = exchange(sends[:4], sends[4:])
-    (packets,) = call(
+    (packet,) = call(
         part(coarse_kernel, dims, z_count),
         "coarse",
-        [(owners, 8, rows)],
-        [pltpu.VMEM((8, rows), f32), pltpu.VMEM(vector, f32)],
+        [(1, 8, rows)],
+        [pltpu.VMEM(vector, f32)],
         rhs,
         sums,
         couplings,
         second,
-        agg_ids,
+        ids,
         *thin,
         *thin_z,
     )
-    packets = lax.all_to_all(packets, ("gy", "gz"), 0, 0, tiled=True)
+    z_words, y_words = words_of(n_z), words_of(n_y)
+    packet = jnp.concatenate([fetch(packet, (), z) if z else packet for z in z_words], axis=0)
+    packets = [fetch(packet, y, ()) if y else packet for y in y_words]
     stack, y_z = call(
         part(solve_kernel, dims, (n_y, n_z), own),
         "solve",
         [(4 * 8, rows), (2 * 8, rows)],
-        [pltpu.VMEM((owners * 8, own), f32)] * 2 + [pltpu.VMEM((owners * 36, own), f32)],
-        packets,
-        coarse_inv,
+        [pltpu.VMEM((owners * 8, own), f32)] * 2 + [pltpu.VMEM((owners * 36, own), f32)]
+        + [pltpu.VMEM((owners, 8, rows), f32)],
+        *packets,
+        own_inv,
         fat[2],
         fat[3],
         fat_z[0],

time: 60 us -> 51.4 us (0.86)
  local copies, waits for them, and re-layouts: 10.2 us -> 0.01 us
  waiting for transfers between devices: 15 us -> 20 us
  starting transfers between devices: 25 us -> 20.8 us
  Pallas kernels: 9.07 us -> 10.3 us
    unnamed x34 -> x2, local copies, waits for them, and re-layouts: 10.2 us -> 0.01 us
    ppermute x1 -> x5, waiting for transfers between devices: 2.29 us -> 6.45 us  [fetch(): return lax.ppermute(value, ('gy', 'gz'), which)]
    all_to_all x1 -> x0, starting transfers between devices: 3.91 us -> none  [shards(): packets = lax.all_to_all(packets, ('gy', 'gz'), 0, 0, tiled=True)]
    pallas_call x6, Pallas kernels: 9.07 us -> 10.3 us  [call(): pl.pallas_call(body, name=name, out_shape=[jax.ShapeDtypeStruct(s, jnp.fl...]
    ppermute x13, starting transfers between devices: 17.2 us -> 16.2 us  [swap(): lax.ppermute(value, axis, [(partner(i, count, odd), i) for i in range(cou...]
    ppermute x13, waiting for transfers between devices: 12.5 us -> 13.6 us  [swap(): lax.ppermute(value, axis, [(partner(i, count, odd), i) for i in range(cou...]
    ppermute x1 -> x5, starting transfers between devices: 3.82 us -> 4.68 us  [fetch(): return lax.ppermute(value, ('gy', 'gz'), which)]
  transfers between devices with their start and end apart: 15 -> 18, of which waited for: 8 -> 10; matrix products, arithmetic and copies ran while one was open for 0% -> 0% of each run, Pallas kernels for 0% -> 0%
where the time goes in v5:
time: 51.4 us; the launch traced here: 51.2 us
  starting transfers between devices  20.8 us (40%)
  waiting for transfers between devices  20 us (39%)
  Pallas kernels  10.3 us (20%)
    ppermute x13, starting transfers between devices, swap(): lax.ppermute(value, axis, [(partner(i, count, odd), i) for i in range(cou...  16.2 us
    ppermute x13, waiting for transfers between devices, swap(): lax.ppermute(value, axis, [(partner(i, count, odd), i) for i in range(cou...  13.6 us
    pallas_call x6, Pallas kernels, call(): pl.pallas_call(body, name=name, out_shape=[jax.ShapeDtypeStruct(s, jnp.fl...  10.3 us
    ppermute x5, waiting for transfers between devices, fetch(): return lax.ppermute(value, ('gy', 'gz'), which)  6.45 us
    ppermute x5, starting transfers between devices, fetch(): return lax.ppermute(value, ('gy', 'gz'), which)  4.68 us
  transfers between devices with their start and end apart: 18, of which 10 were waited for; matrix products, arithmetic and copies ran while one was open for 0% of the time, Pallas kernels for 0%

profile of v5, /device:TPU:0, one launch (start us, length us, event | category | flops | bytes accessed | tf_op | source)
XLA Modules:
  0.0 51.2 jit_solution(2950217156232518364)
XLA Ops:
  0.0 2.0 %first.1 = (f32[3,256,128]{2,1,0:T(8,128)S(1)}, f32[9,256,128]{2,1,0:T(8,128)S(1)}, f32[3,256,128]{2,1,0:T(8,128)S(1)}, f32[6,256,128]{2,1,0:T(8,128)S(1)}, f32[...) custom-call(f32[3,256,128]{2,1,0:T(8,128)} %bitcast.6, ...), custom_call_target="tpu_custom_call" | custom-call | tf_op jit(solution)/shard_map/first/pallas_call | solution.py:657
  2.0 3.1 %collective-permute-start.2 = (f32[324,128]{1,0:T(8,128)S(1)}, f32[324,128]{1,0:T(8,128)S(1)}, u32[]{:S(2)}, u32[]{:S(2)}) collective-permute-start(f32[324,128]{1,0:T(8,128)S(1)} %get-tuple-element.34), channel_id=1, source_target_pairs={{2,0},{0,2},{6,4},{4,6},{3,1},{1,3},{7,5},{5,7},{10,8},{8,10},{14,... | collective-permute-start | bytes 497672 | tf_op jit(solution)/shard_map/ppermute | solution.py:632
  5.2 2.5 %collective-permute-start.3 = (f32[324,128]{1,0:T(8,128)S(1)}, f32[324,128]{1,0:T(8,128)S(1)}, u32[]{:S(2)}, u32[]{:S(2)}) collective-permute-start(f32[324,128]{1,0:T(8,128)S(1)} %get-tuple-element.35), channel_id=1, source_target_pairs={{6,0},{4,2},{2,4},{0,6},{7,1},{5,3},{3,5},{1,7},{14,8},{12,10},{10... | collective-permute-start | bytes 497672 | tf_op jit(solution)/shard_map/ppermute | solution.py:632
  7.6 1.6 %collective-permute-start.1 = (f32[288,128]{1,0:T(8,128)S(1)}, f32[288,128]{1,0:T(8,128)S(1)}, u32[]{:S(2)}, u32[]{:S(2)}) collective-permute-start(f32[288,128]{1,0:T(8,128)S(1)} %get-tuple-element.33), channel_id=1, source_target_pairs={{24,0},{16,8},{8,16},{0,24},{25,1},{17,9},{9,17},{1,25},{26,2},{18... | collective-permute-start | bytes 442376 | tf_op jit(solution)/shard_map/ppermute | solution.py:632
  9.3 1.5 %collective-permute-start.4 = (f32[44,128]{1,0:T(8,128)S(1)}, f32[44,128]{1,0:T(8,128)S(1)}, u32[]{:S(2)}, u32[]{:S(2)}) collective-permute-start(f32[44,128]{1,0:T(8,128)S(1)} %get-tuple-element.36), channel_id=1, source_target_pairs={{1,0},{0,1},{3,2},{2,3},{5,4},{4,5},{7,6},{6,7},{9,8},{8,9},{11,10... | collective-permute-start | bytes 67592 | tf_op jit(solution)/shard_map/ppermute | solution.py:632
  10.8 2.3 %collective-permute-done.4.refs_4_.refs_7_ = f32[44,128]{1,0:T(8,128)S(1)} collective-permute-done((f32[44,128]{1,0:T(8,128)S(1)}, f32[44,128]{1,0:T(8,128)S(1)}, u32[]{:S(2)}, u32[]{:S(2)}) %collective-permute-start.4) | collective-permute-done | bytes 22560 | tf_op jit(solution)/shard_map/ppermute | solution.py:632
  13.1 2.2 %collective-permute-done.3.refs_3_.refs_6_.refs_5_ = f32[324,128]{1,0:T(8,128)S(1)} collective-permute-done((f32[324,128]{1,0:T(8,128)S(1)}, f32[324,128]{1,0:T(8,128)S(1)}, u32[]{:S(2)}, u32[]{:S(2)}) %collective-permute-start.3) | collective-permute-done | bytes 165920 | tf_op jit(solution)/shard_map/ppermute | solution.py:632
  15.3 1.8 %second.1 = (f32[3,256,128]{2,1,0:T(8,128)S(1)}, f32[3,256,128]{2,1,0:T(8,128)S(1)}, f32[48,128]{1,0:T(8,128)S(1)}, f32[48,128]{1,0:T(8,128)S(1)}, f32[84,128]{1...) custom-call(f32[9,256,128]{2,1,0:T(8,128)S(1)} %get-tuple-element.29.inverse, ...), custom_call_target="tpu_custom_call" | custom-call | tf_op jit(solution)/shard_map/second/pallas_call | solution.py:657
  17.7 1.5 %collective-permute-start.9 = (f32[80,128]{1,0:T(8,128)S(1)}, f32[80,128]{1,0:T(8,128)S(1)}, u32[]{:S(2)}, u32[]{:S(2)}) collective-permute-start(f32[80,128]{1,0:T(8,128)S(1)} %get-tuple-element.45), channel_id=1, source_target_pairs={{1,0},{0,1},{3,2},{2,3},{5,4},{4,5},{7,6},{6,7},{9,8},{8,9},{11,10... | collective-permute-start | bytes 122888 | tf_op jit(solution)/shard_map/ppermute | solution.py:632
  19.2 1.6 %collective-permute-start.6 = (f32[48,128]{1,0:T(8,128)S(1)}, f32[48,128]{1,0:T(8,128)S(1)}, u32[]{:S(2)}, u32[]{:S(2)}) collective-permute-start(f32[48,128]{1,0:T(8,128)S(1)} %get-tuple-element.42), channel_id=1, source_target_pairs={{24,0},{16,8},{8,16},{0,24},{25,1},{17,9},{9,17},{1,25},{26,2},{18... | collective-permute-start | bytes 73736 | tf_op jit(solution)/shard_map/ppermute | solution.py:632
  20.9 2.6 %collective-permute-start.8 = (f32[48,128]{1,0:T(8,128)S(1)}, f32[48,128]{1,0:T(8,128)S(1)}, u32[]{:S(2)}, u32[]{:S(2)}) collective-permute-start(f32[48,128]{1,0:T(8,128)S(1)} %get-tuple-element.44), channel_id=1, source_target_pairs={{6,0},{4,2},{2,4},{0,6},{7,1},{5,3},{3,5},{1,7},{14,8},{12,10},{10... | collective-permute-start | bytes 73736 | tf_op jit(solution)/shard_map/ppermute | solution.py:632
  23.5 3.0 %collective-permute-done.8.refs_3_.refs_9_ = f32[48,128]{1,0:T(8,128)S(1)} collective-permute-done((f32[48,128]{1,0:T(8,128)S(1)}, f32[48,128]{1,0:T(8,128)S(1)}, u32[]{:S(2)}, u32[]{:S(2)}) %collective-permute-start.8) | collective-permute-done | bytes 24608 | tf_op jit(solution)/shard_map/ppermute | solution.py:632
  26.5 0.8 %coarse.1 = f32[1,8,256]{2,1,0:T(8,128)S(1)} custom-call(f32[3,256,128]{2,1,0:T(8,128)S(1)} %get-tuple-element.38.rhs, f32[3,256,128]{2,1,0:T(8,128)S(1)} %get-tuple-element.39.sums, f32[6,256,128]{2,1,0:T(8,128)S(1)} %get-tuple-element.30.couplings, f32[3,256,128]{2,1,0:T(8,128)S(1)} %get-tuple-element.37.second, f32[1,256]{1,0:T(1,128)S(1)} %get-tuple-element.40.ids, ...), custom_call_target="tpu_custom_call" | custom-call | tf_op jit(solution)/shard_map/coarse/pallas_call | solution.py:657
  28.5 2.6 %collective-permute-done.10 = f32[1,8,256]{2,1,0:T(8,128)S(1)} collective-permute-done((f32[1,8,256]{2,1,0:T(8,128)S(1)}, f32[1,8,256]{2,1,0:T(8,128)S(1)}, u32[]{:S(2)}, u32[]{:S(2)}) %collective-permute-start.10) | collective-permute-done | bytes 8224 | tf_op jit(solution)/shard_map/ppermute | solution.py:651
  31.1 0.9 %collective-permute-start.11 = (f32[2,8,256]{2,1,0:T(8,128)S(1)}, f32[2,8,256]{2,1,0:T(8,128)S(1)}, u32[]{:S(2)}, u32[]{:S(2)}) collective-permute-start(f32[2,8,256]{2,1,0:T(8,128)S(1)} %pad_maximum_fusion.refs_0_), channel_id=1, source_target_pairs={{2,0},{3,1},{0,2},{1,3},{6,4},{7,5},{4,6},{5,7},{10,8},{11,9},{8,1... | collective-permute-start | bytes 49160 | tf_op jit(solution)/shard_map/ppermute | solution.py:651
  32.1 1.8 %collective-permute-start.12 = (f32[2,8,256]{2,1,0:T(8,128)S(1)}, f32[2,8,256]{2,1,0:T(8,128)S(1)}, u32[]{:S(2)}, u32[]{:S(2)}) collective-permute-start(f32[2,8,256]{2,1,0:T(8,128)S(1)} %pad_maximum_fusion.refs_0_), channel_id=1, source_target_pairs={{6,0},{7,1},{4,2},{5,3},{2,4},{3,5},{0,6},{1,7},{14,8},{15,9},{12,... | collective-permute-start | bytes 49160 | tf_op jit(solution)/shard_map/ppermute | solution.py:651
  33.8 0.8 %collective-permute-start.13 = (f32[2,8,256]{2,1,0:T(8,128)S(1)}, f32[2,8,256]{2,1,0:T(8,128)S(1)}, u32[]{:S(2)}, u32[]{:S(2)}) collective-permute-start(f32[2,8,256]{2,1,0:T(8,128)S(1)} %pad_maximum_fusion.refs_0_), channel_id=1, source_target_pairs={{4,0},{5,1},{6,2},{7,3},{0,4},{1,5},{2,6},{3,7},{12,8},{13,9},{14,... | collective-permute-start | bytes 49160 | tf_op jit(solution)/shard_map/ppermute | solution.py:651
  35.0 2.6 %collective-permute-done.12.refs_2_ = f32[2,8,256]{2,1,0:T(8,128)S(1)} collective-permute-done((f32[2,8,256]{2,1,0:T(8,128)S(1)}, f32[2,8,256]{2,1,0:T(8,128)S(1)}, u32[]{:S(2)}, u32[]{:S(2)}) %collective-permute-start.12) | collective-permute-done | bytes 16416 | tf_op jit(solution)/shard_map/ppermute | solution.py:651
  37.6 0.9 %collective-permute-done.13.refs_3_ = f32[2,8,256]{2,1,0:T(8,128)S(1)} collective-permute-done((f32[2,8,256]{2,1,0:T(8,128)S(1)}, f32[2,8,256]{2,1,0:T(8,128)S(1)}, u32[]{:S(2)}, u32[]{:S(2)}) %collective-permute-start.13) | collective-permute-done | bytes 16416 | tf_op jit(solution)/shard_map/ppermute | solution.py:651
  38.5 2.3 %solve.1 = (f32[32,256]{1,0:T(8,128)S(1)}, f32[16,256]{1,0:T(8,128)S(1)}) custom-call(f32[2,8,256]{2,1,0:T(8,128)S(1)} %pad_maximum_fusion.refs_0_, f32[2,8,256]{2,1,0:T(8,128)S(1)} %collective-permute-done.11.refs_1_, f32[2,8,256]{2,1,0:T(8,128)S(1)} %collective-permute-done.12.refs_2_, f32[2,8,256]{2,1,0:T(8,128)S(1)} %collective-permute-done.13.refs_3_, ...), custom_call_target="tpu_custom_call" | custom-call | tf_op jit(solution)/shard_map/solve/pallas_call | solution.py:657
  42.1 2.2 %collective-permute-done.16.refs_1_ = f32[32,256]{1,0:T(8,128)S(1)} collective-permute-done((f32[32,256]{1,0:T(8,128)S(1)}, f32[32,256]{1,0:T(8,128)S(1)}, u32[]{:S(2)}, u32[]{:S(2)}) %collective-permute-start.16) | collective-permute-done | bytes 32800 | tf_op jit(solution)/shard_map/ppermute | solution.py:632
  44.3 1.2 %third.1 = (f32[3,256,128]{2,1,0:T(8,128)S(1)}, f32[2,48,128]{2,1,0:T(8,128)S(1)}, f32[2,48,128]{2,1,0:T(8,128)S(1)}, f32[8,128]{1,0:T(8,128)S(1)}) custom-call(f32[9,256,128]{2,1,0:T(8,128)S(1)} %get-tuple-element.29.inverse, f32[6,256,128]{2,1,0:T(8,128)S(1)} %get-tuple-element.30.couplings, f32[3,256,128]{2,1,0:T(8,128)S(1)} %get-tuple-element.37.second, ...), custom_call_target="tpu_custom_call" | custom-call | tf_op jit(solution)/shard_map/third/pallas_call | solution.py:657
  45.9 3.2 %collective-permute-done.17.refs_0_ = f32[8,128]{1,0:T(8,128)S(1)} collective-permute-done((f32[8,128]{1,0:T(8,128)S(1)}, f32[8,128]{1,0:T(8,128)S(1)}, u32[]{:S(2)}, u32[]{:S(2)}) %collective-permute-start.17) | collective-permute-done | bytes 4128 | tf_op jit(solution)/shard_map/ppermute | solution.py:632
  49.1 2.1 %last.1 = f32[3,256,128]{2,1,0:T(8,128)} custom-call(f32[9,256,128]{2,1,0:T(8,128)S(1)} %get-tuple-element.29.inverse, f32[6,256,128]{2,1,0:T(8,128)S(1)} %get-tuple-element.30.couplings, f32[3,256,128]{2,1,0:T(8,128)S(1)} %get-tuple-element.31.first, f32[3,256,128]{2,1,0:T(8,128)S(1)} %get-tuple-element.49.third, ...), custom_call_target="tpu_custom_call" | custom-call | tf_op jit(solution)/shard_map/last/pallas_call | solution.py:657
  (21 shorter events, 3.9 us)
Async XLA Ops:
  2.0 11.1 %collective-permute-start.2 = (f32[324,128]{1,0:T(8,128)S(1)}, f32[324,128]{1,0:T(8,128)S(1)}, u32[]{:S(2)}, u32[]{:S(2)}) collective-permute-start(f32[324,128]{1,0:T(8,128)S(1)} %get-tuple-element.34), channel_id=1, source_target_pairs={{2,0},{0,2},{6,4},{4,6},{3,1},{1,3},{7,5},{5,7},{10,8},{8,10},{14,... | collective-permute-start | bytes 497672 | tf_op jit(solution)/shard_map/ppermute | solution.py:632
  5.2 10.2 %collective-permute-start.3 = (f32[324,128]{1,0:T(8,128)S(1)}, f32[324,128]{1,0:T(8,128)S(1)}, u32[]{:S(2)}, u32[]{:S(2)}) collective-permute-start(f32[324,128]{1,0:T(8,128)S(1)} %get-tuple-element.35), channel_id=1, source_target_pairs={{6,0},{4,2},{2,4},{0,6},{7,1},{5,3},{3,5},{1,7},{14,8},{12,10},{10... | collective-permute-start | bytes 497672 | tf_op jit(solution)/shard_map/ppermute | solution.py:632
  7.6 5.5 %collective-permute-start = (f32[288,128]{1,0:T(8,128)S(1)}, f32[288,128]{1,0:T(8,128)S(1)}, u32[]{:S(2)}, u32[]{:S(2)}) collective-permute-start(f32[288,128]{1,0:T(8,128)S(1)} %get-tuple-element.32), channel_id=1, source_target_pairs={{8,0},{0,8},{24,16},{16,24},{9,1},{1,9},{25,17},{17,25},{10,2},{2,... | collective-permute-start | bytes 442376 | tf_op jit(solution)/shard_map/ppermute | solution.py:632
  7.6 5.5 %collective-permute-start.1 = (f32[288,128]{1,0:T(8,128)S(1)}, f32[288,128]{1,0:T(8,128)S(1)}, u32[]{:S(2)}, u32[]{:S(2)}) collective-permute-start(f32[288,128]{1,0:T(8,128)S(1)} %get-tuple-element.33), channel_id=1, source_target_pairs={{24,0},{16,8},{8,16},{0,24},{25,1},{17,9},{9,17},{1,25},{26,2},{18... | collective-permute-start | bytes 442376 | tf_op jit(solution)/shard_map/ppermute | solution.py:632
  9.3 3.8 %collective-permute-start.4 = (f32[44,128]{1,0:T(8,128)S(1)}, f32[44,128]{1,0:T(8,128)S(1)}, u32[]{:S(2)}, u32[]{:S(2)}) collective-permute-start(f32[44,128]{1,0:T(8,128)S(1)} %get-tuple-element.36), channel_id=1, source_target_pairs={{1,0},{0,1},{3,2},{2,3},{5,4},{4,5},{7,6},{6,7},{9,8},{8,9},{11,10... | collective-permute-start | bytes 67592 | tf_op jit(solution)/shard_map/ppermute | solution.py:632
  17.1 10.8 %copy-start = (f32[36,1,128]{2,1,0:T(1,128)S(1)}, f32[36,1,128]{2,1,0:T(1,128)}, u32[]{:S(2)}) copy-start(f32[36,1,128]{2,1,0:T(1,128)} %refs_3_.1) | copy-start | bytes 55300
  17.1 9.3 %collective-permute-start.7 = (f32[84,128]{1,0:T(8,128)S(1)}, f32[84,128]{1,0:T(8,128)S(1)}, u32[]{:S(2)}, u32[]{:S(2)}) collective-permute-start(f32[84,128]{1,0:T(8,128)S(1)} %get-tuple-element.43), channel_id=1, source_target_pairs={{2,0},{0,2},{6,4},{4,6},{3,1},{1,3},{7,5},{5,7},{10,8},{8,10},{14,... | collective-permute-start | bytes 129032 | tf_op jit(solution)/shard_map/ppermute | solution.py:632
  17.7 8.8 %collective-permute-start.9 = (f32[80,128]{1,0:T(8,128)S(1)}, f32[80,128]{1,0:T(8,128)S(1)}, u32[]{:S(2)}, u32[]{:S(2)}) collective-permute-start(f32[80,128]{1,0:T(8,128)S(1)} %get-tuple-element.45), channel_id=1, source_target_pairs={{1,0},{0,1},{3,2},{2,3},{5,4},{4,5},{7,6},{6,7},{9,8},{8,9},{11,10... | collective-permute-start | bytes 122888 | tf_op jit(solution)/shard_map/ppermute | solution.py:632
  19.2 4.3 %collective-permute-start.5 = (f32[48,128]{1,0:T(8,128)S(1)}, f32[48,128]{1,0:T(8,128)S(1)}, u32[]{:S(2)}, u32[]{:S(2)}) collective-permute-start(f32[48,128]{1,0:T(8,128)S(1)} %get-tuple-element.41), channel_id=1, source_target_pairs={{8,0},{0,8},{24,16},{16,24},{9,1},{1,9},{25,17},{17,25},{10,2},{2,... | collective-permute-start | bytes 73736 | tf_op jit(solution)/shard_map/ppermute | solution.py:632
  19.2 4.3 %collective-permute-start.6 = (f32[48,128]{1,0:T(8,128)S(1)}, f32[48,128]{1,0:T(8,128)S(1)}, u32[]{:S(2)}, u32[]{:S(2)}) collective-permute-start(f32[48,128]{1,0:T(8,128)S(1)} %get-tuple-element.42), channel_id=1, source_target_pairs={{24,0},{16,8},{8,16},{0,24},{25,1},{17,9},{9,17},{1,25},{26,2},{18... | collective-permute-start | bytes 73736 | tf_op jit(solution)/shard_map/ppermute | solution.py:632
  20.9 5.6 %collective-permute-start.8 = (f32[48,128]{1,0:T(8,128)S(1)}, f32[48,128]{1,0:T(8,128)S(1)}, u32[]{:S(2)}, u32[]{:S(2)}) collective-permute-start(f32[48,128]{1,0:T(8,128)S(1)} %get-tuple-element.44), channel_id=1, source_target_pairs={{6,0},{4,2},{2,4},{0,6},{7,1},{5,3},{3,5},{1,7},{14,8},{12,10},{10... | collective-permute-start | bytes 73736 | tf_op jit(solution)/shard_map/ppermute | solution.py:632
  27.3 3.8 %collective-permute-start.10 = (f32[1,8,256]{2,1,0:T(8,128)S(1)}, f32[1,8,256]{2,1,0:T(8,128)S(1)}, u32[]{:S(2)}, u32[]{:S(2)}) collective-permute-start(f32[1,8,256]{2,1,0:T(8,128)S(1)} %coarse.1), channel_id=1, source_target_pairs={{1,0},{0,1},{3,2},{2,3},{5,4},{4,5},{7,6},{6,7},{9,8},{8,9},{11,10... | collective-permute-start | bytes 24584 | tf_op jit(solution)/shard_map/ppermute | solution.py:651
  27.9 6.7 %collective-permute-start.14 = (f32[36,1,128]{2,1,0:T(1,128)S(1)}, f32[36,1,128]{2,1,0:T(1,128)S(1)}, u32[]{:S(2)}, u32[]{:S(2)}) collective-permute-start(f32[36,1,128]{2,1,0:T(1,128)S(1)} %copy-done), channel_id=1, source_target_pairs={{5,0},{4,1},{7,2},{6,3},{1,4},{0,5},{3,6},{2,7},{13,8},{12,9},{15,... | collective-permute-start | bytes 55304 | tf_op jit(solution)/shard_map/ppermute | solution.py:651
  31.1 3.9 %collective-permute-start.11 = (f32[2,8,256]{2,1,0:T(8,128)S(1)}, f32[2,8,256]{2,1,0:T(8,128)S(1)}, u32[]{:S(2)}, u32[]{:S(2)}) collective-permute-start(f32[2,8,256]{2,1,0:T(8,128)S(1)} %pad_maximum_fusion.refs_0_), channel_id=1, source_target_pairs={{2,0},{3,1},{0,2},{1,3},{6,4},{7,5},{4,6},{5,7},{10,8},{11,9},{8,1... | collective-permute-start | bytes 49160 | tf_op jit(solution)/shard_map/ppermute | solution.py:651
  32.1 5.5 %collective-permute-start.12 = (f32[2,8,256]{2,1,0:T(8,128)S(1)}, f32[2,8,256]{2,1,0:T(8,128)S(1)}, u32[]{:S(2)}, u32[]{:S(2)}) collective-permute-start(f32[2,8,256]{2,1,0:T(8,128)S(1)} %pad_maximum_fusion.refs_0_), channel_id=1, source_target_pairs={{6,0},{7,1},{4,2},{5,3},{2,4},{3,5},{0,6},{1,7},{14,8},{15,9},{12,... | collective-permute-start | bytes 49160 | tf_op jit(solution)/shard_map/ppermute | solution.py:651
  33.8 4.6 %collective-permute-start.13 = (f32[2,8,256]{2,1,0:T(8,128)S(1)}, f32[2,8,256]{2,1,0:T(8,128)S(1)}, u32[]{:S(2)}, u32[]{:S(2)}) collective-permute-start(f32[2,8,256]{2,1,0:T(8,128)S(1)} %pad_maximum_fusion.refs_0_), channel_id=1, source_target_pairs={{4,0},{5,1},{6,2},{7,3},{0,4},{1,5},{2,6},{3,7},{12,8},{13,9},{14,... | collective-permute-start | bytes 49160 | tf_op jit(solution)/shard_map/ppermute | solution.py:651
  40.8 1.3 %collective-permute-start.15 = (f32[32,256]{1,0:T(8,128)S(1)}, f32[32,256]{1,0:T(8,128)S(1)}, u32[]{:S(2)}, u32[]{:S(2)}) collective-permute-start(f32[32,256]{1,0:T(8,128)S(1)} %get-tuple-element.47.stack), channel_id=1, source_target_pairs={{8,0},{0,8},{24,16},{16,24},{9,1},{1,9},{25,17},{17,25},{10,2},{2,... | collective-permute-start | bytes 98312 | tf_op jit(solution)/shard_map/ppermute | solution.py:632
  40.9 3.4 %collective-permute-start.16 = (f32[32,256]{1,0:T(8,128)S(1)}, f32[32,256]{1,0:T(8,128)S(1)}, u32[]{:S(2)}, u32[]{:S(2)}) collective-permute-start(f32[32,256]{1,0:T(8,128)S(1)} %get-tuple-element.47.stack), channel_id=1, source_target_pairs={{24,0},{16,8},{8,16},{0,24},{25,1},{17,9},{9,17},{1,25},{26,2},{18... | collective-permute-start | bytes 98312 | tf_op jit(solution)/shard_map/ppermute | solution.py:632
  45.5 3.6 %collective-permute-start.17 = (f32[8,128]{1,0:T(8,128)S(1)}, f32[8,128]{1,0:T(8,128)S(1)}, u32[]{:S(2)}, u32[]{:S(2)}) collective-permute-start(f32[8,128]{1,0:T(8,128)S(1)} %get-tuple-element.52), channel_id=1, source_target_pairs={{1,0},{0,1},{3,2},{2,3},{5,4},{4,5},{7,6},{6,7},{9,8},{8,9},{11,10... | collective-permute-start | bytes 12296 | tf_op jit(solution)/shard_map/ppermute | solution.py:632

commit v6 on v5

--- a/solution.py
+++ b/solution.py
@@ -160,34 +160,27 @@
     return jnp.where(even, e, o) if high else jnp.where(even, o, e)
 
 
-class ZHalo:
-    def __init__(self, dims, recv):
-        self.dims = dims
-        self.recv = [r[0:8, :] for r in recv]
-        if len(recv) == 2:
-            self.low = neighbour("gz", self.recv, False)
-            self.high = neighbour("gz", self.recv, True)
-        else:
-            self.low = self.high = None
-            self.at = jnp.where(is_even("gz"), 0, dims.nz - 1)
-            self.moved = pltpu.roll(self.recv[0], self.at, 1)
-
-    def tile(self, c, x):
-        dims = self.dims
-        nz = dims.nz
-        lane = lane_iota(8, nz)
-        per = dims.ny // 8
-        out = []
-        for g in range(x * per, (x + 1) * per):
-            at = c * dims.groups + g
-            if self.low is None:
-                v = pltpu.roll(self.moved, (nz - at) % nz, 1)
-                out.append(jnp.where(lane == self.at, v, 0.0))
+def place_z(dims, recv, out):
+    nz = dims.nz
+    lane = lane_iota(8, nz)
+    recv = [r[0:8, :] for r in recv]
+    if len(recv) == 2:
+        low, high = neighbour("gz", recv, False), neighbour("gz", recv, True)
+    else:
+        at = jnp.where(is_even("gz"), 0, nz - 1)
+        moved = pltpu.roll(recv[0], at, 1)
+    for c in range(3):
+        for g in range(dims.groups):
+            k = c * dims.groups + g
+            if len(recv) == 2:
+                v = jnp.where(
+                    lane == nz - 1,
+                    pltpu.roll(low, (nz - 1 - k) % nz, 1),
+                    pltpu.roll(high, (nz - k) % nz, 1),
+                )
             else:
-                low = pltpu.roll(self.low, (nz - 1 - at) % nz, 1)
-                high = pltpu.roll(self.high, (nz - at) % nz, 1)
-                out.append(jnp.where(lane == nz - 1, low, high))
-        return jnp.concatenate(out, axis=0) if per > 1 else out[0]
+                v = jnp.where(lane == at, pltpu.roll(moved, (nz - k) % nz, 1), 0.0)
+            out[c, 8 * g : 8 * g + 8, :] = v
 
 
 def shifted(v, low, high, axis):
@@ -215,7 +208,7 @@
         low = tile(field, c, x - 1, ny) if x > 0 else x_halo(c, False)
         high = tile(field, c, x + 1, ny) if x < nx - 1 else x_halo(c, True)
         y_pair = shifted(center[c], y_halo(c, x, False), y_halo(c, x, True), 0)
-        z = z_halo.tile(c, x)
+        z = tile(z_halo, c, x, ny)
         z_pair = shifted(center[c], z, z, 1)
         out.append(beside(coup, (low, high), y_pair, z_pair))
     return center, out
@@ -294,9 +287,9 @@
 def second_kernel(dims, n_z, inverse, couplings, first, *refs):
     recv, z_recv, refs = refs[:4], refs[4 : 4 + n_z], refs[4 + n_z :]
     second, sums, *sends = refs[:6]
-    z_sends = refs[6:]
+    z_sends, z_halo = refs[6:-1], refs[-1]
     x_halo, y_halo = received(dims, recv)
-    z_halo = ZHalo(dims, z_recv)
+    place_z(dims, z_recv, z_halo)
     for x in range(dims.nx):
         coup = tiles(couplings, 6, x, dims.ny)
         center, total = sums_at(dims, x, first, x_halo, y_halo, z_halo, coup)
@@ -313,9 +306,11 @@
 
 
 def coarse_kernel(dims, n_z, rhs, sums, couplings, second, ids, *refs):
-    recv, z_recv, (packet, resid) = refs[:4], refs[4 : 4 + n_z], refs[4 + n_z :]
+    half = dims.rows // 2
+    recv, z_recv, refs = refs[:4], refs[4 : 4 + n_z], refs[4 + n_z :]
+    packet, resid, z_halo = refs
     x_halo, y_halo = received(dims, recv)
-    z_halo = ZHalo(dims, z_recv)
+    place_z(dims, z_recv, z_halo)
     rest = 1.0 - DAMPING * (2.0 - DAMPING)
     for x in range(dims.nx):
         coup = tiles(couplings, 6, x, dims.ny)
@@ -328,9 +323,13 @@
     modes = split3(jnp.where(row == 0, m0, jnp.where(row == 1, m1, 0.0)))
     for c in range(3):
         s = sum(dot_tt(modes, part) for part in parts3(resid[c]))
-        packet[0, 2 * c : 2 * c + 2, :] = (s[0:8] + (s[8:16] + s[16:24]))[0:2]
-    packet[0, 6:7, :] = ids[...]
-    packet[0, 7:8, :] = jnp.zeros((1, dims.rows), jnp.float32)
+        s = (s[0:8] + (s[8:16] + s[16:24]))[0:2]
+        packet[2 * c : 2 * c + 2, :] = s[:, :half]
+        packet[8 + 2 * c : 10 + 2 * c, :] = s[:, half:]
+    for k in range(2):
+        packet[8 * k + 6 : 8 * k + 7, :] = ids[:, k * half : (k + 1) * half]
+        packet[8 * k + 7 : 8 * k + 8, :] = jnp.zeros((1, half), jnp.float32)
+    put_inverses(packet, 16, [recv[2][3 * dims.nx : 3 * dims.nx + 36, :]])
 
 
 def pencil_row(dims, square):
@@ -375,7 +374,7 @@
 
 def blocks_of(n_y, n_z):
     e, o, none = (False,), (True,), ()
-    held = [(none, none), (e, none), (o, none), (none, e), (e, e), (o, e), (e + o, none)]
+    held = [(none, none), (e, none), (o, none), (none, e), (e, e), (o, e), (e + o, none), (e + o, e)]
     found = {(follow(0, n_y, y), follow(0, n_z, z)) for y, z in held}
     rest = []
     for y in words_of(n_y):
@@ -394,27 +393,31 @@
     my_y, my_z = lax.axis_index("gy"), lax.axis_index("gz")
     arrived, coarse_inv, refs = refs[:n_y], refs[n_y], refs[n_y + 1 :]
     held, rest = blocks_of(n_y, n_z)
-    pieces, refs = refs[: 5 + len(rest)], refs[5 + len(rest) :]
+    pieces, refs = refs[: 6 + len(rest)], refs[6 + len(rest) :]
     stack, y_z, coarse, correction, inverses, packets = refs
     put_inverses(inverses, 0, [coarse_inv[...]])
     at = 36
-    fat_ye, fat_yo, fat_z, thin_ye, thin_z = pieces[:5]
+    fat_ye, fat_yo, fat_z, thin_ye, thin_z, first_z = pieces[:6]
     for ref, start, count in (
         (fat_ye, 18 * dims.nx, 36),
         (fat_yo, 18 * dims.nx, 36),
         (fat_z, 8, 36),
         (thin_z, 8, 72),
         (thin_ye, 3 * dims.nx, 36),
+        (first_z, 16, 36),
     ):
         inverses[at : at + count, :] = ref[start : start + count, :]
         at += count
-    for piece in pieces[5:]:
+    for piece in pieces[6:]:
         put_inverses(inverses, at, [piece[:, 0, :]])
         at += 36
     order = held + rest
     for y, ref in zip(words_of(n_y), arrived):
         for k, z in enumerate(words_of(n_z)):
-            packets[follow(my_y, n_y, y) * n_z + follow(my_z, n_z, z)] = ref[k]
+            at = follow(my_y, n_y, y) * n_z + follow(my_z, n_z, z)
+            for side in range(2):
+                v = ref[16 * k + 8 * side : 16 * k + 8 * side + 8, :]
+                packets[at, :, side * rows // 2 : (side + 1) * rows // 2] = v
     local = row_iota(own, rows).astype(jnp.bfloat16)
     one_b = jnp.ones((own, rows), jnp.bfloat16)
     zero_b = jnp.zeros((own, rows), jnp.bfloat16)
@@ -608,7 +611,9 @@
 
 
 def last_kernel(dims, inverse, couplings, first, third, x_third, y_third, *refs):
-    z_recv, out = refs[:-1], refs[-1]
+    z_recv, (out, z_halo, result, sems) = refs[:-4], refs[-4:]
+    copies = []
+    step = dims.nx // CHUNKS
     nx, ny = dims.nx, dims.ny
 
     def x_halo(c, high):
@@ -617,14 +622,21 @@
     def y_halo(c, x, high):
         return y_third[int(high), c * nx + x : c * nx + x + 1, :]
 
-    z_halo = ZHalo(dims, z_recv)
+    place_z(dims, z_recv, z_halo)
     for x in range(nx):
         coup = tiles(couplings, 6, x, ny)
         center, total = sums_at(dims, x, third, x_halo, y_halo, z_halo, coup)
-        step = times(tiles(inverse, 9, x, ny), total)
+        change = times(tiles(inverse, 9, x, ny), total)
         at = rows_at(dims, x)
         for c in range(3):
-            out[c, at, :] = first[c, at, :] + ((1.0 - DAMPING) * center[c] + step[c])
+            result[c, at, :] = first[c, at, :] + ((1.0 - DAMPING) * center[c] + change[c])
+        if (x + 1) % step == 0:
+            at = pl.ds((x + 1 - step) * ny, step * ny)
+            copy = (result.at[:, at, :], out.at[:, at, :], sems.at[x // step])
+            copies.append(pltpu.make_async_copy(*copy))
+            copies[-1].start()
+    for copy in copies:
+        copy.wait()
 
 
 def swap(value, axis, odd):
@@ -651,7 +663,7 @@
     return lax.ppermute(value, ("gy", "gz"), which)
 
 
-def call(body, name, out_shapes, scratch, *args, in_hbm=0):
+def call(body, name, out_shapes, scratch, *args, in_hbm=0, out_hbm=False):
     near = pl.BlockSpec(memory_space=pltpu.VMEM)
     far = pl.BlockSpec(memory_space=pltpu.HBM)
     return pl.pallas_call(
@@ -659,7 +671,7 @@
         name=name,
         out_shape=[jax.ShapeDtypeStruct(s, jnp.float32) for s in out_shapes],
         in_specs=[far] * in_hbm + [near] * (len(args) - in_hbm),
-        out_specs=[near] * len(out_shapes),
+        out_specs=[far if out_hbm else near] * len(out_shapes),
         scratch_shapes=scratch,
         compiler_params=pltpu.CompilerParams(vmem_limit_bytes=VMEM_LIMIT),
     )(*args)
@@ -711,7 +723,7 @@
         part(second_kernel, dims, z_count),
         "second",
         [vector, vector] + faces(3, 36, 0) + z_faces(72),
-        [],
+        [pltpu.VMEM(vector, f32)],
         inverse,
         couplings,
         first,
@@ -722,8 +734,8 @@
     (packet,) = call(
         part(coarse_kernel, dims, z_count),
         "coarse",
-        [(1, 8, rows)],
-        [pltpu.VMEM(vector, f32)],
+        [(16 + 36, rows // 2)],
+        [pltpu.VMEM(vector, f32)] * 2,
         rhs,
         sums,
         couplings,
@@ -733,7 +745,10 @@
         *thin_z,
     )
     z_words, y_words = words_of(n_z), words_of(n_y)
-    packet = jnp.concatenate([fetch(packet, (), z) if z else packet for z in z_words], axis=0)
+    first_z = fetch(packet, (), z_words[1])
+    packet = packet[:16]
+    others = [fetch(packet, (), z) for z in z_words[2:]]
+    packet = jnp.concatenate([packet, first_z[:16]] + others, axis=0)
     packets = [fetch(packet, y, ()) if y else packet for y in y_words]
     stack, y_z = call(
         part(solve_kernel, dims, (n_y, n_z), own),
@@ -748,6 +763,7 @@
         fat_z[0],
         thin[2],
         thin_z[0],
+        first_z,
         *pieces,
     )
     xe, xo = swap(stack, "gx", 0), swap(stack, "gx", 1)
@@ -771,7 +787,7 @@
         part(last_kernel, dims),
         "last",
         [vector],
-        [],
+        [pltpu.VMEM(vector, f32)] * 2 + [pltpu.SemaphoreType.DMA((CHUNKS,))],
         inverse,
         couplings,
         first,
@@ -779,6 +795,7 @@
         x_third,
         y_third,
         *z_recv,
+        out_hbm=True,
     )
     return out.reshape(3, nx, ny, nz)
 

time: 51.4 us -> 48.8 us (0.949)
  Pallas kernels: 10.3 us -> 8.53 us
    pallas_call x6, Pallas kernels: 10.3 us -> 8.53 us  [call(): pl.pallas_call(body, name=name, out_shape=[jax.ShapeDtypeStruct(s, jnp.fl...]
    ppermute x5 -> x4, starting transfers between devices: 4.68 us -> 4.09 us  [fetch(): return lax.ppermute(value, ('gy', 'gz'), which)]
    ppermute x5 -> x4, waiting for transfers between devices: 6.45 us -> 6.29 us  [fetch(): return lax.ppermute(value, ('gy', 'gz'), which)]
  transfers between devices with their start and end apart: 18 -> 17, of which waited for: 10 -> 9; matrix products, arithmetic and copies ran while one was open for 0% -> 0% of each run, Pallas kernels for 0% -> 0%
where the time goes in v6:
time: 48.8 us; the launch traced here: 48.6 us
  starting transfers between devices  20.4 us (42%)
  waiting for transfers between devices  19.6 us (40%)
  Pallas kernels  8.53 us (17%)
    ppermute x13, starting transfers between devices, swap(): lax.ppermute(value, axis, [(partner(i, count, odd), i) for i in range(cou...  16.3 us
    ppermute x13, waiting for transfers between devices, swap(): lax.ppermute(value, axis, [(partner(i, count, odd), i) for i in range(cou...  13.3 us
    pallas_call x6, Pallas kernels, call(): pl.pallas_call(body, name=name, out_shape=[jax.ShapeDtypeStruct(s, jnp.fl...  8.53 us
    ppermute x4, waiting for transfers between devices, fetch(): return lax.ppermute(value, ('gy', 'gz'), which)  6.29 us
    ppermute x4, starting transfers between devices, fetch(): return lax.ppermute(value, ('gy', 'gz'), which)  4.09 us
  transfers between devices with their start and end apart: 17, of which 9 were waited for; matrix products, arithmetic and copies ran while one was open for 0% of the time, Pallas kernels for 0%

profile of v6, /device:TPU:0, one launch (start us, length us, event | category | flops | bytes accessed | tf_op | source)
XLA Modules:
  0.0 48.6 jit_solution(14157797148590851861)
XLA Ops:
  0.0 2.0 %first.1 = (f32[3,256,128]{2,1,0:T(8,128)S(1)}, f32[9,256,128]{2,1,0:T(8,128)S(1)}, f32[3,256,128]{2,1,0:T(8,128)S(1)}, f32[6,256,128]{2,1,0:T(8,128)S(1)}, f32[...) custom-call(f32[3,256,128]{2,1,0:T(8,128)} %bitcast.6, ...), custom_call_target="tpu_custom_call" | custom-call | tf_op jit(solution)/shard_map/first/pallas_call | solution.py:669
  2.0 3.1 %collective-permute-start.2 = (f32[324,128]{1,0:T(8,128)S(1)}, f32[324,128]{1,0:T(8,128)S(1)}, u32[]{:S(2)}, u32[]{:S(2)}) collective-permute-start(f32[324,128]{1,0:T(8,128)S(1)} %get-tuple-element.34), channel_id=1, source_target_pairs={{2,0},{0,2},{6,4},{4,6},{3,1},{1,3},{7,5},{5,7},{10,8},{8,10},{14,... | collective-permute-start | bytes 497672 | tf_op jit(solution)/shard_map/ppermute | solution.py:644
  5.2 2.5 %collective-permute-start.3 = (f32[324,128]{1,0:T(8,128)S(1)}, f32[324,128]{1,0:T(8,128)S(1)}, u32[]{:S(2)}, u32[]{:S(2)}) collective-permute-start(f32[324,128]{1,0:T(8,128)S(1)} %get-tuple-element.35), channel_id=1, source_target_pairs={{6,0},{4,2},{2,4},{0,6},{7,1},{5,3},{3,5},{1,7},{14,8},{12,10},{10... | collective-permute-start | bytes 497672 | tf_op jit(solution)/shard_map/ppermute | solution.py:644
  7.6 1.6 %collective-permute-start.1 = (f32[288,128]{1,0:T(8,128)S(1)}, f32[288,128]{1,0:T(8,128)S(1)}, u32[]{:S(2)}, u32[]{:S(2)}) collective-permute-start(f32[288,128]{1,0:T(8,128)S(1)} %get-tuple-element.33), channel_id=1, source_target_pairs={{24,0},{16,8},{8,16},{0,24},{25,1},{17,9},{9,17},{1,25},{26,2},{18... | collective-permute-start | bytes 442376 | tf_op jit(solution)/shard_map/ppermute | solution.py:644
  9.3 1.5 %collective-permute-start.4 = (f32[44,128]{1,0:T(8,128)S(1)}, f32[44,128]{1,0:T(8,128)S(1)}, u32[]{:S(2)}, u32[]{:S(2)}) collective-permute-start(f32[44,128]{1,0:T(8,128)S(1)} %get-tuple-element.36), channel_id=1, source_target_pairs={{1,0},{0,1},{3,2},{2,3},{5,4},{4,5},{7,6},{6,7},{9,8},{8,9},{11,10... | collective-permute-start | bytes 67592 | tf_op jit(solution)/shard_map/ppermute | solution.py:644
  10.8 2.3 %collective-permute-done.4.refs_4_.refs_7_ = f32[44,128]{1,0:T(8,128)S(1)} collective-permute-done((f32[44,128]{1,0:T(8,128)S(1)}, f32[44,128]{1,0:T(8,128)S(1)}, u32[]{:S(2)}, u32[]{:S(2)}) %collective-permute-start.4) | collective-permute-done | bytes 22560 | tf_op jit(solution)/shard_map/ppermute | solution.py:644
  13.1 2.2 %collective-permute-done.3.refs_3_.refs_6_.refs_5_ = f32[324,128]{1,0:T(8,128)S(1)} collective-permute-done((f32[324,128]{1,0:T(8,128)S(1)}, f32[324,128]{1,0:T(8,128)S(1)}, u32[]{:S(2)}, u32[]{:S(2)}) %collective-permute-start.3) | collective-permute-done | bytes 165920 | tf_op jit(solution)/shard_map/ppermute | solution.py:644
  15.3 0.8 %second.1 = (f32[3,256,128]{2,1,0:T(8,128)S(1)}, f32[3,256,128]{2,1,0:T(8,128)S(1)}, f32[48,128]{1,0:T(8,128)S(1)}, f32[48,128]{1,0:T(8,128)S(1)}, f32[84,128]{1...) custom-call(f32[9,256,128]{2,1,0:T(8,128)S(1)} %get-tuple-element.29.inverse, ...), custom_call_target="tpu_custom_call" | custom-call | tf_op jit(solution)/shard_map/second/pallas_call | solution.py:669
  16.8 1.5 %collective-permute-start.9 = (f32[80,128]{1,0:T(8,128)S(1)}, f32[80,128]{1,0:T(8,128)S(1)}, u32[]{:S(2)}, u32[]{:S(2)}) collective-permute-start(f32[80,128]{1,0:T(8,128)S(1)} %get-tuple-element.45), channel_id=1, source_target_pairs={{1,0},{0,1},{3,2},{2,3},{5,4},{4,5},{7,6},{6,7},{9,8},{8,9},{11,10... | collective-permute-start | bytes 122888 | tf_op jit(solution)/shard_map/ppermute | solution.py:644
  18.3 1.6 %collective-permute-start.6 = (f32[48,128]{1,0:T(8,128)S(1)}, f32[48,128]{1,0:T(8,128)S(1)}, u32[]{:S(2)}, u32[]{:S(2)}) collective-permute-start(f32[48,128]{1,0:T(8,128)S(1)} %get-tuple-element.42), channel_id=1, source_target_pairs={{24,0},{16,8},{8,16},{0,24},{25,1},{17,9},{9,17},{1,25},{26,2},{18... | collective-permute-start | bytes 73736 | tf_op jit(solution)/shard_map/ppermute | solution.py:644
  19.9 2.6 %collective-permute-start.8 = (f32[48,128]{1,0:T(8,128)S(1)}, f32[48,128]{1,0:T(8,128)S(1)}, u32[]{:S(2)}, u32[]{:S(2)}) collective-permute-start(f32[48,128]{1,0:T(8,128)S(1)} %get-tuple-element.44), channel_id=1, source_target_pairs={{6,0},{4,2},{2,4},{0,6},{7,1},{5,3},{3,5},{1,7},{14,8},{12,10},{10... | collective-permute-start | bytes 73736 | tf_op jit(solution)/shard_map/ppermute | solution.py:644
  22.5 3.0 %collective-permute-done.8.refs_3_.refs_9_ = f32[48,128]{1,0:T(8,128)S(1)} collective-permute-done((f32[48,128]{1,0:T(8,128)S(1)}, f32[48,128]{1,0:T(8,128)S(1)}, u32[]{:S(2)}, u32[]{:S(2)}) %collective-permute-start.8) | collective-permute-done | bytes 24608 | tf_op jit(solution)/shard_map/ppermute | solution.py:644
  25.5 0.8 %coarse.1 = f32[52,128]{1,0:T(8,128)S(1)} custom-call(f32[3,256,128]{2,1,0:T(8,128)S(1)} %get-tuple-element.38.rhs, f32[3,256,128]{2,1,0:T(8,128)S(1)} %get-tuple-element.39.sums, f32[6,256,128]{2,1,0:T(8,128)S(1)} %get-tuple-element.30.couplings, f32[3,256,128]{2,1,0:T(8,128)S(1)} %get-tuple-element.37.second, f32[1,256]{1,0:T(1,128)S(1)} %get-tuple-element.40.ids, ...), custom_call_target="tpu_custom_call" | custom-call | tf_op jit(solution)/shard_map/coarse/pallas_call | solution.py:669
  27.0 3.3 %collective-permute-done.10.refs_10_ = f32[52,128]{1,0:T(8,128)S(1)} collective-permute-done((f32[52,128]{1,0:T(8,128)S(1)}, f32[52,128]{1,0:T(8,128)S(1)}, u32[]{:S(2)}, u32[]{:S(2)}) %collective-permute-start.10) | collective-permute-done | bytes 26656 | tf_op jit(solution)/shard_map/ppermute | solution.py:663
  30.3 2.7 %collective-permute-start.12 = (f32[32,128]{1,0:T(8,128)S(1)}, f32[32,128]{1,0:T(8,128)S(1)}, u32[]{:S(2)}, u32[]{:S(2)}) collective-permute-start(f32[32,128]{1,0:T(8,128)S(1)} %pad_maximum_fusion.refs_0_), channel_id=1, source_target_pairs={{6,0},{7,1},{4,2},{5,3},{2,4},{3,5},{0,6},{1,7},{14,8},{15,9},{12,... | collective-permute-start | bytes 49160 | tf_op jit(solution)/shard_map/ppermute | solution.py:663
  33.0 0.8 %collective-permute-start.11 = (f32[32,128]{1,0:T(8,128)S(1)}, f32[32,128]{1,0:T(8,128)S(1)}, u32[]{:S(2)}, u32[]{:S(2)}) collective-permute-start(f32[32,128]{1,0:T(8,128)S(1)} %pad_maximum_fusion.refs_0_), channel_id=1, source_target_pairs={{2,0},{3,1},{0,2},{1,3},{6,4},{7,5},{4,6},{5,7},{10,8},{11,9},{8,1... | collective-permute-start | bytes 49160 | tf_op jit(solution)/shard_map/ppermute | solution.py:663
  33.8 1.1 %collective-permute-done.13.refs_3_ = f32[32,128]{1,0:T(8,128)S(1)} collective-permute-done((f32[32,128]{1,0:T(8,128)S(1)}, f32[32,128]{1,0:T(8,128)S(1)}, u32[]{:S(2)}, u32[]{:S(2)}) %collective-permute-start.13) | collective-permute-done | bytes 16416 | tf_op jit(solution)/shard_map/ppermute | solution.py:663
  34.9 1.0 %collective-permute-done.12.refs_2_ = f32[32,128]{1,0:T(8,128)S(1)} collective-permute-done((f32[32,128]{1,0:T(8,128)S(1)}, f32[32,128]{1,0:T(8,128)S(1)}, u32[]{:S(2)}, u32[]{:S(2)}) %collective-permute-start.12) | collective-permute-done | bytes 16416 | tf_op jit(solution)/shard_map/ppermute | solution.py:663
  35.9 0.8 %collective-permute-done.11.refs_1_ = f32[32,128]{1,0:T(8,128)S(1)} collective-permute-done((f32[32,128]{1,0:T(8,128)S(1)}, f32[32,128]{1,0:T(8,128)S(1)}, u32[]{:S(2)}, u32[]{:S(2)}) %collective-permute-start.11) | collective-permute-done | bytes 16416 | tf_op jit(solution)/shard_map/ppermute | solution.py:663
  36.7 2.3 %solve.1 = (f32[32,256]{1,0:T(8,128)S(1)}, f32[16,256]{1,0:T(8,128)S(1)}) custom-call(f32[32,128]{1,0:T(8,128)S(1)} %pad_maximum_fusion.refs_0_, f32[32,128]{1,0:T(8,128)S(1)} %collective-permute-done.11.refs_1_, f32[32,128]{1,0:T(8,128)S(1)} %collective-permute-done.12.refs_2_, f32[32,128]{1,0:T(8,128)S(1)} %collective-permute-done.13.refs_3_, ...), custom_call_target="tpu_custom_call" | custom-call | tf_op jit(solution)/shard_map/solve/pallas_call | solution.py:669
  39.8 2.7 %collective-permute-done.15.refs_1_ = f32[32,256]{1,0:T(8,128)S(1)} collective-permute-done((f32[32,256]{1,0:T(8,128)S(1)}, f32[32,256]{1,0:T(8,128)S(1)}, u32[]{:S(2)}, u32[]{:S(2)}) %collective-permute-start.15) | collective-permute-done | bytes 32800 | tf_op jit(solution)/shard_map/ppermute | solution.py:644
  42.5 1.1 %third.1 = (f32[3,256,128]{2,1,0:T(8,128)S(1)}, f32[2,48,128]{2,1,0:T(8,128)S(1)}, f32[2,48,128]{2,1,0:T(8,128)S(1)}, f32[8,128]{1,0:T(8,128)S(1)}) custom-call(f32[9,256,128]{2,1,0:T(8,128)S(1)} %get-tuple-element.29.inverse, f32[6,256,128]{2,1,0:T(8,128)S(1)} %get-tuple-element.30.couplings, f32[3,256,128]{2,1,0:T(8,128)S(1)} %get-tuple-element.37.second, ...), custom_call_target="tpu_custom_call" | custom-call | tf_op jit(solution)/shard_map/third/pallas_call | solution.py:669
  44.2 3.1 %collective-permute-done.16.refs_0_ = f32[8,128]{1,0:T(8,128)S(1)} collective-permute-done((f32[8,128]{1,0:T(8,128)S(1)}, f32[8,128]{1,0:T(8,128)S(1)}, u32[]{:S(2)}, u32[]{:S(2)}) %collective-permute-start.16) | collective-permute-done | bytes 4128 | tf_op jit(solution)/shard_map/ppermute | solution.py:644
  47.3 1.3 %last.1 = f32[3,256,128]{2,1,0:T(8,128)} custom-call(f32[9,256,128]{2,1,0:T(8,128)S(1)} %get-tuple-element.29.inverse, f32[6,256,128]{2,1,0:T(8,128)S(1)} %get-tuple-element.30.couplings, f32[3,256,128]{2,1,0:T(8,128)S(1)} %get-tuple-element.31.first, f32[3,256,128]{2,1,0:T(8,128)S(1)} %get-tuple-element.49.third, ...), custom_call_target="tpu_custom_call" | custom-call | tf_op jit(solution)/shard_map/last/pallas_call | solution.py:669
  (19 shorter events, 2.5 us)
Async XLA Ops:
  2.0 11.1 %collective-permute-start.2 = (f32[324,128]{1,0:T(8,128)S(1)}, f32[324,128]{1,0:T(8,128)S(1)}, u32[]{:S(2)}, u32[]{:S(2)}) collective-permute-start(f32[324,128]{1,0:T(8,128)S(1)} %get-tuple-element.34), channel_id=1, source_target_pairs={{2,0},{0,2},{6,4},{4,6},{3,1},{1,3},{7,5},{5,7},{10,8},{8,10},{14,... | collective-permute-start | bytes 497672 | tf_op jit(solution)/shard_map/ppermute | solution.py:644
  5.2 10.2 %collective-permute-start.3 = (f32[324,128]{1,0:T(8,128)S(1)}, f32[324,128]{1,0:T(8,128)S(1)}, u32[]{:S(2)}, u32[]{:S(2)}) collective-permute-start(f32[324,128]{1,0:T(8,128)S(1)} %get-tuple-element.35), channel_id=1, source_target_pairs={{6,0},{4,2},{2,4},{0,6},{7,1},{5,3},{3,5},{1,7},{14,8},{12,10},{10... | collective-permute-start | bytes 497672 | tf_op jit(solution)/shard_map/ppermute | solution.py:644
  7.6 5.5 %collective-permute-start = (f32[288,128]{1,0:T(8,128)S(1)}, f32[288,128]{1,0:T(8,128)S(1)}, u32[]{:S(2)}, u32[]{:S(2)}) collective-permute-start(f32[288,128]{1,0:T(8,128)S(1)} %get-tuple-element.32), channel_id=1, source_target_pairs={{8,0},{0,8},{24,16},{16,24},{9,1},{1,9},{25,17},{17,25},{10,2},{2,... | collective-permute-start | bytes 442376 | tf_op jit(solution)/shard_map/ppermute | solution.py:644
  7.6 5.5 %collective-permute-start.1 = (f32[288,128]{1,0:T(8,128)S(1)}, f32[288,128]{1,0:T(8,128)S(1)}, u32[]{:S(2)}, u32[]{:S(2)}) collective-permute-start(f32[288,128]{1,0:T(8,128)S(1)} %get-tuple-element.33), channel_id=1, source_target_pairs={{24,0},{16,8},{8,16},{0,24},{25,1},{17,9},{9,17},{1,25},{26,2},{18... | collective-permute-start | bytes 442376 | tf_op jit(solution)/shard_map/ppermute | solution.py:644
  9.3 3.8 %collective-permute-start.4 = (f32[44,128]{1,0:T(8,128)S(1)}, f32[44,128]{1,0:T(8,128)S(1)}, u32[]{:S(2)}, u32[]{:S(2)}) collective-permute-start(f32[44,128]{1,0:T(8,128)S(1)} %get-tuple-element.36), channel_id=1, source_target_pairs={{1,0},{0,1},{3,2},{2,3},{5,4},{4,5},{7,6},{6,7},{9,8},{8,9},{11,10... | collective-permute-start | bytes 67592 | tf_op jit(solution)/shard_map/ppermute | solution.py:644
  16.2 9.3 %collective-permute-start.7 = (f32[84,128]{1,0:T(8,128)S(1)}, f32[84,128]{1,0:T(8,128)S(1)}, u32[]{:S(2)}, u32[]{:S(2)}) collective-permute-start(f32[84,128]{1,0:T(8,128)S(1)} %get-tuple-element.43), channel_id=1, source_target_pairs={{2,0},{0,2},{6,4},{4,6},{3,1},{1,3},{7,5},{5,7},{10,8},{8,10},{14,... | collective-permute-start | bytes 129032 | tf_op jit(solution)/shard_map/ppermute | solution.py:644
  16.8 8.8 %collective-permute-start.9 = (f32[80,128]{1,0:T(8,128)S(1)}, f32[80,128]{1,0:T(8,128)S(1)}, u32[]{:S(2)}, u32[]{:S(2)}) collective-permute-start(f32[80,128]{1,0:T(8,128)S(1)} %get-tuple-element.45), channel_id=1, source_target_pairs={{1,0},{0,1},{3,2},{2,3},{5,4},{4,5},{7,6},{6,7},{9,8},{8,9},{11,10... | collective-permute-start | bytes 122888 | tf_op jit(solution)/shard_map/ppermute | solution.py:644
  18.3 4.3 %collective-permute-start.5 = (f32[48,128]{1,0:T(8,128)S(1)}, f32[48,128]{1,0:T(8,128)S(1)}, u32[]{:S(2)}, u32[]{:S(2)}) collective-permute-start(f32[48,128]{1,0:T(8,128)S(1)} %get-tuple-element.41), channel_id=1, source_target_pairs={{8,0},{0,8},{24,16},{16,24},{9,1},{1,9},{25,17},{17,25},{10,2},{2,... | collective-permute-start | bytes 73736 | tf_op jit(solution)/shard_map/ppermute | solution.py:644
  18.3 4.3 %collective-permute-start.6 = (f32[48,128]{1,0:T(8,128)S(1)}, f32[48,128]{1,0:T(8,128)S(1)}, u32[]{:S(2)}, u32[]{:S(2)}) collective-permute-start(f32[48,128]{1,0:T(8,128)S(1)} %get-tuple-element.42), channel_id=1, source_target_pairs={{24,0},{16,8},{8,16},{0,24},{25,1},{17,9},{9,17},{1,25},{26,2},{18... | collective-permute-start | bytes 73736 | tf_op jit(solution)/shard_map/ppermute | solution.py:644
  19.9 5.6 %collective-permute-start.8 = (f32[48,128]{1,0:T(8,128)S(1)}, f32[48,128]{1,0:T(8,128)S(1)}, u32[]{:S(2)}, u32[]{:S(2)}) collective-permute-start(f32[48,128]{1,0:T(8,128)S(1)} %get-tuple-element.44), channel_id=1, source_target_pairs={{6,0},{4,2},{2,4},{0,6},{7,1},{5,3},{3,5},{1,7},{14,8},{12,10},{10... | collective-permute-start | bytes 73736 | tf_op jit(solution)/shard_map/ppermute | solution.py:644
  26.3 3.9 %collective-permute-start.10 = (f32[52,128]{1,0:T(8,128)S(1)}, f32[52,128]{1,0:T(8,128)S(1)}, u32[]{:S(2)}, u32[]{:S(2)}) collective-permute-start(f32[52,128]{1,0:T(8,128)S(1)} %coarse.1), channel_id=1, source_target_pairs={{1,0},{0,1},{3,2},{2,3},{5,4},{4,5},{7,6},{6,7},{9,8},{8,9},{11,10... | collective-permute-start | bytes 79880 | tf_op jit(solution)/shard_map/ppermute | solution.py:663
  30.3 4.6 %collective-permute-start.13 = (f32[32,128]{1,0:T(8,128)S(1)}, f32[32,128]{1,0:T(8,128)S(1)}, u32[]{:S(2)}, u32[]{:S(2)}) collective-permute-start(f32[32,128]{1,0:T(8,128)S(1)} %pad_maximum_fusion.refs_0_), channel_id=1, source_target_pairs={{4,0},{5,1},{6,2},{7,3},{0,4},{1,5},{2,6},{3,7},{12,8},{13,9},{14,... | collective-permute-start | bytes 49160 | tf_op jit(solution)/shard_map/ppermute | solution.py:663
  30.3 5.6 %collective-permute-start.12 = (f32[32,128]{1,0:T(8,128)S(1)}, f32[32,128]{1,0:T(8,128)S(1)}, u32[]{:S(2)}, u32[]{:S(2)}) collective-permute-start(f32[32,128]{1,0:T(8,128)S(1)} %pad_maximum_fusion.refs_0_), channel_id=1, source_target_pairs={{6,0},{7,1},{4,2},{5,3},{2,4},{3,5},{0,6},{1,7},{14,8},{15,9},{12,... | collective-permute-start | bytes 49160 | tf_op jit(solution)/shard_map/ppermute | solution.py:663
  33.0 3.7 %collective-permute-start.11 = (f32[32,128]{1,0:T(8,128)S(1)}, f32[32,128]{1,0:T(8,128)S(1)}, u32[]{:S(2)}, u32[]{:S(2)}) collective-permute-start(f32[32,128]{1,0:T(8,128)S(1)} %pad_maximum_fusion.refs_0_), channel_id=1, source_target_pairs={{2,0},{3,1},{0,2},{1,3},{6,4},{7,5},{4,6},{5,7},{10,8},{11,9},{8,1... | collective-permute-start | bytes 49160 | tf_op jit(solution)/shard_map/ppermute | solution.py:663
  39.1 3.4 %collective-permute-start.15 = (f32[32,256]{1,0:T(8,128)S(1)}, f32[32,256]{1,0:T(8,128)S(1)}, u32[]{:S(2)}, u32[]{:S(2)}) collective-permute-start(f32[32,256]{1,0:T(8,128)S(1)} %get-tuple-element.47.stack), channel_id=1, source_target_pairs={{24,0},{16,8},{8,16},{0,24},{25,1},{17,9},{9,17},{1,25},{26,2},{18... | collective-permute-start | bytes 98312 | tf_op jit(solution)/shard_map/ppermute | solution.py:644
  39.2 3.3 %collective-permute-start.14 = (f32[32,256]{1,0:T(8,128)S(1)}, f32[32,256]{1,0:T(8,128)S(1)}, u32[]{:S(2)}, u32[]{:S(2)}) collective-permute-start(f32[32,256]{1,0:T(8,128)S(1)} %get-tuple-element.47.stack), channel_id=1, source_target_pairs={{8,0},{0,8},{24,16},{16,24},{9,1},{1,9},{25,17},{17,25},{10,2},{2,... | collective-permute-start | bytes 98312 | tf_op jit(solution)/shard_map/ppermute | solution.py:644
  43.7 3.6 %collective-permute-start.16 = (f32[8,128]{1,0:T(8,128)S(1)}, f32[8,128]{1,0:T(8,128)S(1)}, u32[]{:S(2)}, u32[]{:S(2)}) collective-permute-start(f32[8,128]{1,0:T(8,128)S(1)} %get-tuple-element.52), channel_id=1, source_target_pairs={{1,0},{0,1},{3,2},{2,3},{5,4},{4,5},{7,6},{6,7},{9,8},{8,9},{11,10... | collective-permute-start | bytes 12296 | tf_op jit(solution)/shard_map/ppermute | solution.py:644

commit v7 on v6

--- a/solution.py
+++ b/solution.py
@@ -120,22 +120,19 @@
     return jnp.where((at > 0) & (at < count - 1), value, 0.0)
 
 
-def put_faces(dims, fields, sends):
+def put_faces(dims, field, sends):
     xe, xo, ye, yo = sends
     nx, ny = dims.nx, dims.ny
     x_e, x_o = face_index("gx", nx)
     y_e, y_o = face_index("gy", ny)
-    at = 0
-    for field in fields:
-        for c in range(field.shape[0]):
-            x_rows = slice(at * ny, (at + 1) * ny)
-            y_rows = slice(at * nx, (at + 1) * nx)
-            xe[x_rows, :] = field[c, pl.ds(pl.multiple_of(x_e * ny, ny), ny), :]
-            v = field[c, pl.ds(pl.multiple_of(x_o * ny, ny), ny), :]
-            xo[x_rows, :] = inner_odd("gx", v)
-            ye[y_rows, :] = field[c, pl.ds(y_e, nx, stride=ny), :]
-            yo[y_rows, :] = inner_odd("gy", field[c, pl.ds(y_o, nx, stride=ny), :])
-            at += 1
+    for c in range(3):
+        x_rows = slice(c * ny, (c + 1) * ny)
+        y_rows = slice(c * nx, (c + 1) * nx)
+        xe[x_rows, :] = field[c, pl.ds(pl.multiple_of(x_e * ny, ny), ny), :]
+        v = field[c, pl.ds(pl.multiple_of(x_o * ny, ny), ny), :]
+        xo[x_rows, :] = inner_odd("gx", v)
+        ye[y_rows, :] = field[c, pl.ds(y_e, nx, stride=ny), :]
+        yo[y_rows, :] = inner_odd("gy", field[c, pl.ds(y_o, nx, stride=ny), :])
 
 
 def put_z(dims, field, sends):
@@ -275,11 +272,11 @@
             first[c, at, :] = v[c]
     for c in copies[-3:]:
         c.wait()
-    put_faces(dims, (first, inverse, couplings), (xe, xo, ye, yo))
+    put_faces(dims, first, (xe, xo, ye, yo))
     put_z(dims, first, z_sends)
     own[...] = coarse_inv[:, 0, :]
-    put_inverses(ye, 18 * dims.nx, [own[...]])
-    put_inverses(yo, 18 * dims.nx, [own[...]])
+    put_inverses(ye, 3 * dims.nx, [own[...]])
+    put_inverses(yo, 3 * dims.nx, [own[...]])
     put_inverses(z_sends[0], 8, [own[...]])
     ids[...] = pencil_row(dims, square[0].astype(jnp.float32))
 
@@ -298,9 +295,9 @@
         for c in range(3):
             sums[c, at, :] = total[c]
             second[c, at, :] = (2.0 - DAMPING) * center[c] + step[c]
-    put_faces(dims, (second,), sends)
+    put_faces(dims, second, sends)
     put_z(dims, second, z_sends)
-    even_block, odd_block = [r[18 * dims.nx : 18 * dims.nx + 36, :] for r in recv[2:]]
+    even_block, odd_block = [r[3 * dims.nx : 3 * dims.nx + 36, :] for r in recv[2:]]
     put_inverses(sends[2], 3 * dims.nx, [odd_block])
     put_inverses(z_sends[0], 8, [even_block, odd_block])
 
@@ -394,13 +391,13 @@
     arrived, coarse_inv, refs = refs[:n_y], refs[n_y], refs[n_y + 1 :]
     held, rest = blocks_of(n_y, n_z)
     pieces, refs = refs[: 6 + len(rest)], refs[6 + len(rest) :]
-    stack, y_z, coarse, correction, inverses, packets = refs
+    stack, beyond_out, coarse, correction, inverses, packets = refs
     put_inverses(inverses, 0, [coarse_inv[...]])
     at = 36
     fat_ye, fat_yo, fat_z, thin_ye, thin_z, first_z = pieces[:6]
     for ref, start, count in (
-        (fat_ye, 18 * dims.nx, 36),
-        (fat_yo, 18 * dims.nx, 36),
+        (fat_ye, 3 * dims.nx, 36),
+        (fat_yo, 3 * dims.nx, 36),
         (fat_z, 8, 36),
         (thin_z, 8, 72),
         (thin_ye, 3 * dims.nx, 36),
@@ -468,7 +465,7 @@
 
     beyond = [1 - my_z] if n_z == 2 else [my_z - 1, my_z + 1]
     wanted = [ids_of(my_y, my_z), y_ids(my_z)]
-    wanted += [ids_of(my_y, z) for z in beyond] + [y_ids(z) for z in beyond]
+    wanted += [ids_of(my_y, z) for z in beyond]
     totals = [jnp.zeros((24, rows), jnp.float32) for _ in wanted]
     for j in range(owners):
         left = split3(correction[8 * j : 8 * j + 8])
@@ -480,23 +477,18 @@
                 preferred_element_type=jnp.float32,
             )
     totals = [s[0:8] + (s[8:16] + s[16:24]) for s in totals]
-    stack[0:8] = totals[0]
-    stack[8:16] = totals[1]
+    stack[...] = totals[0]
+    beyond_out[0:8] = totals[1]
     if n_z == 2:
-        low = my_z == 1
-        for ref, at, value in ((stack, 16, totals[2]), (y_z, 0, totals[3])):
-            ref[at : at + 8] = jnp.where(low, value, 0.0)
-            ref[at + 8 : at + 16] = jnp.where(low, 0.0, value)
+        beyond_out[8:16] = jnp.where(my_z == 1, totals[2], 0.0)
+        beyond_out[16:24] = jnp.where(my_z == 0, totals[2], 0.0)
     else:
-        stack[16:24], stack[24:32] = totals[2], totals[3]
-        y_z[0:8], y_z[8:16] = totals[4], totals[5]
-
-
-def third_kernel(dims, n_z, inverse, couplings, second, stack, y_z, *refs):
-    stacks, fat, thin, refs = refs[:2], refs[2:6], refs[6:10], refs[10:]
-    third, x_third, y_third = refs[:3]
-    z_sends, refs = refs[3 : 3 + n_z], refs[3 + n_z :]
-    field, y_field, z_field, yz_field, x_field, xy_field, xz_field = refs
+        beyond_out[8:16], beyond_out[16:24] = totals[2], totals[3]
+
+
+def third_kernel(dims, n_z, inverse, couplings, second, stack, beyond, *refs):
+    stacks, third, sends = refs[:2], refs[2], refs[3:7]
+    z_sends, (field, y_field, z_field) = refs[7 : 7 + n_z], refs[7 + n_z :]
     nx, ny, nz = dims.nx, dims.ny, dims.nz
     side = nx * ny // 2
     m0, m1 = mode_rows(8, nz)
@@ -517,111 +509,40 @@
     x_high = neighbour("gx", [s[:, :side] for s in stacks], True)
     x_low = jnp.where(my_x > 0, x_low, 0.0)
     x_high = jnp.where(my_x < n_x - 1, x_high, 0.0)
-    x_mix = jnp.where(lane_iota(4 * 8, side) < side // 2, x_high, x_low)
-
-    def expand(v, ends=None):
-        if ends is None:
-            return dot_00(pairs6(v), wide)
-        return dot_00(pairs6(v), last) + dot_00(pairs6(ends), start)
-
+    x_mix = jnp.where(lane_iota(8, side) < side // 2, x_high, x_low)
+    x_field = dot_00(pairs6(x_mix), wide)
     for ref, value in (
-        (field, expand(stack[0:8])),
-        (y_field, expand(stack[8:16])),
-        (z_field, expand(stack[16:24], stack[24:32])),
-        (yz_field, expand(y_z[0:8], y_z[8:16])),
-        (x_field, expand(x_mix[0:8])),
-        (xy_field, expand(x_mix[8:16])),
-        (xz_field, expand(x_mix[16:24], x_mix[24:32])),
+        (field, dot_00(pairs6(stack[...]), wide)),
+        (y_field, dot_00(pairs6(beyond[0:8]), wide)),
+        (z_field, dot_00(pairs6(beyond[8:16]), last) + dot_00(pairs6(beyond[16:24]), start)),
     ):
         for c in range(3):
             ref[c] = value[:, c * nz : (c + 1) * nz]
 
-    def at_x(own, outer, c, x):
-        if 0 <= x < nx:
-            return tile(own, c, x, ny)
-        return tile(outer, c, side // ny + x if x < 0 else x - nx, ny)
-
-    def update(inv, coup, center, base, pairs):
-        step = times(inv, [beside(coup, *pairs(c)) for c in range(3)])
-        return [base[c] + ((1.0 - DAMPING) * center[c] + step[c]) for c in range(3)]
-
-    for x in range(-1, nx + 1):
-        center = [at_x(field, x_field, c, x) for c in range(3)]
-
-        def pairs(c, x=x, center=center):
-            y = at_x(y_field, xy_field, c, x)
-            z = at_x(z_field, xz_field, c, x)
-            x_pair = (at_x(field, x_field, c, x - 1), at_x(field, x_field, c, x + 1))
-            return x_pair, shifted(center[c], y, y, 0), shifted(center[c], z, z, 1)
-
-        if 0 <= x < nx:
-            out = update(
-                tiles(inverse, 9, x, ny),
-                tiles(couplings, 6, x, ny),
-                center,
-                tiles(second, 3, x, ny),
-                pairs,
-            )
-            for c in range(3):
-                third[c, rows_at(dims, x), :] = out[c]
-        else:
-            high = x == nx
-            halo = [
-                neighbour("gx", [r[c * ny : (c + 1) * ny, :] for r in fat[:2]], high)
-                for c in range(3, 18)
-            ]
-            base = [
-                neighbour("gx", [r[c * ny : (c + 1) * ny, :] for r in thin[:2]], high)
-                for c in range(3)
-            ]
-            out = update(halo[:9], halo[9:], center, base, pairs)
-            for c in range(3):
-                x_third[int(high), c * ny : (c + 1) * ny, :] = out[c]
-    for high in (False, True):
-        inner, near, far = (ny - 1, 0, 1) if high else (0, ny - 1, ny - 2)
-
-        def line(ref, c, y):
-            return ref[c, pl.ds(y, nx, stride=ny), :]
-
-        center = [line(y_field, c, near) for c in range(3)]
-
-        def pairs(c, center=center, inner=inner, near=near, far=far, high=high):
-            low_row = xy_field[c, side - ny + near : side - ny + near + 1, :]
-            high_row = xy_field[c, near : near + 1, :]
-            y_pair = (line(y_field, c, far), line(field, c, inner))
-            z = line(yz_field, c, near)
-            return (
-                shifted(center[c], low_row, high_row, 0),
-                y_pair[::-1] if high else y_pair,
-                shifted(center[c], z, z, 1),
-            )
-
-        halo = [
-            neighbour("gy", [r[c * nx : (c + 1) * nx, :] for r in fat[2:]], high)
-            for c in range(3, 18)
-        ]
-        base = [
-            neighbour("gy", [r[c * nx : (c + 1) * nx, :] for r in thin[2:]], high)
-            for c in range(3)
-        ]
-        out = update(halo[:9], halo[9:], center, base, pairs)
+    def x_halo(c, high):
+        v = x_field[:, c * nz : (c + 1) * nz]
+        return v[0:ny] if high else v[side - ny : side]
+
+    def y_halo(c, x, high):
+        return tile(y_field, c, x, ny)
+
+    for x in range(nx):
+        coup = tiles(couplings, 6, x, ny)
+        center, total = sums_at(dims, x, field, x_halo, y_halo, z_field, coup)
+        change = times(tiles(inverse, 9, x, ny), total)
+        at = rows_at(dims, x)
         for c in range(3):
-            y_third[int(high), c * nx : (c + 1) * nx, :] = out[c]
+            third[c, at, :] = second[c, at, :] + ((1.0 - DAMPING) * center[c] + change[c])
+    put_faces(dims, third, sends)
     put_z(dims, third, z_sends)
 
 
-def last_kernel(dims, inverse, couplings, first, third, x_third, y_third, *refs):
-    z_recv, (out, z_halo, result, sems) = refs[:-4], refs[-4:]
+def last_kernel(dims, n_z, inverse, couplings, first, third, *refs):
+    recv, z_recv, (out, z_halo, result, sems) = refs[:4], refs[4 : 4 + n_z], refs[4 + n_z :]
+    nx, ny = dims.nx, dims.ny
     copies = []
-    step = dims.nx // CHUNKS
-    nx, ny = dims.nx, dims.ny
-
-    def x_halo(c, high):
-        return x_third[int(high), c * ny : (c + 1) * ny, :]
-
-    def y_halo(c, x, high):
-        return y_third[int(high), c * nx + x : c * nx + x + 1, :]
-
+    step = nx // CHUNKS
+    x_halo, y_halo = received(dims, recv)
     place_z(dims, z_recv, z_halo)
     for x in range(nx):
         coup = tiles(couplings, 6, x, ny)
@@ -644,11 +565,23 @@
     return lax.ppermute(value, axis, [(partner(i, count, odd), i) for i in range(count)])
 
 
-def exchange(sends, z_sends):
+def swap_inner(value, axis, spare):
+    count, other = lax.axis_size(axis), lax.axis_size(spare)
+    which = []
+    for i in range(count):
+        for k in range(other):
+            inside = 0 < i < count - 1
+            source = (partner(i, count, True), k) if inside else (i, partner(k, other, False))
+            which.append((source[0] * other + source[1], i * other + k))
+    return lax.ppermute(value, (axis, spare), which)
+
+
+def exchange(sends, z_sends, ring):
     xe, xo, ye, yo = sends
     xe = swap(xe, "gx", 0)
     z_recv = [swap(v, "gz", k) for k, v in enumerate(z_sends)]
-    ye, yo = swap(ye, "gy", 0), swap(yo, "gy", 1)
+    ye = swap(ye, "gy", 0)
+    yo = swap(yo, "gy", 1) if ring else swap_inner(yo, "gy", "gz")
     xo = swap(xo, "gx", 1)
     return [xe, xo, ye, yo], z_recv
 
@@ -704,7 +637,7 @@
         part(first_kernel, dims, z_count),
         "first",
         [vector, (9, rows, nz), vector, (6, rows, nz), (36, own), (1, rows)]
-        + faces(18, 36, 36)
+        + faces(3, 36, 36)
         + z_faces(36),
         [
             pltpu.VMEM((9, rows, nz), f32),
@@ -718,7 +651,7 @@
         ],
         in_hbm=5,
     )
-    fat, fat_z = exchange(sends[:4], sends[4:])
+    fat, fat_z = exchange(sends[:4], sends[4:], True)
     second, sums, *sends = call(
         part(second_kernel, dims, z_count),
         "second",
@@ -730,7 +663,7 @@
         *fat,
         *fat_z,
     )
-    thin, thin_z = exchange(sends[:4], sends[4:])
+    thin, thin_z = exchange(sends[:4], sends[4:], False)
     (packet,) = call(
         part(coarse_kernel, dims, z_count),
         "coarse",
@@ -750,10 +683,10 @@
     others = [fetch(packet, (), z) for z in z_words[2:]]
     packet = jnp.concatenate([packet, first_z[:16]] + others, axis=0)
     packets = [fetch(packet, y, ()) if y else packet for y in y_words]
-    stack, y_z = call(
+    stack, beyond = call(
         part(solve_kernel, dims, (n_y, n_z), own),
         "solve",
-        [(4 * 8, rows), (2 * 8, rows)],
+        [(8, rows), (24, rows)],
         [pltpu.VMEM((owners * 8, own), f32)] * 2 + [pltpu.VMEM((owners * 36, own), f32)]
         + [pltpu.VMEM((owners, 8, rows), f32)],
         *packets,
@@ -767,24 +700,22 @@
         *pieces,
     )
     xe, xo = swap(stack, "gx", 0), swap(stack, "gx", 1)
-    third, x_third, y_third, *z_sends = call(
+    third, *sends = call(
         part(third_kernel, dims, z_count),
         "third",
-        [vector, (2, 3 * ny, nz), (2, 3 * nx, nz)] + z_faces(0),
-        [pltpu.VMEM(vector, f32)] * 4 + [pltpu.VMEM((3, rows // 2, nz), f32)] * 3,
+        [vector] + faces(3, 0, 0) + z_faces(0),
+        [pltpu.VMEM(vector, f32)] * 3,
         inverse,
         couplings,
         second,
         stack,
-        y_z,
+        beyond,
         xe,
         xo,
-        *fat,
-        *thin,
-    )
-    z_recv = [swap(v, "gz", k) for k, v in enumerate(z_sends)]
+    )
+    recv, z_recv = exchange(sends[:4], sends[4:], False)
     (out,) = call(
-        part(last_kernel, dims),
+        part(last_kernel, dims, z_count),
         "last",
         [vector],
         [pltpu.VMEM(vector, f32)] * 2 + [pltpu.SemaphoreType.DMA((CHUNKS,))],
@@ -792,8 +723,7 @@
         couplings,
         first,
         third,
-        x_third,
-        y_third,
+        *recv,
         *z_recv,
         out_hbm=True,
     )

time: 48.8 us -> 46.6 us (0.955)
  waiting for transfers between devices: 19.6 us -> 16.3 us
  starting transfers between devices: 20.4 us -> 21.9 us
    ppermute x13 -> x15, waiting for transfers between devices: 13.3 us -> 8.03 us  [swap(): lax.ppermute(value, axis, [(partner(i, count, odd), i) for i in range(cou...]
    ppermute x0 -> x2, waiting for transfers between devices: none -> 1.2 us  [swap_inner(): return lax.ppermute(value, (axis, spare), which)]
    ppermute x0 -> x2, starting transfers between devices: none -> 1.07 us  [swap_inner(): return lax.ppermute(value, (axis, spare), which)]
    ppermute x4, waiting for transfers between devices: 6.29 us -> 7.07 us  [fetch(): return lax.ppermute(value, ('gy', 'gz'), which)]
    ppermute x13 -> x15, starting transfers between devices: 16.3 us -> 16.5 us  [swap(): lax.ppermute(value, axis, [(partner(i, count, odd), i) for i in range(cou...]
  transfers between devices with their start and end apart: 17 -> 21, of which waited for: 9 -> 9; matrix products, arithmetic and copies ran while one was open for 0% -> 0% of each run, Pallas kernels for 0% -> 0%
where the time goes in v7:
time: 46.6 us; the launch traced here: 46.5 us
  starting transfers between devices  21.9 us (47%)
  waiting for transfers between devices  16.3 us (35%)
  Pallas kernels  8.21 us (18%)
    ppermute x15, starting transfers between devices, swap(): lax.ppermute(value, axis, [(partner(i, count, odd), i) for i in range(cou...  16.5 us
    pallas_call x6, Pallas kernels, call(): pl.pallas_call(body, name=name, out_shape=[jax.ShapeDtypeStruct(s, jnp.fl...  8.21 us
    ppermute x15, waiting for transfers between devices, swap(): lax.ppermute(value, axis, [(partner(i, count, odd), i) for i in range(cou...  8.03 us
    ppermute x4, waiting for transfers between devices, fetch(): return lax.ppermute(value, ('gy', 'gz'), which)  7.07 us
    ppermute x4, starting transfers between devices, fetch(): return lax.ppermute(value, ('gy', 'gz'), which)  4.32 us
    ppermute x2, waiting for transfers between devices, swap_inner(): return lax.ppermute(value, (axis, spare), which)  1.2 us
    ppermute x2, starting transfers between devices, swap_inner(): return lax.ppermute(value, (axis, spare), which)  1.07 us
  transfers between devices with their start and end apart: 21, of which 9 were waited for; matrix products, arithmetic and copies ran while one was open for 0% of the time, Pallas kernels for 0%

profile of v7, /device:TPU:0, one launch (start us, length us, event | category | flops | bytes accessed | tf_op | source)
XLA Modules:
  0.0 46.5 jit_solution(13329015419229044104)
XLA Ops:
  0.0 2.0 %first.1 = (f32[3,256,128]{2,1,0:T(8,128)S(1)}, f32[9,256,128]{2,1,0:T(8,128)S(1)}, f32[3,256,128]{2,1,0:T(8,128)S(1)}, f32[6,256,128]{2,1,0:T(8,128)S(1)}, f32[...) custom-call(f32[3,256,128]{2,1,0:T(8,128)} %bitcast.6, ...), custom_call_target="tpu_custom_call" | custom-call | tf_op jit(solution)/shard_map/first/pallas_call | solution.py:602
  2.0 3.1 %collective-permute-start.2 = (f32[84,128]{1,0:T(8,128)S(1)}, f32[84,128]{1,0:T(8,128)S(1)}, u32[]{:S(2)}, u32[]{:S(2)}) collective-permute-start(f32[84,128]{1,0:T(8,128)S(1)} %get-tuple-element.36), channel_id=1, source_target_pairs={{2,0},{0,2},{6,4},{4,6},{3,1},{1,3},{7,5},{5,7},{10,8},{8,10},{14,... | collective-permute-start | bytes 129032 | tf_op jit(solution)/shard_map/ppermute | solution.py:565
  5.1 2.5 %collective-permute-start.3 = (f32[84,128]{1,0:T(8,128)S(1)}, f32[84,128]{1,0:T(8,128)S(1)}, u32[]{:S(2)}, u32[]{:S(2)}) collective-permute-start(f32[84,128]{1,0:T(8,128)S(1)} %get-tuple-element.37), channel_id=1, source_target_pairs={{6,0},{4,2},{2,4},{0,6},{7,1},{5,3},{3,5},{1,7},{14,8},{12,10},{10... | collective-permute-start | bytes 129032 | tf_op jit(solution)/shard_map/ppermute | solution.py:565
  7.6 1.6 %collective-permute-start.1 = (f32[48,128]{1,0:T(8,128)S(1)}, f32[48,128]{1,0:T(8,128)S(1)}, u32[]{:S(2)}, u32[]{:S(2)}) collective-permute-start(f32[48,128]{1,0:T(8,128)S(1)} %get-tuple-element.35), channel_id=1, source_target_pairs={{24,0},{16,8},{8,16},{0,24},{25,1},{17,9},{9,17},{1,25},{26,2},{18... | collective-permute-start | bytes 73736 | tf_op jit(solution)/shard_map/ppermute | solution.py:565
  9.2 1.5 %collective-permute-start.4 = (f32[44,128]{1,0:T(8,128)S(1)}, f32[44,128]{1,0:T(8,128)S(1)}, u32[]{:S(2)}, u32[]{:S(2)}) collective-permute-start(f32[44,128]{1,0:T(8,128)S(1)} %get-tuple-element.38), channel_id=1, source_target_pairs={{1,0},{0,1},{3,2},{2,3},{5,4},{4,5},{7,6},{6,7},{9,8},{8,9},{11,10... | collective-permute-start | bytes 67592 | tf_op jit(solution)/shard_map/ppermute | solution.py:565
  10.7 2.3 %collective-permute-done.4.refs_4_.refs_7_ = f32[44,128]{1,0:T(8,128)S(1)} collective-permute-done((f32[44,128]{1,0:T(8,128)S(1)}, f32[44,128]{1,0:T(8,128)S(1)}, u32[]{:S(2)}, u32[]{:S(2)}) %collective-permute-start.4) | collective-permute-done | bytes 22560 | tf_op jit(solution)/shard_map/ppermute | solution.py:565
  13.1 0.8 %second.1 = (f32[3,256,128]{2,1,0:T(8,128)S(1)}, f32[3,256,128]{2,1,0:T(8,128)S(1)}, f32[48,128]{1,0:T(8,128)S(1)}, f32[48,128]{1,0:T(8,128)S(1)}, f32[84,128]{1...) custom-call(f32[9,256,128]{2,1,0:T(8,128)S(1)} %get-tuple-element.31.inverse, ...), custom_call_target="tpu_custom_call" | custom-call | tf_op jit(solution)/shard_map/second/pallas_call | solution.py:602
  14.6 1.5 %collective-permute-start.9 = (f32[80,128]{1,0:T(8,128)S(1)}, f32[80,128]{1,0:T(8,128)S(1)}, u32[]{:S(2)}, u32[]{:S(2)}) collective-permute-start(f32[80,128]{1,0:T(8,128)S(1)} %get-tuple-element.47), channel_id=1, source_target_pairs={{1,0},{0,1},{3,2},{2,3},{5,4},{4,5},{7,6},{6,7},{9,8},{8,9},{11,10... | collective-permute-start | bytes 122888 | tf_op jit(solution)/shard_map/ppermute | solution.py:565
  17.2 2.1 %collective-permute-done.6.refs_1_ = f32[48,128]{1,0:T(8,128)S(1)} collective-permute-done((f32[48,128]{1,0:T(8,128)S(1)}, f32[48,128]{1,0:T(8,128)S(1)}, u32[]{:S(2)}, u32[]{:S(2)}) %collective-permute-start.6) | collective-permute-done | bytes 24608 | tf_op jit(solution)/shard_map/ppermute | solution.py:565
  19.3 1.2 %collective-permute-done.8.refs_3_ = f32[48,128]{1,0:T(8,128)S(1)} collective-permute-done((f32[48,128]{1,0:T(8,128)S(1)}, f32[48,128]{1,0:T(8,128)S(1)}, u32[]{:S(2)}, u32[]{:S(2)}) %collective-permute-start.8) | collective-permute-done | bytes 24608 | tf_op jit(solution)/shard_map/ppermute | solution.py:576
  20.5 0.8 %coarse.1 = f32[52,128]{1,0:T(8,128)S(1)} custom-call(f32[3,256,128]{2,1,0:T(8,128)S(1)} %get-tuple-element.40.rhs, f32[3,256,128]{2,1,0:T(8,128)S(1)} %get-tuple-element.41.sums, f32[6,256,128]{2,1,0:T(8,128)S(1)} %get-tuple-element.32.couplings, f32[3,256,128]{2,1,0:T(8,128)S(1)} %get-tuple-element.39.second, f32[1,256]{1,0:T(1,128)S(1)} %get-tuple-element.42.ids, ...), custom_call_target="tpu_custom_call" | custom-call | tf_op jit(solution)/shard_map/coarse/pallas_call | solution.py:602
  21.9 3.3 %collective-permute-done.10.refs_10_ = f32[52,128]{1,0:T(8,128)S(1)} collective-permute-done((f32[52,128]{1,0:T(8,128)S(1)}, f32[52,128]{1,0:T(8,128)S(1)}, u32[]{:S(2)}, u32[]{:S(2)}) %collective-permute-start.10) | collective-permute-done | bytes 26656 | tf_op jit(solution)/shard_map/ppermute | solution.py:596
  25.3 1.2 %collective-permute-start.13 = (f32[32,128]{1,0:T(8,128)S(1)}, f32[32,128]{1,0:T(8,128)S(1)}, u32[]{:S(2)}, u32[]{:S(2)}) collective-permute-start(f32[32,128]{1,0:T(8,128)S(1)} %pad_maximum_fusion.refs_0_), channel_id=1, source_target_pairs={{4,0},{5,1},{6,2},{7,3},{0,4},{1,5},{2,6},{3,7},{12,8},{13,9},{14,... | collective-permute-start | bytes 49160 | tf_op jit(solution)/shard_map/ppermute | solution.py:596
  26.5 2.5 %collective-permute-start.12 = (f32[32,128]{1,0:T(8,128)S(1)}, f32[32,128]{1,0:T(8,128)S(1)}, u32[]{:S(2)}, u32[]{:S(2)}) collective-permute-start(f32[32,128]{1,0:T(8,128)S(1)} %pad_maximum_fusion.refs_0_), channel_id=1, source_target_pairs={{6,0},{7,1},{4,2},{5,3},{2,4},{3,5},{0,6},{1,7},{14,8},{15,9},{12,... | collective-permute-start | bytes 49160 | tf_op jit(solution)/shard_map/ppermute | solution.py:596
  29.0 0.9 %collective-permute-done.13.refs_3_ = f32[32,128]{1,0:T(8,128)S(1)} collective-permute-done((f32[32,128]{1,0:T(8,128)S(1)}, f32[32,128]{1,0:T(8,128)S(1)}, u32[]{:S(2)}, u32[]{:S(2)}) %collective-permute-start.13) | collective-permute-done | bytes 16416 | tf_op jit(solution)/shard_map/ppermute | solution.py:596
  29.9 2.1 %collective-permute-done.12.refs_2_ = f32[32,128]{1,0:T(8,128)S(1)} collective-permute-done((f32[32,128]{1,0:T(8,128)S(1)}, f32[32,128]{1,0:T(8,128)S(1)}, u32[]{:S(2)}, u32[]{:S(2)}) %collective-permute-start.12) | collective-permute-done | bytes 16416 | tf_op jit(solution)/shard_map/ppermute | solution.py:596
  32.7 2.3 %solve.1 = (f32[8,256]{1,0:T(8,128)S(1)}, f32[24,256]{1,0:T(8,128)S(1)}) custom-call(f32[32,128]{1,0:T(8,128)S(1)} %pad_maximum_fusion.refs_0_, f32[32,128]{1,0:T(8,128)S(1)} %collective-permute-done.11.refs_1_, f32[32,128]{1,0:T(8,128)S(1)} %collective-permute-done.12.refs_2_, f32[32,128]{1,0:T(8,128)S(1)} %collective-permute-done.13.refs_3_, ...), custom_call_target="tpu_custom_call" | custom-call | tf_op jit(solution)/shard_map/solve/pallas_call | solution.py:602
  35.1 1.6 %collective-permute-start.14 = (f32[8,256]{1,0:T(8,128)S(1)}, f32[8,256]{1,0:T(8,128)S(1)}, u32[]{:S(2)}, u32[]{:S(2)}) collective-permute-start(f32[8,256]{1,0:T(8,128)S(1)} %get-tuple-element.49.stack), channel_id=1, source_target_pairs={{8,0},{0,8},{24,16},{16,24},{9,1},{1,9},{25,17},{17,25},{10,2},{2,... | collective-permute-start | bytes 24584 | tf_op jit(solution)/shard_map/ppermute | solution.py:565
  36.7 1.5 %collective-permute-done.15.refs_1_ = f32[8,256]{1,0:T(8,128)S(1)} collective-permute-done((f32[8,256]{1,0:T(8,128)S(1)}, f32[8,256]{1,0:T(8,128)S(1)}, u32[]{:S(2)}, u32[]{:S(2)}) %collective-permute-start.15) | collective-permute-done | bytes 8224 | tf_op jit(solution)/shard_map/ppermute | solution.py:565
  38.2 1.0 %third.1 = (f32[3,256,128]{2,1,0:T(8,128)S(1)}, f32[48,128]{1,0:T(8,128)S(1)}, f32[48,128]{1,0:T(8,128)S(1)}, f32[48,128]{1,0:T(8,128)S(1)}, f32[48,128]{1,0:T(8,128)S(1)}, /*index=5*/f32[8,128]{1,0:T(8,128)S(1)}) custom-call(f32[9,256,128]{2,1,0:T(8,128)S(1)} %get-tuple-element.31.inverse, f32[6,256,128]{2,1,0:T(8,128)S(1)} %get-tuple-element.32.couplings, ...), custom_call_target="tpu_custom_call" | custom-call | tf_op jit(solution)/shard_map/third/pallas_call | solution.py:602
  39.3 1.5 %collective-permute-start.17 = (f32[48,128]{1,0:T(8,128)S(1)}, f32[48,128]{1,0:T(8,128)S(1)}, u32[]{:S(2)}, u32[]{:S(2)}) collective-permute-start(f32[48,128]{1,0:T(8,128)S(1)} %get-tuple-element.53), channel_id=1, source_target_pairs={{24,0},{16,8},{8,16},{0,24},{25,1},{17,9},{9,17},{1,25},{26,2},{18... | collective-permute-start | bytes 73736 | tf_op jit(solution)/shard_map/ppermute | solution.py:565
  41.5 1.5 %collective-permute-start.20 = (f32[8,128]{1,0:T(8,128)S(1)}, f32[8,128]{1,0:T(8,128)S(1)}, u32[]{:S(2)}, u32[]{:S(2)}) collective-permute-start(f32[8,128]{1,0:T(8,128)S(1)} %get-tuple-element.56), channel_id=1, source_target_pairs={{1,0},{0,1},{3,2},{2,3},{5,4},{4,5},{7,6},{6,7},{9,8},{8,9},{11,10... | collective-permute-start | bytes 12296 | tf_op jit(solution)/shard_map/ppermute | solution.py:565
  43.0 2.1 %collective-permute-done.20.refs_4_ = f32[8,128]{1,0:T(8,128)S(1)} collective-permute-done((f32[8,128]{1,0:T(8,128)S(1)}, f32[8,128]{1,0:T(8,128)S(1)}, u32[]{:S(2)}, u32[]{:S(2)}) %collective-permute-start.20) | collective-permute-done | bytes 4128 | tf_op jit(solution)/shard_map/ppermute | solution.py:565
  45.1 1.3 %last.1 = f32[3,256,128]{2,1,0:T(8,128)} custom-call(f32[9,256,128]{2,1,0:T(8,128)S(1)} %get-tuple-element.31.inverse, f32[6,256,128]{2,1,0:T(8,128)S(1)} %get-tuple-element.32.couplings, f32[3,256,128]{2,1,0:T(8,128)S(1)} %get-tuple-element.33.first, f32[3,256,128]{2,1,0:T(8,128)S(1)} %get-tuple-element.51.third, ...), custom_call_target="tpu_custom_call" | custom-call | tf_op jit(solution)/shard_map/last/pallas_call | solution.py:602
  (27 shorter events, 4.1 us)
Async XLA Ops:
  2.0 11.1 %collective-permute-start.2 = (f32[84,128]{1,0:T(8,128)S(1)}, f32[84,128]{1,0:T(8,128)S(1)}, u32[]{:S(2)}, u32[]{:S(2)}) collective-permute-start(f32[84,128]{1,0:T(8,128)S(1)} %get-tuple-element.36), channel_id=1, source_target_pairs={{2,0},{0,2},{6,4},{4,6},{3,1},{1,3},{7,5},{5,7},{10,8},{8,10},{14,... | collective-permute-start | bytes 129032 | tf_op jit(solution)/shard_map/ppermute | solution.py:565
  5.1 8.0 %collective-permute-start.3 = (f32[84,128]{1,0:T(8,128)S(1)}, f32[84,128]{1,0:T(8,128)S(1)}, u32[]{:S(2)}, u32[]{:S(2)}) collective-permute-start(f32[84,128]{1,0:T(8,128)S(1)} %get-tuple-element.37), channel_id=1, source_target_pairs={{6,0},{4,2},{2,4},{0,6},{7,1},{5,3},{3,5},{1,7},{14,8},{12,10},{10... | collective-permute-start | bytes 129032 | tf_op jit(solution)/shard_map/ppermute | solution.py:565
  7.6 5.5 %collective-permute-start = (f32[48,128]{1,0:T(8,128)S(1)}, f32[48,128]{1,0:T(8,128)S(1)}, u32[]{:S(2)}, u32[]{:S(2)}) collective-permute-start(f32[48,128]{1,0:T(8,128)S(1)} %get-tuple-element.34), channel_id=1, source_target_pairs={{8,0},{0,8},{24,16},{16,24},{9,1},{1,9},{25,17},{17,25},{10,2},{2,... | collective-permute-start | bytes 73736 | tf_op jit(solution)/shard_map/ppermute | solution.py:565
  7.6 5.5 %collective-permute-start.1 = (f32[48,128]{1,0:T(8,128)S(1)}, f32[48,128]{1,0:T(8,128)S(1)}, u32[]{:S(2)}, u32[]{:S(2)}) collective-permute-start(f32[48,128]{1,0:T(8,128)S(1)} %get-tuple-element.35), channel_id=1, source_target_pairs={{24,0},{16,8},{8,16},{0,24},{25,1},{17,9},{9,17},{1,25},{26,2},{18... | collective-permute-start | bytes 73736 | tf_op jit(solution)/shard_map/ppermute | solution.py:565
  9.2 3.8 %collective-permute-start.4 = (f32[44,128]{1,0:T(8,128)S(1)}, f32[44,128]{1,0:T(8,128)S(1)}, u32[]{:S(2)}, u32[]{:S(2)}) collective-permute-start(f32[44,128]{1,0:T(8,128)S(1)} %get-tuple-element.38), channel_id=1, source_target_pairs={{1,0},{0,1},{3,2},{2,3},{5,4},{4,5},{7,6},{6,7},{9,8},{8,9},{11,10... | collective-permute-start | bytes 67592 | tf_op jit(solution)/shard_map/ppermute | solution.py:565
  13.9 6.6 %collective-permute-start.7 = (f32[84,128]{1,0:T(8,128)S(1)}, f32[84,128]{1,0:T(8,128)S(1)}, u32[]{:S(2)}, u32[]{:S(2)}) collective-permute-start(f32[84,128]{1,0:T(8,128)S(1)} %get-tuple-element.45), channel_id=1, source_target_pairs={{2,0},{0,2},{6,4},{4,6},{3,1},{1,3},{7,5},{5,7},{10,8},{8,10},{14,... | collective-permute-start | bytes 129032 | tf_op jit(solution)/shard_map/ppermute | solution.py:565
  14.6 5.9 %collective-permute-start.9 = (f32[80,128]{1,0:T(8,128)S(1)}, f32[80,128]{1,0:T(8,128)S(1)}, u32[]{:S(2)}, u32[]{:S(2)}) collective-permute-start(f32[80,128]{1,0:T(8,128)S(1)} %get-tuple-element.47), channel_id=1, source_target_pairs={{1,0},{0,1},{3,2},{2,3},{5,4},{4,5},{7,6},{6,7},{9,8},{8,9},{11,10... | collective-permute-start | bytes 122888 | tf_op jit(solution)/shard_map/ppermute | solution.py:565
  16.1 1.2 %collective-permute-start.5 = (f32[48,128]{1,0:T(8,128)S(1)}, f32[48,128]{1,0:T(8,128)S(1)}, u32[]{:S(2)}, u32[]{:S(2)}) collective-permute-start(f32[48,128]{1,0:T(8,128)S(1)} %get-tuple-element.43), channel_id=1, source_target_pairs={{8,0},{0,8},{24,16},{16,24},{9,1},{1,9},{25,17},{17,25},{10,2},{2,... | collective-permute-start | bytes 73736 | tf_op jit(solution)/shard_map/ppermute | solution.py:565
  16.1 3.3 %collective-permute-start.6 = (f32[48,128]{1,0:T(8,128)S(1)}, f32[48,128]{1,0:T(8,128)S(1)}, u32[]{:S(2)}, u32[]{:S(2)}) collective-permute-start(f32[48,128]{1,0:T(8,128)S(1)} %get-tuple-element.44), channel_id=1, source_target_pairs={{24,0},{16,8},{8,16},{0,24},{25,1},{17,9},{9,17},{1,25},{26,2},{18... | collective-permute-start | bytes 73736 | tf_op jit(solution)/shard_map/ppermute | solution.py:565
  16.7 3.8 %collective-permute-start.8 = (f32[48,128]{1,0:T(8,128)S(1)}, f32[48,128]{1,0:T(8,128)S(1)}, u32[]{:S(2)}, u32[]{:S(2)}) collective-permute-start(f32[48,128]{1,0:T(8,128)S(1)} %get-tuple-element.46), channel_id=1, source_target_pairs={{1,0},{0,1},{4,2},{5,3},{2,4},{3,5},{7,6},{6,7},{9,8},{8,9},{12,10... | collective-permute-start | bytes 73736 | tf_op jit(solution)/shard_map/ppermute | solution.py:576
  21.3 3.9 %collective-permute-start.10 = (f32[52,128]{1,0:T(8,128)S(1)}, f32[52,128]{1,0:T(8,128)S(1)}, u32[]{:S(2)}, u32[]{:S(2)}) collective-permute-start(f32[52,128]{1,0:T(8,128)S(1)} %coarse.1), channel_id=1, source_target_pairs={{1,0},{0,1},{3,2},{2,3},{5,4},{4,5},{7,6},{6,7},{9,8},{8,9},{11,10... | collective-permute-start | bytes 79880 | tf_op jit(solution)/shard_map/ppermute | solution.py:596
  25.3 4.6 %collective-permute-start.13 = (f32[32,128]{1,0:T(8,128)S(1)}, f32[32,128]{1,0:T(8,128)S(1)}, u32[]{:S(2)}, u32[]{:S(2)}) collective-permute-start(f32[32,128]{1,0:T(8,128)S(1)} %pad_maximum_fusion.refs_0_), channel_id=1, source_target_pairs={{4,0},{5,1},{6,2},{7,3},{0,4},{1,5},{2,6},{3,7},{12,8},{13,9},{14,... | collective-permute-start | bytes 49160 | tf_op jit(solution)/shard_map/ppermute | solution.py:596
  26.5 5.5 %collective-permute-start.12 = (f32[32,128]{1,0:T(8,128)S(1)}, f32[32,128]{1,0:T(8,128)S(1)}, u32[]{:S(2)}, u32[]{:S(2)}) collective-permute-start(f32[32,128]{1,0:T(8,128)S(1)} %pad_maximum_fusion.refs_0_), channel_id=1, source_target_pairs={{6,0},{7,1},{4,2},{5,3},{2,4},{3,5},{0,6},{1,7},{14,8},{15,9},{12,... | collective-permute-start | bytes 49160 | tf_op jit(solution)/shard_map/ppermute | solution.py:596
  29.0 3.7 %collective-permute-start.11 = (f32[32,128]{1,0:T(8,128)S(1)}, f32[32,128]{1,0:T(8,128)S(1)}, u32[]{:S(2)}, u32[]{:S(2)}) collective-permute-start(f32[32,128]{1,0:T(8,128)S(1)} %pad_maximum_fusion.refs_0_), channel_id=1, source_target_pairs={{2,0},{3,1},{0,2},{1,3},{6,4},{7,5},{4,6},{5,7},{10,8},{11,9},{8,1... | collective-permute-start | bytes 49160 | tf_op jit(solution)/shard_map/ppermute | solution.py:596
  35.0 3.2 %collective-permute-start.15 = (f32[8,256]{1,0:T(8,128)S(1)}, f32[8,256]{1,0:T(8,128)S(1)}, u32[]{:S(2)}, u32[]{:S(2)}) collective-permute-start(f32[8,256]{1,0:T(8,128)S(1)} %get-tuple-element.49.stack), channel_id=1, source_target_pairs={{24,0},{16,8},{8,16},{0,24},{25,1},{17,9},{9,17},{1,25},{26,2},{18... | collective-permute-start | bytes 24584 | tf_op jit(solution)/shard_map/ppermute | solution.py:565
  35.1 3.1 %collective-permute-start.14 = (f32[8,256]{1,0:T(8,128)S(1)}, f32[8,256]{1,0:T(8,128)S(1)}, u32[]{:S(2)}, u32[]{:S(2)}) collective-permute-start(f32[8,256]{1,0:T(8,128)S(1)} %get-tuple-element.49.stack), channel_id=1, source_target_pairs={{8,0},{0,8},{24,16},{16,24},{9,1},{1,9},{25,17},{17,25},{10,2},{2,... | collective-permute-start | bytes 24584 | tf_op jit(solution)/shard_map/ppermute | solution.py:565
  39.2 6.0 %collective-permute-start.16 = (f32[48,128]{1,0:T(8,128)S(1)}, f32[48,128]{1,0:T(8,128)S(1)}, u32[]{:S(2)}, u32[]{:S(2)}) collective-permute-start(f32[48,128]{1,0:T(8,128)S(1)} %get-tuple-element.52), channel_id=1, source_target_pairs={{8,0},{0,8},{24,16},{16,24},{9,1},{1,9},{25,17},{17,25},{10,2},{2,... | collective-permute-start | bytes 73736 | tf_op jit(solution)/shard_map/ppermute | solution.py:565
  39.3 5.8 %collective-permute-start.17 = (f32[48,128]{1,0:T(8,128)S(1)}, f32[48,128]{1,0:T(8,128)S(1)}, u32[]{:S(2)}, u32[]{:S(2)}) collective-permute-start(f32[48,128]{1,0:T(8,128)S(1)} %get-tuple-element.53), channel_id=1, source_target_pairs={{24,0},{16,8},{8,16},{0,24},{25,1},{17,9},{9,17},{1,25},{26,2},{18... | collective-permute-start | bytes 73736 | tf_op jit(solution)/shard_map/ppermute | solution.py:565
  40.8 4.3 %collective-permute-start.18 = (f32[48,128]{1,0:T(8,128)S(1)}, f32[48,128]{1,0:T(8,128)S(1)}, u32[]{:S(2)}, u32[]{:S(2)}) collective-permute-start(f32[48,128]{1,0:T(8,128)S(1)} %get-tuple-element.54), channel_id=1, source_target_pairs={{2,0},{0,2},{6,4},{4,6},{3,1},{1,3},{7,5},{5,7},{10,8},{8,10},{14,... | collective-permute-start | bytes 73736 | tf_op jit(solution)/shard_map/ppermute | solution.py:565
  41.0 4.2 %collective-permute-start.19 = (f32[48,128]{1,0:T(8,128)S(1)}, f32[48,128]{1,0:T(8,128)S(1)}, u32[]{:S(2)}, u32[]{:S(2)}) collective-permute-start(f32[48,128]{1,0:T(8,128)S(1)} %get-tuple-element.55), channel_id=1, source_target_pairs={{1,0},{0,1},{4,2},{5,3},{2,4},{3,5},{7,6},{6,7},{9,8},{8,9},{12,10... | collective-permute-start | bytes 73736 | tf_op jit(solution)/shard_map/ppermute | solution.py:576
  41.5 3.6 %collective-permute-start.20 = (f32[8,128]{1,0:T(8,128)S(1)}, f32[8,128]{1,0:T(8,128)S(1)}, u32[]{:S(2)}, u32[]{:S(2)}) collective-permute-start(f32[8,128]{1,0:T(8,128)S(1)} %get-tuple-element.56), channel_id=1, source_target_pairs={{1,0},{0,1},{3,2},{2,3},{5,4},{4,5},{7,6},{6,7},{9,8},{8,9},{11,10... | collective-permute-start | bytes 12296 | tf_op jit(solution)/shard_map/ppermute | solution.py:565

commit v8 on v7

--- a/solution.py
+++ b/solution.py
@@ -120,34 +120,42 @@
     return jnp.where((at > 0) & (at < count - 1), value, 0.0)
 
 
+def put_x(dims, field, sends):
+    ny = dims.ny
+    for odd, (ref, x) in enumerate(zip(sends, face_index("gx", dims.nx))):
+        for c in range(3):
+            v = field[c, pl.ds(pl.multiple_of(x * ny, ny), ny), :]
+            ref[c * ny : (c + 1) * ny, :] = inner_odd("gx", v) if odd else v
+
+
 def put_faces(dims, field, sends):
-    xe, xo, ye, yo = sends
     nx, ny = dims.nx, dims.ny
-    x_e, x_o = face_index("gx", nx)
-    y_e, y_o = face_index("gy", ny)
-    for c in range(3):
-        x_rows = slice(c * ny, (c + 1) * ny)
-        y_rows = slice(c * nx, (c + 1) * nx)
-        xe[x_rows, :] = field[c, pl.ds(pl.multiple_of(x_e * ny, ny), ny), :]
-        v = field[c, pl.ds(pl.multiple_of(x_o * ny, ny), ny), :]
-        xo[x_rows, :] = inner_odd("gx", v)
-        ye[y_rows, :] = field[c, pl.ds(y_e, nx, stride=ny), :]
-        yo[y_rows, :] = inner_odd("gy", field[c, pl.ds(y_o, nx, stride=ny), :])
-
-
-def put_z(dims, field, sends):
+    put_x(dims, field, sends[:2])
+    for odd, (ref, y) in enumerate(zip(sends[2:], face_index("gy", ny))):
+        for c in range(3):
+            v = field[c, pl.ds(y, nx, stride=ny), :]
+            ref[c * nx : (c + 1) * nx, :] = inner_odd("gy", v) if odd else v
+
+
+def pack_z(dims, planes, k):
     groups, nz = dims.groups, dims.nz
-    lane = lane_iota(8, nz)
-    for odd, (ref, k) in enumerate(zip(sends, face_index("gz", nz))):
-        to = lax.rem(lane + nz - k, nz)
-        total = []
-        for c in range(3):
-            face = jnp.zeros((8, nz), jnp.float32)
-            for g in range(groups):
-                at = c * groups + g
-                face = jnp.where(to == at, pltpu.roll(field[c, 8 * g : 8 * g + 8, :], at, 1), face)
-            total.append(face)
-        face = pltpu.roll(total[0] + total[1] + total[2], lax.rem(nz - k, nz), 1)
+    to = lax.rem(lane_iota(8, nz) + nz - k, nz)
+    total = None
+    for c, plane in enumerate(planes):
+        face = jnp.zeros((8, nz), jnp.float32)
+        for g in range(groups):
+            at = c * groups + g
+            face = jnp.where(to == at, pltpu.roll(plane[8 * g : 8 * g + 8, :], at, 1), face)
+        total = face if total is None else total + face
+    return pltpu.roll(total, lax.rem(nz - k, nz), 1)
+
+
+def put_z(dims, field, sends, couplings=None):
+    for odd, (ref, k) in enumerate(zip(sends, face_index("gz", dims.nz))):
+        planes = [field.at[c] for c in range(3)]
+        if couplings is not None:
+            planes.append(couplings.at[jnp.where(k > 0, 5, 4)])
+        face = pack_z(dims, planes, k)
         ref[0:8, :] = inner_odd("gz", face) if odd else face
 
 
@@ -273,18 +281,21 @@
     for c in copies[-3:]:
         c.wait()
     put_faces(dims, first, (xe, xo, ye, yo))
-    put_z(dims, first, z_sends)
+    put_z(dims, first, z_sends, couplings)
+    for odd, (ref, y) in enumerate(zip((ye, yo), face_index("gy", dims.ny))):
+        v = couplings[jnp.where(y > 0, 3, 2), pl.ds(y, dims.nx, stride=dims.ny), :]
+        ref[3 * dims.nx : 4 * dims.nx, :] = inner_odd("gy", v) if odd else v
     own[...] = coarse_inv[:, 0, :]
-    put_inverses(ye, 3 * dims.nx, [own[...]])
-    put_inverses(yo, 3 * dims.nx, [own[...]])
+    put_inverses(ye, 4 * dims.nx, [own[...]])
+    put_inverses(yo, 4 * dims.nx, [own[...]])
     put_inverses(z_sends[0], 8, [own[...]])
     ids[...] = pencil_row(dims, square[0].astype(jnp.float32))
 
 
 def second_kernel(dims, n_z, inverse, couplings, first, *refs):
     recv, z_recv, refs = refs[:4], refs[4 : 4 + n_z], refs[4 + n_z :]
-    second, sums, *sends = refs[:6]
-    z_sends, z_halo = refs[6:-1], refs[-1]
+    second, sums, *sends = refs[:4]
+    z_halo = refs[4]
     x_halo, y_halo = received(dims, recv)
     place_z(dims, z_recv, z_halo)
     for x in range(dims.nx):
@@ -295,38 +306,92 @@
         for c in range(3):
             sums[c, at, :] = total[c]
             second[c, at, :] = (2.0 - DAMPING) * center[c] + step[c]
-    put_faces(dims, second, sends)
-    put_z(dims, second, z_sends)
-    even_block, odd_block = [r[3 * dims.nx : 3 * dims.nx + 36, :] for r in recv[2:]]
-    put_inverses(sends[2], 3 * dims.nx, [odd_block])
-    put_inverses(z_sends[0], 8, [even_block, odd_block])
+    put_x(dims, second, sends)
 
 
 def coarse_kernel(dims, n_z, rhs, sums, couplings, second, ids, *refs):
-    half = dims.rows // 2
-    recv, z_recv, refs = refs[:4], refs[4 : 4 + n_z], refs[4 + n_z :]
-    packet, resid, z_halo = refs
-    x_halo, y_halo = received(dims, recv)
-    place_z(dims, z_recv, z_halo)
+    nx, ny, nz, rows = dims.nx, dims.ny, dims.nz, dims.rows
+    half = rows // 2
+    (xe, xo, ye, yo), z_recv, refs = refs[:4], refs[4 : 4 + n_z], refs[4 + n_z :]
+    packet, z_more, (resid, wide) = refs[0], refs[1:n_z], refs[n_z:]
+
+    def x_halo(c, high):
+        return neighbour("gx", [r[c * ny : (c + 1) * ny, :] for r in (xe, xo)], high)
+
     rest = 1.0 - DAMPING * (2.0 - DAMPING)
-    for x in range(dims.nx):
-        coup = tiles(couplings, 6, x, dims.ny)
-        _, total = sums_at(dims, x, second, x_halo, y_halo, z_halo, coup)
+    row = row_iota(ny, nz)
+    lane = lane_iota(ny, nz)
+    for x in range(nx):
+        coup = tiles(couplings, 6, x, ny)
+        coup[2] = jnp.where(row == 0, 0.0, coup[2])
+        coup[3] = jnp.where(row == ny - 1, 0.0, coup[3])
+        coup[4] = jnp.where(lane == 0, 0.0, coup[4])
+        coup[5] = jnp.where(lane == nz - 1, 0.0, coup[5])
         at = rows_at(dims, x)
         for c in range(3):
-            resid[c, at, :] = rest * rhs[c, at, :] + (total[c] - DAMPING * sums[c, at, :])
-    m0, m1 = mode_rows(8, dims.nz)
-    row = row_iota(8, dims.nz)
+            v = tile(second, c, x, ny)
+            low = tile(second, c, x - 1, ny) if x > 0 else x_halo(c, False)
+            high = tile(second, c, x + 1, ny) if x < nx - 1 else x_halo(c, True)
+            y_pair = (pltpu.roll(v, 1, 0), pltpu.roll(v, ny - 1, 0))
+            z_pair = (pltpu.roll(v, 1, 1), pltpu.roll(v, nz - 1, 1))
+            total = beside(coup, (low, high), y_pair, z_pair)
+            resid[c, at, :] = rest * rhs[c, at, :] + (total - DAMPING * sums[c, at, :])
+    m0, m1 = mode_rows(8, nz)
+    row = row_iota(8, nz)
     modes = split3(jnp.where(row == 0, m0, jnp.where(row == 1, m1, 0.0)))
+
+    def mode_sums(v):
+        s = sum(dot_tt(modes, part) for part in parts3(v))
+        return s[0:8] + (s[8:16] + s[16:24])
+
     for c in range(3):
-        s = sum(dot_tt(modes, part) for part in parts3(resid[c]))
-        s = (s[0:8] + (s[8:16] + s[16:24]))[0:2]
-        packet[2 * c : 2 * c + 2, :] = s[:, :half]
-        packet[8 + 2 * c : 10 + 2 * c, :] = s[:, half:]
+        s = mode_sums(resid[c])
+        packet[2 * c : 2 * c + 2, :] = s[0:2, :half]
+        packet[8 + 2 * c : 10 + 2 * c, :] = s[0:2, half:]
+    toward = [
+        neighbour("gy", [r[3 * nx : 4 * nx, :] for r in (ye, yo)], high) for high in (False, True)
+    ]
+    wide[...] = jnp.zeros_like(wide)
+    for c in range(3):
+        for side, y in enumerate((0, ny - 1)):
+            at = (2 * c + side) * nx
+            wide[at : at + nx, :] = toward[side] * second[c, pl.ds(y, nx, stride=ny), :]
+    s = mode_sums(wide[...])
     for k in range(2):
         packet[8 * k + 6 : 8 * k + 7, :] = ids[:, k * half : (k + 1) * half]
-        packet[8 * k + 7 : 8 * k + 8, :] = jnp.zeros((1, half), jnp.float32)
-    put_inverses(packet, 16, [recv[2][3 * dims.nx : 3 * dims.nx + 36, :]])
+        packet[8 * k + 7 : 8 * k + 8, :] = s[k : k + 1, :]
+    groups = dims.groups
+    lane = lane_iota(nz, 3 * rows)
+    c_of, p_of = lax.div(lane, rows), lax.rem(lane, rows)
+    spread = jnp.where(row_iota(nz, 3 * rows) == c_of * groups + lax.div(p_of, 8), 1.0, 0.0)
+    spread = spread.astype(jnp.bfloat16)
+    keep = lax.rem(lane_iota(8, 3 * rows), 8) == row_iota(8, 3 * rows)
+    steps = [(packet, 16), *[(ref, 0) for ref in z_more]]
+    for (ref, at), recv, k in zip(steps, z_recv, face_index("gz", nz)):
+        face = pack_z(dims, [second.at[c] for c in range(3)], k)
+        beyond = recv[0:8, :]
+        coup = jnp.zeros_like(beyond)
+        lane = lane_iota(8, nz)
+        for c in range(3):
+            inside = (lane >= c * groups) & (lane < (c + 1) * groups)
+            coup = jnp.where(inside, pltpu.roll(beyond, (nz - (3 - c) * groups) % nz, 1), coup)
+        s = lax.dot_general(
+            split3(coup * face),
+            spread,
+            (((1,), (0,)), ((), ())),
+            preferred_element_type=jnp.float32,
+        )
+        s = jnp.where(keep, s[0:8] + (s[8:16] + s[16:24]), 0.0)
+        s = jnp.sum(s, axis=0, keepdims=True)
+        mode = ((nz - 1 - k).astype(jnp.float32) - (nz - 1) / 2.0) / (nz / 2.0) * (3.0 / nz) ** 0.5
+        ref[at : at + 16, :] = jnp.zeros((16, half), jnp.float32)
+        for c in range(3):
+            for side in range(2):
+                v = s[:, c * rows + side * half : c * rows + (side + 1) * half]
+                to = at + 8 * side + 2 * c
+                ref[to : to + 1, :] = v * nz ** (-0.5)
+                ref[to + 1 : to + 2, :] = v * mode
+    put_inverses(packet, 32, [r[4 * nx : 4 * nx + 36, :] for r in (ye, yo)])
 
 
 def pencil_row(dims, square):
@@ -383,6 +448,35 @@
     return held, rest
 
 
+def add_beside(dims, sizes, packets):
+    n_y, n_z = sizes
+    owners = n_y * n_z
+    nx, ny, nz, rows = dims.nx, dims.ny, dims.nz, dims.rows
+    half = rows // 2
+    lane = lane_iota(half, 3 * rows)
+    row = row_iota(half, 3 * rows)
+    c, p = lax.div(lane, rows), lax.rem(lane, rows)
+    x, y = lax.div(p, ny), lax.rem(p, ny)
+    low, high = row == 2 * c * nx + x, row == (2 * c + 1) * nx + x
+    spread = jnp.where(((y == ny - 1) & low) | ((y == 0) & high), 1.0, 0.0).astype(jnp.bfloat16)
+    y = lax.rem(lane_iota(owners, 3 * rows), ny)
+    for m in range(2):
+        parts = parts3(packets[m][pl.ds(7, owners, stride=8), :])
+        s = sum(
+            lax.dot_general(
+                part, spread, (((1,), (0,)), ((), ())), preferred_element_type=jnp.float32
+            )
+            for part in parts
+        )
+        above, below = pltpu.roll(s, owners - n_z, 0), pltpu.roll(s, n_z, 0)
+        s = jnp.where(y == ny - 1, above, jnp.where(y == 0, below, 0.0))
+        for c in range(3):
+            at = pl.ds(2 * c + m, owners, stride=8)
+            for side in range(2):
+                v = s[:, c * rows + side * half : c * rows + (side + 1) * half]
+                packets[side][at, :] = packets[side][at, :] + v
+
+
 def solve_kernel(dims, sizes, own, *refs):
     n_y, n_z = sizes
     owners = n_y * n_z
@@ -390,31 +484,36 @@
     my_y, my_z = lax.axis_index("gy"), lax.axis_index("gz")
     arrived, coarse_inv, refs = refs[:n_y], refs[n_y], refs[n_y + 1 :]
     held, rest = blocks_of(n_y, n_z)
-    pieces, refs = refs[: 6 + len(rest)], refs[6 + len(rest) :]
-    stack, beyond_out, coarse, correction, inverses, packets = refs
+    pieces, refs = refs[: 5 + len(rest)], refs[5 + len(rest) :]
+    stack, beyond_out, coarse, correction, inverses, *packets = refs
     put_inverses(inverses, 0, [coarse_inv[...]])
     at = 36
-    fat_ye, fat_yo, fat_z, thin_ye, thin_z, first_z = pieces[:6]
+    ye, yo, z, more_z, more_e = pieces[:5]
     for ref, start, count in (
-        (fat_ye, 3 * dims.nx, 36),
-        (fat_yo, 3 * dims.nx, 36),
-        (fat_z, 8, 36),
-        (thin_z, 8, 72),
-        (thin_ye, 3 * dims.nx, 36),
-        (first_z, 16, 36),
+        (ye, 4 * dims.nx, 36),
+        (yo, 4 * dims.nx, 36),
+        (z, 8, 36),
+        (more_z, 32, 72),
+        (more_e, 16 * n_z, 72),
     ):
         inverses[at : at + count, :] = ref[start : start + count, :]
         at += count
-    for piece in pieces[6:]:
+    for piece in pieces[5:]:
         put_inverses(inverses, at, [piece[:, 0, :]])
         at += 36
     order = held + rest
     for y, ref in zip(words_of(n_y), arrived):
         for k, z in enumerate(words_of(n_z)):
             at = follow(my_y, n_y, y) * n_z + follow(my_z, n_z, z)
+            at = pl.ds(pl.multiple_of(8 * at, 8), 8)
             for side in range(2):
-                v = ref[16 * k + 8 * side : 16 * k + 8 * side + 8, :]
-                packets[at, :, side * rows // 2 : (side + 1) * rows // 2] = v
+                packets[side][at, :] = ref[16 * k + 8 * side : 16 * k + 8 * side + 8, :]
+    add_beside(dims, sizes, packets)
+
+    def packet_of(d):
+        at = pl.ds(pl.multiple_of(8 * d, 8), 8)
+        return jnp.concatenate([packets[0][at, :], packets[1][at, :]], axis=1)
+
     local = row_iota(own, rows).astype(jnp.bfloat16)
     one_b = jnp.ones((own, rows), jnp.bfloat16)
     zero_b = jnp.zeros((own, rows), jnp.bfloat16)
@@ -431,7 +530,7 @@
     coarse[...] = jnp.zeros_like(coarse)
 
     def add(d, carry):
-        pack = packets[d]
+        pack = packet_of(d)
         ids = pack[6:7]
         parts = split3(jnp.where(row_iota(8, rows) < 6, pack, 0.0))
         for j in range(owners):
@@ -456,7 +555,7 @@
         inside = (y >= 0) & (y < n_y) & (z >= 0) & (z < n_z)
         y = jnp.clip(y, 0, n_y - 1)
         z = jnp.clip(z, 0, n_z - 1)
-        return jnp.where(inside, packets[y * n_z + z, 6:7, :], -1.0)
+        return jnp.where(inside, packet_of(y * n_z + z)[6:7], -1.0)
 
     upper = lax.rem(lane_iota(1, rows), dims.ny) >= dims.ny // 2
 
@@ -637,7 +736,7 @@
         part(first_kernel, dims, z_count),
         "first",
         [vector, (9, rows, nz), vector, (6, rows, nz), (36, own), (1, rows)]
-        + faces(3, 36, 36)
+        + faces(3, nx + 36, nx + 36)
         + z_faces(36),
         [
             pltpu.VMEM((9, rows, nz), f32),
@@ -655,7 +754,7 @@
     second, sums, *sends = call(
         part(second_kernel, dims, z_count),
         "second",
-        [vector, vector] + faces(3, 36, 0) + z_faces(72),
+        [vector, vector] + faces(3, 0, 0)[:2],
         [pltpu.VMEM(vector, f32)],
         inverse,
         couplings,
@@ -663,40 +762,49 @@
         *fat,
         *fat_z,
     )
-    thin, thin_z = exchange(sends[:4], sends[4:], False)
-    (packet,) = call(
+    second_x = [swap(sends[0], "gx", 0), swap(sends[1], "gx", 1)]
+    half = rows // 2
+    packet, *z_more = call(
         part(coarse_kernel, dims, z_count),
         "coarse",
-        [(16 + 36, rows // 2)],
-        [pltpu.VMEM(vector, f32)] * 2,
+        [(32 + 72, half)] + [(16, half)] * (z_count - 1),
+        [pltpu.VMEM(vector, f32), pltpu.VMEM((half, nz), f32)],
         rhs,
         sums,
         couplings,
         second,
         ids,
-        *thin,
-        *thin_z,
+        *second_x,
+        *fat[2:],
+        *fat_z,
     )
     z_words, y_words = words_of(n_z), words_of(n_y)
-    first_z = fetch(packet, (), z_words[1])
-    packet = packet[:16]
-    others = [fetch(packet, (), z) for z in z_words[2:]]
-    packet = jnp.concatenate([packet, first_z[:16]] + others, axis=0)
-    packets = [fetch(packet, y, ()) if y else packet for y in y_words]
+    if n_z == 2:
+        more_z = fetch(packet, (), z_words[1])
+        mine = packet[:16] + more_z[16:32]
+        theirs = more_z[:16] + packet[16:32]
+        joined = jnp.concatenate([mine, theirs], axis=0)
+    else:
+        mine = packet[:16] + swap(packet[16:32], "gz", 0) + swap(z_more[0], "gz", 1)
+        more_z = fetch(jnp.concatenate([mine, packet[16:]], axis=0), (), z_words[1])
+        others = [fetch(mine, (), z) for z in z_words[2:]]
+        joined = jnp.concatenate([mine, more_z[:16]] + others, axis=0)
+    with_more = jnp.concatenate([joined, packet[68:], more_z[68:]], axis=0)
+    packets = [joined, fetch(with_more, y_words[1], ())]
+    packets += [fetch(joined, y, ()) for y in y_words[2:]]
     stack, beyond = call(
         part(solve_kernel, dims, (n_y, n_z), own),
         "solve",
         [(8, rows), (24, rows)],
         [pltpu.VMEM((owners * 8, own), f32)] * 2 + [pltpu.VMEM((owners * 36, own), f32)]
-        + [pltpu.VMEM((owners, 8, rows), f32)],
+        + [pltpu.VMEM((owners * 8, half), f32)] * 2,
         *packets,
         own_inv,
         fat[2],
         fat[3],
         fat_z[0],
-        thin[2],
-        thin_z[0],
-        first_z,
+        more_z,
+        packets[1],
         *pieces,
     )
     xe, xo = swap(stack, "gx", 0), swap(stack, "gx", 1)

time: 46.6 us -> 43.7 us (0.938)
  starting transfers between devices: 21.9 us -> 19 us
    ppermute x15 -> x13, starting transfers between devices: 16.5 us -> 11.5 us  [swap(): lax.ppermute(value, axis, [(partner(i, count, odd), i) for i in range(cou...]
    ppermute x15 -> x13, waiting for transfers between devices: 8.03 us -> 10.5 us  [swap(): lax.ppermute(value, axis, [(partner(i, count, odd), i) for i in range(cou...]
    ppermute x4, starting transfers between devices: 4.32 us -> 6.01 us  [fetch(): return lax.ppermute(value, ('gy', 'gz'), which)]
    ppermute x4, waiting for transfers between devices: 7.07 us -> 5.73 us  [fetch(): return lax.ppermute(value, ('gy', 'gz'), which)]
    ppermute x2 -> x1, waiting for transfers between devices: 1.2 us -> 0.01 us  [swap_inner(): return lax.ppermute(value, (axis, spare), which)]
    ppermute x2 -> x1, starting transfers between devices: 1.07 us -> 1.49 us  [swap_inner(): return lax.ppermute(value, (axis, spare), which)]
  transfers between devices with their start and end apart: 21 -> 18, of which waited for: 9 -> 8; matrix products, arithmetic and copies ran while one was open for 0% -> 0% of each run, Pallas kernels for 0% -> 0%
where the time goes in v8:
time: 43.7 us; the launch traced here: 43.5 us
  starting transfers between devices  19 us (43%)
  waiting for transfers between devices  16.2 us (37%)
  Pallas kernels  8.16 us (19%)
    ppermute x13, starting transfers between devices, swap(): lax.ppermute(value, axis, [(partner(i, count, odd), i) for i in range(cou...  11.5 us
    ppermute x13, waiting for transfers between devices, swap(): lax.ppermute(value, axis, [(partner(i, count, odd), i) for i in range(cou...  10.5 us
    pallas_call x6, Pallas kernels, call(): pl.pallas_call(body, name=name, out_shape=[jax.ShapeDtypeStruct(s, jnp.fl...  8.16 us
    ppermute x4, starting transfers between devices, fetch(): return lax.ppermute(value, ('gy', 'gz'), which)  6.01 us
    ppermute x4, waiting for transfers between devices, fetch(): return lax.ppermute(value, ('gy', 'gz'), which)  5.73 us
    ppermute x1, starting transfers between devices, swap_inner(): return lax.ppermute(value, (axis, spare), which)  1.49 us
  transfers between devices with their start and end apart: 18, of which 8 were waited for; matrix products, arithmetic and copies ran while one was open for 0% of the time, Pallas kernels for 0%

profile of v8, /device:TPU:0, one launch (start us, length us, event | category | flops | bytes accessed | tf_op | source)
XLA Modules:
  0.0 43.5 jit_solution(14722126560315269818)
XLA Ops:
  0.0 2.0 %first.1 = (f32[3,256,128]{2,1,0:T(8,128)S(1)}, f32[9,256,128]{2,1,0:T(8,128)S(1)}, f32[3,256,128]{2,1,0:T(8,128)S(1)}, f32[6,256,128]{2,1,0:T(8,128)S(1)}, f32[...) custom-call(f32[3,256,128]{2,1,0:T(8,128)} %bitcast.6, ...), custom_call_target="tpu_custom_call" | custom-call | tf_op jit(solution)/shard_map/first/pallas_call | solution.py:701
  2.0 3.1 %collective-permute-start.2 = (f32[100,128]{1,0:T(8,128)S(1)}, f32[100,128]{1,0:T(8,128)S(1)}, u32[]{:S(2)}, u32[]{:S(2)}) collective-permute-start(f32[100,128]{1,0:T(8,128)S(1)} %get-tuple-element.33), channel_id=1, source_target_pairs={{2,0},{0,2},{6,4},{4,6},{3,1},{1,3},{7,5},{5,7},{10,8},{8,10},{14,... | collective-permute-start | bytes 153608 | tf_op jit(solution)/shard_map/ppermute | solution.py:664
  5.2 2.5 %collective-permute-start.3 = (f32[100,128]{1,0:T(8,128)S(1)}, f32[100,128]{1,0:T(8,128)S(1)}, u32[]{:S(2)}, u32[]{:S(2)}) collective-permute-start(f32[100,128]{1,0:T(8,128)S(1)} %get-tuple-element.34), channel_id=1, source_target_pairs={{6,0},{4,2},{2,4},{0,6},{7,1},{5,3},{3,5},{1,7},{14,8},{12,10},{10... | collective-permute-start | bytes 153608 | tf_op jit(solution)/shard_map/ppermute | solution.py:664
  7.6 1.6 %collective-permute-start.1 = (f32[48,128]{1,0:T(8,128)S(1)}, f32[48,128]{1,0:T(8,128)S(1)}, u32[]{:S(2)}, u32[]{:S(2)}) collective-permute-start(f32[48,128]{1,0:T(8,128)S(1)} %get-tuple-element.32), channel_id=1, source_target_pairs={{24,0},{16,8},{8,16},{0,24},{25,1},{17,9},{9,17},{1,25},{26,2},{18... | collective-permute-start | bytes 73736 | tf_op jit(solution)/shard_map/ppermute | solution.py:664
  9.3 1.5 %collective-permute-start.4 = (f32[44,128]{1,0:T(8,128)S(1)}, f32[44,128]{1,0:T(8,128)S(1)}, u32[]{:S(2)}, u32[]{:S(2)}) collective-permute-start(f32[44,128]{1,0:T(8,128)S(1)} %get-tuple-element.35), channel_id=1, source_target_pairs={{1,0},{0,1},{3,2},{2,3},{5,4},{4,5},{7,6},{6,7},{9,8},{8,9},{11,10... | collective-permute-start | bytes 67592 | tf_op jit(solution)/shard_map/ppermute | solution.py:664
  10.8 2.3 %collective-permute-done.4.refs_4_.refs_7_ = f32[44,128]{1,0:T(8,128)S(1)} collective-permute-done((f32[44,128]{1,0:T(8,128)S(1)}, f32[44,128]{1,0:T(8,128)S(1)}, u32[]{:S(2)}, u32[]{:S(2)}) %collective-permute-start.4) | collective-permute-done | bytes 22560 | tf_op jit(solution)/shard_map/ppermute | solution.py:664
  13.8 0.6 %collective-permute-start.6 = (f32[48,128]{1,0:T(8,128)S(1)}, f32[48,128]{1,0:T(8,128)S(1)}, u32[]{:S(2)}, u32[]{:S(2)}) collective-permute-start(f32[48,128]{1,0:T(8,128)S(1)} %get-tuple-element.41), channel_id=1, source_target_pairs={{24,0},{16,8},{8,16},{0,24},{25,1},{17,9},{9,17},{1,25},{26,2},{18... | collective-permute-start | bytes 73736 | tf_op jit(solution)/shard_map/ppermute | solution.py:664
  15.0 2.1 %collective-permute-done.6.refs_1_ = f32[48,128]{1,0:T(8,128)S(1)} collective-permute-done((f32[48,128]{1,0:T(8,128)S(1)}, f32[48,128]{1,0:T(8,128)S(1)}, u32[]{:S(2)}, u32[]{:S(2)}) %collective-permute-start.6) | collective-permute-done | bytes 24608 | tf_op jit(solution)/shard_map/ppermute | solution.py:664
  17.1 0.7 %coarse.1 = f32[104,128]{1,0:T(8,128)S(1)} custom-call(f32[3,256,128]{2,1,0:T(8,128)S(1)} %get-tuple-element.37.rhs, f32[3,256,128]{2,1,0:T(8,128)S(1)} %get-tuple-element.38.sums, f32[6,256,128]{2,1,0:T(8,128)S(1)} %get-tuple-element.29.couplings, f32[3,256,128]{2,1,0:T(8,128)S(1)} %get-tuple-element.36.second, f32[1,256]{1,0:T(1,128)S(1)} %get-tuple-element.39.ids, ...), custom_call_target="tpu_custom_call" | custom-call | tf_op jit(solution)/shard_map/coarse/pallas_call | solution.py:701
  17.8 1.6 %collective-permute-start.7 = (f32[104,128]{1,0:T(8,128)S(1)}, f32[104,128]{1,0:T(8,128)S(1)}, u32[]{:S(2)}, u32[]{:S(2)}) collective-permute-start(f32[104,128]{1,0:T(8,128)S(1)} %coarse.1), channel_id=1, source_target_pairs={{1,0},{0,1},{3,2},{2,3},{5,4},{4,5},{7,6},{6,7},{9,8},{8,9},{11,10... | collective-permute-start | bytes 159752 | tf_op jit(solution)/shard_map/ppermute | solution.py:695
  19.4 2.7 %collective-permute-done.7.refs_8_ = f32[104,128]{1,0:T(8,128)S(1)} collective-permute-done((f32[104,128]{1,0:T(8,128)S(1)}, f32[104,128]{1,0:T(8,128)S(1)}, u32[]{:S(2)}, u32[]{:S(2)}) %collective-permute-start.7) | collective-permute-done | bytes 53280 | tf_op jit(solution)/shard_map/ppermute | solution.py:695
  22.1 0.7 %collective-permute-start.8 = (f32[104,128]{1,0:T(8,128)S(1)}, f32[104,128]{1,0:T(8,128)S(1)}, u32[]{:S(2)}, u32[]{:S(2)}) collective-permute-start(f32[104,128]{1,0:T(8,128)S(1)} %pad_maximum_fusion), channel_id=1, source_target_pairs={{2,0},{3,1},{0,2},{1,3},{6,4},{7,5},{4,6},{5,7},{10,8},{11,9},{8,1... | collective-permute-start | bytes 159752 | tf_op jit(solution)/shard_map/ppermute | solution.py:695
  22.8 1.2 %collective-permute-start.10 = (f32[32,128]{1,0:T(8,128)S(1)}, f32[32,128]{1,0:T(8,128)S(1)}, u32[]{:S(2)}, u32[]{:S(2)}) collective-permute-start(f32[32,128]{1,0:T(8,128)S(1)} %pad_maximum_fusion.1.refs_0_), channel_id=1, source_target_pairs={{4,0},{5,1},{6,2},{7,3},{0,4},{1,5},{2,6},{3,7},{12,8},{13,9},{14,... | collective-permute-start | bytes 49160 | tf_op jit(solution)/shard_map/ppermute | solution.py:695
  24.1 2.5 %collective-permute-start.9 = (f32[32,128]{1,0:T(8,128)S(1)}, f32[32,128]{1,0:T(8,128)S(1)}, u32[]{:S(2)}, u32[]{:S(2)}) collective-permute-start(f32[32,128]{1,0:T(8,128)S(1)} %pad_maximum_fusion.1.refs_0_), channel_id=1, source_target_pairs={{6,0},{7,1},{4,2},{5,3},{2,4},{3,5},{0,6},{1,7},{14,8},{15,9},{12,... | collective-permute-start | bytes 49160 | tf_op jit(solution)/shard_map/ppermute | solution.py:695
  26.5 0.9 %collective-permute-done.10.refs_3_ = f32[32,128]{1,0:T(8,128)S(1)} collective-permute-done((f32[32,128]{1,0:T(8,128)S(1)}, f32[32,128]{1,0:T(8,128)S(1)}, u32[]{:S(2)}, u32[]{:S(2)}) %collective-permute-start.10) | collective-permute-done | bytes 16416 | tf_op jit(solution)/shard_map/ppermute | solution.py:695
  27.5 2.1 %collective-permute-done.9.refs_2_ = f32[32,128]{1,0:T(8,128)S(1)} collective-permute-done((f32[32,128]{1,0:T(8,128)S(1)}, f32[32,128]{1,0:T(8,128)S(1)}, u32[]{:S(2)}, u32[]{:S(2)}) %collective-permute-start.9) | collective-permute-done | bytes 16416 | tf_op jit(solution)/shard_map/ppermute | solution.py:695
  29.6 2.7 %solve.1 = (f32[8,256]{1,0:T(8,128)S(1)}, f32[24,256]{1,0:T(8,128)S(1)}) custom-call(f32[32,128]{1,0:T(8,128)S(1)} %pad_maximum_fusion.1.refs_0_, f32[104,128]{1,0:T(8,128)S(1)} %collective-permute-done.8.refs_1_.refs_9_, f32[32,128]{1,0:T(8,128)S(1)} %collective-permute-done.9.refs_2_, f32[32,128]{1,0:T(8,128)S(1)} %collective-permute-done.10.refs_3_, ...), custom_call_target="tpu_custom_call" | custom-call | tf_op jit(solution)/shard_map/solve/pallas_call | solution.py:701
  32.4 0.7 %collective-permute-start.11 = (f32[8,256]{1,0:T(8,128)S(1)}, f32[8,256]{1,0:T(8,128)S(1)}, u32[]{:S(2)}, u32[]{:S(2)}) collective-permute-start(f32[8,256]{1,0:T(8,128)S(1)} %get-tuple-element.43.stack), channel_id=1, source_target_pairs={{8,0},{0,8},{24,16},{16,24},{9,1},{1,9},{25,17},{17,25},{10,2},{2,... | collective-permute-start | bytes 24584 | tf_op jit(solution)/shard_map/ppermute | solution.py:664
  33.1 2.4 %collective-permute-done.12.refs_1_ = f32[8,256]{1,0:T(8,128)S(1)} collective-permute-done((f32[8,256]{1,0:T(8,128)S(1)}, f32[8,256]{1,0:T(8,128)S(1)}, u32[]{:S(2)}, u32[]{:S(2)}) %collective-permute-start.12) | collective-permute-done | bytes 8224 | tf_op jit(solution)/shard_map/ppermute | solution.py:664
  35.4 0.9 %third.1 = (f32[3,256,128]{2,1,0:T(8,128)S(1)}, f32[48,128]{1,0:T(8,128)S(1)}, f32[48,128]{1,0:T(8,128)S(1)}, f32[48,128]{1,0:T(8,128)S(1)}, f32[48,128]{1,0:T(8,128)S(1)}, /*index=5*/f32[8,128]{1,0:T(8,128)S(1)}) custom-call(f32[9,256,128]{2,1,0:T(8,128)S(1)} %get-tuple-element.28.inverse, f32[6,256,128]{2,1,0:T(8,128)S(1)} %get-tuple-element.29.couplings, ...), custom_call_target="tpu_custom_call" | custom-call | tf_op jit(solution)/shard_map/third/pallas_call | solution.py:701
  36.3 0.8 %collective-permute-start.14 = (f32[48,128]{1,0:T(8,128)S(1)}, f32[48,128]{1,0:T(8,128)S(1)}, u32[]{:S(2)}, u32[]{:S(2)}) collective-permute-start(f32[48,128]{1,0:T(8,128)S(1)} %get-tuple-element.47), channel_id=1, source_target_pairs={{24,0},{16,8},{8,16},{0,24},{25,1},{17,9},{9,17},{1,25},{26,2},{18... | collective-permute-start | bytes 73736 | tf_op jit(solution)/shard_map/ppermute | solution.py:664
  37.1 1.5 %collective-permute-start.16 = (f32[48,128]{1,0:T(8,128)S(1)}, f32[48,128]{1,0:T(8,128)S(1)}, u32[]{:S(2)}, u32[]{:S(2)}) collective-permute-start(f32[48,128]{1,0:T(8,128)S(1)} %get-tuple-element.49), channel_id=1, source_target_pairs={{1,0},{0,1},{4,2},{5,3},{2,4},{3,5},{7,6},{6,7},{9,8},{8,9},{12,10... | collective-permute-start | bytes 73736 | tf_op jit(solution)/shard_map/ppermute | solution.py:675
  39.1 3.1 %collective-permute-done.17.refs_4_ = f32[8,128]{1,0:T(8,128)S(1)} collective-permute-done((f32[8,128]{1,0:T(8,128)S(1)}, f32[8,128]{1,0:T(8,128)S(1)}, u32[]{:S(2)}, u32[]{:S(2)}) %collective-permute-start.17) | collective-permute-done | bytes 4128 | tf_op jit(solution)/shard_map/ppermute | solution.py:664
  42.2 1.3 %last.1 = f32[3,256,128]{2,1,0:T(8,128)} custom-call(f32[9,256,128]{2,1,0:T(8,128)S(1)} %get-tuple-element.28.inverse, f32[6,256,128]{2,1,0:T(8,128)S(1)} %get-tuple-element.29.couplings, f32[3,256,128]{2,1,0:T(8,128)S(1)} %get-tuple-element.30.first, f32[3,256,128]{2,1,0:T(8,128)S(1)} %get-tuple-element.45.third, ...), custom_call_target="tpu_custom_call" | custom-call | tf_op jit(solution)/shard_map/last/pallas_call | solution.py:701
  (23 shorter events, 1.9 us)
Async XLA Ops:
  2.0 11.1 %collective-permute-start.2 = (f32[100,128]{1,0:T(8,128)S(1)}, f32[100,128]{1,0:T(8,128)S(1)}, u32[]{:S(2)}, u32[]{:S(2)}) collective-permute-start(f32[100,128]{1,0:T(8,128)S(1)} %get-tuple-element.33), channel_id=1, source_target_pairs={{2,0},{0,2},{6,4},{4,6},{3,1},{1,3},{7,5},{5,7},{10,8},{8,10},{14,... | collective-permute-start | bytes 153608 | tf_op jit(solution)/shard_map/ppermute | solution.py:664
  5.2 8.0 %collective-permute-start.3 = (f32[100,128]{1,0:T(8,128)S(1)}, f32[100,128]{1,0:T(8,128)S(1)}, u32[]{:S(2)}, u32[]{:S(2)}) collective-permute-start(f32[100,128]{1,0:T(8,128)S(1)} %get-tuple-element.34), channel_id=1, source_target_pairs={{6,0},{4,2},{2,4},{0,6},{7,1},{5,3},{3,5},{1,7},{14,8},{12,10},{10... | collective-permute-start | bytes 153608 | tf_op jit(solution)/shard_map/ppermute | solution.py:664
  7.6 5.5 %collective-permute-start = (f32[48,128]{1,0:T(8,128)S(1)}, f32[48,128]{1,0:T(8,128)S(1)}, u32[]{:S(2)}, u32[]{:S(2)}) collective-permute-start(f32[48,128]{1,0:T(8,128)S(1)} %get-tuple-element.31), channel_id=1, source_target_pairs={{8,0},{0,8},{24,16},{16,24},{9,1},{1,9},{25,17},{17,25},{10,2},{2,... | collective-permute-start | bytes 73736 | tf_op jit(solution)/shard_map/ppermute | solution.py:664
  7.6 5.5 %collective-permute-start.1 = (f32[48,128]{1,0:T(8,128)S(1)}, f32[48,128]{1,0:T(8,128)S(1)}, u32[]{:S(2)}, u32[]{:S(2)}) collective-permute-start(f32[48,128]{1,0:T(8,128)S(1)} %get-tuple-element.32), channel_id=1, source_target_pairs={{24,0},{16,8},{8,16},{0,24},{25,1},{17,9},{9,17},{1,25},{26,2},{18... | collective-permute-start | bytes 73736 | tf_op jit(solution)/shard_map/ppermute | solution.py:664
  9.3 3.8 %collective-permute-start.4 = (f32[44,128]{1,0:T(8,128)S(1)}, f32[44,128]{1,0:T(8,128)S(1)}, u32[]{:S(2)}, u32[]{:S(2)}) collective-permute-start(f32[44,128]{1,0:T(8,128)S(1)} %get-tuple-element.35), channel_id=1, source_target_pairs={{1,0},{0,1},{3,2},{2,3},{5,4},{4,5},{7,6},{6,7},{9,8},{8,9},{11,10... | collective-permute-start | bytes 67592 | tf_op jit(solution)/shard_map/ppermute | solution.py:664
  13.7 1.3 %collective-permute-start.5 = (f32[48,128]{1,0:T(8,128)S(1)}, f32[48,128]{1,0:T(8,128)S(1)}, u32[]{:S(2)}, u32[]{:S(2)}) collective-permute-start(f32[48,128]{1,0:T(8,128)S(1)} %get-tuple-element.40), channel_id=1, source_target_pairs={{8,0},{0,8},{24,16},{16,24},{9,1},{1,9},{25,17},{17,25},{10,2},{2,... | collective-permute-start | bytes 73736 | tf_op jit(solution)/shard_map/ppermute | solution.py:664
  13.8 3.3 %collective-permute-start.6 = (f32[48,128]{1,0:T(8,128)S(1)}, f32[48,128]{1,0:T(8,128)S(1)}, u32[]{:S(2)}, u32[]{:S(2)}) collective-permute-start(f32[48,128]{1,0:T(8,128)S(1)} %get-tuple-element.41), channel_id=1, source_target_pairs={{24,0},{16,8},{8,16},{0,24},{25,1},{17,9},{9,17},{1,25},{26,2},{18... | collective-permute-start | bytes 73736 | tf_op jit(solution)/shard_map/ppermute | solution.py:664
  17.8 4.2 %collective-permute-start.7 = (f32[104,128]{1,0:T(8,128)S(1)}, f32[104,128]{1,0:T(8,128)S(1)}, u32[]{:S(2)}, u32[]{:S(2)}) collective-permute-start(f32[104,128]{1,0:T(8,128)S(1)} %coarse.1), channel_id=1, source_target_pairs={{1,0},{0,1},{3,2},{2,3},{5,4},{4,5},{7,6},{6,7},{9,8},{8,9},{11,10... | collective-permute-start | bytes 159752 | tf_op jit(solution)/shard_map/ppermute | solution.py:695
  22.1 7.5 %collective-permute-start.8 = (f32[104,128]{1,0:T(8,128)S(1)}, f32[104,128]{1,0:T(8,128)S(1)}, u32[]{:S(2)}, u32[]{:S(2)}) collective-permute-start(f32[104,128]{1,0:T(8,128)S(1)} %pad_maximum_fusion), channel_id=1, source_target_pairs={{2,0},{3,1},{0,2},{1,3},{6,4},{7,5},{4,6},{5,7},{10,8},{11,9},{8,1... | collective-permute-start | bytes 159752 | tf_op jit(solution)/shard_map/ppermute | solution.py:695
  22.8 4.6 %collective-permute-start.10 = (f32[32,128]{1,0:T(8,128)S(1)}, f32[32,128]{1,0:T(8,128)S(1)}, u32[]{:S(2)}, u32[]{:S(2)}) collective-permute-start(f32[32,128]{1,0:T(8,128)S(1)} %pad_maximum_fusion.1.refs_0_), channel_id=1, source_target_pairs={{4,0},{5,1},{6,2},{7,3},{0,4},{1,5},{2,6},{3,7},{12,8},{13,9},{14,... | collective-permute-start | bytes 49160 | tf_op jit(solution)/shard_map/ppermute | solution.py:695
  24.1 5.5 %collective-permute-start.9 = (f32[32,128]{1,0:T(8,128)S(1)}, f32[32,128]{1,0:T(8,128)S(1)}, u32[]{:S(2)}, u32[]{:S(2)}) collective-permute-start(f32[32,128]{1,0:T(8,128)S(1)} %pad_maximum_fusion.1.refs_0_), channel_id=1, source_target_pairs={{6,0},{7,1},{4,2},{5,3},{2,4},{3,5},{0,6},{1,7},{14,8},{15,9},{12,... | collective-permute-start | bytes 49160 | tf_op jit(solution)/shard_map/ppermute | solution.py:695
  32.3 3.1 %collective-permute-start.12 = (f32[8,256]{1,0:T(8,128)S(1)}, f32[8,256]{1,0:T(8,128)S(1)}, u32[]{:S(2)}, u32[]{:S(2)}) collective-permute-start(f32[8,256]{1,0:T(8,128)S(1)} %get-tuple-element.43.stack), channel_id=1, source_target_pairs={{24,0},{16,8},{8,16},{0,24},{25,1},{17,9},{9,17},{1,25},{26,2},{18... | collective-permute-start | bytes 24584 | tf_op jit(solution)/shard_map/ppermute | solution.py:664
  32.4 3.1 %collective-permute-start.11 = (f32[8,256]{1,0:T(8,128)S(1)}, f32[8,256]{1,0:T(8,128)S(1)}, u32[]{:S(2)}, u32[]{:S(2)}) collective-permute-start(f32[8,256]{1,0:T(8,128)S(1)} %get-tuple-element.43.stack), channel_id=1, source_target_pairs={{8,0},{0,8},{24,16},{16,24},{9,1},{1,9},{25,17},{17,25},{10,2},{2,... | collective-permute-start | bytes 24584 | tf_op jit(solution)/shard_map/ppermute | solution.py:664
  36.3 5.9 %collective-permute-start.13 = (f32[48,128]{1,0:T(8,128)S(1)}, f32[48,128]{1,0:T(8,128)S(1)}, u32[]{:S(2)}, u32[]{:S(2)}) collective-permute-start(f32[48,128]{1,0:T(8,128)S(1)} %get-tuple-element.46), channel_id=1, source_target_pairs={{8,0},{0,8},{24,16},{16,24},{9,1},{1,9},{25,17},{17,25},{10,2},{2,... | collective-permute-start | bytes 73736 | tf_op jit(solution)/shard_map/ppermute | solution.py:664
  36.3 5.9 %collective-permute-start.14 = (f32[48,128]{1,0:T(8,128)S(1)}, f32[48,128]{1,0:T(8,128)S(1)}, u32[]{:S(2)}, u32[]{:S(2)}) collective-permute-start(f32[48,128]{1,0:T(8,128)S(1)} %get-tuple-element.47), channel_id=1, source_target_pairs={{24,0},{16,8},{8,16},{0,24},{25,1},{17,9},{9,17},{1,25},{26,2},{18... | collective-permute-start | bytes 73736 | tf_op jit(solution)/shard_map/ppermute | solution.py:664
  37.1 5.1 %collective-permute-start.15 = (f32[48,128]{1,0:T(8,128)S(1)}, f32[48,128]{1,0:T(8,128)S(1)}, u32[]{:S(2)}, u32[]{:S(2)}) collective-permute-start(f32[48,128]{1,0:T(8,128)S(1)} %get-tuple-element.48), channel_id=1, source_target_pairs={{2,0},{0,2},{6,4},{4,6},{3,1},{1,3},{7,5},{5,7},{10,8},{8,10},{14,... | collective-permute-start | bytes 73736 | tf_op jit(solution)/shard_map/ppermute | solution.py:664
  37.1 5.1 %collective-permute-start.16 = (f32[48,128]{1,0:T(8,128)S(1)}, f32[48,128]{1,0:T(8,128)S(1)}, u32[]{:S(2)}, u32[]{:S(2)}) collective-permute-start(f32[48,128]{1,0:T(8,128)S(1)} %get-tuple-element.49), channel_id=1, source_target_pairs={{1,0},{0,1},{4,2},{5,3},{2,4},{3,5},{7,6},{6,7},{9,8},{8,9},{12,10... | collective-permute-start | bytes 73736 | tf_op jit(solution)/shard_map/ppermute | solution.py:675
  38.6 3.6 %collective-permute-start.17 = (f32[8,128]{1,0:T(8,128)S(1)}, f32[8,128]{1,0:T(8,128)S(1)}, u32[]{:S(2)}, u32[]{:S(2)}) collective-permute-start(f32[8,128]{1,0:T(8,128)S(1)} %get-tuple-element.50), channel_id=1, source_target_pairs={{1,0},{0,1},{3,2},{2,3},{5,4},{4,5},{7,6},{6,7},{9,8},{8,9},{11,10... | collective-permute-start | bytes 12296 | tf_op jit(solution)/shard_map/ppermute | solution.py:664

commit v9 on v8

--- a/solution.py
+++ b/solution.py
@@ -7,9 +7,10 @@
 from jax.experimental.pallas import tpu as pltpu
 from jax.sharding import PartitionSpec as P
 
+
 DAMPING = 0.8
-AXES = ("gx", "gy", "gz")
 VMEM_LIMIT = 12 * 1024 * 1024
+EO = (False, True)
 
 
 def dot_tt(a, b):
@@ -103,10 +104,6 @@
 
 def tiles(ref, count, x, size):
     return [tile(ref, c, x, size) for c in range(count)]
-
-
-def flat_tiles(ref, start, count, size):
-    return [ref[(start + c) * size : (start + c + 1) * size, :] for c in range(count)]
 
 
 def face_index(axis, count):
@@ -244,13 +241,27 @@
         start += 36
 
 
+def put_tables(dims, spread_y, spread_z):
+    nx, ny, rows = dims.nx, dims.ny, dims.rows
+    half = rows // 2
+    for c in range(3):
+        row, p = row_iota(half, rows), lane_iota(half, rows)
+        x, y = lax.div(p, ny), lax.rem(p, ny)
+        low, high = row == 2 * c * nx + x, row == (2 * c + 1) * nx + x
+        at = slice(c * rows, (c + 1) * rows)
+        hit = ((y == ny - 1) & low) | ((y == 0) & high)
+        spread_y[:, at] = jnp.where(hit, 1.0, 0.0).astype(jnp.bfloat16)
+        hit = row == c * dims.groups + lax.div(p, 8)
+        spread_z[:, at] = jnp.where(hit, 1.0, 0.0).astype(jnp.bfloat16)
+
+
 CHUNKS = 4
 
 
 def first_kernel(dims, n_z, *refs):
     rhs_in, blocks_in, couplings_in, coarse_inv_in, ids_in = refs[:5]
-    first, inverse, rhs, couplings, own, ids, xe, xo, ye, yo = refs[5:15]
-    z_sends, (blocks, coarse_inv, square, sems) = refs[15 : 15 + n_z], refs[15 + n_z :]
+    first, inverse, rhs, couplings, own, ids, spread_y, spread_z, xe, xo, ye, yo = refs[5:17]
+    z_sends, (blocks, coarse_inv, square, sems) = refs[17 : 17 + n_z], refs[17 + n_z :]
     step = dims.rows // CHUNKS
 
     def copy(k, src, dst, rows):
@@ -266,6 +277,7 @@
     copies.append(pltpu.make_async_copy(ids_in, square, sems.at[2 * CHUNKS + 2]))
     for c in copies:
         c.start()
+    put_tables(dims, spread_y, spread_z)
     for x in range(dims.nx):
         if x % (dims.nx // CHUNKS) == 0:
             k = x // (dims.nx // CHUNKS)
@@ -287,15 +299,16 @@
         ref[3 * dims.nx : 4 * dims.nx, :] = inner_odd("gy", v) if odd else v
     own[...] = coarse_inv[:, 0, :]
     put_inverses(ye, 4 * dims.nx, [own[...]])
-    put_inverses(yo, 4 * dims.nx, [own[...]])
     put_inverses(z_sends[0], 8, [own[...]])
     ids[...] = pencil_row(dims, square[0].astype(jnp.float32))
 
 
-def second_kernel(dims, n_z, inverse, couplings, first, *refs):
+def second_kernel(dims, n_z, inverse, couplings, first, own, *refs):
     recv, z_recv, refs = refs[:4], refs[4 : 4 + n_z], refs[4 + n_z :]
     second, sums, *sends = refs[:4]
-    z_halo = refs[4]
+    inverses, z_halo = refs[4:]
+    e_block = recv[2][4 * dims.nx : 4 * dims.nx + 36, :]
+    put_inverses(inverses, 0, [own[...], z_recv[0][8:44, :], e_block])
     x_halo, y_halo = received(dims, recv)
     place_z(dims, z_recv, z_halo)
     for x in range(dims.nx):
@@ -309,7 +322,7 @@
     put_x(dims, second, sends)
 
 
-def coarse_kernel(dims, n_z, rhs, sums, couplings, second, ids, *refs):
+def coarse_kernel(dims, n_z, rhs, sums, couplings, second, ids, spread, *refs):
     nx, ny, nz, rows = dims.nx, dims.ny, dims.nz, dims.rows
     half = rows // 2
     (xe, xo, ye, yo), z_recv, refs = refs[:4], refs[4 : 4 + n_z], refs[4 + n_z :]
@@ -361,10 +374,6 @@
         packet[8 * k + 6 : 8 * k + 7, :] = ids[:, k * half : (k + 1) * half]
         packet[8 * k + 7 : 8 * k + 8, :] = s[k : k + 1, :]
     groups = dims.groups
-    lane = lane_iota(nz, 3 * rows)
-    c_of, p_of = lax.div(lane, rows), lax.rem(lane, rows)
-    spread = jnp.where(row_iota(nz, 3 * rows) == c_of * groups + lax.div(p_of, 8), 1.0, 0.0)
-    spread = spread.astype(jnp.bfloat16)
     keep = lax.rem(lane_iota(8, 3 * rows), 8) == row_iota(8, 3 * rows)
     steps = [(packet, 16), *[(ref, 0) for ref in z_more]]
     for (ref, at), recv, k in zip(steps, z_recv, face_index("gz", nz)):
@@ -377,7 +386,7 @@
             coup = jnp.where(inside, pltpu.roll(beyond, (nz - (3 - c) * groups) % nz, 1), coup)
         s = lax.dot_general(
             split3(coup * face),
-            spread,
+            spread[...],
             (((1,), (0,)), ((), ())),
             preferred_element_type=jnp.float32,
         )
@@ -391,7 +400,6 @@
                 to = at + 8 * side + 2 * c
                 ref[to : to + 1, :] = v * nz ** (-0.5)
                 ref[to + 1 : to + 2, :] = v * mode
-    put_inverses(packet, 32, [r[4 * nx : 4 * nx + 36, :] for r in (ye, yo)])
 
 
 def pencil_row(dims, square):
@@ -436,7 +444,7 @@
 
 def blocks_of(n_y, n_z):
     e, o, none = (False,), (True,), ()
-    held = [(none, none), (e, none), (o, none), (none, e), (e, e), (o, e), (e + o, none), (e + o, e)]
+    held = [(none, none), (e, none), (none, e), (EO, none), (EO, e), (EO + e, none), (e, e), (o, e)]
     found = {(follow(0, n_y, y), follow(0, n_z, z)) for y, z in held}
     rest = []
     for y in words_of(n_y):
@@ -448,23 +456,17 @@
     return held, rest
 
 
-def add_beside(dims, sizes, packets):
+def add_beside(dims, sizes, packets, spread):
     n_y, n_z = sizes
     owners = n_y * n_z
-    nx, ny, nz, rows = dims.nx, dims.ny, dims.nz, dims.rows
+    ny, rows = dims.ny, dims.rows
     half = rows // 2
-    lane = lane_iota(half, 3 * rows)
-    row = row_iota(half, 3 * rows)
-    c, p = lax.div(lane, rows), lax.rem(lane, rows)
-    x, y = lax.div(p, ny), lax.rem(p, ny)
-    low, high = row == 2 * c * nx + x, row == (2 * c + 1) * nx + x
-    spread = jnp.where(((y == ny - 1) & low) | ((y == 0) & high), 1.0, 0.0).astype(jnp.bfloat16)
     y = lax.rem(lane_iota(owners, 3 * rows), ny)
     for m in range(2):
         parts = parts3(packets[m][pl.ds(7, owners, stride=8), :])
         s = sum(
             lax.dot_general(
-                part, spread, (((1,), (0,)), ((), ())), preferred_element_type=jnp.float32
+                part, spread[...], (((1,), (0,)), ((), ())), preferred_element_type=jnp.float32
             )
             for part in parts
         )
@@ -482,23 +484,23 @@
     owners = n_y * n_z
     rows = dims.rows
     my_y, my_z = lax.axis_index("gy"), lax.axis_index("gz")
-    arrived, coarse_inv, refs = refs[:n_y], refs[n_y], refs[n_y + 1 :]
+    arrived, coarse_inv, spread, refs = refs[:n_y], refs[n_y], refs[n_y + 1], refs[n_y + 2 :]
     held, rest = blocks_of(n_y, n_z)
-    pieces, refs = refs[: 5 + len(rest)], refs[5 + len(rest) :]
-    stack, beyond_out, coarse, correction, inverses, *packets = refs
+    pieces, refs = refs[: 4 + len(rest)], refs[4 + len(rest) :]
+    stack, beyond_out, coarse, correction, inverses, low_half, high_half, parts, members = refs
+    packets = (low_half, high_half)
     put_inverses(inverses, 0, [coarse_inv[...]])
     at = 36
-    ye, yo, z, more_z, more_e = pieces[:5]
+    ye, z, far, more_e = pieces[:4]
     for ref, start, count in (
         (ye, 4 * dims.nx, 36),
-        (yo, 4 * dims.nx, 36),
         (z, 8, 36),
-        (more_z, 32, 72),
+        (far, 0, 108),
         (more_e, 16 * n_z, 72),
     ):
         inverses[at : at + count, :] = ref[start : start + count, :]
         at += count
-    for piece in pieces[5:]:
+    for piece in pieces[4:]:
         put_inverses(inverses, at, [piece[:, 0, :]])
         at += 36
     order = held + rest
@@ -508,7 +510,7 @@
             at = pl.ds(pl.multiple_of(8 * at, 8), 8)
             for side in range(2):
                 packets[side][at, :] = ref[16 * k + 8 * side : 16 * k + 8 * side + 8, :]
-    add_beside(dims, sizes, packets)
+    add_beside(dims, sizes, packets, spread)
 
     def packet_of(d):
         at = pl.ds(pl.multiple_of(8 * d, 8), 8)
@@ -527,18 +529,19 @@
         rel = jnp.clip(ids - base, -1.0, float(own)).astype(jnp.bfloat16)
         return jnp.where(local == rel, one_b, zero_b)
 
-    coarse[...] = jnp.zeros_like(coarse)
-
-    def add(d, carry):
+    for d in range(owners):
         pack = packet_of(d)
-        ids = pack[6:7]
-        parts = split3(jnp.where(row_iota(8, rows) < 6, pack, 0.0))
-        for j in range(owners):
-            s = dot_tt(parts, member(j, ids))
-            coarse[8 * j : 8 * j + 8] = coarse[8 * j : 8 * j + 8] + (s[0:8] + (s[8:16] + s[16:24]))
-        return carry
-
-    lax.fori_loop(0, owners, add, 0, unroll=2)
+        parts[:, d * rows : (d + 1) * rows] = split3(jnp.where(row_iota(8, rows) < 6, pack, 0.0))
+    for j in range(owners):
+
+        def fill(d, carry, j=j):
+            at = pl.ds(pl.multiple_of(d * rows, rows), rows)
+            members[:, at] = member(j, packet_of(d)[6:7])
+            return carry
+
+        lax.fori_loop(0, owners, fill, 0, unroll=8)
+        s = jnp.transpose(dot_tt(members[...], parts[...]))
+        coarse[8 * j : 8 * j + 8] = s[0:8] + (s[8:16] + s[16:24])
 
     for block in range(owners // 8):
         v = [coarse[pl.ds(64 * block + k, 8, stride=8), :] for k in range(6)]
@@ -675,14 +678,20 @@
     return lax.ppermute(value, (axis, spare), which)
 
 
-def exchange(sends, z_sends, ring):
+def exchange(sends, z_sends):
     xe, xo, ye, yo = sends
-    xe = swap(xe, "gx", 0)
-    z_recv = [swap(v, "gz", k) for k, v in enumerate(z_sends)]
+    z_recv = []
+    for k, v in enumerate(z_sends):
+        z_recv.append(swap(v, "gz", k))
     ye = swap(ye, "gy", 0)
-    yo = swap(yo, "gy", 1) if ring else swap_inner(yo, "gy", "gz")
-    xo = swap(xo, "gx", 1)
-    return [xe, xo, ye, yo], z_recv
+    yo = swap_inner(yo, "gy", "gz")
+    return exchange_x([xe, xo]) + [ye, yo], z_recv
+
+
+def exchange_x(sends):
+    xo = swap(sends[1], "gx", 1)
+    xe = swap(sends[0], "gx", 0)
+    return [xe, xo]
 
 
 def fetch(value, word_y, word_z):
@@ -695,13 +704,14 @@
     return lax.ppermute(value, ("gy", "gz"), which)
 
 
-def call(body, name, out_shapes, scratch, *args, in_hbm=0, out_hbm=False):
+def call(body, out_shapes, scratch, *args, in_hbm=0, out_hbm=False):
     near = pl.BlockSpec(memory_space=pltpu.VMEM)
     far = pl.BlockSpec(memory_space=pltpu.HBM)
     return pl.pallas_call(
         body,
-        name=name,
-        out_shape=[jax.ShapeDtypeStruct(s, jnp.float32) for s in out_shapes],
+        out_shape=[
+            s if hasattr(s, "dtype") else jax.ShapeDtypeStruct(s, jnp.float32) for s in out_shapes
+        ],
         in_specs=[far] * in_hbm + [near] * (len(args) - in_hbm),
         out_specs=[far if out_hbm else near] * len(out_shapes),
         scratch_shapes=scratch,
@@ -709,7 +719,7 @@
     )(*args)
 
 
-def shards(rhs, blocks, couplings, agg_ids, coarse_inv):
+def cycle(rhs, blocks, couplings, agg_ids, coarse_inv):
     _, nx, ny, nz = rhs.shape
     dims = Dims(nx, ny, nz)
     rows = nx * ny
@@ -732,11 +742,11 @@
 
     _, rest = blocks_of(n_y, n_z)
     pieces = [fetch(coarse_inv, y, z) for y, z in rest]
-    first, inverse, rhs, couplings, own_inv, ids, *sends = call(
+    first, inverse, rhs, couplings, own_inv, ids, spread_y, spread_z, *sends = call(
         part(first_kernel, dims, z_count),
-        "first",
         [vector, (9, rows, nz), vector, (6, rows, nz), (36, own), (1, rows)]
-        + faces(3, nx + 36, nx + 36)
+        + [jax.ShapeDtypeStruct((rows // 2, 3 * rows), jnp.bfloat16)] * 2
+        + faces(3, nx + 36, nx)
         + z_faces(36),
         [
             pltpu.VMEM((9, rows, nz), f32),
@@ -750,30 +760,31 @@
         ],
         in_hbm=5,
     )
-    fat, fat_z = exchange(sends[:4], sends[4:], True)
-    second, sums, *sends = call(
+    fat, fat_z = exchange(sends[:4], sends[4:])
+    second, sums, *sends, inv_out = call(
         part(second_kernel, dims, z_count),
-        "second",
-        [vector, vector] + faces(3, 0, 0)[:2],
+        [vector, vector] + faces(3, 0, 0)[:2] + [(3 * 36, own)],
         [pltpu.VMEM(vector, f32)],
         inverse,
         couplings,
         first,
+        own_inv,
         *fat,
         *fat_z,
     )
-    second_x = [swap(sends[0], "gx", 0), swap(sends[1], "gx", 1)]
+    second_x = exchange_x(sends)
+    far_inv = fetch(inv_out, EO, ())
     half = rows // 2
     packet, *z_more = call(
         part(coarse_kernel, dims, z_count),
-        "coarse",
-        [(32 + 72, half)] + [(16, half)] * (z_count - 1),
+        [(32, half)] + [(16, half)] * (z_count - 1),
         [pltpu.VMEM(vector, f32), pltpu.VMEM((half, nz), f32)],
         rhs,
         sums,
         couplings,
         second,
         ids,
+        spread_z,
         *second_x,
         *fat[2:],
         *fat_z,
@@ -786,31 +797,29 @@
         joined = jnp.concatenate([mine, theirs], axis=0)
     else:
         mine = packet[:16] + swap(packet[16:32], "gz", 0) + swap(z_more[0], "gz", 1)
-        more_z = fetch(jnp.concatenate([mine, packet[16:]], axis=0), (), z_words[1])
-        others = [fetch(mine, (), z) for z in z_words[2:]]
-        joined = jnp.concatenate([mine, more_z[:16]] + others, axis=0)
-    with_more = jnp.concatenate([joined, packet[68:], more_z[68:]], axis=0)
-    packets = [joined, fetch(with_more, y_words[1], ())]
-    packets += [fetch(joined, y, ()) for y in y_words[2:]]
+        joined = jnp.concatenate([mine] + [fetch(mine, (), z) for z in z_words[1:]], axis=0)
+    with_more = jnp.concatenate([joined, fat_z[0][8:44], far_inv[36:72]], axis=0)
+    packets = [joined]
+    for k, y in enumerate(y_words[1:]):
+        packets.append(fetch(joined if k else with_more, y, ()))
     stack, beyond = call(
         part(solve_kernel, dims, (n_y, n_z), own),
-        "solve",
         [(8, rows), (24, rows)],
         [pltpu.VMEM((owners * 8, own), f32)] * 2 + [pltpu.VMEM((owners * 36, own), f32)]
-        + [pltpu.VMEM((owners * 8, half), f32)] * 2,
+        + [pltpu.VMEM((owners * 8, half), f32)] * 2
+        + [pltpu.VMEM((n, owners * rows), jnp.bfloat16) for n in (24, own)],
         *packets,
         own_inv,
+        spread_y,
         fat[2],
-        fat[3],
         fat_z[0],
-        more_z,
+        far_inv,
         packets[1],
         *pieces,
     )
-    xe, xo = swap(stack, "gx", 0), swap(stack, "gx", 1)
+    xe, xo = exchange_x([stack, stack])
     third, *sends = call(
         part(third_kernel, dims, z_count),
-        "third",
         [vector] + faces(3, 0, 0) + z_faces(0),
         [pltpu.VMEM(vector, f32)] * 3,
         inverse,
@@ -821,10 +830,9 @@
         xe,
         xo,
     )
-    recv, z_recv = exchange(sends[:4], sends[4:], False)
+    recv, z_recv = exchange(sends[:4], sends[4:])
     (out,) = call(
         part(last_kernel, dims, z_count),
-        "last",
         [vector],
         [pltpu.VMEM(vector, f32)] * 2 + [pltpu.SemaphoreType.DMA((CHUNKS,))],
         inverse,
@@ -840,7 +848,7 @@
 
 def solution(mesh):
     return jax.shard_map(
-        shards,
+        cycle,
         mesh=mesh,
         in_specs=(
             P(None, "gx", "gy", "gz"),

time: 43.7 us -> 45.2 us (1.034)
  waiting for transfers between devices: 16.2 us -> 18.3 us
    ppermute x13 -> x12, starting transfers between devices: 11.5 us -> 9.2 us  [swap(): lax.ppermute(value, axis, [(partner(i, count, odd), i) for i in range(cou...]
    ppermute x4 -> x5, waiting for transfers between devices: 5.73 us -> 7.18 us  [fetch(): return lax.ppermute(value, ('gy', 'gz'), which)]
    ppermute x1 -> x2, starting transfers between devices: 1.49 us -> 2.51 us  [swap_inner(): return lax.ppermute(value, (axis, spare), which)]
    ppermute x4 -> x5, starting transfers between devices: 6.01 us -> 6.89 us  [fetch(): return lax.ppermute(value, ('gy', 'gz'), which)]
    ppermute x13 -> x12, waiting for transfers between devices: 10.5 us -> 11.2 us  [swap(): lax.ppermute(value, axis, [(partner(i, count, odd), i) for i in range(cou...]
  transfers between devices with their start and end apart: 18 -> 19, of which waited for: 8 -> 10; matrix products, arithmetic and copies ran while one was open for 0% -> 0% of each run, Pallas kernels for 0% -> 0%
where the time goes in v9:
time: 45.2 us; the launch traced here: 45.1 us
  starting transfers between devices  18.6 us (41%)
  waiting for transfers between devices  18.3 us (40%)
  Pallas kernels  8.02 us (18%)
    ppermute x12, waiting for transfers between devices, swap(): lax.ppermute(value, axis, [(partner(i, count, odd), i) for i in range(cou...  11.2 us
    ppermute x12, starting transfers between devices, swap(): lax.ppermute(value, axis, [(partner(i, count, odd), i) for i in range(cou...  9.2 us
    pallas_call x6, Pallas kernels, call(): pl.pallas_call(body, out_shape=[s if hasattr(s, 'dtype') else jax.ShapeDt...  8.02 us
    ppermute x5, waiting for transfers between devices, fetch(): return lax.ppermute(value, ('gy', 'gz'), which)  7.18 us
    ppermute x5, starting transfers between devices, fetch(): return lax.ppermute(value, ('gy', 'gz'), which)  6.89 us
    ppermute x2, starting transfers between devices, swap_inner(): return lax.ppermute(value, (axis, spare), which)  2.51 us
  transfers between devices with their start and end apart: 19, of which 10 were waited for; matrix products, arithmetic and copies ran while one was open for 0% of the time, Pallas kernels for 0%

profile of v9, /device:TPU:0, one launch (start us, length us, event | category | flops | bytes accessed | tf_op | source)
XLA Modules:
  0.0 45.1 jit_solution(12391499739136951017)
XLA Ops:
  0.0 2.0 %shard_map.55 = (f32[3,256,128]{2,1,0:T(8,128)S(1)}, f32[9,256,128]{2,1,0:T(8,128)S(1)}, f32[3,256,128]{2,1,0:T(8,128)S(1)}, f32[6,256,128]{2,1,0:T(8,128)S(1)},...) custom-call(f32[3,256,128]{2,1,0:T(8,128)} %bitcast.6, ...), custom_call_target="tpu_custom_call" | custom-call | tf_op jit(solution)/shard_map/pallas_call | solution.py:710
  2.0 3.1 %collective-permute-start.2 = (f32[100,128]{1,0:T(8,128)S(1)}, f32[100,128]{1,0:T(8,128)S(1)}, u32[]{:S(2)}, u32[]{:S(2)}) collective-permute-start(f32[100,128]{1,0:T(8,128)S(1)} %get-tuple-element.37), channel_id=1, source_target_pairs={{2,0},{0,2},{6,4},{4,6},{3,1},{1,3},{7,5},{5,7},{10,8},{8,10},{14,... | collective-permute-start | bytes 153608 | tf_op jit(solution)/shard_map/ppermute | solution.py:667
  5.2 1.5 %collective-permute-start.3 = (f32[64,128]{1,0:T(8,128)S(1)}, f32[64,128]{1,0:T(8,128)S(1)}, u32[]{:S(2)}, u32[]{:S(2)}) collective-permute-start(f32[64,128]{1,0:T(8,128)S(1)} %get-tuple-element.38), channel_id=1, source_target_pairs={{1,0},{0,1},{4,2},{5,3},{2,4},{3,5},{7,6},{6,7},{9,8},{8,9},{12,10... | collective-permute-start | bytes 98312 | tf_op jit(solution)/shard_map/ppermute | solution.py:678
  6.7 1.6 %collective-permute-start.1 = (f32[48,128]{1,0:T(8,128)S(1)}, f32[48,128]{1,0:T(8,128)S(1)}, u32[]{:S(2)}, u32[]{:S(2)}) collective-permute-start(f32[48,128]{1,0:T(8,128)S(1)} %get-tuple-element.36), channel_id=1, source_target_pairs={{24,0},{16,8},{8,16},{0,24},{25,1},{17,9},{9,17},{1,25},{26,2},{18... | collective-permute-start | bytes 73736 | tf_op jit(solution)/shard_map/ppermute | solution.py:667
  8.8 3.3 %collective-permute-done.4.refs_4_.refs_7_ = f32[44,128]{1,0:T(8,128)S(1)} collective-permute-done((f32[44,128]{1,0:T(8,128)S(1)}, f32[44,128]{1,0:T(8,128)S(1)}, u32[]{:S(2)}, u32[]{:S(2)}) %collective-permute-start.4) | collective-permute-done | bytes 22560 | tf_op jit(solution)/shard_map/ppermute | solution.py:667
  12.1 0.7 %shard_map.56 = (f32[3,256,128]{2,1,0:T(8,128)S(1)}, f32[3,256,128]{2,1,0:T(8,128)S(1)}, f32[48,128]{1,0:T(8,128)S(1)}, f32[48,128]{1,0:T(8,128)S(1)}, f32[108,128]{1,0:T(8,128)S(1)}) custom-call(f32[9,256,128]{2,1,0:T(8,128)S(1)} %get-tuple-element.31.inverse, f32[6,256,128]{2,1,0:T(8,128)S(1)} %get-tuple-element.32.couplings, ...), custom_call_target="tpu_custom_call" | custom-call | tf_op jit(solution)/shard_map/pallas_call | solution.py:710
  12.9 0.6 %collective-permute-start.6 = (f32[48,128]{1,0:T(8,128)S(1)}, f32[48,128]{1,0:T(8,128)S(1)}, u32[]{:S(2)}, u32[]{:S(2)}) collective-permute-start(f32[48,128]{1,0:T(8,128)S(1)} %get-tuple-element.46), channel_id=1, source_target_pairs={{24,0},{16,8},{8,16},{0,24},{25,1},{17,9},{9,17},{1,25},{26,2},{18... | collective-permute-start | bytes 73736 | tf_op jit(solution)/shard_map/ppermute | solution.py:667
  14.1 2.1 %collective-permute-done.6.refs_1_ = f32[48,128]{1,0:T(8,128)S(1)} collective-permute-done((f32[48,128]{1,0:T(8,128)S(1)}, f32[48,128]{1,0:T(8,128)S(1)}, u32[]{:S(2)}, u32[]{:S(2)}) %collective-permute-start.6) | collective-permute-done | bytes 24608 | tf_op jit(solution)/shard_map/ppermute | solution.py:667
  16.2 0.7 %shard_map.57 = f32[32,128]{1,0:T(8,128)S(1)} custom-call(f32[3,256,128]{2,1,0:T(8,128)S(1)} %get-tuple-element.41.rhs, f32[3,256,128]{2,1,0:T(8,128)S(1)} %get-tuple-element.42.sums, f32[6,256,128]{2,1,0:T(8,128)S(1)} %get-tuple-element.32.couplings, f32[3,256,128]{2,1,0:T(8,128)S(1)} %get-tuple-element.40.second, f32[1,256]{1,0:T(1,128)S(1)} %get-tuple-element.43.ids, ...), custom_call_target="tpu_custom_call" | custom-call | tf_op jit(solution)/shard_map/pallas_call | solution.py:710
  16.9 0.6 %collective-permute-start.7 = (f32[32,128]{1,0:T(8,128)S(1)}, f32[32,128]{1,0:T(8,128)S(1)}, u32[]{:S(2)}, u32[]{:S(2)}) collective-permute-start(f32[32,128]{1,0:T(8,128)S(1)} %shard_map.57), channel_id=1, source_target_pairs={{1,0},{0,1},{3,2},{2,3},{5,4},{4,5},{7,6},{6,7},{9,8},{8,9},{11,10... | collective-permute-start | bytes 49160 | tf_op jit(solution)/shard_map/ppermute | solution.py:704
  17.6 2.1 %collective-permute-start.8 = (f32[108,128]{1,0:T(8,128)S(1)}, f32[108,128]{1,0:T(8,128)S(1)}, u32[]{:S(2)}, u32[]{:S(2)}) collective-permute-start(f32[108,128]{1,0:T(8,128)S(1)} %get-tuple-element.47), channel_id=1, source_target_pairs={{4,0},{5,1},{6,2},{7,3},{0,4},{1,5},{2,6},{3,7},{12,8},{13,9},{14,... | collective-permute-start | bytes 165896 | tf_op jit(solution)/shard_map/ppermute | solution.py:704
  19.6 1.1 %collective-permute-done.7 = f32[32,128]{1,0:T(8,128)S(1)} collective-permute-done((f32[32,128]{1,0:T(8,128)S(1)}, f32[32,128]{1,0:T(8,128)S(1)}, u32[]{:S(2)}, u32[]{:S(2)}) %collective-permute-start.7) | collective-permute-done | bytes 16416 | tf_op jit(solution)/shard_map/ppermute | solution.py:704
  20.8 1.9 %collective-permute-done.8.refs_8_ = f32[108,128]{1,0:T(8,128)S(1)} collective-permute-done((f32[108,128]{1,0:T(8,128)S(1)}, f32[108,128]{1,0:T(8,128)S(1)}, u32[]{:S(2)}, u32[]{:S(2)}) %collective-permute-start.8) | collective-permute-done | bytes 55328 | tf_op jit(solution)/shard_map/ppermute | solution.py:704
  22.6 2.7 %collective-permute-start.9 = (f32[104,128]{1,0:T(8,128)S(1)}, f32[104,128]{1,0:T(8,128)S(1)}, u32[]{:S(2)}, u32[]{:S(2)}) collective-permute-start(f32[104,128]{1,0:T(8,128)S(1)} %pad_maximum_fusion), channel_id=1, source_target_pairs={{2,0},{3,1},{0,2},{1,3},{6,4},{7,5},{4,6},{5,7},{10,8},{11,9},{8,1... | collective-permute-start | bytes 159752 | tf_op jit(solution)/shard_map/ppermute | solution.py:704
  25.3 1.0 %collective-permute-start.10 = (f32[32,128]{1,0:T(8,128)S(1)}, f32[32,128]{1,0:T(8,128)S(1)}, u32[]{:S(2)}, u32[]{:S(2)}) collective-permute-start(f32[32,128]{1,0:T(8,128)S(1)} %pad_maximum_fusion.1.refs_0_), channel_id=1, source_target_pairs={{6,0},{7,1},{4,2},{5,3},{2,4},{3,5},{0,6},{1,7},{14,8},{15,9},{12,... | collective-permute-start | bytes 49160 | tf_op jit(solution)/shard_map/ppermute | solution.py:704
  26.9 4.0 %collective-permute-done.10.refs_2_ = f32[32,128]{1,0:T(8,128)S(1)} collective-permute-done((f32[32,128]{1,0:T(8,128)S(1)}, f32[32,128]{1,0:T(8,128)S(1)}, u32[]{:S(2)}, u32[]{:S(2)}) %collective-permute-start.10) | collective-permute-done | bytes 16416 | tf_op jit(solution)/shard_map/ppermute | solution.py:704
  31.0 2.3 %shard_map.58 = (f32[8,256]{1,0:T(8,128)S(1)}, f32[24,256]{1,0:T(8,128)S(1)}) custom-call(f32[32,128]{1,0:T(8,128)S(1)} %pad_maximum_fusion.1.refs_0_, f32[104,128]{1,0:T(8,128)S(1)} %collective-permute-done.9.refs_1_.refs_9_, f32[32,128]{1,0:T(8,128)S(1)} %collective-permute-done.10.refs_2_, f32[32,128]{1,0:T(8,128)S(1)} %collective-permute-done.11.refs_3_, ...), custom_call_target="tpu_custom_call" | custom-call | tf_op jit(solution)/shard_map/pallas_call | solution.py:710
  34.6 2.0 %collective-permute-done.13.refs_1_ = f32[8,256]{1,0:T(8,128)S(1)} collective-permute-done((f32[8,256]{1,0:T(8,128)S(1)}, f32[8,256]{1,0:T(8,128)S(1)}, u32[]{:S(2)}, u32[]{:S(2)}) %collective-permute-start.13) | collective-permute-done | bytes 8224 | tf_op jit(solution)/shard_map/ppermute | solution.py:667
  36.6 1.0 %shard_map.59 = (f32[3,256,128]{2,1,0:T(8,128)S(1)}, f32[48,128]{1,0:T(8,128)S(1)}, f32[48,128]{1,0:T(8,128)S(1)}, f32[48,128]{1,0:T(8,128)S(1)}, f32[48,128]{1,0:T(8,128)S(1)}, /*index=5*/f32[8,128]{1,0:T(8,128)S(1)}) custom-call(f32[9,256,128]{2,1,0:T(8,128)S(1)} %get-tuple-element.31.inverse, f32[6,256,128]{2,1,0:T(8,128)S(1)} %get-tuple-element.32.couplings, ...), custom_call_target="tpu_custom_call" | custom-call | tf_op jit(solution)/shard_map/pallas_call | solution.py:710
  38.2 0.9 %collective-permute-start.16 = (f32[48,128]{1,0:T(8,128)S(1)}, f32[48,128]{1,0:T(8,128)S(1)}, u32[]{:S(2)}, u32[]{:S(2)}) collective-permute-start(f32[48,128]{1,0:T(8,128)S(1)} %get-tuple-element.54), channel_id=1, source_target_pairs={{2,0},{0,2},{6,4},{4,6},{3,1},{1,3},{7,5},{5,7},{10,8},{8,10},{14,... | collective-permute-start | bytes 73736 | tf_op jit(solution)/shard_map/ppermute | solution.py:667
  39.1 1.0 %collective-permute-start.17 = (f32[48,128]{1,0:T(8,128)S(1)}, f32[48,128]{1,0:T(8,128)S(1)}, u32[]{:S(2)}, u32[]{:S(2)}) collective-permute-start(f32[48,128]{1,0:T(8,128)S(1)} %get-tuple-element.55), channel_id=1, source_target_pairs={{1,0},{0,1},{4,2},{5,3},{2,4},{3,5},{7,6},{6,7},{9,8},{8,9},{12,10... | collective-permute-start | bytes 73736 | tf_op jit(solution)/shard_map/ppermute | solution.py:678
  40.1 1.0 %collective-permute-start.18 = (f32[8,128]{1,0:T(8,128)S(1)}, f32[8,128]{1,0:T(8,128)S(1)}, u32[]{:S(2)}, u32[]{:S(2)}) collective-permute-start(f32[8,128]{1,0:T(8,128)S(1)} %get-tuple-element.56), channel_id=1, source_target_pairs={{1,0},{0,1},{3,2},{2,3},{5,4},{4,5},{7,6},{6,7},{9,8},{8,9},{11,10... | collective-permute-start | bytes 12296 | tf_op jit(solution)/shard_map/ppermute | solution.py:667
  41.1 2.6 %collective-permute-done.18.refs_4_ = f32[8,128]{1,0:T(8,128)S(1)} collective-permute-done((f32[8,128]{1,0:T(8,128)S(1)}, f32[8,128]{1,0:T(8,128)S(1)}, u32[]{:S(2)}, u32[]{:S(2)}) %collective-permute-start.18) | collective-permute-done | bytes 4128 | tf_op jit(solution)/shard_map/ppermute | solution.py:667
  43.7 1.3 %shard_map.60 = f32[3,256,128]{2,1,0:T(8,128)} custom-call(f32[9,256,128]{2,1,0:T(8,128)S(1)} %get-tuple-element.31.inverse, f32[6,256,128]{2,1,0:T(8,128)S(1)} %get-tuple-element.32.couplings, f32[3,256,128]{2,1,0:T(8,128)S(1)} %get-tuple-element.33.first, f32[3,256,128]{2,1,0:T(8,128)S(1)} %get-tuple-element.51.third, ...), custom_call_target="tpu_custom_call" | custom-call | tf_op jit(solution)/shard_map/pallas_call | solution.py:710
  (25 shorter events, 3.8 us)
Async XLA Ops:
  2.0 10.1 %collective-permute-start.2 = (f32[100,128]{1,0:T(8,128)S(1)}, f32[100,128]{1,0:T(8,128)S(1)}, u32[]{:S(2)}, u32[]{:S(2)}) collective-permute-start(f32[100,128]{1,0:T(8,128)S(1)} %get-tuple-element.37), channel_id=1, source_target_pairs={{2,0},{0,2},{6,4},{4,6},{3,1},{1,3},{7,5},{5,7},{10,8},{8,10},{14,... | collective-permute-start | bytes 153608 | tf_op jit(solution)/shard_map/ppermute | solution.py:667
  5.2 7.0 %collective-permute-start.3 = (f32[64,128]{1,0:T(8,128)S(1)}, f32[64,128]{1,0:T(8,128)S(1)}, u32[]{:S(2)}, u32[]{:S(2)}) collective-permute-start(f32[64,128]{1,0:T(8,128)S(1)} %get-tuple-element.38), channel_id=1, source_target_pairs={{1,0},{0,1},{4,2},{5,3},{2,4},{3,5},{7,6},{6,7},{9,8},{8,9},{12,10... | collective-permute-start | bytes 98312 | tf_op jit(solution)/shard_map/ppermute | solution.py:678
  6.7 5.5 %collective-permute-start = (f32[48,128]{1,0:T(8,128)S(1)}, f32[48,128]{1,0:T(8,128)S(1)}, u32[]{:S(2)}, u32[]{:S(2)}) collective-permute-start(f32[48,128]{1,0:T(8,128)S(1)} %get-tuple-element.35), channel_id=1, source_target_pairs={{8,0},{0,8},{24,16},{16,24},{9,1},{1,9},{25,17},{17,25},{10,2},{2,... | collective-permute-start | bytes 73736 | tf_op jit(solution)/shard_map/ppermute | solution.py:667
  6.7 5.5 %collective-permute-start.1 = (f32[48,128]{1,0:T(8,128)S(1)}, f32[48,128]{1,0:T(8,128)S(1)}, u32[]{:S(2)}, u32[]{:S(2)}) collective-permute-start(f32[48,128]{1,0:T(8,128)S(1)} %get-tuple-element.36), channel_id=1, source_target_pairs={{24,0},{16,8},{8,16},{0,24},{25,1},{17,9},{9,17},{1,25},{26,2},{18... | collective-permute-start | bytes 73736 | tf_op jit(solution)/shard_map/ppermute | solution.py:667
  8.3 3.8 %collective-permute-start.4 = (f32[44,128]{1,0:T(8,128)S(1)}, f32[44,128]{1,0:T(8,128)S(1)}, u32[]{:S(2)}, u32[]{:S(2)}) collective-permute-start(f32[44,128]{1,0:T(8,128)S(1)} %get-tuple-element.39), channel_id=1, source_target_pairs={{1,0},{0,1},{3,2},{2,3},{5,4},{4,5},{7,6},{6,7},{9,8},{8,9},{11,10... | collective-permute-start | bytes 67592 | tf_op jit(solution)/shard_map/ppermute | solution.py:667
  12.8 1.3 %collective-permute-start.5 = (f32[48,128]{1,0:T(8,128)S(1)}, f32[48,128]{1,0:T(8,128)S(1)}, u32[]{:S(2)}, u32[]{:S(2)}) collective-permute-start(f32[48,128]{1,0:T(8,128)S(1)} %get-tuple-element.45), channel_id=1, source_target_pairs={{8,0},{0,8},{24,16},{16,24},{9,1},{1,9},{25,17},{17,25},{10,2},{2,... | collective-permute-start | bytes 73736 | tf_op jit(solution)/shard_map/ppermute | solution.py:667
  12.9 3.3 %collective-permute-start.6 = (f32[48,128]{1,0:T(8,128)S(1)}, f32[48,128]{1,0:T(8,128)S(1)}, u32[]{:S(2)}, u32[]{:S(2)}) collective-permute-start(f32[48,128]{1,0:T(8,128)S(1)} %get-tuple-element.46), channel_id=1, source_target_pairs={{24,0},{16,8},{8,16},{0,24},{25,1},{17,9},{9,17},{1,25},{26,2},{18... | collective-permute-start | bytes 73736 | tf_op jit(solution)/shard_map/ppermute | solution.py:667
  16.9 3.8 %collective-permute-start.7 = (f32[32,128]{1,0:T(8,128)S(1)}, f32[32,128]{1,0:T(8,128)S(1)}, u32[]{:S(2)}, u32[]{:S(2)}) collective-permute-start(f32[32,128]{1,0:T(8,128)S(1)} %shard_map.57), channel_id=1, source_target_pairs={{1,0},{0,1},{3,2},{2,3},{5,4},{4,5},{7,6},{6,7},{9,8},{8,9},{11,10... | collective-permute-start | bytes 49160 | tf_op jit(solution)/shard_map/ppermute | solution.py:704
  17.6 5.1 %collective-permute-start.8 = (f32[108,128]{1,0:T(8,128)S(1)}, f32[108,128]{1,0:T(8,128)S(1)}, u32[]{:S(2)}, u32[]{:S(2)}) collective-permute-start(f32[108,128]{1,0:T(8,128)S(1)} %get-tuple-element.47), channel_id=1, source_target_pairs={{4,0},{5,1},{6,2},{7,3},{0,4},{1,5},{2,6},{3,7},{12,8},{13,9},{14,... | collective-permute-start | bytes 165896 | tf_op jit(solution)/shard_map/ppermute | solution.py:704
  22.6 8.4 %collective-permute-start.9 = (f32[104,128]{1,0:T(8,128)S(1)}, f32[104,128]{1,0:T(8,128)S(1)}, u32[]{:S(2)}, u32[]{:S(2)}) collective-permute-start(f32[104,128]{1,0:T(8,128)S(1)} %pad_maximum_fusion), channel_id=1, source_target_pairs={{2,0},{3,1},{0,2},{1,3},{6,4},{7,5},{4,6},{5,7},{10,8},{11,9},{8,1... | collective-permute-start | bytes 159752 | tf_op jit(solution)/shard_map/ppermute | solution.py:704
  25.3 5.5 %collective-permute-start.10 = (f32[32,128]{1,0:T(8,128)S(1)}, f32[32,128]{1,0:T(8,128)S(1)}, u32[]{:S(2)}, u32[]{:S(2)}) collective-permute-start(f32[32,128]{1,0:T(8,128)S(1)} %pad_maximum_fusion.1.refs_0_), channel_id=1, source_target_pairs={{6,0},{7,1},{4,2},{5,3},{2,4},{3,5},{0,6},{1,7},{14,8},{15,9},{12,... | collective-permute-start | bytes 49160 | tf_op jit(solution)/shard_map/ppermute | solution.py:704
  26.3 4.7 %collective-permute-start.11 = (f32[32,128]{1,0:T(8,128)S(1)}, f32[32,128]{1,0:T(8,128)S(1)}, u32[]{:S(2)}, u32[]{:S(2)}) collective-permute-start(f32[32,128]{1,0:T(8,128)S(1)} %pad_maximum_fusion.1.refs_0_), channel_id=1, source_target_pairs={{4,0},{5,1},{6,2},{7,3},{0,4},{1,5},{2,6},{3,7},{12,8},{13,9},{14,... | collective-permute-start | bytes 49160 | tf_op jit(solution)/shard_map/ppermute | solution.py:704
  33.3 1.2 %collective-permute-start.12 = (f32[8,256]{1,0:T(8,128)S(1)}, f32[8,256]{1,0:T(8,128)S(1)}, u32[]{:S(2)}, u32[]{:S(2)}) collective-permute-start(f32[8,256]{1,0:T(8,128)S(1)} %get-tuple-element.49.stack), channel_id=1, source_target_pairs={{8,0},{0,8},{24,16},{16,24},{9,1},{1,9},{25,17},{17,25},{10,2},{2,... | collective-permute-start | bytes 24584 | tf_op jit(solution)/shard_map/ppermute | solution.py:667
  33.4 3.1 %collective-permute-start.13 = (f32[8,256]{1,0:T(8,128)S(1)}, f32[8,256]{1,0:T(8,128)S(1)}, u32[]{:S(2)}, u32[]{:S(2)}) collective-permute-start(f32[8,256]{1,0:T(8,128)S(1)} %get-tuple-element.49.stack), channel_id=1, source_target_pairs={{24,0},{16,8},{8,16},{0,24},{25,1},{17,9},{9,17},{1,25},{26,2},{18... | collective-permute-start | bytes 24584 | tf_op jit(solution)/shard_map/ppermute | solution.py:667
  37.5 6.2 %collective-permute-start.14 = (f32[48,128]{1,0:T(8,128)S(1)}, f32[48,128]{1,0:T(8,128)S(1)}, u32[]{:S(2)}, u32[]{:S(2)}) collective-permute-start(f32[48,128]{1,0:T(8,128)S(1)} %get-tuple-element.52), channel_id=1, source_target_pairs={{8,0},{0,8},{24,16},{16,24},{9,1},{1,9},{25,17},{17,25},{10,2},{2,... | collective-permute-start | bytes 73736 | tf_op jit(solution)/shard_map/ppermute | solution.py:667
  38.0 5.8 %collective-permute-start.15 = (f32[48,128]{1,0:T(8,128)S(1)}, f32[48,128]{1,0:T(8,128)S(1)}, u32[]{:S(2)}, u32[]{:S(2)}) collective-permute-start(f32[48,128]{1,0:T(8,128)S(1)} %get-tuple-element.53), channel_id=1, source_target_pairs={{24,0},{16,8},{8,16},{0,24},{25,1},{17,9},{9,17},{1,25},{26,2},{18... | collective-permute-start | bytes 73736 | tf_op jit(solution)/shard_map/ppermute | solution.py:667
  38.2 5.6 %collective-permute-start.16 = (f32[48,128]{1,0:T(8,128)S(1)}, f32[48,128]{1,0:T(8,128)S(1)}, u32[]{:S(2)}, u32[]{:S(2)}) collective-permute-start(f32[48,128]{1,0:T(8,128)S(1)} %get-tuple-element.54), channel_id=1, source_target_pairs={{2,0},{0,2},{6,4},{4,6},{3,1},{1,3},{7,5},{5,7},{10,8},{8,10},{14,... | collective-permute-start | bytes 73736 | tf_op jit(solution)/shard_map/ppermute | solution.py:667
  39.1 4.6 %collective-permute-start.17 = (f32[48,128]{1,0:T(8,128)S(1)}, f32[48,128]{1,0:T(8,128)S(1)}, u32[]{:S(2)}, u32[]{:S(2)}) collective-permute-start(f32[48,128]{1,0:T(8,128)S(1)} %get-tuple-element.55), channel_id=1, source_target_pairs={{1,0},{0,1},{4,2},{5,3},{2,4},{3,5},{7,6},{6,7},{9,8},{8,9},{12,10... | collective-permute-start | bytes 73736 | tf_op jit(solution)/shard_map/ppermute | solution.py:678
  40.1 3.6 %collective-permute-start.18 = (f32[8,128]{1,0:T(8,128)S(1)}, f32[8,128]{1,0:T(8,128)S(1)}, u32[]{:S(2)}, u32[]{:S(2)}) collective-permute-start(f32[8,128]{1,0:T(8,128)S(1)} %get-tuple-element.56), channel_id=1, source_target_pairs={{1,0},{0,1},{3,2},{2,3},{5,4},{4,5},{7,6},{6,7},{9,8},{8,9},{11,10... | collective-permute-start | bytes 12296 | tf_op jit(solution)/shard_map/ppermute | solution.py:667

commit v10 on v9

--- a/solution.py
+++ b/solution.py
@@ -322,15 +322,21 @@
     put_x(dims, second, sends)
 
 
+def mode_sums(nz, v):
+    m0, m1 = mode_rows(8, nz)
+    row = row_iota(8, nz)
+    modes = split3(jnp.where(row == 0, m0, jnp.where(row == 1, m1, 0.0)))
+    s = sum(dot_tt(modes, part) for part in parts3(v))
+    return s[0:8] + (s[8:16] + s[16:24])
+
+
 def coarse_kernel(dims, n_z, rhs, sums, couplings, second, ids, spread, *refs):
     nx, ny, nz, rows = dims.nx, dims.ny, dims.nz, dims.rows
     half = rows // 2
-    (xe, xo, ye, yo), z_recv, refs = refs[:4], refs[4 : 4 + n_z], refs[4 + n_z :]
+    (ye, yo), z_recv, refs = refs[:2], refs[2 : 2 + n_z], refs[2 + n_z :]
     packet, z_more, (resid, wide) = refs[0], refs[1:n_z], refs[n_z:]
 
-    def x_halo(c, high):
-        return neighbour("gx", [r[c * ny : (c + 1) * ny, :] for r in (xe, xo)], high)
-
+    zero = jnp.zeros((ny, nz), jnp.float32)
     rest = 1.0 - DAMPING * (2.0 - DAMPING)
     row = row_iota(ny, nz)
     lane = lane_iota(ny, nz)
@@ -343,22 +349,14 @@
         at = rows_at(dims, x)
         for c in range(3):
             v = tile(second, c, x, ny)
-            low = tile(second, c, x - 1, ny) if x > 0 else x_halo(c, False)
-            high = tile(second, c, x + 1, ny) if x < nx - 1 else x_halo(c, True)
+            low = tile(second, c, x - 1, ny) if x > 0 else zero
+            high = tile(second, c, x + 1, ny) if x < nx - 1 else zero
             y_pair = (pltpu.roll(v, 1, 0), pltpu.roll(v, ny - 1, 0))
             z_pair = (pltpu.roll(v, 1, 1), pltpu.roll(v, nz - 1, 1))
             total = beside(coup, (low, high), y_pair, z_pair)
             resid[c, at, :] = rest * rhs[c, at, :] + (total - DAMPING * sums[c, at, :])
-    m0, m1 = mode_rows(8, nz)
-    row = row_iota(8, nz)
-    modes = split3(jnp.where(row == 0, m0, jnp.where(row == 1, m1, 0.0)))
-
-    def mode_sums(v):
-        s = sum(dot_tt(modes, part) for part in parts3(v))
-        return s[0:8] + (s[8:16] + s[16:24])
-
     for c in range(3):
-        s = mode_sums(resid[c])
+        s = mode_sums(nz, resid[c])
         packet[2 * c : 2 * c + 2, :] = s[0:2, :half]
         packet[8 + 2 * c : 10 + 2 * c, :] = s[0:2, half:]
     toward = [
@@ -369,7 +367,7 @@
         for side, y in enumerate((0, ny - 1)):
             at = (2 * c + side) * nx
             wide[at : at + nx, :] = toward[side] * second[c, pl.ds(y, nx, stride=ny), :]
-    s = mode_sums(wide[...])
+    s = mode_sums(nz, wide[...])
     for k in range(2):
         packet[8 * k + 6 : 8 * k + 7, :] = ids[:, k * half : (k + 1) * half]
         packet[8 * k + 7 : 8 * k + 8, :] = s[k : k + 1, :]
@@ -400,6 +398,29 @@
                 to = at + 8 * side + 2 * c
                 ref[to : to + 1, :] = v * nz ** (-0.5)
                 ref[to + 1 : to + 2, :] = v * mode
+
+
+def edges_kernel(dims, inside, couplings, xe, xo, packet, wide):
+    nx, ny, nz = dims.nx, dims.ny, dims.nz
+    half = dims.rows // 2
+    wide[...] = jnp.zeros_like(wide)
+    for c in range(3):
+        for side, x in enumerate((0, nx - 1)):
+            pair = [r[c * ny : (c + 1) * ny, :] for r in (xe, xo)]
+            v = tile(couplings, side, x, ny) * neighbour("gx", pair, side == 1)
+            at = (2 * c + side) * ny
+            wide[at : at + ny, :] = v
+    s = mode_sums(nz, wide[...])
+    row, lane = row_iota(8, half), lane_iota(8, half)
+    packet[16:, :] = inside[16:, :]
+    for side, (start, keep) in enumerate(((0, lane < ny), (half - ny, lane >= half - ny))):
+        total = inside[8 * side : 8 * side + 8, :]
+        for c in range(3):
+            moved = pltpu.roll(s, (start - (2 * c + side) * ny) % half, 1)
+            for m in range(2):
+                hit = keep & (row == 2 * c + m)
+                total = total + jnp.where(hit, moved[m : m + 1], 0.0)
+        packet[8 * side : 8 * side + 8, :] = total
 
 
 def pencil_row(dims, square):
@@ -588,31 +609,23 @@
         beyond_out[8:16], beyond_out[16:24] = totals[2], totals[3]
 
 
-def third_kernel(dims, n_z, inverse, couplings, second, stack, beyond, *refs):
-    stacks, third, sends = refs[:2], refs[2], refs[3:7]
-    z_sends, (field, y_field, z_field) = refs[7 : 7 + n_z], refs[7 + n_z :]
+def mode_columns(dims):
+    m0, m1 = mode_rows(8, dims.nz)
+    row = row_iota(8, dims.nz)
+    parts = [
+        jnp.where(row == 2 * c, m0, jnp.where(row == 2 * c + 1, m1, 0.0)) for c in range(3)
+    ]
+    return jnp.concatenate(parts, axis=1)
+
+
+def third_kernel(dims, inverse, couplings, second, stack, beyond, third, *fields):
+    field, y_field, z_field = fields
     nx, ny, nz = dims.nx, dims.ny, dims.nz
-    side = nx * ny // 2
-    m0, m1 = mode_rows(8, nz)
-    row = row_iota(8, nz)
-    modes = jnp.concatenate(
-        [
-            jnp.where(row == 2 * c, m0, jnp.where(row == 2 * c + 1, m1, 0.0))
-            for c in range(3)
-        ],
-        axis=1,
-    )
+    modes = mode_columns(dims)
     at = lax.rem(lane_iota(8, 3 * nz), nz)
     wide = pairs6_right(modes)
     last = pairs6_right(jnp.where(at == nz - 1, modes, 0.0))
     start = pairs6_right(jnp.where(at == 0, modes, 0.0))
-    my_x, n_x = lax.axis_index("gx"), lax.axis_size("gx")
-    x_low = neighbour("gx", [s[:, side:] for s in stacks], False)
-    x_high = neighbour("gx", [s[:, :side] for s in stacks], True)
-    x_low = jnp.where(my_x > 0, x_low, 0.0)
-    x_high = jnp.where(my_x < n_x - 1, x_high, 0.0)
-    x_mix = jnp.where(lane_iota(8, side) < side // 2, x_high, x_low)
-    x_field = dot_00(pairs6(x_mix), wide)
     for ref, value in (
         (field, dot_00(pairs6(stack[...]), wide)),
         (y_field, dot_00(pairs6(beyond[0:8]), wide)),
@@ -622,8 +635,7 @@
             ref[c] = value[:, c * nz : (c + 1) * nz]
 
     def x_halo(c, high):
-        v = x_field[:, c * nz : (c + 1) * nz]
-        return v[0:ny] if high else v[side - ny : side]
+        return jnp.zeros((ny, nz), jnp.float32)
 
     def y_halo(c, x, high):
         return tile(y_field, c, x, ny)
@@ -635,8 +647,27 @@
         at = rows_at(dims, x)
         for c in range(3):
             third[c, at, :] = second[c, at, :] + ((1.0 - DAMPING) * center[c] + change[c])
-    put_faces(dims, third, sends)
-    put_z(dims, third, z_sends)
+
+
+def faces_kernel(dims, inside, inverse, couplings, xe, xo, third, *sends):
+    nx, ny, nz = dims.nx, dims.ny, dims.nz
+    side = nx * ny // 2
+    my_x, n_x = lax.axis_index("gx"), lax.axis_size("gx")
+    x_low = neighbour("gx", [s[:, side:] for s in (xe, xo)], False)
+    x_high = neighbour("gx", [s[:, :side] for s in (xe, xo)], True)
+    x_low = jnp.where(my_x > 0, x_low, 0.0)
+    x_high = jnp.where(my_x < n_x - 1, x_high, 0.0)
+    x_mix = jnp.where(lane_iota(8, side) < side // 2, x_high, x_low)
+    x_field = dot_00(pairs6(x_mix), pairs6_right(mode_columns(dims)))
+    for x, toward, rows in ((0, 0, slice(side - ny, side)), (nx - 1, 1, slice(0, ny))):
+        coup = tile(couplings, toward, x, ny)
+        v = [coup * x_field[rows, c * nz : (c + 1) * nz] for c in range(3)]
+        change = times(tiles(inverse, 9, x, ny), v)
+        at = rows_at(dims, x)
+        for c in range(3):
+            third[c, at, :] = inside[c, at, :] + change[c]
+    put_faces(dims, third, sends[:4])
+    put_z(dims, third, sends[4:])
 
 
 def last_kernel(dims, n_z, inverse, couplings, first, third, *refs):
@@ -704,7 +735,7 @@
     return lax.ppermute(value, ("gy", "gz"), which)
 
 
-def call(body, out_shapes, scratch, *args, in_hbm=0, out_hbm=False):
+def call(body, out_shapes, scratch, *args, in_hbm=0, out_hbm=False, alias=None):
     near = pl.BlockSpec(memory_space=pltpu.VMEM)
     far = pl.BlockSpec(memory_space=pltpu.HBM)
     return pl.pallas_call(
@@ -715,6 +746,7 @@
         in_specs=[far] * in_hbm + [near] * (len(args) - in_hbm),
         out_specs=[far if out_hbm else near] * len(out_shapes),
         scratch_shapes=scratch,
+        input_output_aliases=alias or {},
         compiler_params=pltpu.CompilerParams(vmem_limit_bytes=VMEM_LIMIT),
     )(*args)
 
@@ -775,7 +807,7 @@
     second_x = exchange_x(sends)
     far_inv = fetch(inv_out, EO, ())
     half = rows // 2
-    packet, *z_more = call(
+    inside, *z_more = call(
         part(coarse_kernel, dims, z_count),
         [(32, half)] + [(16, half)] * (z_count - 1),
         [pltpu.VMEM(vector, f32), pltpu.VMEM((half, nz), f32)],
@@ -785,9 +817,16 @@
         second,
         ids,
         spread_z,
-        *second_x,
         *fat[2:],
         *fat_z,
+    )
+    (packet,) = call(
+        part(edges_kernel, dims),
+        [(32, half)],
+        [pltpu.VMEM((half, nz), f32)],
+        inside,
+        couplings,
+        *second_x,
     )
     z_words, y_words = words_of(n_z), words_of(n_y)
     if n_z == 2:
@@ -818,17 +857,26 @@
         *pieces,
     )
     xe, xo = exchange_x([stack, stack])
-    third, *sends = call(
-        part(third_kernel, dims, z_count),
-        [vector] + faces(3, 0, 0) + z_faces(0),
+    (inside,) = call(
+        part(third_kernel, dims),
+        [vector],
         [pltpu.VMEM(vector, f32)] * 3,
         inverse,
         couplings,
         second,
         stack,
         beyond,
+    )
+    third, *sends = call(
+        part(faces_kernel, dims),
+        [vector] + faces(3, 0, 0) + z_faces(0),
+        [],
+        inside,
+        inverse,
+        couplings,
         xe,
         xo,
+        alias={0: 0},
     )
     recv, z_recv = exchange(sends[:4], sends[4:])
     (out,) = call(

time: 45.2 us -> 44.2 us (0.978)
  waiting for transfers between devices: 18.3 us -> 16.9 us
    ppermute x12, waiting for transfers between devices: 11.2 us -> 9.68 us  [swap(): lax.ppermute(value, axis, [(partner(i, count, odd), i) for i in range(cou...]
    pallas_call x6 -> x8, Pallas kernels: 8.02 us -> 8.37 us  [call(): pl.pallas_call(body, out_shape=[s if hasattr(s, 'dtype') else jax.ShapeDt...]
  transfers between devices with their start and end apart: 19 -> 19, of which waited for: 10 -> 8; matrix products, arithmetic and copies ran while one was open for 0% -> 0% of each run, Pallas kernels for 0% -> 3%
where the time goes in v10:
time: 44.2 us; the launch traced here: 44 us
  starting transfers between devices  18.6 us (42%)
  waiting for transfers between devices  16.9 us (38%)
  Pallas kernels  8.37 us (19%)
    ppermute x12, waiting for transfers between devices, swap(): lax.ppermute(value, axis, [(partner(i, count, odd), i) for i in range(cou...  9.68 us
    ppermute x12, starting transfers between devices, swap(): lax.ppermute(value, axis, [(partner(i, count, odd), i) for i in range(cou...  9.23 us
    pallas_call x8, Pallas kernels, call(): pl.pallas_call(body, out_shape=[s if hasattr(s, 'dtype') else jax.ShapeDt...  8.37 us
    ppermute x5, waiting for transfers between devices, fetch(): return lax.ppermute(value, ('gy', 'gz'), which)  7.18 us
    ppermute x5, starting transfers between devices, fetch(): return lax.ppermute(value, ('gy', 'gz'), which)  6.9 us
    ppermute x2, starting transfers between devices, swap_inner(): return lax.ppermute(value, (axis, spare), which)  2.51 us
  transfers between devices with their start and end apart: 19, of which 8 were waited for; matrix products, arithmetic and copies ran while one was open for 0% of the time, Pallas kernels for 3%

profile of v10, /device:TPU:0, one launch (start us, length us, event | category | flops | bytes accessed | tf_op | source)
XLA Modules:
  0.0 44.0 jit_solution(6288747076909792134)
XLA Ops:
  0.0 2.0 %shard_map.55 = (f32[3,256,128]{2,1,0:T(8,128)S(1)}, f32[9,256,128]{2,1,0:T(8,128)S(1)}, f32[3,256,128]{2,1,0:T(8,128)S(1)}, f32[6,256,128]{2,1,0:T(8,128)S(1)},...) custom-call(f32[3,256,128]{2,1,0:T(8,128)} %bitcast.6, ...), custom_call_target="tpu_custom_call" | custom-call | tf_op jit(solution)/shard_map/pallas_call | solution.py:741
  2.0 3.1 %collective-permute-start.2 = (f32[100,128]{1,0:T(8,128)S(1)}, f32[100,128]{1,0:T(8,128)S(1)}, u32[]{:S(2)}, u32[]{:S(2)}) collective-permute-start(f32[100,128]{1,0:T(8,128)S(1)} %get-tuple-element.37), channel_id=1, source_target_pairs={{2,0},{0,2},{6,4},{4,6},{3,1},{1,3},{7,5},{5,7},{10,8},{8,10},{14,... | collective-permute-start | bytes 153608 | tf_op jit(solution)/shard_map/ppermute | solution.py:698
  5.2 1.5 %collective-permute-start.3 = (f32[64,128]{1,0:T(8,128)S(1)}, f32[64,128]{1,0:T(8,128)S(1)}, u32[]{:S(2)}, u32[]{:S(2)}) collective-permute-start(f32[64,128]{1,0:T(8,128)S(1)} %get-tuple-element.38), channel_id=1, source_target_pairs={{1,0},{0,1},{4,2},{5,3},{2,4},{3,5},{7,6},{6,7},{9,8},{8,9},{12,10... | collective-permute-start | bytes 98312 | tf_op jit(solution)/shard_map/ppermute | solution.py:709
  6.7 1.6 %collective-permute-start.1 = (f32[48,128]{1,0:T(8,128)S(1)}, f32[48,128]{1,0:T(8,128)S(1)}, u32[]{:S(2)}, u32[]{:S(2)}) collective-permute-start(f32[48,128]{1,0:T(8,128)S(1)} %get-tuple-element.36), channel_id=1, source_target_pairs={{24,0},{16,8},{8,16},{0,24},{25,1},{17,9},{9,17},{1,25},{26,2},{18... | collective-permute-start | bytes 73736 | tf_op jit(solution)/shard_map/ppermute | solution.py:698
  8.8 3.3 %collective-permute-done.4.refs_4_.refs_2_.refs_7_ = f32[44,128]{1,0:T(8,128)S(1)} collective-permute-done((f32[44,128]{1,0:T(8,128)S(1)}, f32[44,128]{1,0:T(8,128)S(1)}, u32[]{:S(2)}, u32[]{:S(2)}) %collective-permute-start.4) | collective-permute-done | bytes 22560 | tf_op jit(solution)/shard_map/ppermute | solution.py:698
  12.1 0.6 %shard_map.56 = (f32[3,256,128]{2,1,0:T(8,128)S(1)}, f32[3,256,128]{2,1,0:T(8,128)S(1)}, f32[48,128]{1,0:T(8,128)S(1)}, f32[48,128]{1,0:T(8,128)S(1)}, f32[108,128]{1,0:T(8,128)S(1)}) custom-call(f32[9,256,128]{2,1,0:T(8,128)S(1)} %get-tuple-element.31.inverse, f32[6,256,128]{2,1,0:T(8,128)S(1)} %get-tuple-element.32.couplings, ...), custom_call_target="tpu_custom_call" | custom-call | tf_op jit(solution)/shard_map/pallas_call | solution.py:741
  13.5 0.7 %shard_map.57.inside = f32[32,128]{1,0:T(8,128)S(1)} custom-call(f32[3,256,128]{2,1,0:T(8,128)S(1)} %get-tuple-element.41.rhs, f32[3,256,128]{2,1,0:T(8,128)S(1)} %get-tuple-element.42.sums, f32[6,256,128]{2,1,0:T(8,128)S(1)} %get-tuple-element.32.couplings, f32[3,256,128]{2,1,0:T(8,128)S(1)} %get-tuple-element.40.second, ...), custom_call_target="tpu_custom_call" | custom-call | tf_op jit(solution)/shard_map/pallas_call | solution.py:741
  14.2 2.0 %collective-permute-done.6.xo = f32[48,128]{1,0:T(8,128)S(1)} collective-permute-done((f32[48,128]{1,0:T(8,128)S(1)}, f32[48,128]{1,0:T(8,128)S(1)}, u32[]{:S(2)}, u32[]{:S(2)}) %collective-permute-start.6) | collective-permute-done | bytes 24608 | tf_op jit(solution)/shard_map/ppermute | solution.py:698
  16.4 0.6 %collective-permute-start.7 = (f32[32,128]{1,0:T(8,128)S(1)}, f32[32,128]{1,0:T(8,128)S(1)}, u32[]{:S(2)}, u32[]{:S(2)}) collective-permute-start(f32[32,128]{1,0:T(8,128)S(1)} %shard_map.58), channel_id=1, source_target_pairs={{1,0},{0,1},{3,2},{2,3},{5,4},{4,5},{7,6},{6,7},{9,8},{8,9},{11,10... | collective-permute-start | bytes 49160 | tf_op jit(solution)/shard_map/ppermute | solution.py:735
  17.0 2.1 %collective-permute-start.8 = (f32[108,128]{1,0:T(8,128)S(1)}, f32[108,128]{1,0:T(8,128)S(1)}, u32[]{:S(2)}, u32[]{:S(2)}) collective-permute-start(f32[108,128]{1,0:T(8,128)S(1)} %get-tuple-element.47), channel_id=1, source_target_pairs={{4,0},{5,1},{6,2},{7,3},{0,4},{1,5},{2,6},{3,7},{12,8},{13,9},{14,... | collective-permute-start | bytes 165896 | tf_op jit(solution)/shard_map/ppermute | solution.py:735
  19.1 1.1 %collective-permute-done.7 = f32[32,128]{1,0:T(8,128)S(1)} collective-permute-done((f32[32,128]{1,0:T(8,128)S(1)}, f32[32,128]{1,0:T(8,128)S(1)}, u32[]{:S(2)}, u32[]{:S(2)}) %collective-permute-start.7) | collective-permute-done | bytes 16416 | tf_op jit(solution)/shard_map/ppermute | solution.py:735
  20.2 1.9 %collective-permute-done.8.refs_8_ = f32[108,128]{1,0:T(8,128)S(1)} collective-permute-done((f32[108,128]{1,0:T(8,128)S(1)}, f32[108,128]{1,0:T(8,128)S(1)}, u32[]{:S(2)}, u32[]{:S(2)}) %collective-permute-start.8) | collective-permute-done | bytes 55328 | tf_op jit(solution)/shard_map/ppermute | solution.py:735
  22.1 2.7 %collective-permute-start.9 = (f32[104,128]{1,0:T(8,128)S(1)}, f32[104,128]{1,0:T(8,128)S(1)}, u32[]{:S(2)}, u32[]{:S(2)}) collective-permute-start(f32[104,128]{1,0:T(8,128)S(1)} %pad_maximum_fusion), channel_id=1, source_target_pairs={{2,0},{3,1},{0,2},{1,3},{6,4},{7,5},{4,6},{5,7},{10,8},{11,9},{8,1... | collective-permute-start | bytes 159752 | tf_op jit(solution)/shard_map/ppermute | solution.py:735
  24.8 1.0 %collective-permute-start.10 = (f32[32,128]{1,0:T(8,128)S(1)}, f32[32,128]{1,0:T(8,128)S(1)}, u32[]{:S(2)}, u32[]{:S(2)}) collective-permute-start(f32[32,128]{1,0:T(8,128)S(1)} %pad_maximum_fusion.1.refs_0_), channel_id=1, source_target_pairs={{6,0},{7,1},{4,2},{5,3},{2,4},{3,5},{0,6},{1,7},{14,8},{15,9},{12,... | collective-permute-start | bytes 49160 | tf_op jit(solution)/shard_map/ppermute | solution.py:735
  26.4 4.0 %collective-permute-done.10.refs_2_ = f32[32,128]{1,0:T(8,128)S(1)} collective-permute-done((f32[32,128]{1,0:T(8,128)S(1)}, f32[32,128]{1,0:T(8,128)S(1)}, u32[]{:S(2)}, u32[]{:S(2)}) %collective-permute-start.10) | collective-permute-done | bytes 16416 | tf_op jit(solution)/shard_map/ppermute | solution.py:735
  30.5 2.3 %shard_map.59 = (f32[8,256]{1,0:T(8,128)S(1)}, f32[24,256]{1,0:T(8,128)S(1)}) custom-call(f32[32,128]{1,0:T(8,128)S(1)} %pad_maximum_fusion.1.refs_0_, f32[104,128]{1,0:T(8,128)S(1)} %collective-permute-done.9.refs_1_.refs_9_, f32[32,128]{1,0:T(8,128)S(1)} %collective-permute-done.10.refs_2_, f32[32,128]{1,0:T(8,128)S(1)} %collective-permute-done.11.refs_3_, ...), custom_call_target="tpu_custom_call" | custom-call | tf_op jit(solution)/shard_map/pallas_call | solution.py:741
  32.9 0.6 %collective-permute-start.13 = (f32[8,256]{1,0:T(8,128)S(1)}, f32[8,256]{1,0:T(8,128)S(1)}, u32[]{:S(2)}, u32[]{:S(2)}) collective-permute-start(f32[8,256]{1,0:T(8,128)S(1)} %get-tuple-element.49.stack), channel_id=1, source_target_pairs={{24,0},{16,8},{8,16},{0,24},{25,1},{17,9},{9,17},{1,25},{26,2},{18... | collective-permute-start | bytes 24584 | tf_op jit(solution)/shard_map/ppermute | solution.py:698
  33.5 0.7 %shard_map.60.inside = f32[3,256,128]{2,1,0:T(8,128)S(1)} custom-call(f32[9,256,128]{2,1,0:T(8,128)S(1)} %get-tuple-element.31.inverse, f32[6,256,128]{2,1,0:T(8,128)S(1)} %get-tuple-element.32.couplings, f32[3,256,128]{2,1,0:T(8,128)S(1)} %get-tuple-element.40.second, f32[8,256]{1,0:T(8,128)S(1)} %get-tuple-element.49.stack, ...), custom_call_target="tpu_custom_call" | custom-call | tf_op jit(solution)/shard_map/pallas_call | solution.py:741
  34.2 1.8 %collective-permute-done.13.xo = f32[8,256]{1,0:T(8,128)S(1)} collective-permute-done((f32[8,256]{1,0:T(8,128)S(1)}, f32[8,256]{1,0:T(8,128)S(1)}, u32[]{:S(2)}, u32[]{:S(2)}) %collective-permute-start.13) | collective-permute-done | bytes 8224 | tf_op jit(solution)/shard_map/ppermute | solution.py:698
  37.1 0.9 %collective-permute-start.16 = (f32[48,128]{1,0:T(8,128)S(1)}, f32[48,128]{1,0:T(8,128)S(1)}, u32[]{:S(2)}, u32[]{:S(2)}) collective-permute-start(f32[48,128]{1,0:T(8,128)S(1)} %get-tuple-element.54), channel_id=1, source_target_pairs={{2,0},{0,2},{6,4},{4,6},{3,1},{1,3},{7,5},{5,7},{10,8},{8,10},{14,... | collective-permute-start | bytes 73736 | tf_op jit(solution)/shard_map/ppermute | solution.py:698
  38.0 1.0 %collective-permute-start.17 = (f32[48,128]{1,0:T(8,128)S(1)}, f32[48,128]{1,0:T(8,128)S(1)}, u32[]{:S(2)}, u32[]{:S(2)}) collective-permute-start(f32[48,128]{1,0:T(8,128)S(1)} %get-tuple-element.55), channel_id=1, source_target_pairs={{1,0},{0,1},{4,2},{5,3},{2,4},{3,5},{7,6},{6,7},{9,8},{8,9},{12,10... | collective-permute-start | bytes 73736 | tf_op jit(solution)/shard_map/ppermute | solution.py:709
  39.0 1.0 %collective-permute-start.18 = (f32[8,128]{1,0:T(8,128)S(1)}, f32[8,128]{1,0:T(8,128)S(1)}, u32[]{:S(2)}, u32[]{:S(2)}) collective-permute-start(f32[8,128]{1,0:T(8,128)S(1)} %get-tuple-element.56), channel_id=1, source_target_pairs={{1,0},{0,1},{3,2},{2,3},{5,4},{4,5},{7,6},{6,7},{9,8},{8,9},{11,10... | collective-permute-start | bytes 12296 | tf_op jit(solution)/shard_map/ppermute | solution.py:698
  40.0 2.6 %collective-permute-done.18.refs_4_ = f32[8,128]{1,0:T(8,128)S(1)} collective-permute-done((f32[8,128]{1,0:T(8,128)S(1)}, f32[8,128]{1,0:T(8,128)S(1)}, u32[]{:S(2)}, u32[]{:S(2)}) %collective-permute-start.18) | collective-permute-done | bytes 4128 | tf_op jit(solution)/shard_map/ppermute | solution.py:698
  42.7 1.3 %shard_map.62 = f32[3,256,128]{2,1,0:T(8,128)} custom-call(f32[9,256,128]{2,1,0:T(8,128)S(1)} %get-tuple-element.31.inverse, f32[6,256,128]{2,1,0:T(8,128)S(1)} %get-tuple-element.32.couplings, f32[3,256,128]{2,1,0:T(8,128)S(1)} %get-tuple-element.33.first, f32[3,256,128]{2,1,0:T(8,128)S(1)} %get-tuple-element.51.third, ...), custom_call_target="tpu_custom_call" | custom-call | tf_op jit(solution)/shard_map/pallas_call | solution.py:741
  (27 shorter events, 3.4 us)
Async XLA Ops:
  2.0 10.1 %collective-permute-start.2 = (f32[100,128]{1,0:T(8,128)S(1)}, f32[100,128]{1,0:T(8,128)S(1)}, u32[]{:S(2)}, u32[]{:S(2)}) collective-permute-start(f32[100,128]{1,0:T(8,128)S(1)} %get-tuple-element.37), channel_id=1, source_target_pairs={{2,0},{0,2},{6,4},{4,6},{3,1},{1,3},{7,5},{5,7},{10,8},{8,10},{14,... | collective-permute-start | bytes 153608 | tf_op jit(solution)/shard_map/ppermute | solution.py:698
  5.2 7.0 %collective-permute-start.3 = (f32[64,128]{1,0:T(8,128)S(1)}, f32[64,128]{1,0:T(8,128)S(1)}, u32[]{:S(2)}, u32[]{:S(2)}) collective-permute-start(f32[64,128]{1,0:T(8,128)S(1)} %get-tuple-element.38), channel_id=1, source_target_pairs={{1,0},{0,1},{4,2},{5,3},{2,4},{3,5},{7,6},{6,7},{9,8},{8,9},{12,10... | collective-permute-start | bytes 98312 | tf_op jit(solution)/shard_map/ppermute | solution.py:709
  6.7 5.5 %collective-permute-start = (f32[48,128]{1,0:T(8,128)S(1)}, f32[48,128]{1,0:T(8,128)S(1)}, u32[]{:S(2)}, u32[]{:S(2)}) collective-permute-start(f32[48,128]{1,0:T(8,128)S(1)} %get-tuple-element.35), channel_id=1, source_target_pairs={{8,0},{0,8},{24,16},{16,24},{9,1},{1,9},{25,17},{17,25},{10,2},{2,... | collective-permute-start | bytes 73736 | tf_op jit(solution)/shard_map/ppermute | solution.py:698
  6.7 5.5 %collective-permute-start.1 = (f32[48,128]{1,0:T(8,128)S(1)}, f32[48,128]{1,0:T(8,128)S(1)}, u32[]{:S(2)}, u32[]{:S(2)}) collective-permute-start(f32[48,128]{1,0:T(8,128)S(1)} %get-tuple-element.36), channel_id=1, source_target_pairs={{24,0},{16,8},{8,16},{0,24},{25,1},{17,9},{9,17},{1,25},{26,2},{18... | collective-permute-start | bytes 73736 | tf_op jit(solution)/shard_map/ppermute | solution.py:698
  8.3 3.8 %collective-permute-start.4 = (f32[44,128]{1,0:T(8,128)S(1)}, f32[44,128]{1,0:T(8,128)S(1)}, u32[]{:S(2)}, u32[]{:S(2)}) collective-permute-start(f32[44,128]{1,0:T(8,128)S(1)} %get-tuple-element.39), channel_id=1, source_target_pairs={{1,0},{0,1},{3,2},{2,3},{5,4},{4,5},{7,6},{6,7},{9,8},{8,9},{11,10... | collective-permute-start | bytes 67592 | tf_op jit(solution)/shard_map/ppermute | solution.py:698
  12.8 1.4 %collective-permute-start.5 = (f32[48,128]{1,0:T(8,128)S(1)}, f32[48,128]{1,0:T(8,128)S(1)}, u32[]{:S(2)}, u32[]{:S(2)}) collective-permute-start(f32[48,128]{1,0:T(8,128)S(1)} %get-tuple-element.45), channel_id=1, source_target_pairs={{8,0},{0,8},{24,16},{16,24},{9,1},{1,9},{25,17},{17,25},{10,2},{2,... | collective-permute-start | bytes 73736 | tf_op jit(solution)/shard_map/ppermute | solution.py:698
  12.9 3.3 %collective-permute-start.6 = (f32[48,128]{1,0:T(8,128)S(1)}, f32[48,128]{1,0:T(8,128)S(1)}, u32[]{:S(2)}, u32[]{:S(2)}) collective-permute-start(f32[48,128]{1,0:T(8,128)S(1)} %get-tuple-element.46), channel_id=1, source_target_pairs={{24,0},{16,8},{8,16},{0,24},{25,1},{17,9},{9,17},{1,25},{26,2},{18... | collective-permute-start | bytes 73736 | tf_op jit(solution)/shard_map/ppermute | solution.py:698
  16.4 3.8 %collective-permute-start.7 = (f32[32,128]{1,0:T(8,128)S(1)}, f32[32,128]{1,0:T(8,128)S(1)}, u32[]{:S(2)}, u32[]{:S(2)}) collective-permute-start(f32[32,128]{1,0:T(8,128)S(1)} %shard_map.58), channel_id=1, source_target_pairs={{1,0},{0,1},{3,2},{2,3},{5,4},{4,5},{7,6},{6,7},{9,8},{8,9},{11,10... | collective-permute-start | bytes 49160 | tf_op jit(solution)/shard_map/ppermute | solution.py:735
  17.0 5.1 %collective-permute-start.8 = (f32[108,128]{1,0:T(8,128)S(1)}, f32[108,128]{1,0:T(8,128)S(1)}, u32[]{:S(2)}, u32[]{:S(2)}) collective-permute-start(f32[108,128]{1,0:T(8,128)S(1)} %get-tuple-element.47), channel_id=1, source_target_pairs={{4,0},{5,1},{6,2},{7,3},{0,4},{1,5},{2,6},{3,7},{12,8},{13,9},{14,... | collective-permute-start | bytes 165896 | tf_op jit(solution)/shard_map/ppermute | solution.py:735
  22.1 8.4 %collective-permute-start.9 = (f32[104,128]{1,0:T(8,128)S(1)}, f32[104,128]{1,0:T(8,128)S(1)}, u32[]{:S(2)}, u32[]{:S(2)}) collective-permute-start(f32[104,128]{1,0:T(8,128)S(1)} %pad_maximum_fusion), channel_id=1, source_target_pairs={{2,0},{3,1},{0,2},{1,3},{6,4},{7,5},{4,6},{5,7},{10,8},{11,9},{8,1... | collective-permute-start | bytes 159752 | tf_op jit(solution)/shard_map/ppermute | solution.py:735
  24.8 5.5 %collective-permute-start.10 = (f32[32,128]{1,0:T(8,128)S(1)}, f32[32,128]{1,0:T(8,128)S(1)}, u32[]{:S(2)}, u32[]{:S(2)}) collective-permute-start(f32[32,128]{1,0:T(8,128)S(1)} %pad_maximum_fusion.1.refs_0_), channel_id=1, source_target_pairs={{6,0},{7,1},{4,2},{5,3},{2,4},{3,5},{0,6},{1,7},{14,8},{15,9},{12,... | collective-permute-start | bytes 49160 | tf_op jit(solution)/shard_map/ppermute | solution.py:735
  25.8 4.7 %collective-permute-start.11 = (f32[32,128]{1,0:T(8,128)S(1)}, f32[32,128]{1,0:T(8,128)S(1)}, u32[]{:S(2)}, u32[]{:S(2)}) collective-permute-start(f32[32,128]{1,0:T(8,128)S(1)} %pad_maximum_fusion.1.refs_0_), channel_id=1, source_target_pairs={{4,0},{5,1},{6,2},{7,3},{0,4},{1,5},{2,6},{3,7},{12,8},{13,9},{14,... | collective-permute-start | bytes 49160 | tf_op jit(solution)/shard_map/ppermute | solution.py:735
  32.8 1.4 %collective-permute-start.12 = (f32[8,256]{1,0:T(8,128)S(1)}, f32[8,256]{1,0:T(8,128)S(1)}, u32[]{:S(2)}, u32[]{:S(2)}) collective-permute-start(f32[8,256]{1,0:T(8,128)S(1)} %get-tuple-element.49.stack), channel_id=1, source_target_pairs={{8,0},{0,8},{24,16},{16,24},{9,1},{1,9},{25,17},{17,25},{10,2},{2,... | collective-permute-start | bytes 24584 | tf_op jit(solution)/shard_map/ppermute | solution.py:698
  32.9 3.1 %collective-permute-start.13 = (f32[8,256]{1,0:T(8,128)S(1)}, f32[8,256]{1,0:T(8,128)S(1)}, u32[]{:S(2)}, u32[]{:S(2)}) collective-permute-start(f32[8,256]{1,0:T(8,128)S(1)} %get-tuple-element.49.stack), channel_id=1, source_target_pairs={{24,0},{16,8},{8,16},{0,24},{25,1},{17,9},{9,17},{1,25},{26,2},{18... | collective-permute-start | bytes 24584 | tf_op jit(solution)/shard_map/ppermute | solution.py:698
  36.4 6.2 %collective-permute-start.14 = (f32[48,128]{1,0:T(8,128)S(1)}, f32[48,128]{1,0:T(8,128)S(1)}, u32[]{:S(2)}, u32[]{:S(2)}) collective-permute-start(f32[48,128]{1,0:T(8,128)S(1)} %get-tuple-element.52), channel_id=1, source_target_pairs={{8,0},{0,8},{24,16},{16,24},{9,1},{1,9},{25,17},{17,25},{10,2},{2,... | collective-permute-start | bytes 73736 | tf_op jit(solution)/shard_map/ppermute | solution.py:698
  36.9 5.8 %collective-permute-start.15 = (f32[48,128]{1,0:T(8,128)S(1)}, f32[48,128]{1,0:T(8,128)S(1)}, u32[]{:S(2)}, u32[]{:S(2)}) collective-permute-start(f32[48,128]{1,0:T(8,128)S(1)} %get-tuple-element.53), channel_id=1, source_target_pairs={{24,0},{16,8},{8,16},{0,24},{25,1},{17,9},{9,17},{1,25},{26,2},{18... | collective-permute-start | bytes 73736 | tf_op jit(solution)/shard_map/ppermute | solution.py:698
  37.1 5.6 %collective-permute-start.16 = (f32[48,128]{1,0:T(8,128)S(1)}, f32[48,128]{1,0:T(8,128)S(1)}, u32[]{:S(2)}, u32[]{:S(2)}) collective-permute-start(f32[48,128]{1,0:T(8,128)S(1)} %get-tuple-element.54), channel_id=1, source_target_pairs={{2,0},{0,2},{6,4},{4,6},{3,1},{1,3},{7,5},{5,7},{10,8},{8,10},{14,... | collective-permute-start | bytes 73736 | tf_op jit(solution)/shard_map/ppermute | solution.py:698
  38.0 4.6 %collective-permute-start.17 = (f32[48,128]{1,0:T(8,128)S(1)}, f32[48,128]{1,0:T(8,128)S(1)}, u32[]{:S(2)}, u32[]{:S(2)}) collective-permute-start(f32[48,128]{1,0:T(8,128)S(1)} %get-tuple-element.55), channel_id=1, source_target_pairs={{1,0},{0,1},{4,2},{5,3},{2,4},{3,5},{7,6},{6,7},{9,8},{8,9},{12,10... | collective-permute-start | bytes 73736 | tf_op jit(solution)/shard_map/ppermute | solution.py:709
  39.0 3.6 %collective-permute-start.18 = (f32[8,128]{1,0:T(8,128)S(1)}, f32[8,128]{1,0:T(8,128)S(1)}, u32[]{:S(2)}, u32[]{:S(2)}) collective-permute-start(f32[8,128]{1,0:T(8,128)S(1)} %get-tuple-element.56), channel_id=1, source_target_pairs={{1,0},{0,1},{3,2},{2,3},{5,4},{4,5},{7,6},{6,7},{9,8},{8,9},{11,10... | collective-permute-start | bytes 12296 | tf_op jit(solution)/shard_map/ppermute | solution.py:698
